TPU v7x, 128 devices: a whole 4x4x4 slice. The times are simulated.
128 devices in a mesh: row: 16 (over y_lo, z, core), col: 8 (over x, y_hi).
Axes of the slice: x: 4, y: 4 (y_hi: 2, y_lo: 2; y = y_hi * 2 + y_lo), z: 4, core: 2. Of those that a mesh axis runs over, the one named last changes fastest.
Arguments:
- mode_basis: bfloat16 [16384, 4096], P('row'), may hold values from -0.0625 to 0.0625
- node_coords: float32 [3, 16384], P(None, 'row'), may hold values from -1 to 1
- quad_weights: float32 [16384], P('row'), may hold values from 0.3 to 3
- magnetization: bfloat16 [2, 4096, 128], P(None, 'col', 'row'), may hold values from -6 to 6
- decay_rates: float32 [4096], replicated, may hold values from 0.02 to 1.5
- directions: float32 [6, 3, 128], replicated, may hold values from -3 to 3
Outputs:
- final_magnet: bfloat16 [2, 4096, 128], P(None, 'col', 'row')
All inputs are finite; a program needn't handle non-finite values.
Results may differ from a plain program's by a relative error of at most 0.03.
Values may be sent and summed in bfloat16 or wider, within the bound.
No kernel may reach another device: no remote copies, remote signals or barrier semaphores. Data moves between devices by JAX's collectives and lax.ppermute only.
A program may use at most 64 MiB of HBM per device.

v0:
```python
import jax
import jax.numpy as jnp
from jax import lax
from jax.sharding import PartitionSpec as P

STEPS = 3


def on_device(mode_basis, node_coords, quad_weights, magnetization, decay_rates, directions):
    row_count = lax.axis_size("row")
    col_count = lax.axis_size("col")
    row_index = lax.axis_index("row")
    col_index = lax.axis_index("col")
    mode_count = mode_basis.shape[1]
    node_local = mode_basis.shape[0]
    col_width = mode_count // col_count
    row_width = mode_count // row_count
    moments = node_coords * quad_weights[None, :]
    col_block = lax.dynamic_slice_in_dim(mode_basis, col_index * col_width, col_width, 1)
    right_block = (
        col_block.astype(jnp.float32)[:, None, :] * jnp.transpose(moments)[:, :, None]
    ).astype(jnp.bfloat16)
    right_block = right_block.reshape(node_local, 3 * col_width)
    moment_tiles = lax.psum_scatter(
        lax.dot_general(
            mode_basis, right_block, (((0,), (0,)), ((), ())), preferred_element_type=jnp.float32
        ).astype(jnp.bfloat16),
        "row",
        scatter_dimension=0,
        tiled=True,
    )
    rates_rows = lax.dynamic_slice_in_dim(decay_rates, row_index * row_width, row_width, 0)
    offset = jnp.clip(row_index * row_width - col_index * col_width, 0, col_width - row_width)
    on_diagonal = row_index * row_width // col_width == col_index
    field_now = magnetization
    moment_tiles = moment_tiles.reshape(row_width, 3, col_width)
    for step_index in range(STEPS):
        forward_gathered = lax.all_gather(field_now, "row", axis=2, tiled=True)
        forward_products = jnp.einsum(
            "ikj,xjg->kxig", moment_tiles, forward_gathered, preferred_element_type=jnp.float32
        )
        forward_combined = jnp.einsum("kg,kxig->xig", directions[2 * step_index], forward_products)
        diag_part = lax.dynamic_slice_in_dim(forward_gathered, offset, row_width, 1).astype(
            jnp.float32
        )
        diag_part = diag_part * (1.0 - 0.5 * rates_rows)[None, :, None]
        diag_part = jnp.where(on_diagonal, diag_part, 0.0)
        forward_partial_terms = jnp.stack(
            [0.5 * forward_combined[1] + diag_part[0], -0.5 * forward_combined[0] + diag_part[1]]
        )
        half_field = lax.psum_scatter(
            forward_partial_terms.astype(jnp.bfloat16), "col", scatter_dimension=2, tiled=True
        )
        gathered = lax.all_gather(half_field, "col", axis=2, tiled=True)
        products = jnp.einsum(
            "ikj,xig->kxjg", moment_tiles, gathered, preferred_element_type=jnp.float32
        )
        combined = jnp.einsum("kg,kxjg->xjg", directions[2 * step_index + 1], products)
        diag_rows = gathered.astype(jnp.float32) * (0.0 - 1.0 * rates_rows)[None, :, None]
        placed = lax.dynamic_update_slice_in_dim(
            jnp.zeros(combined.shape, jnp.float32), diag_rows, offset, 1
        )
        placed = jnp.where(on_diagonal, placed, 0.0)
        partial_terms = jnp.stack([1.0 * combined[1] + placed[0], -1.0 * combined[0] + placed[1]])
        update = lax.psum_scatter(
            partial_terms.astype(jnp.bfloat16), "row", scatter_dimension=2, tiled=True
        ).astype(jnp.float32)
        field_now = (field_now.astype(jnp.float32) + update).astype(jnp.bfloat16)
    return field_now


def solution(mesh):
    return jax.shard_map(
        on_device,
        mesh=mesh,
        in_specs=(P("row", None), P(None, "row"), P("row"), P(None, "col", "row"), P(), P()),
        out_specs=P(None, "col", "row"),
        check_vma=False,
    )
```

profile of v0, /device:TPU:1, one launch (start us, length us, event | category | flops | bytes accessed | tf_op | source)
XLA Modules:
  0.0 665.9 jit_solution(4116416778563416400)
XLA Ops:
  6.5 2.9 dynamic-slice_convert_fusion
  9.4 1.9 copy.9
  11.4 0.8 multiply_convert_fusion
  12.2 18.8 %fusion = bf16[4096,1536]{0,1:T(8,128)(2,1)} fusion(bf16[1024,1536]{0,1:T(8,128)(2,1)S(1)} %bitcast.145, bf16[1024,4096]{1,0:T(8,128)(2,1)} %param.6), kind=kOutput, calls=%fused_computation.1 | convolution fusion | flops 12891193344 | bytes 24117248 | tf_op jit(solution)/shard_map/dot_general | solution.py:25
  31.1 0.8 dynamic-slice_subtract_fusion
  31.8 23.4 %all_gather.18 = bf16[2,512,128]{1,2,0:T(8,128)(2,1)S(1)} all-gather(bf16[2,512,8]{1,2,0:T(8,128)(2,1)S(1)} %copy-done.1), channel_id=1, replica_groups=mesh['row'=16,'col'=8] {'row'}, dimensions={2}, use_global_device_ids=true | all-gather | bytes 278528 | tf_op jit(solution)/shard_map/all_gather | solution.py:38
  55.4 58.9 %reduce-scatter.14.cloned.1.call-done = bf16[256,1536]{0,1:T(8,128)(2,1)} async-done(((bf16[4096,1536]{0,1:T(8,128)(2,1)}), bf16[256,1536]{0,1:T(8,128)(2,1)}) %reduce-scatter.14.cloned.1.call-update) | async-done | bytes 786448 | tf_op jit(solution)/shard_map/reduce_scatter | solution.py:24
  114.3 1.6 fusion.8
  116.9 71.1 %reduce-scatter.16.cloned.1.call-done = bf16[2,256,16]{1,2,0:T(8,128)(2,1)} async-done(((bf16[2,256,128]{1,2,0:T(8,128)(2,1)}), bf16[2,256,16]{1,2,0:T(8,128)(2,1)}) %reduce-scatter.16.cloned.1.call-update) | async-done | bytes 16400 | tf_op jit(solution)/shard_map/reduce_scatter | solution.py:51
  188.0 28.0 %all_gather.19 = bf16[2,256,128]{1,2,0:T(8,128)(2,1)S(1)} all-gather(bf16[2,256,16]{1,2,0:T(8,128)(2,1)} %reduce-scatter.16.cloned.1.call-done), channel_id=1, replica_groups=mesh['row'=16,'col'=8] {'col'}, dimensions={2}, use_global_device_ids=true | all-gather | bytes 147456 | tf_op jit(solution)/shard_map/all_gather | solution.py:54
  216.1 1.5 convolution_bitcast_fusion.2
  217.6 0.8 fusion.5
  218.6 0.7 select_n.59
  219.7 0.7 copy.63
  220.7 64.1 %reduce-scatter.22.cloned.1.call-done = bf16[8,1024]{1,0:T(8,128)(2,1)} async-done(((bf16[128,1024]{1,0:T(8,128)(2,1)}), bf16[8,1024]{1,0:T(8,128)(2,1)}) %reduce-scatter.22.cloned.1.call-update) | async-done | bytes 16400
  284.8 0.7 reshape.39
  285.5 21.0 %all_gather.20 = bf16[2,512,128]{1,2,0:T(8,128)(2,1)S(1)} all-gather(bf16[2,512,8]{1,2,0:T(8,128)(2,1)S(1)} %add_convert_fusion.2), channel_id=1, replica_groups=mesh['row'=16,'col'=8] {'row'}, dimensions={2}, use_global_device_ids=true | all-gather | bytes 278528 | tf_op jit(solution)/shard_map/all_gather | solution.py:38
  308.4 67.0 %reduce-scatter.18.cloned.1.call-done = bf16[2,256,16]{1,2,0:T(8,128)(2,1)} async-done(((bf16[2,256,128]{1,2,0:T(8,128)(2,1)}), bf16[2,256,16]{1,2,0:T(8,128)(2,1)}) %reduce-scatter.18.cloned.1.call-update) | async-done | bytes 16400 | tf_op jit(solution)/shard_map/reduce_scatter | solution.py:51
  375.5 28.0 %all_gather.21 = bf16[2,256,128]{1,2,0:T(8,128)(2,1)S(1)} all-gather(bf16[2,256,16]{1,2,0:T(8,128)(2,1)} %reduce-scatter.18.cloned.1.call-done), channel_id=1, replica_groups=mesh['row'=16,'col'=8] {'col'}, dimensions={2}, use_global_device_ids=true | all-gather | bytes 147456 | tf_op jit(solution)/shard_map/all_gather | solution.py:54
  403.9 0.8 fusion.3
  404.9 0.7 select_n.62
  406.0 0.7 copy.64
  407.0 64.1 %reduce-scatter.24.cloned.1.call-done = bf16[8,1024]{1,0:T(8,128)(2,1)} async-done(((bf16[128,1024]{1,0:T(8,128)(2,1)}), bf16[8,1024]{1,0:T(8,128)(2,1)}) %reduce-scatter.24.cloned.1.call-update) | async-done | bytes 16400
  471.1 0.7 reshape.41
  471.8 21.1 %all_gather.22 = bf16[2,512,128]{1,2,0:T(8,128)(2,1)S(1)} all-gather(bf16[2,512,8]{1,2,0:T(8,128)(2,1)S(1)} %add_convert_fusion.1), channel_id=1, replica_groups=mesh['row'=16,'col'=8] {'row'}, dimensions={2}, use_global_device_ids=true | all-gather | bytes 278528 | tf_op jit(solution)/shard_map/all_gather | solution.py:38
  494.8 67.2 %reduce-scatter.20.cloned.1.call-done = bf16[2,256,16]{1,2,0:T(8,128)(2,1)} async-done(((bf16[2,256,128]{1,2,0:T(8,128)(2,1)}), bf16[2,256,16]{1,2,0:T(8,128)(2,1)}) %reduce-scatter.20.cloned.1.call-update) | async-done | bytes 16400 | tf_op jit(solution)/shard_map/reduce_scatter | solution.py:51
  562.1 28.0 %all_gather.23 = bf16[2,256,128]{1,2,0:T(8,128)(2,1)S(1)} all-gather(bf16[2,256,16]{1,2,0:T(8,128)(2,1)} %reduce-scatter.20.cloned.1.call-done), channel_id=1, replica_groups=mesh['row'=16,'col'=8] {'col'}, dimensions={2}, use_global_device_ids=true | all-gather | bytes 147456 | tf_op jit(solution)/shard_map/all_gather | solution.py:54
  590.5 0.8 fusion.1
  591.5 0.7 select_n.65
  592.6 0.7 copy.65
  593.4 64.3 %reduce-scatter.26.cloned.1.call-done = bf16[8,1024]{1,0:T(8,128)(2,1)} async-done(((bf16[128,1024]{1,0:T(8,128)(2,1)}), bf16[8,1024]{1,0:T(8,128)(2,1)}) %reduce-scatter.26.cloned.1.call-update) | async-done | bytes 16400
  657.7 0.7 reshape.43
  (71 shorter events, 8.5 us)
Async XLA Ops:
  6.5 4.8 copy-start.2
  6.5 4.8 copy-start.4
  6.5 107.7 %reduce-scatter.14.cloned.1.call-start = ((), (), s32[]{:S(2)}) async-start(), calls=%async_computation.7 | async-start | bytes 13369344 | tf_op jit(solution)/shard_map/reduce_scatter | solution.py:24
  31.0 0.9 copy-start.1
  31.0 24.3 %copy-start.3 = (f32[6,3,128]{2,1,0:T(4,128)S(1)}, f32[6,3,128]{2,1,0:T(4,128)}, u32[]{:S(2)}) copy-start(f32[6,3,128]{2,1,0:T(4,128)} %param.11) | copy-start | bytes 27652
  31.0 157.0 %reduce-scatter.16.cloned.1.call-start = ((), (), s32[]{:S(2)}) async-start(), calls=%async_computation.8 | async-start | bytes 147456 | tf_op jit(solution)/shard_map/reduce_scatter | solution.py:51
  115.9 190.6 %copy-start = (bf16[256,1536]{0,1:T(8,128)(2,1)S(1)}, bf16[256,1536]{0,1:T(8,128)(2,1)}, u32[]{:S(2)}) copy-start(bf16[256,1536]{0,1:T(8,128)(2,1)} %reduce-scatter.14.cloned.1.call-done) | copy-start | bytes 2359300
  116.7 168.1 %reduce-scatter.22.cloned.1.call-start = ((), (), s32[]{:S(2)}) async-start(), calls=%async_computation.11 | async-start | bytes 278528
  220.5 155.0 %reduce-scatter.18.cloned.1.call-start = ((), (), s32[]{:S(2)}) async-start(), calls=%async_computation.9 | async-start | bytes 147456 | tf_op jit(solution)/shard_map/reduce_scatter | solution.py:51
  308.2 162.9 %reduce-scatter.24.cloned.1.call-start = ((), (), s32[]{:S(2)}) async-start(), calls=%async_computation.12 | async-start | bytes 278528
  406.8 155.3 %reduce-scatter.20.cloned.1.call-start = ((), (), s32[]{:S(2)}) async-start(), calls=%async_computation.10 | async-start | bytes 147456 | tf_op jit(solution)/shard_map/reduce_scatter | solution.py:51
  494.7 163.1 %reduce-scatter.26.cloned.1.call-start = ((), (), s32[]{:S(2)}) async-start(), calls=%async_computation.13 | async-start | bytes 278528
Sparse Core Ops, SparseCore 0:
  31.1 83.1 reduce-scatter.13
  117.8 70.1 reduce-scatter.15
  220.6 64.1 reduce-scatter.21
  308.3 67.0 reduce-scatter.17
  406.9 64.1 reduce-scatter.23
  494.8 67.2 reduce-scatter.19
  593.5 64.1 reduce-scatter.25
where the time goes:
time: 669 us; the launch traced here: 666 us
  waiting for transfers between devices  457 us (68%)
  blocking collectives  150 us (22%)
  matrix products  26.8 us (4%)
  between operations  13.9 us (2%)
  local copies, waits for them, and re-layouts  10.6 us (2%)
  other arithmetic  7.97 us (1%)
    reduce_scatter x3, waiting for transfers between devices, on_device(): lax.psum_scatter(forward_partial_terms.astype(jnp.bfloat16), 'col', scatt...  205 us
    unnamed x10, waiting for transfers between devices  193 us
    all_gather x3, blocking collectives, on_device(): gathered = lax.all_gather(half_field, 'col', axis=2, tiled=True)  84.1 us
    all_gather x3, blocking collectives, on_device(): forward_gathered = lax.all_gather(field_now, 'row', axis=2, tiled=True)  65.5 us
    reduce_scatter x1, waiting for transfers between devices, on_device(): lax.psum_scatter(lax.dot_general(mode_basis, right_block, (((0,), (0,)),...  58.9 us
    dot_general x1, matrix products, on_device(): lax.dot_general(mode_basis, right_block, (((0,), (0,)), ((), ())), prefer...  18.8 us
  transfers between devices with their start and end apart: 7, of which 7 were waited for; matrix products, arithmetic and copies ran while one was open for 0% of the time, Pallas kernels for 0%

commit v1 on v0

v1 whole, which is shorter than its diff:
```python
import jax
import jax.numpy as jnp
from jax import lax
from jax.sharding import PartitionSpec as P

STEPS = 3


def on_device(mode_basis, node_coords, quad_weights, magnetization, decay_rates, directions):
    row_count = lax.axis_size("row")
    col_count = lax.axis_size("col")
    row_index = lax.axis_index("row")
    col_index = lax.axis_index("col")
    mode_count = mode_basis.shape[1]
    node_local = mode_basis.shape[0]
    parts, col_width, own_waves = magnetization.shape
    lanes = mode_count // row_count
    columns = 2 * row_count
    f32, bf16 = jnp.float32, jnp.bfloat16

    mine = lax.dynamic_index_in_dim(
        directions.reshape(2 * STEPS, 3, row_count, own_waves), col_index, 3, keepdims=False
    )
    moments = node_coords * quad_weights[None, :]
    weights = jnp.sum(mine[:, :, :, None] * moments[None, :, None, :], axis=1)
    weights = jnp.concatenate([weights, weights], axis=1)

    def gather_rows(block):
        return lax.all_to_all(
            jnp.broadcast_to(block[None], (row_count,) + block.shape), "row", 0, 0
        )

    sent = jnp.transpose(magnetization, (2, 0, 1))
    own = lax.all_to_all(sent, "col", 0, 0)
    every = gather_rows(own)
    field_all = jnp.transpose(every, (2, 0, 1, 3)).reshape(columns, mode_count)

    def partial_sums(state, step):
        projected = lax.dot_general(
            state, mode_basis, (((1,), (1,)), ((), ())), preferred_element_type=f32
        )
        scaled = (projected * weights[step]).astype(bf16)
        return lax.dot_general(
            scaled, mode_basis, (((1,), (0,)), ((), ())), preferred_element_type=f32
        ).astype(bf16)

    def to_blocks(array):
        return jnp.transpose(array.reshape(columns, row_count, lanes), (1, 0, 2))

    def from_blocks(array):
        return jnp.transpose(array, (1, 0, 2)).reshape(columns, mode_count)

    def mixed(sums, factor):
        half = sums.shape[0] // 2
        return jnp.concatenate([factor * sums[half:], -factor * sums[:half]], axis=0)

    rates = lax.dynamic_slice_in_dim(decay_rates, row_index * lanes, lanes, 0)[None, :]
    field = lax.dynamic_slice_in_dim(field_all, row_index * lanes, lanes, 1)
    for step in range(STEPS):
        sums = lax.all_to_all(to_blocks(partial_sums(field_all, 2 * step)), "row", 0, 0)
        sums = jnp.sum(sums.astype(f32), axis=0)
        half = (mixed(sums, 0.5) + (1.0 - 0.5 * rates) * field.astype(f32)).astype(bf16)
        half_all = from_blocks(gather_rows(half))
        partial = partial_sums(half_all, 2 * step + 1)
        if step + 1 < STEPS:
            sums = lax.all_to_all(to_blocks(partial), "row", 0, 0)
            sums = jnp.sum(sums.astype(f32), axis=0)
            update = mixed(sums, 1.0) + (0.0 - 1.0 * rates) * half.astype(f32)
            field = (field.astype(f32) + update).astype(bf16)
            field_all = from_blocks(gather_rows(field))
        else:
            by_wave = jnp.transpose(partial.reshape(2, row_count, mode_count), (1, 0, 2))
            sums = lax.all_to_all(by_wave, "row", 0, 0)
            sums = jnp.sum(sums.astype(f32), axis=0)
            pick = lambda a: lax.dynamic_index_in_dim(
                a.reshape(2, row_count, mode_count), row_index, 1, keepdims=False
            ).astype(f32)
            update = mixed(sums, 1.0) + (0.0 - 1.0 * decay_rates[None, :]) * pick(half_all)
            own = (pick(field_all) + update).astype(bf16)
    sent = jnp.transpose(own.reshape(2, col_count, col_width), (1, 0, 2))
    return jnp.transpose(lax.all_to_all(sent, "col", 0, 0), (1, 2, 0))


def solution(mesh):
    return jax.shard_map(
        on_device,
        mesh=mesh,
        in_specs=(P("row", None), P(None, "row"), P("row"), P(None, "col", "row"), P(), P()),
        out_specs=P(None, "col", "row"),
        check_vma=False,
    )
```

time: 669 us -> 223 us (0.33)
  waiting for transfers between devices: 457 us -> 25.3 us
  blocking collectives: 150 us -> 105 us
  matrix products: 26.8 us -> 58.8 us
  starting transfers between devices: 0.25 us -> 23.6 us
  between operations: 13.9 us -> 0.35 us
    reduce_scatter x4 -> x0, waiting for transfers between devices: 264 us -> none  [the longest x3 205 us: on_device(): lax.psum_scatter(forward_partial_terms.astype(jnp.bfloat16), 'col', scatt...]
    unnamed x10 -> x0, waiting for transfers between devices: 193 us -> none
    all_gather x6 -> x0, blocking collectives: 150 us -> none  [the longest x3 84.1 us: on_device(): gathered = lax.all_gather(half_field, 'col', axis=2, tiled=True)]
    all_to_all x0 -> x10, blocking collectives: none -> 105 us  [the longest x5 53.2 us: gather_rows(): lax.all_to_all(jnp.broadcast_to(block[None], (row_count,) + block.shape),...]
    dot_general x12 -> x6, matrix products: 26.8 us -> 58.8 us  [partial_sums(): lax.dot_general(scaled, mode_basis, (((1,), (0,)), ((), ())), preferred_e...]
    all_to_all x0 -> x4, waiting for transfers between devices: none -> 25.3 us  [the longest x1 7.16 us: on_device(): lax.all_to_all(to_blocks(partial_sums(field_all, 2 * step)), 'row', 0, 0)]
    all_to_all x0 -> x4, starting transfers between devices: none -> 23.6 us  [the longest x1 7.54 us: gather_rows(): lax.all_to_all(jnp.broadcast_to(block[None], (row_count,) + block.shape),...]
  transfers between devices with their start and end apart: 7 -> 4, of which waited for: 7 -> 4; matrix products, arithmetic and copies ran while one was open for 0% -> 1% of each run, Pallas kernels for 0% -> 0%
where the time goes in v1:
time: 223 us; the launch traced here: 221 us
  blocking collectives  105 us (47%)
  matrix products  58.8 us (26%)
  waiting for transfers between devices  25.3 us (11%)
  starting transfers between devices  23.6 us (11%)
  local copies, waits for them, and re-layouts  6.46 us (3%)
    dot_general x6, matrix products, partial_sums(): lax.dot_general(scaled, mode_basis, (((1,), (0,)), ((), ())), preferred_e...  58.8 us
    all_to_all x5, blocking collectives, gather_rows(): lax.all_to_all(jnp.broadcast_to(block[None], (row_count,) + block.shape),...  53.2 us
    all_to_all x2, blocking collectives, on_device(): sums = lax.all_to_all(to_blocks(partial), 'row', 0, 0)  21.3 us
    all_to_all x2, blocking collectives, on_device(): lax.all_to_all(to_blocks(partial_sums(field_all, 2 * step)), 'row', 0, 0)  21.3 us
    all_to_all x1, blocking collectives, on_device(): return jnp.transpose(lax.all_to_all(sent, 'col', 0, 0), (1, 2, 0))  9.18 us
    all_to_all x1, starting transfers between devices, gather_rows(): lax.all_to_all(jnp.broadcast_to(block[None], (row_count,) + block.shape),...  7.54 us
    all_to_all x1, starting transfers between devices, on_device(): own = lax.all_to_all(sent, 'col', 0, 0)  7.48 us
    all_to_all x1, waiting for transfers between devices, on_device(): lax.all_to_all(to_blocks(partial_sums(field_all, 2 * step)), 'row', 0, 0)  7.16 us
  transfers between devices with their start and end apart: 4, of which 4 were waited for; matrix products, arithmetic and copies ran while one was open for 1% of the time, Pallas kernels for 0%

profile of v1, /device:TPU:1, one launch (start us, length us, event | category | flops | bytes accessed | tf_op | source)
XLA Modules:
  0.0 221.3 jit_solution(8632769204971638214)
XLA Ops:
  0.0 1.3 copy.105
  1.3 7.5 %all-to-all-start = ((bf16[8,2,512]{2,1,0:T(2,128)(2,1)}), bf16[8,2,512]{2,1,0:T(2,128)(2,1)S(1)}, u32[]{:S(2)}, u32[]{:S(2)}) async-start(bf16[8,2,512]{2,1,0:T(2,128)(2,1)} %bitcast.130), calls=%async_computation | async-start | bytes 32768 | tf_op jit(solution)/shard_map/all_to_all | solution.py:34
  8.8 0.7 copy.55
  10.0 5.4 %all-to-all-done = bf16[8,2,512]{2,1,0:T(2,128)(2,1)S(1)} async-done(((bf16[8,2,512]{2,1,0:T(2,128)(2,1)}), bf16[8,2,512]{2,1,0:T(2,128)(2,1)S(1)}, u32[]{:S(2)}, u32[]{:S(2)}) %all-to-all-start) | async-done | bytes 16416 | tf_op jit(solution)/shard_map/all_to_all | solution.py:34
  15.4 0.7 broadcast_in_dim.12
  16.1 7.5 %all-to-all-start.1 = ((bf16[16,8,2,512]{3,1,2,0:T(8,128)(2,1)}), bf16[16,8,2,512]{3,1,2,0:T(8,128)(2,1)S(1)}, u32[]{:S(2)}, u32[]{:S(2)}) async-start(bf16[16,8,2,512]{3,1,2,0:T(8,128)(2,1)} %broadcast_in_dim.12), calls=%async_computation.1 | async-start | bytes 524288 | tf_op jit(solution)/shard_map/all_to_all | solution.py:29
  23.6 0.7 broadcast_multiply_fusion
  24.5 6.3 %all-to-all-done.1 = bf16[16,8,2,512]{3,1,2,0:T(8,128)(2,1)S(1)} async-done(((bf16[16,8,2,512]{3,1,2,0:T(8,128)(2,1)}), bf16[16,8,2,512]{3,1,2,0:T(8,128)(2,1)S(1)}, u32[]{:S(2)}, u32[]{:S(2)}) %all-to-all-start.1) | async-done | bytes 262176 | tf_op jit(solution)/shard_map/all_to_all | solution.py:29
  30.9 9.8 %convolution_convert_fusion.5 = bf16[32,4096]{1,0:T(8,128)(2,1)S(1)} fusion(bf16[1024,4096]{1,0:T(8,128)(2,1)} %param.6, bf16[32,4096]{1,0:T(8,128)(2,1)S(1)} %bitcast.135, f32[6,16,1024]{2,1,0:T(8,128)S(1)} %multiply_reduce_fusion), kind=kOutput, calls=%fused_computation.5 | convolution fusion | flops 537100288 | bytes 17694720 | tf_op jit(solution)/shard_map/dot_general | solution.py:43
  40.7 0.7 copy.103
  41.5 4.3 %all-to-all-start.2 = ((bf16[16,32,256]{2,1,0:T(8,128)(2,1)}), bf16[16,32,256]{2,1,0:T(8,128)(2,1)S(1)}, u32[]{:S(2)}, u32[]{:S(2)}) async-start(bf16[16,32,256]{2,1,0:T(8,128)(2,1)} %bitcast.128), calls=%async_computation.2 | async-start | bytes 524288 | tf_op jit(solution)/shard_map/all_to_all | solution.py:60
  45.8 7.2 %all-to-all-done.2 = bf16[16,32,256]{2,1,0:T(8,128)(2,1)S(1)} async-done(((bf16[16,32,256]{2,1,0:T(8,128)(2,1)}), bf16[16,32,256]{2,1,0:T(8,128)(2,1)S(1)}, u32[]{:S(2)}, u32[]{:S(2)}) %all-to-all-start.2) | async-done | bytes 262176 | tf_op jit(solution)/shard_map/all_to_all | solution.py:60
  53.1 10.6 %all_to_all.70 = bf16[16,32,256]{2,1,0:T(8,128)(2,1)S(1)} all-to-all(bf16[16,32,256]{2,1,0:T(8,128)(2,1)S(1)} %broadcast_in_dim.13), channel_id=1, replica_groups=mesh['row'=16,'col'=8] {'row'}, dimensions={0} | all-to-all | bytes 524288 | tf_op jit(solution)/shard_map/all_to_all | solution.py:29
  63.8 9.8 %convolution_convert_fusion.4 = bf16[32,4096]{1,0:T(8,128)(2,1)S(1)} fusion(bf16[1024,4096]{1,0:T(8,128)(2,1)} %param.6, bf16[32,4096]{1,0:T(8,128)(2,1)S(1)} %bitcast.139, f32[6,16,1024]{2,1,0:T(8,128)S(1)} %multiply_reduce_fusion), kind=kOutput, calls=%fused_computation.4 | convolution fusion | flops 537100288 | bytes 17694720 | tf_op jit(solution)/shard_map/dot_general | solution.py:43
  73.6 10.6 %all_to_all.71 = bf16[16,32,256]{2,1,0:T(8,128)(2,1)S(1)} all-to-all(bf16[16,32,256]{2,1,0:T(8,128)(2,1)S(1)} %bitcast.152), channel_id=1, replica_groups=mesh['row'=16,'col'=8] {'row'}, dimensions={0} | all-to-all | bytes 524288 | tf_op jit(solution)/shard_map/all_to_all | solution.py:66
  84.4 10.6 %all_to_all.72 = bf16[16,32,256]{2,1,0:T(8,128)(2,1)S(1)} all-to-all(bf16[16,32,256]{2,1,0:T(8,128)(2,1)S(1)} %broadcast_in_dim.14), channel_id=1, replica_groups=mesh['row'=16,'col'=8] {'row'}, dimensions={0} | all-to-all | bytes 524288 | tf_op jit(solution)/shard_map/all_to_all | solution.py:29
  95.1 9.8 %convolution_convert_fusion.3 = bf16[32,4096]{1,0:T(8,128)(2,1)S(1)} fusion(bf16[1024,4096]{1,0:T(8,128)(2,1)} %param.6, bf16[32,4096]{1,0:T(8,128)(2,1)S(1)} %bitcast.141, f32[6,16,1024]{2,1,0:T(8,128)S(1)} %multiply_reduce_fusion), kind=kOutput, calls=%fused_computation.3 | convolution fusion | flops 537100288 | bytes 17694720 | tf_op jit(solution)/shard_map/dot_general | solution.py:43
  104.9 10.6 %all_to_all.73 = bf16[16,32,256]{2,1,0:T(8,128)(2,1)S(1)} all-to-all(bf16[16,32,256]{2,1,0:T(8,128)(2,1)S(1)} %bitcast.154), channel_id=1, replica_groups=mesh['row'=16,'col'=8] {'row'}, dimensions={0} | all-to-all | bytes 524288 | tf_op jit(solution)/shard_map/all_to_all | solution.py:60
  115.6 10.6 %all_to_all.74 = bf16[16,32,256]{2,1,0:T(8,128)(2,1)S(1)} all-to-all(bf16[16,32,256]{2,1,0:T(8,128)(2,1)S(1)} %broadcast_in_dim.15), channel_id=1, replica_groups=mesh['row'=16,'col'=8] {'row'}, dimensions={0} | all-to-all | bytes 524288 | tf_op jit(solution)/shard_map/all_to_all | solution.py:29
  126.3 9.8 %convolution_convert_fusion.2 = bf16[32,4096]{1,0:T(8,128)(2,1)S(1)} fusion(bf16[1024,4096]{1,0:T(8,128)(2,1)} %param.6, bf16[32,4096]{1,0:T(8,128)(2,1)S(1)} %bitcast.143, f32[6,16,1024]{2,1,0:T(8,128)S(1)} %multiply_reduce_fusion), kind=kOutput, calls=%fused_computation.2 | convolution fusion | flops 537100288 | bytes 17694720 | tf_op jit(solution)/shard_map/dot_general | solution.py:43
  136.1 10.6 %all_to_all.75 = bf16[16,32,256]{2,1,0:T(8,128)(2,1)S(1)} all-to-all(bf16[16,32,256]{2,1,0:T(8,128)(2,1)S(1)} %bitcast.156), channel_id=1, replica_groups=mesh['row'=16,'col'=8] {'row'}, dimensions={0} | all-to-all | bytes 524288 | tf_op jit(solution)/shard_map/all_to_all | solution.py:66
  146.9 10.6 %all_to_all.76 = bf16[16,32,256]{2,1,0:T(8,128)(2,1)S(1)} all-to-all(bf16[16,32,256]{2,1,0:T(8,128)(2,1)S(1)} %broadcast_in_dim.16), channel_id=1, replica_groups=mesh['row'=16,'col'=8] {'row'}, dimensions={0} | all-to-all | bytes 524288 | tf_op jit(solution)/shard_map/all_to_all | solution.py:29
  157.6 9.8 %convolution_convert_fusion.1 = bf16[32,4096]{1,0:T(8,128)(2,1)S(1)} fusion(bf16[1024,4096]{1,0:T(8,128)(2,1)} %param.6, bf16[32,4096]{1,0:T(8,128)(2,1)S(1)} %bitcast.148, f32[6,16,1024]{2,1,0:T(8,128)S(1)} %multiply_reduce_fusion), kind=kOutput, calls=%fused_computation.1 | convolution fusion | flops 537100288 | bytes 17694720 | tf_op jit(solution)/shard_map/dot_general | solution.py:43
  167.4 10.6 %all_to_all.77 = bf16[16,32,256]{2,1,0:T(8,128)(2,1)S(1)} all-to-all(bf16[16,32,256]{2,1,0:T(8,128)(2,1)S(1)} %bitcast.157), channel_id=1, replica_groups=mesh['row'=16,'col'=8] {'row'}, dimensions={0} | all-to-all | bytes 524288 | tf_op jit(solution)/shard_map/all_to_all | solution.py:60
  178.2 10.6 %all_to_all.78 = bf16[16,32,256]{2,1,0:T(8,128)(2,1)S(1)} all-to-all(bf16[16,32,256]{2,1,0:T(8,128)(2,1)S(1)} %broadcast_in_dim.17), channel_id=1, replica_groups=mesh['row'=16,'col'=8] {'row'}, dimensions={0} | all-to-all | bytes 524288 | tf_op jit(solution)/shard_map/all_to_all | solution.py:29
  188.8 9.8 %convolution_convert_fusion = bf16[32,4096]{1,0:T(8,128)(2,1)S(1)} fusion(bf16[1024,4096]{1,0:T(8,128)(2,1)} %param.6, bf16[32,4096]{1,0:T(8,128)(2,1)S(1)} %bitcast.146, f32[6,16,1024]{2,1,0:T(8,128)S(1)} %multiply_reduce_fusion), kind=kOutput, calls=%fused_computation | convolution fusion | flops 537100288 | bytes 9306112 | tf_op jit(solution)/shard_map/dot_general | solution.py:43
  198.6 1.0 copy.104
  199.6 4.3 %all-to-all-start.12 = ((bf16[16,2,4096]{2,1,0:T(2,128)(2,1)}), bf16[16,2,4096]{2,1,0:T(2,128)(2,1)S(1)}, u32[]{:S(2)}, u32[]{:S(2)}) async-start(bf16[16,2,4096]{2,1,0:T(2,128)(2,1)} %bitcast.129), calls=%async_computation.12 | async-start | bytes 524288 | tf_op jit(solution)/shard_map/all_to_all | solution.py:73
  204.5 0.2 convert_reduce_fusion.6
  204.7 6.4 %all-to-all-done.12 = bf16[16,2,4096]{2,1,0:T(2,128)(2,1)S(1)} async-done(((bf16[16,2,4096]{2,1,0:T(2,128)(2,1)}), bf16[16,2,4096]{2,1,0:T(2,128)(2,1)S(1)}, u32[]{:S(2)}, u32[]{:S(2)}) %all-to-all-start.12) | async-done | bytes 262176 | tf_op jit(solution)/shard_map/all_to_all | solution.py:73
  211.5 9.2 %all_to_all.79 = bf16[8,2,512]{2,1,0:T(2,128)(2,1)S(1)} all-to-all(bf16[8,2,512]{2,1,0:T(2,128)(2,1)S(1)} %copy.70), channel_id=1, replica_groups=mesh['row'=16,'col'=8] {'col'}, dimensions={0} | all-to-all | bytes 32768 | tf_op jit(solution)/shard_map/all_to_all | solution.py:81
  220.7 0.6 copy.71
  (51 shorter events, 2.2 us)
Async XLA Ops:
  1.3 14.0 %all-to-all-start = ((bf16[8,2,512]{2,1,0:T(2,128)(2,1)}), bf16[8,2,512]{2,1,0:T(2,128)(2,1)S(1)}, u32[]{:S(2)}, u32[]{:S(2)}) async-start(bf16[8,2,512]{2,1,0:T(2,128)(2,1)} %bitcast.130), calls=%async_computation | async-start | bytes 32768 | tf_op jit(solution)/shard_map/all_to_all | solution.py:34
  16.1 14.7 %all-to-all-start.1 = ((bf16[16,8,2,512]{3,1,2,0:T(8,128)(2,1)}), bf16[16,8,2,512]{3,1,2,0:T(8,128)(2,1)S(1)}, u32[]{:S(2)}, u32[]{:S(2)}) async-start(bf16[16,8,2,512]{3,1,2,0:T(8,128)(2,1)} %broadcast_in_dim.12), calls=%async_computation.1 | async-start | bytes 524288 | tf_op jit(solution)/shard_map/all_to_all | solution.py:29
  30.9 14.8 %copy-start = (f32[4096]{0:T(1024)S(1)}, f32[4096]{0:T(1024)}, u32[]{:S(2)}) copy-start(f32[4096]{0:T(1024)} %param.10) | copy-start | bytes 49156
  41.5 11.5 %all-to-all-start.2 = ((bf16[16,32,256]{2,1,0:T(8,128)(2,1)}), bf16[16,32,256]{2,1,0:T(8,128)(2,1)S(1)}, u32[]{:S(2)}, u32[]{:S(2)}) async-start(bf16[16,32,256]{2,1,0:T(8,128)(2,1)} %bitcast.128), calls=%async_computation.2 | async-start | bytes 524288 | tf_op jit(solution)/shard_map/all_to_all | solution.py:60
  199.6 11.6 %all-to-all-start.12 = ((bf16[16,2,4096]{2,1,0:T(2,128)(2,1)}), bf16[16,2,4096]{2,1,0:T(2,128)(2,1)S(1)}, u32[]{:S(2)}, u32[]{:S(2)}) async-start(bf16[16,2,4096]{2,1,0:T(2,128)(2,1)} %bitcast.129), calls=%async_computation.12 | async-start | bytes 524288 | tf_op jit(solution)/shard_map/all_to_all | solution.py:73

commit v2 on v1

--- a/solution.py
+++ b/solution.py
@@ -39,7 +39,7 @@
         projected = lax.dot_general(
             state, mode_basis, (((1,), (1,)), ((), ())), preferred_element_type=f32
         )
-        scaled = (projected * weights[step]).astype(bf16)
+        scaled = lax.optimization_barrier((projected * weights[step]).astype(bf16))
         return lax.dot_general(
             scaled, mode_basis, (((1,), (0,)), ((), ())), preferred_element_type=f32
         ).astype(bf16)

time: 223 us -> 200 us (0.90)
  matrix products: 58.8 us -> 35.4 us
    dot_general x6, matrix products: 58.8 us -> 12.8 us  [partial_sums(): lax.dot_general(scaled, mode_basis, (((1,), (0,)), ((), ())), preferred_e...]
    dot_general x0 -> x6, matrix products: none -> 22.5 us  [partial_sums(): lax.dot_general(state, mode_basis, (((1,), (1,)), ((), ())), preferred_el...]
where the time goes in v2:
time: 200 us; the launch traced here: 198 us
  blocking collectives  105 us (52%)
  matrix products  35.4 us (18%)
  waiting for transfers between devices  25.3 us (13%)
  starting transfers between devices  23.6 us (12%)
  local copies, waits for them, and re-layouts  6.53 us (3%)
    all_to_all x5, blocking collectives, gather_rows(): lax.all_to_all(jnp.broadcast_to(block[None], (row_count,) + block.shape),...  53.2 us
    dot_general x6, matrix products, partial_sums(): lax.dot_general(state, mode_basis, (((1,), (1,)), ((), ())), preferred_el...  22.5 us
    all_to_all x2, blocking collectives, on_device(): sums = lax.all_to_all(to_blocks(partial), 'row', 0, 0)  21.3 us
    all_to_all x2, blocking collectives, on_device(): lax.all_to_all(to_blocks(partial_sums(field_all, 2 * step)), 'row', 0, 0)  21.3 us
    dot_general x6, matrix products, partial_sums(): lax.dot_general(scaled, mode_basis, (((1,), (0,)), ((), ())), preferred_e...  12.8 us
    all_to_all x1, blocking collectives, on_device(): return jnp.transpose(lax.all_to_all(sent, 'col', 0, 0), (1, 2, 0))  9.18 us
    all_to_all x1, starting transfers between devices, gather_rows(): lax.all_to_all(jnp.broadcast_to(block[None], (row_count,) + block.shape),...  7.54 us
    all_to_all x1, starting transfers between devices, on_device(): own = lax.all_to_all(sent, 'col', 0, 0)  7.48 us
  transfers between devices with their start and end apart: 4, of which 4 were waited for; matrix products, arithmetic and copies ran while one was open for 1% of the time, Pallas kernels for 0%

profile of v2, /device:TPU:1, one launch (start us, length us, event | category | flops | bytes accessed | tf_op | source)
XLA Modules:
  0.0 198.0 jit_solution(15424577988497662076)
XLA Ops:
  0.0 1.3 copy.105
  1.3 7.5 %all-to-all-start = ((bf16[8,2,512]{2,1,0:T(2,128)(2,1)}), bf16[8,2,512]{2,1,0:T(2,128)(2,1)S(1)}, u32[]{:S(2)}, u32[]{:S(2)}) async-start(bf16[8,2,512]{2,1,0:T(2,128)(2,1)} %bitcast.130), calls=%async_computation | async-start | bytes 32768 | tf_op jit(solution)/shard_map/all_to_all | solution.py:34
  10.0 5.4 %all-to-all-done = bf16[8,2,512]{2,1,0:T(2,128)(2,1)S(1)} async-done(((bf16[8,2,512]{2,1,0:T(2,128)(2,1)}), bf16[8,2,512]{2,1,0:T(2,128)(2,1)S(1)}, u32[]{:S(2)}, u32[]{:S(2)}) %all-to-all-start) | async-done | bytes 16416 | tf_op jit(solution)/shard_map/all_to_all | solution.py:34
  16.1 7.5 %all-to-all-start.1 = ((bf16[16,8,2,512]{3,1,2,0:T(8,128)(2,1)}), bf16[16,8,2,512]{3,1,2,0:T(8,128)(2,1)S(1)}, u32[]{:S(2)}, u32[]{:S(2)}) async-start(bf16[16,8,2,512]{3,1,2,0:T(8,128)(2,1)} %broadcast_in_dim.12), calls=%async_computation.1 | async-start | bytes 524288 | tf_op jit(solution)/shard_map/all_to_all | solution.py:29
  24.5 6.3 %all-to-all-done.1 = bf16[16,8,2,512]{3,1,2,0:T(8,128)(2,1)S(1)} async-done(((bf16[16,8,2,512]{3,1,2,0:T(8,128)(2,1)}), bf16[16,8,2,512]{3,1,2,0:T(8,128)(2,1)S(1)}, u32[]{:S(2)}, u32[]{:S(2)}) %all-to-all-start.1) | async-done | bytes 262176 | tf_op jit(solution)/shard_map/all_to_all | solution.py:29
  30.9 6.1 %fusion = bf16[32,1024]{1,0:T(8,128)(2,1)S(1)} fusion(bf16[32,4096]{1,0:T(8,128)(2,1)S(1)} %bitcast.137, bf16[1024,4096]{1,0:T(8,128)(2,1)} %param.6, f32[6,16,1024]{2,1,0:T(8,128)S(1)} %multiply_reduce_fusion), kind=kOutput, calls=%fused_computation.23 | convolution fusion | flops 268533760 | bytes 9109504 | tf_op jit(solution)/shard_map/dot_general | solution.py:39
  37.1 1.5 convolution_convert_fusion.5
  39.3 4.3 %all-to-all-start.2 = ((bf16[16,32,256]{2,1,0:T(8,128)(2,1)}), bf16[16,32,256]{2,1,0:T(8,128)(2,1)S(1)}, u32[]{:S(2)}, u32[]{:S(2)}) async-start(bf16[16,32,256]{2,1,0:T(8,128)(2,1)} %bitcast.128), calls=%async_computation.2 | async-start | bytes 524288 | tf_op jit(solution)/shard_map/all_to_all | solution.py:60
  43.7 7.2 %all-to-all-done.2 = bf16[16,32,256]{2,1,0:T(8,128)(2,1)S(1)} async-done(((bf16[16,32,256]{2,1,0:T(8,128)(2,1)}), bf16[16,32,256]{2,1,0:T(8,128)(2,1)S(1)}, u32[]{:S(2)}, u32[]{:S(2)}) %all-to-all-start.2) | async-done | bytes 262176 | tf_op jit(solution)/shard_map/all_to_all | solution.py:60
  51.0 10.6 %all_to_all.70 = bf16[16,32,256]{2,1,0:T(8,128)(2,1)S(1)} all-to-all(bf16[16,32,256]{2,1,0:T(8,128)(2,1)S(1)} %broadcast_in_dim.13), channel_id=1, replica_groups=mesh['row'=16,'col'=8] {'row'}, dimensions={0} | all-to-all | bytes 524288 | tf_op jit(solution)/shard_map/all_to_all | solution.py:29
  61.7 6.1 %fusion.1 = bf16[32,1024]{1,0:T(8,128)(2,1)S(1)} fusion(bf16[32,4096]{1,0:T(8,128)(2,1)S(1)} %bitcast.146, bf16[1024,4096]{1,0:T(8,128)(2,1)} %param.6, f32[6,16,1024]{2,1,0:T(8,128)S(1)} %multiply_reduce_fusion), kind=kOutput, calls=%fused_computation.24 | convolution fusion | flops 268533760 | bytes 9109504 | tf_op jit(solution)/shard_map/dot_general | solution.py:39
  67.8 5.1 %convolution_convert_fusion.4 = bf16[32,4096]{1,0:T(8,128)(2,1)S(1)} fusion(bf16[32,1024]{1,0:T(8,128)(2,1)S(1)} %fusion.1, bf16[1024,4096]{1,0:T(8,128)(2,1)} %param.6), kind=kOutput, calls=%fused_computation.4 | convolution fusion | flops 268566528 | bytes 8716288 | tf_op jit(solution)/shard_map/dot_general | solution.py:43
  72.9 10.6 %all_to_all.71 = bf16[16,32,256]{2,1,0:T(8,128)(2,1)S(1)} all-to-all(bf16[16,32,256]{2,1,0:T(8,128)(2,1)S(1)} %bitcast.154), channel_id=1, replica_groups=mesh['row'=16,'col'=8] {'row'}, dimensions={0} | all-to-all | bytes 524288 | tf_op jit(solution)/shard_map/all_to_all | solution.py:66
  83.7 10.6 %all_to_all.72 = bf16[16,32,256]{2,1,0:T(8,128)(2,1)S(1)} all-to-all(bf16[16,32,256]{2,1,0:T(8,128)(2,1)S(1)} %broadcast_in_dim.14), channel_id=1, replica_groups=mesh['row'=16,'col'=8] {'row'}, dimensions={0} | all-to-all | bytes 524288 | tf_op jit(solution)/shard_map/all_to_all | solution.py:29
  94.4 2.6 %fusion.2 = bf16[32,1024]{1,0:T(8,128)(2,1)S(1)} fusion(bf16[32,4096]{1,0:T(8,128)(2,1)S(1)} %bitcast.147, bf16[1024,4096]{1,0:T(8,128)(2,1)S(1)} %bitcast.132, f32[6,16,1024]{2,1,0:T(8,128)S(1)} %multiply_reduce_fusion), kind=kOutput, calls=%fused_computation.25 | convolution fusion | flops 268533760 | bytes 9109504 | tf_op jit(solution)/shard_map/dot_general | solution.py:39
  96.9 1.6 convolution_convert_fusion.3
  98.5 10.6 %all_to_all.73 = bf16[16,32,256]{2,1,0:T(8,128)(2,1)S(1)} all-to-all(bf16[16,32,256]{2,1,0:T(8,128)(2,1)S(1)} %bitcast.156), channel_id=1, replica_groups=mesh['row'=16,'col'=8] {'row'}, dimensions={0} | all-to-all | bytes 524288 | tf_op jit(solution)/shard_map/all_to_all | solution.py:60
  109.3 10.6 %all_to_all.74 = bf16[16,32,256]{2,1,0:T(8,128)(2,1)S(1)} all-to-all(bf16[16,32,256]{2,1,0:T(8,128)(2,1)S(1)} %broadcast_in_dim.15), channel_id=1, replica_groups=mesh['row'=16,'col'=8] {'row'}, dimensions={0} | all-to-all | bytes 524288 | tf_op jit(solution)/shard_map/all_to_all | solution.py:29
  120.0 2.6 %fusion.3 = bf16[32,1024]{1,0:T(8,128)(2,1)S(1)} fusion(bf16[32,4096]{1,0:T(8,128)(2,1)S(1)} %bitcast.148, bf16[1024,4096]{1,0:T(8,128)(2,1)S(1)} %bitcast.132, f32[6,16,1024]{2,1,0:T(8,128)S(1)} %multiply_reduce_fusion), kind=kOutput, calls=%fused_computation.26 | convolution fusion | flops 268533760 | bytes 9109504 | tf_op jit(solution)/shard_map/dot_general | solution.py:39
  122.5 1.6 convolution_convert_fusion.2
  124.1 10.7 %all_to_all.75 = bf16[16,32,256]{2,1,0:T(8,128)(2,1)S(1)} all-to-all(bf16[16,32,256]{2,1,0:T(8,128)(2,1)S(1)} %bitcast.158), channel_id=1, replica_groups=mesh['row'=16,'col'=8] {'row'}, dimensions={0} | all-to-all | bytes 524288 | tf_op jit(solution)/shard_map/all_to_all | solution.py:66
  134.9 10.6 %all_to_all.76 = bf16[16,32,256]{2,1,0:T(8,128)(2,1)S(1)} all-to-all(bf16[16,32,256]{2,1,0:T(8,128)(2,1)S(1)} %broadcast_in_dim.16), channel_id=1, replica_groups=mesh['row'=16,'col'=8] {'row'}, dimensions={0} | all-to-all | bytes 524288 | tf_op jit(solution)/shard_map/all_to_all | solution.py:29
  145.6 2.6 %fusion.4 = bf16[32,1024]{1,0:T(8,128)(2,1)S(1)} fusion(bf16[32,4096]{1,0:T(8,128)(2,1)S(1)} %bitcast.150, bf16[1024,4096]{1,0:T(8,128)(2,1)S(1)} %bitcast.132, f32[6,16,1024]{2,1,0:T(8,128)S(1)} %multiply_reduce_fusion), kind=kOutput, calls=%fused_computation.27 | convolution fusion | flops 268533760 | bytes 9109504 | tf_op jit(solution)/shard_map/dot_general | solution.py:39
  148.1 1.6 convolution_convert_fusion.1
  149.7 10.6 %all_to_all.77 = bf16[16,32,256]{2,1,0:T(8,128)(2,1)S(1)} all-to-all(bf16[16,32,256]{2,1,0:T(8,128)(2,1)S(1)} %bitcast.159), channel_id=1, replica_groups=mesh['row'=16,'col'=8] {'row'}, dimensions={0} | all-to-all | bytes 524288 | tf_op jit(solution)/shard_map/all_to_all | solution.py:60
  160.5 10.6 %all_to_all.78 = bf16[16,32,256]{2,1,0:T(8,128)(2,1)S(1)} all-to-all(bf16[16,32,256]{2,1,0:T(8,128)(2,1)S(1)} %broadcast_in_dim.17), channel_id=1, replica_groups=mesh['row'=16,'col'=8] {'row'}, dimensions={0} | all-to-all | bytes 524288 | tf_op jit(solution)/shard_map/all_to_all | solution.py:29
  171.1 2.6 %fusion.5 = bf16[32,1024]{1,0:T(8,128)(2,1)S(1)} fusion(bf16[32,4096]{1,0:T(8,128)(2,1)S(1)} %bitcast.149, bf16[1024,4096]{1,0:T(8,128)(2,1)S(1)} %bitcast.132, f32[6,16,1024]{2,1,0:T(8,128)S(1)} %multiply_reduce_fusion), kind=kOutput, calls=%fused_computation.28 | convolution fusion | flops 268533760 | bytes 9109504 | tf_op jit(solution)/shard_map/dot_general | solution.py:39
  173.7 1.6 convolution_convert_fusion
  175.3 1.0 copy.104
  176.3 4.3 %all-to-all-start.12 = ((bf16[16,2,4096]{2,1,0:T(2,128)(2,1)}), bf16[16,2,4096]{2,1,0:T(2,128)(2,1)S(1)}, u32[]{:S(2)}, u32[]{:S(2)}) async-start(bf16[16,2,4096]{2,1,0:T(2,128)(2,1)} %bitcast.129), calls=%async_computation.12 | async-start | bytes 524288 | tf_op jit(solution)/shard_map/all_to_all | solution.py:73
  181.4 6.4 %all-to-all-done.12 = bf16[16,2,4096]{2,1,0:T(2,128)(2,1)S(1)} async-done(((bf16[16,2,4096]{2,1,0:T(2,128)(2,1)}), bf16[16,2,4096]{2,1,0:T(2,128)(2,1)S(1)}, u32[]{:S(2)}, u32[]{:S(2)}) %all-to-all-start.12) | async-done | bytes 262176 | tf_op jit(solution)/shard_map/all_to_all | solution.py:73
  188.2 9.2 %all_to_all.79 = bf16[8,2,512]{2,1,0:T(2,128)(2,1)S(1)} all-to-all(bf16[8,2,512]{2,1,0:T(2,128)(2,1)S(1)} %copy.70), channel_id=1, replica_groups=mesh['row'=16,'col'=8] {'col'}, dimensions={0} | all-to-all | bytes 32768 | tf_op jit(solution)/shard_map/all_to_all | solution.py:81
  (64 shorter events, 6.0 us)
Async XLA Ops:
  1.3 14.0 %all-to-all-start = ((bf16[8,2,512]{2,1,0:T(2,128)(2,1)}), bf16[8,2,512]{2,1,0:T(2,128)(2,1)S(1)}, u32[]{:S(2)}, u32[]{:S(2)}) async-start(bf16[8,2,512]{2,1,0:T(2,128)(2,1)} %bitcast.130), calls=%async_computation | async-start | bytes 32768 | tf_op jit(solution)/shard_map/all_to_all | solution.py:34
  16.1 14.7 %all-to-all-start.1 = ((bf16[16,8,2,512]{3,1,2,0:T(8,128)(2,1)}), bf16[16,8,2,512]{3,1,2,0:T(8,128)(2,1)S(1)}, u32[]{:S(2)}, u32[]{:S(2)}) async-start(bf16[16,8,2,512]{3,1,2,0:T(8,128)(2,1)} %broadcast_in_dim.12), calls=%async_computation.1 | async-start | bytes 524288 | tf_op jit(solution)/shard_map/all_to_all | solution.py:29
  30.8 6.2 %copy-start = (bf16[1024,4096]{1,0:T(8,128)(2,1)S(1)}, bf16[1024,4096]{1,0:T(8,128)(2,1)}, u32[]{:S(2)}) copy-start(bf16[1024,4096]{1,0:T(8,128)(2,1)} %param.6) | copy-start | bytes 25165828
  37.0 6.6 %copy-start.1 = (f32[4096]{0:T(1024)S(1)}, f32[4096]{0:T(1024)}, u32[]{:S(2)}) copy-start(f32[4096]{0:T(1024)} %param.10) | copy-start | bytes 49156
  39.3 11.5 %all-to-all-start.2 = ((bf16[16,32,256]{2,1,0:T(8,128)(2,1)}), bf16[16,32,256]{2,1,0:T(8,128)(2,1)S(1)}, u32[]{:S(2)}, u32[]{:S(2)}) async-start(bf16[16,32,256]{2,1,0:T(8,128)(2,1)} %bitcast.128), calls=%async_computation.2 | async-start | bytes 524288 | tf_op jit(solution)/shard_map/all_to_all | solution.py:60
  61.6 32.7 %slice-start = ((s8[8388608]{0:T(1024)(128)(4,1)}), s8[4194304]{0:T(1024)(128)(4,1)S(1)}, s32[]{:S(2)}) async-start(s8[8388608]{0:T(1024)(128)(4,1)} %bitcast.131), calls=%async_computation.14 | async-start | bytes 8388608
  67.8 26.6 %slice-start.1 = ((s8[8388608]{0:T(1024)(128)(4,1)}), s8[4194304]{0:T(1024)(128)(4,1)S(1)}, s32[]{:S(2)}) async-start(s8[8388608]{0:T(1024)(128)(4,1)} %bitcast.131), calls=%async_computation.15 | async-start | bytes 8388608
  176.3 11.6 %all-to-all-start.12 = ((bf16[16,2,4096]{2,1,0:T(2,128)(2,1)}), bf16[16,2,4096]{2,1,0:T(2,128)(2,1)S(1)}, u32[]{:S(2)}, u32[]{:S(2)}) async-start(bf16[16,2,4096]{2,1,0:T(2,128)(2,1)} %bitcast.129), calls=%async_computation.12 | async-start | bytes 524288 | tf_op jit(solution)/shard_map/all_to_all | solution.py:73

commit v3 on v2

v3 whole, which is shorter than its diff:
```python
import jax
import jax.numpy as jnp
from jax import lax
from jax.sharding import PartitionSpec as P

STEPS = 3


def on_device(mode_basis, node_coords, quad_weights, magnetization, decay_rates, directions):
    row_count = lax.axis_size("row")
    col_count = lax.axis_size("col")
    row_index = lax.axis_index("row")
    col_index = lax.axis_index("col")
    core = row_index % 2
    mode_count = mode_basis.shape[1]
    parts, col_width, own_waves = magnetization.shape
    columns = 2 * row_count
    width = mode_count // 2
    f32, bf16 = jnp.float32, jnp.bfloat16

    def move(array, target):
        return lax.ppermute(array, "row", [(r, target(r)) for r in range(row_count)])

    def to_other_core(array):
        return move(array, lambda r: r ^ 1)

    def along_y(array):
        return move(array, lambda r: r ^ 8)

    def along_z(array, hops):
        return move(array, lambda r: (r & 9) | ((r + 2 * hops) & 6))

    mine = lax.dynamic_index_in_dim(
        directions.reshape(2 * STEPS, 3, row_count, own_waves), col_index, 3, keepdims=False
    )
    moments = node_coords * quad_weights[None, :]
    weights = jnp.sum(mine[:, :, :, None] * moments[None, :, None, :], axis=1)
    weights = jnp.concatenate([weights, weights], axis=1)

    def half_of(array, which, axis):
        return lax.dynamic_slice_in_dim(array, which * width, width, axis)

    basis_own = lax.optimization_barrier(half_of(mode_basis, core, 1))
    basis_other = lax.optimization_barrier(half_of(mode_basis, 1 - core, 1))
    rates = half_of(decay_rates, core, 0)[None, :]

    sent = jnp.transpose(magnetization, (2, 0, 1))
    sent = jnp.broadcast_to(sent[None], (row_count,) + sent.shape)
    sent = sent.reshape(row_count * col_count, parts, col_width)
    every = lax.all_to_all(sent, ("row", "col"), 0, 0)
    every = every.reshape(row_count, col_count, parts, col_width)
    every = jnp.transpose(every, (2, 0, 1, 3)).reshape(columns, mode_count)
    field = half_of(every, core, 1)
    field_other = half_of(every, 1 - core, 1)

    def scaled_nodes(own, other, step):
        nodes = lax.dot_general(
            own, basis_own, (((1,), (1,)), ((), ())), preferred_element_type=f32
        ) + lax.dot_general(
            other, basis_other, (((1,), (1,)), ((), ())), preferred_element_type=f32
        )
        return lax.optimization_barrier((nodes * weights[step]).astype(bf16))

    def back(nodes, basis):
        return lax.dot_general(
            nodes, basis, (((1,), (0,)), ((), ())), preferred_element_type=f32
        )

    def reduced(own, other, step):
        nodes = scaled_nodes(own, other, step)
        arrived = to_other_core(back(nodes, basis_other).astype(bf16))
        total = lax.optimization_barrier(back(nodes, basis_own)) + arrived.astype(f32)
        total = total + along_y(total.astype(bf16)).astype(f32)
        sent = total.astype(bf16)
        for hops in (1, 3, 2):
            total = total + along_z(sent, hops).astype(f32)
        return total

    def mixed(sums, factor):
        half = sums.shape[0] // 2
        return jnp.concatenate([factor * sums[half:], -factor * sums[:half]], axis=0)

    for step in range(STEPS):
        sums = reduced(field, field_other, 2 * step)
        half = (mixed(sums, 0.5) + (1.0 - 0.5 * rates) * field.astype(f32)).astype(bf16)
        half_other = to_other_core(half)
        if step + 1 < STEPS:
            sums = reduced(half, half_other, 2 * step + 1)
            update = mixed(sums, 1.0) + (0.0 - 1.0 * rates) * half.astype(f32)
            field = (field.astype(f32) + update).astype(bf16)
            field_other = to_other_core(field)

    nodes = scaled_nodes(half, half_other, 2 * STEPS - 1)
    local = field.astype(f32) + (0.0 - 1.0 * rates) * half.astype(f32)
    local = jnp.where(row_index < 2, local, 0.0)
    part_own = (mixed(back(nodes, basis_own), 1.0) + local).astype(bf16)
    part_other = mixed(back(nodes, basis_other), 1.0).astype(bf16)
    low = jnp.where(core == 0, part_own, part_other)
    high = jnp.where(core == 0, part_other, part_own)
    sent = jnp.concatenate([low, high], axis=1)
    sent = sent.reshape(parts, row_count, col_count, col_width)
    sent = jnp.transpose(sent, (1, 2, 0, 3)).reshape(row_count * col_count, parts, col_width)
    every = lax.all_to_all(sent, ("row", "col"), 0, 0)
    every = every.reshape(row_count, col_count, parts, col_width)
    final = jnp.sum(every.astype(f32), axis=0).astype(bf16)
    return jnp.transpose(final, (1, 2, 0))


def solution(mesh):
    return jax.shard_map(
        on_device,
        mesh=mesh,
        in_specs=(P("row", None), P(None, "row"), P("row"), P(None, "col", "row"), P(), P()),
        out_specs=P(None, "col", "row"),
        check_vma=False,
    )
```

time: 200 us -> 157 us (0.79)
  blocking collectives: 105 us -> 16.9 us
  waiting for transfers between devices: 25.3 us -> 57.8 us
  starting transfers between devices: 23.6 us -> 36.4 us
  local copies, waits for them, and re-layouts: 6.53 us -> 12.4 us
  matrix products: 35.4 us -> 30.4 us
    all_to_all x10 -> x1, blocking collectives: 105 us -> 16.9 us  [on_device(): every = lax.all_to_all(sent, ('row', 'col'), 0, 0)]
    ppermute x0 -> x30, waiting for transfers between devices: none -> 57.1 us  [move(): lax.ppermute(array, 'row', [(r, target(r)) for r in range(row_count)])]
    ppermute x0 -> x30, starting transfers between devices: none -> 24.9 us  [move(): lax.ppermute(array, 'row', [(r, target(r)) for r in range(row_count)])]
    all_to_all x4 -> x1, waiting for transfers between devices: 25.3 us -> 0.77 us  [on_device(): every = lax.all_to_all(sent, ('row', 'col'), 0, 0)]
    all_to_all x4 -> x1, starting transfers between devices: 23.6 us -> 11.5 us  [on_device(): every = lax.all_to_all(sent, ('row', 'col'), 0, 0)]
    dynamic_slice x0 -> x1, local copies, waits for them, and re-layouts: none -> 8.44 us  [half_of(): return lax.dynamic_slice_in_dim(array, which * width, width, axis)]
    dot_general x12 -> x24, matrix products: 35.4 us -> 30.4 us  [the longest x6 12.5 us: scaled_nodes(): lax.dot_general(own, basis_own, (((1,), (1,)), ((), ())), preferred_eleme...]
  transfers between devices with their start and end apart: 4 -> 31, of which waited for: 4 -> 26; matrix products, arithmetic and copies ran while one was open for 1% -> 15% of each run, Pallas kernels for 0% -> 0%
where the time goes in v3:
time: 157 us; the launch traced here: 156 us
  waiting for transfers between devices  57.8 us (37%)
  starting transfers between devices  36.4 us (23%)
  matrix products  30.4 us (19%)
  blocking collectives  16.9 us (11%)
  local copies, waits for them, and re-layouts  12.4 us (8%)
  other arithmetic  1.78 us (1%)
    ppermute x30, waiting for transfers between devices, move(): lax.ppermute(array, 'row', [(r, target(r)) for r in range(row_count)])  57.1 us
    ppermute x30, starting transfers between devices, move(): lax.ppermute(array, 'row', [(r, target(r)) for r in range(row_count)])  24.9 us
    all_to_all x1, blocking collectives, on_device(): every = lax.all_to_all(sent, ('row', 'col'), 0, 0)  16.9 us
    dot_general x6, matrix products, scaled_nodes(): lax.dot_general(own, basis_own, (((1,), (1,)), ((), ())), preferred_eleme...  12.5 us
    all_to_all x1, starting transfers between devices, on_device(): every = lax.all_to_all(sent, ('row', 'col'), 0, 0)  11.5 us
    dot_general x12, matrix products, back(): lax.dot_general(nodes, basis, (((1,), (0,)), ((), ())), preferred_element...  9.88 us
    dynamic_slice x1, local copies, waits for them, and re-layouts, half_of(): return lax.dynamic_slice_in_dim(array, which * width, width, axis)  8.44 us
    dot_general x6, matrix products, scaled_nodes(): lax.dot_general(other, basis_other, (((1,), (1,)), ((), ())), preferred_e...  8.06 us
  transfers between devices with their start and end apart: 31, of which 26 were waited for; matrix products, arithmetic and copies ran while one was open for 15% of the time, Pallas kernels for 0%

profile of v3, /device:TPU:1, one launch (start us, length us, event | category | flops | bytes accessed | tf_op | source)
XLA Modules:
  0.0 156.2 jit_solution(14781979723556775873)
XLA Ops:
  1.7 11.5 %all-to-all-start = ((bf16[128,2,512]{2,1,0:T(2,128)(2,1)}), bf16[128,2,512]{2,1,0:T(2,128)(2,1)S(1)}, u32[]{:S(2)}, u32[]{:S(2)}) async-start(bf16[128,2,512]{2,1,0:T(2,128)(2,1)} %bitcast.1), calls=%async_computation | async-start | bytes 524288 | tf_op jit(solution)/shard_map/all_to_all | solution.py:50
  14.4 8.4 %constant_dynamic-slice_fusion.1 = (bf16[1024,2048]{1,0:T(8,128)(2,1)}, bf16[1024,2048]{1,0:T(8,128)(2,1)}) fusion(bf16[1024,4096]{1,0:T(8,128)(2,1)} %param.6, s32[]{:T(128)S(6)} %select_n.43, s32[]{:T(128)S(6)} %select_n.42), kind=kLoop, calls=%fused_computation.115 | loop fusion | bytes 16777224 | tf_op jit(solution)/shard_map/dynamic_slice | solution.py:41
  23.9 3.7 %fusion.46 = f32[32,1024]{1,0:T(8,128)S(1)} fusion(bf16[1024,2048]{1,0:T(8,128)(2,1)} %get-tuple-element.8, bf16[32,4096]{1,0:T(8,128)(2,1)S(1)} %bitcast.90, s32[]{:T(128)S(6)} %select_n.42), kind=kOutput, calls=%fused_computation.108 | convolution fusion | flops 134217728 | bytes 4456452 | tf_op jit(solution)/shard_map/dot_general | solution.py:57
  27.6 1.3 fusion.6
  32.5 4.4 %collective-permute-done.1 = bf16[32,2048]{1,0:T(8,128)(2,1)S(1)} collective-permute-done((bf16[32,2048]{1,0:T(8,128)(2,1)S(1)}, bf16[32,2048]{1,0:T(8,128)(2,1)S(1)}, u32[]{:S(2)}, u32[]{:S(2)}) %collective-permute-start.1) | collective-permute-done | bytes 131104 | tf_op jit(solution)/shard_map/ppermute | solution.py:22
  36.9 1.7 %collective-permute-start.4 = (bf16[32,2048]{1,0:T(8,128)(2,1)S(1)}, bf16[32,2048]{1,0:T(8,128)(2,1)S(1)}, u32[]{:S(2)}, u32[]{:S(2)}) collective-permute-start(bf16[32,2048]{1,0:T(8,128)(2,1)S(1)} %fusion.41), channel_id=1, source_target_pairs={{0,32},{8,40},{16,48},{24,56},{32,0},{40,8},{48,16},{56,24},{64,96... | collective-permute-start | bytes 393224 | tf_op jit(solution)/shard_map/ppermute | solution.py:22
  40.1 2.2 %collective-permute-done.4 = bf16[32,2048]{1,0:T(8,128)(2,1)S(1)} collective-permute-done((bf16[32,2048]{1,0:T(8,128)(2,1)S(1)}, bf16[32,2048]{1,0:T(8,128)(2,1)S(1)}, u32[]{:S(2)}, u32[]{:S(2)}) %collective-permute-start.4) | collective-permute-done | bytes 131104 | tf_op jit(solution)/shard_map/ppermute | solution.py:22
  42.3 2.0 %collective-permute-done.3 = bf16[32,2048]{1,0:T(8,128)(2,1)S(1)} collective-permute-done((bf16[32,2048]{1,0:T(8,128)(2,1)S(1)}, bf16[32,2048]{1,0:T(8,128)(2,1)S(1)}, u32[]{:S(2)}, u32[]{:S(2)}) %collective-permute-start.3) | collective-permute-done | bytes 131104 | tf_op jit(solution)/shard_map/ppermute | solution.py:22
  44.3 1.9 %collective-permute-done.2 = bf16[32,2048]{1,0:T(8,128)(2,1)S(1)} collective-permute-done((bf16[32,2048]{1,0:T(8,128)(2,1)S(1)}, bf16[32,2048]{1,0:T(8,128)(2,1)S(1)}, u32[]{:S(2)}, u32[]{:S(2)}) %collective-permute-start.2) | collective-permute-done | bytes 131104 | tf_op jit(solution)/shard_map/ppermute | solution.py:22
  46.4 1.8 %collective-permute-start.5 = (bf16[32,2048]{1,0:T(8,128)(2,1)S(1)}, bf16[32,2048]{1,0:T(8,128)(2,1)S(1)}, u32[]{:S(2)}, u32[]{:S(2)}) collective-permute-start(bf16[32,2048]{1,0:T(8,128)(2,1)S(1)} %fusion.13), channel_id=1, source_target_pairs={{0,8},{8,0},{16,24},{24,16},{32,40},{40,32},{48,56},{56,48},{64,72... | collective-permute-start | bytes 393224 | tf_op jit(solution)/shard_map/ppermute | solution.py:22
  49.6 1.3 fusion.7
  53.7 4.5 %collective-permute-done.7 = bf16[32,2048]{1,0:T(8,128)(2,1)S(1)} collective-permute-done((bf16[32,2048]{1,0:T(8,128)(2,1)S(1)}, bf16[32,2048]{1,0:T(8,128)(2,1)S(1)}, u32[]{:S(2)}, u32[]{:S(2)}) %collective-permute-start.7) | collective-permute-done | bytes 131104 | tf_op jit(solution)/shard_map/ppermute | solution.py:22
  60.7 3.0 %collective-permute-done.10 = bf16[32,2048]{1,0:T(8,128)(2,1)S(1)} collective-permute-done((bf16[32,2048]{1,0:T(8,128)(2,1)S(1)}, bf16[32,2048]{1,0:T(8,128)(2,1)S(1)}, u32[]{:S(2)}, u32[]{:S(2)}) %collective-permute-start.10) | collective-permute-done | bytes 131104 | tf_op jit(solution)/shard_map/ppermute | solution.py:22
  63.7 1.5 collective-permute-done.9
  65.1 2.2 %collective-permute-done.8 = bf16[32,2048]{1,0:T(8,128)(2,1)S(1)} collective-permute-done((bf16[32,2048]{1,0:T(8,128)(2,1)S(1)}, bf16[32,2048]{1,0:T(8,128)(2,1)S(1)}, u32[]{:S(2)}, u32[]{:S(2)}) %collective-permute-start.8) | collective-permute-done | bytes 131104 | tf_op jit(solution)/shard_map/ppermute | solution.py:22
  67.5 1.5 collective-permute-start.11
  70.4 1.3 fusion.8
  74.8 4.3 %collective-permute-done.13 = bf16[32,2048]{1,0:T(8,128)(2,1)S(1)} collective-permute-done((bf16[32,2048]{1,0:T(8,128)(2,1)S(1)}, bf16[32,2048]{1,0:T(8,128)(2,1)S(1)}, u32[]{:S(2)}, u32[]{:S(2)}) %collective-permute-start.13) | collective-permute-done | bytes 131104 | tf_op jit(solution)/shard_map/ppermute | solution.py:22
  81.3 3.2 %collective-permute-done.16 = bf16[32,2048]{1,0:T(8,128)(2,1)S(1)} collective-permute-done((bf16[32,2048]{1,0:T(8,128)(2,1)S(1)}, bf16[32,2048]{1,0:T(8,128)(2,1)S(1)}, u32[]{:S(2)}, u32[]{:S(2)}) %collective-permute-start.16) | collective-permute-done | bytes 131104 | tf_op jit(solution)/shard_map/ppermute | solution.py:22
  85.7 2.3 %collective-permute-done.14 = bf16[32,2048]{1,0:T(8,128)(2,1)S(1)} collective-permute-done((bf16[32,2048]{1,0:T(8,128)(2,1)S(1)}, bf16[32,2048]{1,0:T(8,128)(2,1)S(1)}, u32[]{:S(2)}, u32[]{:S(2)}) %collective-permute-start.14) | collective-permute-done | bytes 131104 | tf_op jit(solution)/shard_map/ppermute | solution.py:22
  88.3 1.5 collective-permute-start.17
  91.1 1.3 fusion.9
  95.6 4.2 %collective-permute-done.19 = bf16[32,2048]{1,0:T(8,128)(2,1)S(1)} collective-permute-done((bf16[32,2048]{1,0:T(8,128)(2,1)S(1)}, bf16[32,2048]{1,0:T(8,128)(2,1)S(1)}, u32[]{:S(2)}, u32[]{:S(2)}) %collective-permute-start.19) | collective-permute-done | bytes 131104 | tf_op jit(solution)/shard_map/ppermute | solution.py:22
  101.9 3.3 %collective-permute-done.22 = bf16[32,2048]{1,0:T(8,128)(2,1)S(1)} collective-permute-done((bf16[32,2048]{1,0:T(8,128)(2,1)S(1)}, bf16[32,2048]{1,0:T(8,128)(2,1)S(1)}, u32[]{:S(2)}, u32[]{:S(2)}) %collective-permute-start.22) | collective-permute-done | bytes 131104 | tf_op jit(solution)/shard_map/ppermute | solution.py:22
  106.3 2.4 %collective-permute-done.20 = bf16[32,2048]{1,0:T(8,128)(2,1)S(1)} collective-permute-done((bf16[32,2048]{1,0:T(8,128)(2,1)S(1)}, bf16[32,2048]{1,0:T(8,128)(2,1)S(1)}, u32[]{:S(2)}, u32[]{:S(2)}) %collective-permute-start.20) | collective-permute-done | bytes 131104 | tf_op jit(solution)/shard_map/ppermute | solution.py:22
  108.9 1.8 %collective-permute-start.23 = (bf16[32,2048]{1,0:T(8,128)(2,1)S(1)}, bf16[32,2048]{1,0:T(8,128)(2,1)S(1)}, u32[]{:S(2)}, u32[]{:S(2)}) collective-permute-start(bf16[32,2048]{1,0:T(8,128)(2,1)S(1)} %fusion.17), channel_id=1, source_target_pairs={{0,8},{8,0},{16,24},{24,16},{32,40},{40,32},{48,56},{56,48},{64,72... | collective-permute-start | bytes 393224 | tf_op jit(solution)/shard_map/ppermute | solution.py:22
  116.5 4.1 %collective-permute-done.25 = bf16[32,2048]{1,0:T(8,128)(2,1)S(1)} collective-permute-done((bf16[32,2048]{1,0:T(8,128)(2,1)S(1)}, bf16[32,2048]{1,0:T(8,128)(2,1)S(1)}, u32[]{:S(2)}, u32[]{:S(2)}) %collective-permute-start.25) | collective-permute-done | bytes 131104 | tf_op jit(solution)/shard_map/ppermute | solution.py:22
  122.7 3.4 %collective-permute-done.28 = bf16[32,2048]{1,0:T(8,128)(2,1)S(1)} collective-permute-done((bf16[32,2048]{1,0:T(8,128)(2,1)S(1)}, bf16[32,2048]{1,0:T(8,128)(2,1)S(1)}, u32[]{:S(2)}, u32[]{:S(2)}) %collective-permute-start.28) | collective-permute-done | bytes 131104 | tf_op jit(solution)/shard_map/ppermute | solution.py:22
  127.1 2.4 %collective-permute-done.26 = bf16[32,2048]{1,0:T(8,128)(2,1)S(1)} collective-permute-done((bf16[32,2048]{1,0:T(8,128)(2,1)S(1)}, bf16[32,2048]{1,0:T(8,128)(2,1)S(1)}, u32[]{:S(2)}, u32[]{:S(2)}) %collective-permute-start.26) | collective-permute-done | bytes 131104 | tf_op jit(solution)/shard_map/ppermute | solution.py:22
  129.7 1.5 collective-permute-start.29
  131.3 3.5 %fusion.63 = f32[32,1024]{1,0:T(8,128)S(1)} fusion(bf16[32,2048]{1,0:T(8,128)(2,1)S(1)} %fusion.19, bf16[1024,2048]{1,0:T(8,128)(2,1)} %get-tuple-element.8), kind=kOutput, calls=%fused_computation.130 | convolution fusion | flops 134217728 | bytes 4456448 | tf_op jit(solution)/shard_map/dot_general | solution.py:57
  138.4 16.9 %all_to_all.10 = bf16[128,2,512]{2,1,0:T(2,128)(2,1)S(1)} all-to-all(bf16[128,2,512]{2,1,0:T(2,128)(2,1)S(1)} %bitcast.99), channel_id=1, replica_groups=mesh['row'=16,'col'=8] {'row','col'}, dimensions={0} | all-to-all | bytes 524288 | tf_op jit(solution)/shard_map/all_to_all | solution.py:103
  (116 shorter events, 45.1 us)
Async XLA Ops:
  1.7 22.1 %all-to-all-start = ((bf16[128,2,512]{2,1,0:T(2,128)(2,1)}), bf16[128,2,512]{2,1,0:T(2,128)(2,1)S(1)}, u32[]{:S(2)}, u32[]{:S(2)}) async-start(bf16[128,2,512]{2,1,0:T(2,128)(2,1)} %bitcast.1), calls=%async_computation | async-start | bytes 524288 | tf_op jit(solution)/shard_map/all_to_all | solution.py:50
  29.7 2.3 %collective-permute-start = (bf16[32,2048]{1,0:T(8,128)(2,1)S(1)}, bf16[32,2048]{1,0:T(8,128)(2,1)S(1)}, u32[]{:S(2)}, u32[]{:S(2)}) collective-permute-start(bf16[32,2048]{1,0:T(8,128)(2,1)S(1)} %convolution_convert_fusion.4), channel_id=1, source_target_pairs={{0,8},{8,0},{16,24},{24,16},{32,40},{40,32},{48,56},{56,48},{64,72... | collective-permute-start | bytes 393224 | tf_op jit(solution)/shard_map/ppermute | solution.py:22
  32.1 4.8 %collective-permute-start.1 = (bf16[32,2048]{1,0:T(8,128)(2,1)S(1)}, bf16[32,2048]{1,0:T(8,128)(2,1)S(1)}, u32[]{:S(2)}, u32[]{:S(2)}) collective-permute-start(bf16[32,2048]{1,0:T(8,128)(2,1)S(1)} %fusion.23), channel_id=1, source_target_pairs={{0,64},{8,72},{16,80},{24,88},{32,96},{40,104},{48,112},{56,120},{... | collective-permute-start | bytes 393224 | tf_op jit(solution)/shard_map/ppermute | solution.py:22
  36.9 5.4 %collective-permute-start.4 = (bf16[32,2048]{1,0:T(8,128)(2,1)S(1)}, bf16[32,2048]{1,0:T(8,128)(2,1)S(1)}, u32[]{:S(2)}, u32[]{:S(2)}) collective-permute-start(bf16[32,2048]{1,0:T(8,128)(2,1)S(1)} %fusion.41), channel_id=1, source_target_pairs={{0,32},{8,40},{16,48},{24,56},{32,0},{40,8},{48,16},{56,24},{64,96... | collective-permute-start | bytes 393224 | tf_op jit(solution)/shard_map/ppermute | solution.py:22
  38.6 5.7 %collective-permute-start.3 = (bf16[32,2048]{1,0:T(8,128)(2,1)S(1)}, bf16[32,2048]{1,0:T(8,128)(2,1)S(1)}, u32[]{:S(2)}, u32[]{:S(2)}) collective-permute-start(bf16[32,2048]{1,0:T(8,128)(2,1)S(1)} %fusion.41), channel_id=1, source_target_pairs={{0,48},{8,56},{16,0},{24,8},{32,16},{40,24},{48,32},{56,40},{64,11... | collective-permute-start | bytes 393224 | tf_op jit(solution)/shard_map/ppermute | solution.py:22
  40.0 6.3 %collective-permute-start.2 = (bf16[32,2048]{1,0:T(8,128)(2,1)S(1)}, bf16[32,2048]{1,0:T(8,128)(2,1)S(1)}, u32[]{:S(2)}, u32[]{:S(2)}) collective-permute-start(bf16[32,2048]{1,0:T(8,128)(2,1)S(1)} %fusion.41), channel_id=1, source_target_pairs={{0,16},{8,24},{16,32},{24,40},{32,48},{40,56},{48,0},{56,8},{64,80... | collective-permute-start | bytes 393224 | tf_op jit(solution)/shard_map/ppermute | solution.py:22
  46.4 3.2 %collective-permute-start.5 = (bf16[32,2048]{1,0:T(8,128)(2,1)S(1)}, bf16[32,2048]{1,0:T(8,128)(2,1)S(1)}, u32[]{:S(2)}, u32[]{:S(2)}) collective-permute-start(bf16[32,2048]{1,0:T(8,128)(2,1)S(1)} %fusion.13), channel_id=1, source_target_pairs={{0,8},{8,0},{16,24},{24,16},{32,40},{40,32},{48,56},{56,48},{64,72... | collective-permute-start | bytes 393224 | tf_op jit(solution)/shard_map/ppermute | solution.py:22
  51.8 1.4 collective-permute-start.6
  53.2 5.0 %collective-permute-start.7 = (bf16[32,2048]{1,0:T(8,128)(2,1)S(1)}, bf16[32,2048]{1,0:T(8,128)(2,1)S(1)}, u32[]{:S(2)}, u32[]{:S(2)}) collective-permute-start(bf16[32,2048]{1,0:T(8,128)(2,1)S(1)} %fusion.24), channel_id=1, source_target_pairs={{0,64},{8,72},{16,80},{24,88},{32,96},{40,104},{48,112},{56,120},{... | collective-permute-start | bytes 393224 | tf_op jit(solution)/shard_map/ppermute | solution.py:22
  58.3 5.4 %collective-permute-start.10 = (bf16[32,2048]{1,0:T(8,128)(2,1)S(1)}, bf16[32,2048]{1,0:T(8,128)(2,1)S(1)}, u32[]{:S(2)}, u32[]{:S(2)}) collective-permute-start(bf16[32,2048]{1,0:T(8,128)(2,1)S(1)} %fusion.42), channel_id=1, source_target_pairs={{0,32},{8,40},{16,48},{24,56},{32,0},{40,8},{48,16},{56,24},{64,96... | collective-permute-start | bytes 393224 | tf_op jit(solution)/shard_map/ppermute | solution.py:22
  59.2 5.9 %collective-permute-start.9 = (bf16[32,2048]{1,0:T(8,128)(2,1)S(1)}, bf16[32,2048]{1,0:T(8,128)(2,1)S(1)}, u32[]{:S(2)}, u32[]{:S(2)}) collective-permute-start(bf16[32,2048]{1,0:T(8,128)(2,1)S(1)} %fusion.42), channel_id=1, source_target_pairs={{0,48},{8,56},{16,0},{24,8},{32,16},{40,24},{48,32},{56,40},{64,11... | collective-permute-start | bytes 393224 | tf_op jit(solution)/shard_map/ppermute | solution.py:22
  60.5 6.8 %collective-permute-start.8 = (bf16[32,2048]{1,0:T(8,128)(2,1)S(1)}, bf16[32,2048]{1,0:T(8,128)(2,1)S(1)}, u32[]{:S(2)}, u32[]{:S(2)}) collective-permute-start(bf16[32,2048]{1,0:T(8,128)(2,1)S(1)} %fusion.42), channel_id=1, source_target_pairs={{0,16},{8,24},{16,32},{24,40},{32,48},{40,56},{48,0},{56,8},{64,80... | collective-permute-start | bytes 393224 | tf_op jit(solution)/shard_map/ppermute | solution.py:22
  67.5 2.9 %collective-permute-start.11 = (bf16[32,2048]{1,0:T(8,128)(2,1)S(1)}, bf16[32,2048]{1,0:T(8,128)(2,1)S(1)}, u32[]{:S(2)}, u32[]{:S(2)}) collective-permute-start(bf16[32,2048]{1,0:T(8,128)(2,1)S(1)} %fusion.14), channel_id=1, source_target_pairs={{0,8},{8,0},{16,24},{24,16},{32,40},{40,32},{48,56},{56,48},{64,72... | collective-permute-start | bytes 393224 | tf_op jit(solution)/shard_map/ppermute | solution.py:22
  72.6 1.4 collective-permute-start.12
  74.0 5.0 %collective-permute-start.13 = (bf16[32,2048]{1,0:T(8,128)(2,1)S(1)}, bf16[32,2048]{1,0:T(8,128)(2,1)S(1)}, u32[]{:S(2)}, u32[]{:S(2)}) collective-permute-start(bf16[32,2048]{1,0:T(8,128)(2,1)S(1)} %fusion.25), channel_id=1, source_target_pairs={{0,64},{8,72},{16,80},{24,88},{32,96},{40,104},{48,112},{56,120},{... | collective-permute-start | bytes 393224 | tf_op jit(solution)/shard_map/ppermute | solution.py:22
  79.1 5.4 %collective-permute-start.16 = (bf16[32,2048]{1,0:T(8,128)(2,1)S(1)}, bf16[32,2048]{1,0:T(8,128)(2,1)S(1)}, u32[]{:S(2)}, u32[]{:S(2)}) collective-permute-start(bf16[32,2048]{1,0:T(8,128)(2,1)S(1)} %fusion.43), channel_id=1, source_target_pairs={{0,32},{8,40},{16,48},{24,56},{32,0},{40,8},{48,16},{56,24},{64,96... | collective-permute-start | bytes 393224 | tf_op jit(solution)/shard_map/ppermute | solution.py:22
  79.8 5.9 %collective-permute-start.15 = (bf16[32,2048]{1,0:T(8,128)(2,1)S(1)}, bf16[32,2048]{1,0:T(8,128)(2,1)S(1)}, u32[]{:S(2)}, u32[]{:S(2)}) collective-permute-start(bf16[32,2048]{1,0:T(8,128)(2,1)S(1)} %fusion.43), channel_id=1, source_target_pairs={{0,48},{8,56},{16,0},{24,8},{32,16},{40,24},{48,32},{56,40},{64,11... | collective-permute-start | bytes 393224 | tf_op jit(solution)/shard_map/ppermute | solution.py:22
  81.1 6.9 %collective-permute-start.14 = (bf16[32,2048]{1,0:T(8,128)(2,1)S(1)}, bf16[32,2048]{1,0:T(8,128)(2,1)S(1)}, u32[]{:S(2)}, u32[]{:S(2)}) collective-permute-start(bf16[32,2048]{1,0:T(8,128)(2,1)S(1)} %fusion.43), channel_id=1, source_target_pairs={{0,16},{8,24},{16,32},{24,40},{32,48},{40,56},{48,0},{56,8},{64,80... | collective-permute-start | bytes 393224 | tf_op jit(solution)/shard_map/ppermute | solution.py:22
  88.3 2.9 %collective-permute-start.17 = (bf16[32,2048]{1,0:T(8,128)(2,1)S(1)}, bf16[32,2048]{1,0:T(8,128)(2,1)S(1)}, u32[]{:S(2)}, u32[]{:S(2)}) collective-permute-start(bf16[32,2048]{1,0:T(8,128)(2,1)S(1)} %fusion.16), channel_id=1, source_target_pairs={{0,8},{8,0},{16,24},{24,16},{32,40},{40,32},{48,56},{56,48},{64,72... | collective-permute-start | bytes 393224 | tf_op jit(solution)/shard_map/ppermute | solution.py:22
  93.3 1.4 collective-permute-start.18
  94.7 5.0 %collective-permute-start.19 = (bf16[32,2048]{1,0:T(8,128)(2,1)S(1)}, bf16[32,2048]{1,0:T(8,128)(2,1)S(1)}, u32[]{:S(2)}, u32[]{:S(2)}) collective-permute-start(bf16[32,2048]{1,0:T(8,128)(2,1)S(1)} %fusion.26), channel_id=1, source_target_pairs={{0,64},{8,72},{16,80},{24,88},{32,96},{40,104},{48,112},{56,120},{... | collective-permute-start | bytes 393224 | tf_op jit(solution)/shard_map/ppermute | solution.py:22
  99.8 5.4 %collective-permute-start.22 = (bf16[32,2048]{1,0:T(8,128)(2,1)S(1)}, bf16[32,2048]{1,0:T(8,128)(2,1)S(1)}, u32[]{:S(2)}, u32[]{:S(2)}) collective-permute-start(bf16[32,2048]{1,0:T(8,128)(2,1)S(1)} %fusion.44), channel_id=1, source_target_pairs={{0,32},{8,40},{16,48},{24,56},{32,0},{40,8},{48,16},{56,24},{64,96... | collective-permute-start | bytes 393224 | tf_op jit(solution)/shard_map/ppermute | solution.py:22
  100.4 5.9 %collective-permute-start.21 = (bf16[32,2048]{1,0:T(8,128)(2,1)S(1)}, bf16[32,2048]{1,0:T(8,128)(2,1)S(1)}, u32[]{:S(2)}, u32[]{:S(2)}) collective-permute-start(bf16[32,2048]{1,0:T(8,128)(2,1)S(1)} %fusion.44), channel_id=1, source_target_pairs={{0,48},{8,56},{16,0},{24,8},{32,16},{40,24},{48,32},{56,40},{64,11... | collective-permute-start | bytes 393224 | tf_op jit(solution)/shard_map/ppermute | solution.py:22
  101.7 7.0 %collective-permute-start.20 = (bf16[32,2048]{1,0:T(8,128)(2,1)S(1)}, bf16[32,2048]{1,0:T(8,128)(2,1)S(1)}, u32[]{:S(2)}, u32[]{:S(2)}) collective-permute-start(bf16[32,2048]{1,0:T(8,128)(2,1)S(1)} %fusion.44), channel_id=1, source_target_pairs={{0,16},{8,24},{16,32},{24,40},{32,48},{40,56},{48,0},{56,8},{64,80... | collective-permute-start | bytes 393224 | tf_op jit(solution)/shard_map/ppermute | solution.py:22
  108.9 3.1 %collective-permute-start.23 = (bf16[32,2048]{1,0:T(8,128)(2,1)S(1)}, bf16[32,2048]{1,0:T(8,128)(2,1)S(1)}, u32[]{:S(2)}, u32[]{:S(2)}) collective-permute-start(bf16[32,2048]{1,0:T(8,128)(2,1)S(1)} %fusion.17), channel_id=1, source_target_pairs={{0,8},{8,0},{16,24},{24,16},{32,40},{40,32},{48,56},{56,48},{64,72... | collective-permute-start | bytes 393224 | tf_op jit(solution)/shard_map/ppermute | solution.py:22
  114.2 1.4 collective-permute-start.24
  115.6 5.0 %collective-permute-start.25 = (bf16[32,2048]{1,0:T(8,128)(2,1)S(1)}, bf16[32,2048]{1,0:T(8,128)(2,1)S(1)}, u32[]{:S(2)}, u32[]{:S(2)}) collective-permute-start(bf16[32,2048]{1,0:T(8,128)(2,1)S(1)} %fusion.27), channel_id=1, source_target_pairs={{0,64},{8,72},{16,80},{24,88},{32,96},{40,104},{48,112},{56,120},{... | collective-permute-start | bytes 393224 | tf_op jit(solution)/shard_map/ppermute | solution.py:22
  120.7 5.4 %collective-permute-start.28 = (bf16[32,2048]{1,0:T(8,128)(2,1)S(1)}, bf16[32,2048]{1,0:T(8,128)(2,1)S(1)}, u32[]{:S(2)}, u32[]{:S(2)}) collective-permute-start(bf16[32,2048]{1,0:T(8,128)(2,1)S(1)} %fusion.45), channel_id=1, source_target_pairs={{0,32},{8,40},{16,48},{24,56},{32,0},{40,8},{48,16},{56,24},{64,96... | collective-permute-start | bytes 393224 | tf_op jit(solution)/shard_map/ppermute | solution.py:22
  121.2 5.9 %collective-permute-start.27 = (bf16[32,2048]{1,0:T(8,128)(2,1)S(1)}, bf16[32,2048]{1,0:T(8,128)(2,1)S(1)}, u32[]{:S(2)}, u32[]{:S(2)}) collective-permute-start(bf16[32,2048]{1,0:T(8,128)(2,1)S(1)} %fusion.45), channel_id=1, source_target_pairs={{0,48},{8,56},{16,0},{24,8},{32,16},{40,24},{48,32},{56,40},{64,11... | collective-permute-start | bytes 393224 | tf_op jit(solution)/shard_map/ppermute | solution.py:22
  122.5 7.0 %collective-permute-start.26 = (bf16[32,2048]{1,0:T(8,128)(2,1)S(1)}, bf16[32,2048]{1,0:T(8,128)(2,1)S(1)}, u32[]{:S(2)}, u32[]{:S(2)}) collective-permute-start(bf16[32,2048]{1,0:T(8,128)(2,1)S(1)} %fusion.45), channel_id=1, source_target_pairs={{0,16},{8,24},{16,32},{24,40},{32,48},{40,56},{48,0},{56,8},{64,80... | collective-permute-start | bytes 393224 | tf_op jit(solution)/shard_map/ppermute | solution.py:22
  122.7 12.1 %copy-start.3 = (bf16[1024,2048]{1,0:T(8,128)(2,1)S(1)}, bf16[1024,2048]{1,0:T(8,128)(2,1)}, u32[]{:S(2)}) copy-start(bf16[1024,2048]{1,0:T(8,128)(2,1)} %get-tuple-element.7) | copy-start | bytes 12582916
  129.7 5.1 %collective-permute-start.29 = (bf16[32,2048]{1,0:T(8,128)(2,1)S(1)}, bf16[32,2048]{1,0:T(8,128)(2,1)S(1)}, u32[]{:S(2)}, u32[]{:S(2)}) collective-permute-start(bf16[32,2048]{1,0:T(8,128)(2,1)S(1)} %fusion.19), channel_id=1, source_target_pairs={{0,8},{8,0},{16,24},{24,16},{32,40},{40,32},{48,56},{56,48},{64,72... | collective-permute-start | bytes 393224 | tf_op jit(solution)/shard_map/ppermute | solution.py:22
  (6 other events, 37.6 us)

commit v4 on v3

v4 whole, which is shorter than its diff:
```python
import jax
import jax.numpy as jnp
from jax import lax
from jax.sharding import PartitionSpec as P

STEPS = 3


def on_device(mode_basis, node_coords, quad_weights, magnetization, decay_rates, directions):
    row_count = lax.axis_size("row")
    col_count = lax.axis_size("col")
    row_index = lax.axis_index("row")
    col_index = lax.axis_index("col")
    core = row_index % 2
    mode_count = mode_basis.shape[1]
    node_local = mode_basis.shape[0]
    parts, col_width, own_waves = magnetization.shape
    columns = 2 * row_count
    width = mode_count // 2
    f32, bf16 = jnp.float32, jnp.bfloat16

    def move(array, target):
        return lax.ppermute(array, "row", [(r, target(r)) for r in range(row_count)])

    def to_other_core(array):
        return move(array, lambda r: r ^ 1)

    def y_of(r):
        return r ^ 8

    def z_of(r, hops):
        return (r & 9) | ((r + 2 * hops) & 6)

    def exchanged(array, z_core):
        sent = array.astype(bf16)
        pairs = [(r, z_of(r, 1) if r % 2 == z_core else y_of(r)) for r in range(row_count)]
        total = array + lax.ppermute(sent, "row", pairs).astype(f32)
        for hops in (3, 2):
            pairs = [(r, z_of(r, hops)) for r in range(row_count) if r % 2 == z_core]
            total = total + lax.ppermute(sent, "row", pairs).astype(f32)
        return total

    def over_chips(array):
        return exchanged(exchanged(array, 1), 0)

    mine = lax.dynamic_index_in_dim(
        directions.reshape(2 * STEPS, 3, row_count, own_waves), col_index, 3, keepdims=False
    )
    moments = node_coords * quad_weights[None, :]
    weights = jnp.sum(mine[:, :, :, None] * moments[None, :, None, :], axis=1)

    sent = jnp.transpose(magnetization, (2, 0, 1))
    sent = jnp.broadcast_to(sent[None], (row_count,) + sent.shape)
    sent = sent.reshape(row_count * col_count, parts, col_width)
    every = lax.all_to_all(sent, ("row", "col"), 0, 0)
    every = every.reshape(row_count, col_count, parts, col_width)
    every = lax.optimization_barrier(
        jnp.transpose(every, (2, 0, 1, 3)).reshape(columns, mode_count)
    )

    def to_nodes(array, basis):
        return lax.dot_general(
            array, basis, (((1,), (1,)), ((), ())), preferred_element_type=f32
        )

    def to_modes(nodes, basis):
        return lax.dot_general(
            nodes, basis, (((1,), (0,)), ((), ())), preferred_element_type=f32
        )

    def turned(nodes, half_step):
        factor = 0.5 if half_step % 2 == 0 else 1.0
        scale = factor * weights[half_step]
        real, imag = nodes[:row_count], nodes[row_count:]
        rows = jnp.concatenate([scale * imag, -scale * real], axis=0)
        return lax.optimization_barrier(rows.astype(bf16))

    def half_of(array, which, axis):
        return lax.dynamic_slice_in_dim(array, which * width, width, axis)

    basis_own, rest = lax.optimization_barrier((half_of(mode_basis, core, 1), mode_basis))
    basis_other = lax.optimization_barrier(half_of(rest, 1 - core, 1))
    rates = half_of(decay_rates, core, 0)[None, :]
    field = half_of(every, core, 1)
    field_other = half_of(every, 1 - core, 1)

    def weighted(own, other, half_step):
        kept = lax.optimization_barrier(to_nodes(own, basis_own))
        return turned(kept + to_nodes(other, basis_other), half_step)

    def summed(nodes):
        arrived = to_other_core(to_modes(nodes, basis_other).astype(bf16))
        kept = lax.optimization_barrier(to_modes(nodes, basis_own))
        return over_chips(kept + arrived.astype(f32))

    for step in range(STEPS):
        sums = summed(weighted(field, field_other, 2 * step))
        half = (sums + (1.0 - 0.5 * rates) * field.astype(f32)).astype(bf16)
        nodes = weighted(half, to_other_core(half), 2 * step + 1)
        if step + 1 < STEPS:
            update = summed(nodes) + (0.0 - 1.0 * rates) * half.astype(f32)
            field = (field.astype(f32) + update).astype(bf16)
            field_other = to_other_core(field)

    local = field.astype(f32) + (0.0 - 1.0 * rates) * half.astype(f32)
    local = jnp.where(row_index < 2, local, 0.0)
    part_own = (to_modes(nodes, basis_own) + local).astype(bf16)
    part_other = to_modes(nodes, basis_other).astype(bf16)
    low = jnp.where(core == 0, part_own, part_other)
    high = jnp.where(core == 0, part_other, part_own)
    sent = jnp.concatenate([low, high], axis=1)
    sent = sent.reshape(parts, row_count, col_count, col_width)
    sent = jnp.transpose(sent, (1, 2, 0, 3)).reshape(row_count * col_count, parts, col_width)
    every = lax.all_to_all(sent, ("row", "col"), 0, 0)
    every = every.reshape(row_count, col_count, parts, col_width)
    final = jnp.sum(every.astype(f32), axis=0).astype(bf16)
    return jnp.transpose(final, (1, 2, 0))


def solution(mesh):
    return jax.shard_map(
        on_device,
        mesh=mesh,
        in_specs=(P("row", None), P(None, "row"), P("row"), P(None, "col", "row"), P(), P()),
        out_specs=P(None, "col", "row"),
        check_vma=False,
    )
```

time: 157 us -> 175 us (1.11)
  starting transfers between devices: 36.4 us -> 72.7 us
  waiting for transfers between devices: 57.8 us -> 38.4 us
    ppermute x30 -> x10, waiting for transfers between devices: 57.1 us -> 2.24 us  [move(): lax.ppermute(array, 'row', [(r, target(r)) for r in range(row_count)])]
    ppermute x0 -> x30, starting transfers between devices: none -> 44.4 us  [the longest x20 35.1 us: exchanged(): total = total + lax.ppermute(sent, 'row', pairs).astype(f32)]
    ppermute x0 -> x30, waiting for transfers between devices: none -> 36.2 us  [the longest x10 24.9 us: exchanged(): total = array + lax.ppermute(sent, 'row', pairs).astype(f32)]
    ppermute x30 -> x10, starting transfers between devices: 24.9 us -> 16.8 us  [move(): lax.ppermute(array, 'row', [(r, target(r)) for r in range(row_count)])]
    dynamic_slice x1 -> x2, local copies, waits for them, and re-layouts: 8.44 us -> 9.57 us  [half_of(): return lax.dynamic_slice_in_dim(array, which * width, width, axis)]
  transfers between devices with their start and end apart: 31 -> 41, of which waited for: 26 -> 24; matrix products, arithmetic and copies ran while one was open for 15% -> 14% of each run, Pallas kernels for 0% -> 0%
where the time goes in v4:
time: 175 us; the launch traced here: 174 us
  starting transfers between devices  72.7 us (42%)
  waiting for transfers between devices  38.4 us (22%)
  matrix products  30.4 us (17%)
  blocking collectives  16.8 us (10%)
  local copies, waits for them, and re-layouts  13.5 us (8%)
  other arithmetic  2.01 us (1%)
    ppermute x20, starting transfers between devices, exchanged(): total = total + lax.ppermute(sent, 'row', pairs).astype(f32)  35.1 us
    ppermute x10, waiting for transfers between devices, exchanged(): total = array + lax.ppermute(sent, 'row', pairs).astype(f32)  24.9 us
    dot_general x12, matrix products, to_nodes(): lax.dot_general(array, basis, (((1,), (1,)), ((), ())), preferred_element...  20.5 us
    ppermute x10, starting transfers between devices, move(): lax.ppermute(array, 'row', [(r, target(r)) for r in range(row_count)])  16.8 us
    all_to_all x1, blocking collectives, on_device(): every = lax.all_to_all(sent, ('row', 'col'), 0, 0)  16.8 us
    all_to_all x1, starting transfers between devices, on_device(): every = lax.all_to_all(sent, ('row', 'col'), 0, 0)  11.5 us
    ppermute x20, waiting for transfers between devices, exchanged(): total = total + lax.ppermute(sent, 'row', pairs).astype(f32)  11.3 us
    dot_general x12, matrix products, to_modes(): lax.dot_general(nodes, basis, (((1,), (0,)), ((), ())), preferred_element...  9.95 us
  transfers between devices with their start and end apart: 41, of which 24 were waited for; matrix products, arithmetic and copies ran while one was open for 14% of the time, Pallas kernels for 0%

profile of v4, /device:TPU:1, one launch (start us, length us, event | category | flops | bytes accessed | tf_op | source)
XLA Modules:
  0.0 174.4 jit_solution(1114934237779659956)
XLA Ops:
  1.7 11.5 %all-to-all-start = ((bf16[128,2,512]{2,1,0:T(2,128)(2,1)}), bf16[128,2,512]{2,1,0:T(2,128)(2,1)S(1)}, u32[]{:S(2)}, u32[]{:S(2)}) async-start(bf16[128,2,512]{2,1,0:T(2,128)(2,1)} %bitcast.4), calls=%async_computation | async-start | bytes 524288 | tf_op jit(solution)/shard_map/all_to_all | solution.py:55
  14.3 4.8 %constant_dynamic-slice_fusion.1 = bf16[1024,2048]{1,0:T(8,128)(2,1)} fusion(bf16[1024,4096]{1,0:T(8,128)(2,1)} %param.6, s32[]{:T(128)S(6)} %select_n.43), kind=kLoop, calls=%fused_computation.97 | loop fusion | bytes 8388612 | tf_op jit(solution)/shard_map/dynamic_slice | solution.py:79
  19.1 4.8 %constant_dynamic-slice_fusion = bf16[1024,2048]{1,0:T(8,128)(2,1)} fusion(bf16[1024,4096]{1,0:T(8,128)(2,1)} %param.6, s32[]{:T(128)S(6)} %select_n.44), kind=kLoop, calls=%fused_computation.95 | loop fusion | bytes 8388612 | tf_op jit(solution)/shard_map/dynamic_slice | solution.py:79
  24.2 3.7 %fusion.16 = f32[32,1024]{1,0:T(8,128)S(1)} fusion(bf16[1024,2048]{1,0:T(8,128)(2,1)} %constant_dynamic-slice_fusion.1, bf16[32,4096]{1,0:T(8,128)(2,1)S(1)} %bitcast.102, s32[]{:T(128)S(6)} %select_n.43), kind=kOutput, calls=%fused_computation.50 | convolution fusion | flops 134217728 | bytes 4456452 | tf_op jit(solution)/shard_map/dot_general | solution.py:62
  32.3 4.5 %collective-permute-start.3 = (bf16[32,2048]{1,0:T(8,128)(2,1)S(1)}, bf16[32,2048]{1,0:T(8,128)(2,1)S(1)}, u32[]{:S(2)}, u32[]{:S(2)}) collective-permute-start(bf16[32,2048]{1,0:T(8,128)(2,1)S(1)} %fusion.10), channel_id=1, source_target_pairs={{8,40},{24,56},{40,8},{56,24},{72,104},{88,120},{104,72},{120,88},... | collective-permute-start | bytes 393224 | tf_op jit(solution)/shard_map/ppermute | solution.py:40
  36.8 2.5 %collective-permute-start.2 = (bf16[32,2048]{1,0:T(8,128)(2,1)S(1)}, bf16[32,2048]{1,0:T(8,128)(2,1)S(1)}, u32[]{:S(2)}, u32[]{:S(2)}) collective-permute-start(bf16[32,2048]{1,0:T(8,128)(2,1)S(1)} %fusion.10), channel_id=1, source_target_pairs={{8,56},{24,8},{40,24},{56,40},{72,120},{88,72},{104,88},{120,104},... | collective-permute-start | bytes 393224 | tf_op jit(solution)/shard_map/ppermute | solution.py:40
  40.2 2.3 %collective-permute-done.2 = bf16[32,2048]{1,0:T(8,128)(2,1)S(1)} collective-permute-done((bf16[32,2048]{1,0:T(8,128)(2,1)S(1)}, bf16[32,2048]{1,0:T(8,128)(2,1)S(1)}, u32[]{:S(2)}, u32[]{:S(2)}) %collective-permute-start.2) | collective-permute-done | bytes 131104 | tf_op jit(solution)/shard_map/ppermute | solution.py:40
  42.5 1.9 %collective-permute-done.1 = bf16[32,2048]{1,0:T(8,128)(2,1)S(1)} collective-permute-done((bf16[32,2048]{1,0:T(8,128)(2,1)S(1)}, bf16[32,2048]{1,0:T(8,128)(2,1)S(1)}, u32[]{:S(2)}, u32[]{:S(2)}) %collective-permute-start.1) | collective-permute-done | bytes 131104 | tf_op jit(solution)/shard_map/ppermute | solution.py:37
  47.2 2.8 %collective-permute-done.4 = bf16[32,2048]{1,0:T(8,128)(2,1)S(1)} collective-permute-done((bf16[32,2048]{1,0:T(8,128)(2,1)S(1)}, bf16[32,2048]{1,0:T(8,128)(2,1)S(1)}, u32[]{:S(2)}, u32[]{:S(2)}) %collective-permute-start.4) | collective-permute-done | bytes 131104 | tf_op jit(solution)/shard_map/ppermute | solution.py:37
  50.2 3.0 %collective-permute-start.7 = (bf16[32,2048]{1,0:T(8,128)(2,1)S(1)}, bf16[32,2048]{1,0:T(8,128)(2,1)S(1)}, u32[]{:S(2)}, u32[]{:S(2)}) collective-permute-start(bf16[32,2048]{1,0:T(8,128)(2,1)S(1)} %fusion.2), channel_id=1, source_target_pairs={{0,8},{8,0},{16,24},{24,16},{32,40},{40,32},{48,56},{56,48},{64,72... | collective-permute-start | bytes 393224 | tf_op jit(solution)/shard_map/ppermute | solution.py:23
  58.2 2.4 %collective-permute-start.11 = (bf16[32,2048]{1,0:T(8,128)(2,1)S(1)}, bf16[32,2048]{1,0:T(8,128)(2,1)S(1)}, u32[]{:S(2)}, u32[]{:S(2)}) collective-permute-start(bf16[32,2048]{1,0:T(8,128)(2,1)S(1)} %fusion.11), channel_id=1, source_target_pairs={{8,40},{24,56},{40,8},{56,24},{72,104},{88,120},{104,72},{120,88},... | collective-permute-start | bytes 393224 | tf_op jit(solution)/shard_map/ppermute | solution.py:40
  60.6 3.4 %collective-permute-start.10 = (bf16[32,2048]{1,0:T(8,128)(2,1)S(1)}, bf16[32,2048]{1,0:T(8,128)(2,1)S(1)}, u32[]{:S(2)}, u32[]{:S(2)}) collective-permute-start(bf16[32,2048]{1,0:T(8,128)(2,1)S(1)} %fusion.11), channel_id=1, source_target_pairs={{8,56},{24,8},{40,24},{56,40},{72,120},{88,72},{104,88},{120,104},... | collective-permute-start | bytes 393224 | tf_op jit(solution)/shard_map/ppermute | solution.py:40
  66.3 2.8 %collective-permute-done.9 = bf16[32,2048]{1,0:T(8,128)(2,1)S(1)} collective-permute-done((bf16[32,2048]{1,0:T(8,128)(2,1)S(1)}, bf16[32,2048]{1,0:T(8,128)(2,1)S(1)}, u32[]{:S(2)}, u32[]{:S(2)}) %collective-permute-start.9) | collective-permute-done | bytes 131104 | tf_op jit(solution)/shard_map/ppermute | solution.py:37
  71.9 2.6 %collective-permute-done.12 = bf16[32,2048]{1,0:T(8,128)(2,1)S(1)} collective-permute-done((bf16[32,2048]{1,0:T(8,128)(2,1)S(1)}, bf16[32,2048]{1,0:T(8,128)(2,1)S(1)}, u32[]{:S(2)}, u32[]{:S(2)}) %collective-permute-start.12) | collective-permute-done | bytes 131104 | tf_op jit(solution)/shard_map/ppermute | solution.py:37
  74.6 3.3 %collective-permute-start.15 = (bf16[32,2048]{1,0:T(8,128)(2,1)S(1)}, bf16[32,2048]{1,0:T(8,128)(2,1)S(1)}, u32[]{:S(2)}, u32[]{:S(2)}) collective-permute-start(bf16[32,2048]{1,0:T(8,128)(2,1)S(1)} %fusion.3), channel_id=1, source_target_pairs={{0,8},{8,0},{16,24},{24,16},{32,40},{40,32},{48,56},{56,48},{64,72... | collective-permute-start | bytes 393224 | tf_op jit(solution)/shard_map/ppermute | solution.py:23
  82.9 1.9 %collective-permute-start.19 = (bf16[32,2048]{1,0:T(8,128)(2,1)S(1)}, bf16[32,2048]{1,0:T(8,128)(2,1)S(1)}, u32[]{:S(2)}, u32[]{:S(2)}) collective-permute-start(bf16[32,2048]{1,0:T(8,128)(2,1)S(1)} %fusion.12), channel_id=1, source_target_pairs={{8,40},{24,56},{40,8},{56,24},{72,104},{88,120},{104,72},{120,88},... | collective-permute-start | bytes 393224 | tf_op jit(solution)/shard_map/ppermute | solution.py:40
  84.8 3.0 %collective-permute-start.18 = (bf16[32,2048]{1,0:T(8,128)(2,1)S(1)}, bf16[32,2048]{1,0:T(8,128)(2,1)S(1)}, u32[]{:S(2)}, u32[]{:S(2)}) collective-permute-start(bf16[32,2048]{1,0:T(8,128)(2,1)S(1)} %fusion.12), channel_id=1, source_target_pairs={{8,56},{24,8},{40,24},{56,40},{72,120},{88,72},{104,88},{120,104},... | collective-permute-start | bytes 393224 | tf_op jit(solution)/shard_map/ppermute | solution.py:40
  90.5 2.4 %collective-permute-done.17 = bf16[32,2048]{1,0:T(8,128)(2,1)S(1)} collective-permute-done((bf16[32,2048]{1,0:T(8,128)(2,1)S(1)}, bf16[32,2048]{1,0:T(8,128)(2,1)S(1)}, u32[]{:S(2)}, u32[]{:S(2)}) %collective-permute-start.17) | collective-permute-done | bytes 131104 | tf_op jit(solution)/shard_map/ppermute | solution.py:37
  95.7 2.6 %collective-permute-done.20 = bf16[32,2048]{1,0:T(8,128)(2,1)S(1)} collective-permute-done((bf16[32,2048]{1,0:T(8,128)(2,1)S(1)}, bf16[32,2048]{1,0:T(8,128)(2,1)S(1)}, u32[]{:S(2)}, u32[]{:S(2)}) %collective-permute-start.20) | collective-permute-done | bytes 131104 | tf_op jit(solution)/shard_map/ppermute | solution.py:37
  98.4 3.1 %collective-permute-start.23 = (bf16[32,2048]{1,0:T(8,128)(2,1)S(1)}, bf16[32,2048]{1,0:T(8,128)(2,1)S(1)}, u32[]{:S(2)}, u32[]{:S(2)}) collective-permute-start(bf16[32,2048]{1,0:T(8,128)(2,1)S(1)} %fusion.5), channel_id=1, source_target_pairs={{0,8},{8,0},{16,24},{24,16},{32,40},{40,32},{48,56},{56,48},{64,72... | collective-permute-start | bytes 393224 | tf_op jit(solution)/shard_map/ppermute | solution.py:23
  106.5 2.3 %collective-permute-start.27 = (bf16[32,2048]{1,0:T(8,128)(2,1)S(1)}, bf16[32,2048]{1,0:T(8,128)(2,1)S(1)}, u32[]{:S(2)}, u32[]{:S(2)}) collective-permute-start(bf16[32,2048]{1,0:T(8,128)(2,1)S(1)} %fusion.13), channel_id=1, source_target_pairs={{8,40},{24,56},{40,8},{56,24},{72,104},{88,120},{104,72},{120,88},... | collective-permute-start | bytes 393224 | tf_op jit(solution)/shard_map/ppermute | solution.py:40
  108.8 2.8 %collective-permute-start.26 = (bf16[32,2048]{1,0:T(8,128)(2,1)S(1)}, bf16[32,2048]{1,0:T(8,128)(2,1)S(1)}, u32[]{:S(2)}, u32[]{:S(2)}) collective-permute-start(bf16[32,2048]{1,0:T(8,128)(2,1)S(1)} %fusion.13), channel_id=1, source_target_pairs={{8,56},{24,8},{40,24},{56,40},{72,120},{88,72},{104,88},{120,104},... | collective-permute-start | bytes 393224 | tf_op jit(solution)/shard_map/ppermute | solution.py:40
  114.5 2.2 %collective-permute-done.25 = bf16[32,2048]{1,0:T(8,128)(2,1)S(1)} collective-permute-done((bf16[32,2048]{1,0:T(8,128)(2,1)S(1)}, bf16[32,2048]{1,0:T(8,128)(2,1)S(1)}, u32[]{:S(2)}, u32[]{:S(2)}) %collective-permute-start.25) | collective-permute-done | bytes 131104 | tf_op jit(solution)/shard_map/ppermute | solution.py:37
  119.4 2.7 %collective-permute-done.28 = bf16[32,2048]{1,0:T(8,128)(2,1)S(1)} collective-permute-done((bf16[32,2048]{1,0:T(8,128)(2,1)S(1)}, bf16[32,2048]{1,0:T(8,128)(2,1)S(1)}, u32[]{:S(2)}, u32[]{:S(2)}) %collective-permute-start.28) | collective-permute-done | bytes 131104 | tf_op jit(solution)/shard_map/ppermute | solution.py:37
  122.3 3.2 %collective-permute-start.31 = (bf16[32,2048]{1,0:T(8,128)(2,1)S(1)}, bf16[32,2048]{1,0:T(8,128)(2,1)S(1)}, u32[]{:S(2)}, u32[]{:S(2)}) collective-permute-start(bf16[32,2048]{1,0:T(8,128)(2,1)S(1)} %fusion.6), channel_id=1, source_target_pairs={{0,8},{8,0},{16,24},{24,16},{32,40},{40,32},{48,56},{56,48},{64,72... | collective-permute-start | bytes 393224 | tf_op jit(solution)/shard_map/ppermute | solution.py:23
  130.4 2.7 %collective-permute-start.35 = (bf16[32,2048]{1,0:T(8,128)(2,1)S(1)}, bf16[32,2048]{1,0:T(8,128)(2,1)S(1)}, u32[]{:S(2)}, u32[]{:S(2)}) collective-permute-start(bf16[32,2048]{1,0:T(8,128)(2,1)S(1)} %fusion.14), channel_id=1, source_target_pairs={{8,40},{24,56},{40,8},{56,24},{72,104},{88,120},{104,72},{120,88},... | collective-permute-start | bytes 393224 | tf_op jit(solution)/shard_map/ppermute | solution.py:40
  133.2 2.9 %collective-permute-start.34 = (bf16[32,2048]{1,0:T(8,128)(2,1)S(1)}, bf16[32,2048]{1,0:T(8,128)(2,1)S(1)}, u32[]{:S(2)}, u32[]{:S(2)}) collective-permute-start(bf16[32,2048]{1,0:T(8,128)(2,1)S(1)} %fusion.14), channel_id=1, source_target_pairs={{8,56},{24,8},{40,24},{56,40},{72,120},{88,72},{104,88},{120,104},... | collective-permute-start | bytes 393224 | tf_op jit(solution)/shard_map/ppermute | solution.py:40
  138.9 2.2 %collective-permute-done.33 = bf16[32,2048]{1,0:T(8,128)(2,1)S(1)} collective-permute-done((bf16[32,2048]{1,0:T(8,128)(2,1)S(1)}, bf16[32,2048]{1,0:T(8,128)(2,1)S(1)}, u32[]{:S(2)}, u32[]{:S(2)}) %collective-permute-start.33) | collective-permute-done | bytes 131104 | tf_op jit(solution)/shard_map/ppermute | solution.py:37
  143.9 2.6 %collective-permute-done.36 = bf16[32,2048]{1,0:T(8,128)(2,1)S(1)} collective-permute-done((bf16[32,2048]{1,0:T(8,128)(2,1)S(1)}, bf16[32,2048]{1,0:T(8,128)(2,1)S(1)}, u32[]{:S(2)}, u32[]{:S(2)}) %collective-permute-start.36) | collective-permute-done | bytes 131104 | tf_op jit(solution)/shard_map/ppermute | solution.py:37
  146.7 3.0 %collective-permute-start.39 = (bf16[32,2048]{1,0:T(8,128)(2,1)S(1)}, bf16[32,2048]{1,0:T(8,128)(2,1)S(1)}, u32[]{:S(2)}, u32[]{:S(2)}) collective-permute-start(bf16[32,2048]{1,0:T(8,128)(2,1)S(1)} %fusion.8), channel_id=1, source_target_pairs={{0,8},{8,0},{16,24},{24,16},{32,40},{40,32},{48,56},{56,48},{64,72... | collective-permute-start | bytes 393224 | tf_op jit(solution)/shard_map/ppermute | solution.py:23
  149.7 3.5 %fusion.49 = f32[32,1024]{1,0:T(8,128)S(1)} fusion(bf16[32,2048]{1,0:T(8,128)(2,1)S(1)} %fusion.8, bf16[1024,2048]{1,0:T(8,128)(2,1)} %constant_dynamic-slice_fusion.1), kind=kOutput, calls=%fused_computation.113 | convolution fusion | flops 134217728 | bytes 4456448 | tf_op jit(solution)/shard_map/dot_general | solution.py:62
  156.8 16.8 %all_to_all.10 = bf16[128,2,512]{2,1,0:T(2,128)(2,1)S(1)} all-to-all(bf16[128,2,512]{2,1,0:T(2,128)(2,1)S(1)} %bitcast.111), channel_id=1, replica_groups=mesh['row'=16,'col'=8] {'row','col'}, dimensions={0} | all-to-all | bytes 524288 | tf_op jit(solution)/shard_map/all_to_all | solution.py:114
  (135 shorter events, 57.7 us)
Async XLA Ops:
  1.7 22.4 %all-to-all-start = ((bf16[128,2,512]{2,1,0:T(2,128)(2,1)}), bf16[128,2,512]{2,1,0:T(2,128)(2,1)S(1)}, u32[]{:S(2)}, u32[]{:S(2)}) async-start(bf16[128,2,512]{2,1,0:T(2,128)(2,1)} %bitcast.4), calls=%async_computation | async-start | bytes 524288 | tf_op jit(solution)/shard_map/all_to_all | solution.py:55
  30.2 2.1 %collective-permute-start = (bf16[32,2048]{1,0:T(8,128)(2,1)S(1)}, bf16[32,2048]{1,0:T(8,128)(2,1)S(1)}, u32[]{:S(2)}, u32[]{:S(2)}) collective-permute-start(bf16[32,2048]{1,0:T(8,128)(2,1)S(1)} %convolution_convert_fusion.5), channel_id=1, source_target_pairs={{0,8},{8,0},{16,24},{24,16},{32,40},{40,32},{48,56},{56,48},{64,72... | collective-permute-start | bytes 393224 | tf_op jit(solution)/shard_map/ppermute | solution.py:23
  32.3 7.9 %collective-permute-start.3 = (bf16[32,2048]{1,0:T(8,128)(2,1)S(1)}, bf16[32,2048]{1,0:T(8,128)(2,1)S(1)}, u32[]{:S(2)}, u32[]{:S(2)}) collective-permute-start(bf16[32,2048]{1,0:T(8,128)(2,1)S(1)} %fusion.10), channel_id=1, source_target_pairs={{8,40},{24,56},{40,8},{56,24},{72,104},{88,120},{104,72},{120,88},... | collective-permute-start | bytes 393224 | tf_op jit(solution)/shard_map/ppermute | solution.py:40
  36.8 5.7 %collective-permute-start.2 = (bf16[32,2048]{1,0:T(8,128)(2,1)S(1)}, bf16[32,2048]{1,0:T(8,128)(2,1)S(1)}, u32[]{:S(2)}, u32[]{:S(2)}) collective-permute-start(bf16[32,2048]{1,0:T(8,128)(2,1)S(1)} %fusion.10), channel_id=1, source_target_pairs={{8,56},{24,8},{40,24},{56,40},{72,120},{88,72},{104,88},{120,104},... | collective-permute-start | bytes 393224 | tf_op jit(solution)/shard_map/ppermute | solution.py:40
  39.3 5.1 %collective-permute-start.1 = (bf16[32,2048]{1,0:T(8,128)(2,1)S(1)}, bf16[32,2048]{1,0:T(8,128)(2,1)S(1)}, u32[]{:S(2)}, u32[]{:S(2)}) collective-permute-start(bf16[32,2048]{1,0:T(8,128)(2,1)S(1)} %fusion.10), channel_id=1, source_target_pairs={{0,64},{8,24},{16,80},{24,40},{32,96},{40,56},{48,112},{56,8},{64,... | collective-permute-start | bytes 393224 | tf_op jit(solution)/shard_map/ppermute | solution.py:37
  44.5 2.7 %collective-permute-start.6 = (bf16[32,2048]{1,0:T(8,128)(2,1)S(1)}, bf16[32,2048]{1,0:T(8,128)(2,1)S(1)}, u32[]{:S(2)}, u32[]{:S(2)}) collective-permute-start(bf16[32,2048]{1,0:T(8,128)(2,1)S(1)} %fusion.35), channel_id=1, source_target_pairs={{0,32},{16,48},{32,0},{48,16},{64,96},{80,112},{96,64},{112,80},{1... | collective-permute-start | bytes 393224 | tf_op jit(solution)/shard_map/ppermute | solution.py:40
  45.8 4.2 %collective-permute-start.4 = (bf16[32,2048]{1,0:T(8,128)(2,1)S(1)}, bf16[32,2048]{1,0:T(8,128)(2,1)S(1)}, u32[]{:S(2)}, u32[]{:S(2)}) collective-permute-start(bf16[32,2048]{1,0:T(8,128)(2,1)S(1)} %fusion.35), channel_id=1, source_target_pairs={{0,16},{8,72},{16,32},{24,88},{32,48},{40,104},{48,0},{56,120},{64... | collective-permute-start | bytes 393224 | tf_op jit(solution)/shard_map/ppermute | solution.py:37
  50.2 4.3 %collective-permute-start.7 = (bf16[32,2048]{1,0:T(8,128)(2,1)S(1)}, bf16[32,2048]{1,0:T(8,128)(2,1)S(1)}, u32[]{:S(2)}, u32[]{:S(2)}) collective-permute-start(bf16[32,2048]{1,0:T(8,128)(2,1)S(1)} %fusion.2), channel_id=1, source_target_pairs={{0,8},{8,0},{16,24},{24,16},{32,40},{40,32},{48,56},{56,48},{64,72... | collective-permute-start | bytes 393224 | tf_op jit(solution)/shard_map/ppermute | solution.py:23
  58.2 7.2 %collective-permute-start.11 = (bf16[32,2048]{1,0:T(8,128)(2,1)S(1)}, bf16[32,2048]{1,0:T(8,128)(2,1)S(1)}, u32[]{:S(2)}, u32[]{:S(2)}) collective-permute-start(bf16[32,2048]{1,0:T(8,128)(2,1)S(1)} %fusion.11), channel_id=1, source_target_pairs={{8,40},{24,56},{40,8},{56,24},{72,104},{88,120},{104,72},{120,88},... | collective-permute-start | bytes 393224 | tf_op jit(solution)/shard_map/ppermute | solution.py:40
  60.6 5.7 %collective-permute-start.10 = (bf16[32,2048]{1,0:T(8,128)(2,1)S(1)}, bf16[32,2048]{1,0:T(8,128)(2,1)S(1)}, u32[]{:S(2)}, u32[]{:S(2)}) collective-permute-start(bf16[32,2048]{1,0:T(8,128)(2,1)S(1)} %fusion.11), channel_id=1, source_target_pairs={{8,56},{24,8},{40,24},{56,40},{72,120},{88,72},{104,88},{120,104},... | collective-permute-start | bytes 393224 | tf_op jit(solution)/shard_map/ppermute | solution.py:40
  64.0 5.1 %collective-permute-start.9 = (bf16[32,2048]{1,0:T(8,128)(2,1)S(1)}, bf16[32,2048]{1,0:T(8,128)(2,1)S(1)}, u32[]{:S(2)}, u32[]{:S(2)}) collective-permute-start(bf16[32,2048]{1,0:T(8,128)(2,1)S(1)} %fusion.11), channel_id=1, source_target_pairs={{0,64},{8,24},{16,80},{24,40},{32,96},{40,56},{48,112},{56,8},{64,... | collective-permute-start | bytes 393224 | tf_op jit(solution)/shard_map/ppermute | solution.py:37
  69.2 2.7 %collective-permute-start.14 = (bf16[32,2048]{1,0:T(8,128)(2,1)S(1)}, bf16[32,2048]{1,0:T(8,128)(2,1)S(1)}, u32[]{:S(2)}, u32[]{:S(2)}) collective-permute-start(bf16[32,2048]{1,0:T(8,128)(2,1)S(1)} %fusion.36), channel_id=1, source_target_pairs={{0,32},{16,48},{32,0},{48,16},{64,96},{80,112},{96,64},{112,80},{1... | collective-permute-start | bytes 393224 | tf_op jit(solution)/shard_map/ppermute | solution.py:40
  70.6 3.9 %collective-permute-start.12 = (bf16[32,2048]{1,0:T(8,128)(2,1)S(1)}, bf16[32,2048]{1,0:T(8,128)(2,1)S(1)}, u32[]{:S(2)}, u32[]{:S(2)}) collective-permute-start(bf16[32,2048]{1,0:T(8,128)(2,1)S(1)} %fusion.36), channel_id=1, source_target_pairs={{0,16},{8,72},{16,32},{24,88},{32,48},{40,104},{48,0},{56,120},{64... | collective-permute-start | bytes 393224 | tf_op jit(solution)/shard_map/ppermute | solution.py:37
  74.6 4.6 %collective-permute-start.15 = (bf16[32,2048]{1,0:T(8,128)(2,1)S(1)}, bf16[32,2048]{1,0:T(8,128)(2,1)S(1)}, u32[]{:S(2)}, u32[]{:S(2)}) collective-permute-start(bf16[32,2048]{1,0:T(8,128)(2,1)S(1)} %fusion.3), channel_id=1, source_target_pairs={{0,8},{8,0},{16,24},{24,16},{32,40},{40,32},{48,56},{56,48},{64,72... | collective-permute-start | bytes 393224 | tf_op jit(solution)/shard_map/ppermute | solution.py:23
  82.9 7.2 %collective-permute-start.19 = (bf16[32,2048]{1,0:T(8,128)(2,1)S(1)}, bf16[32,2048]{1,0:T(8,128)(2,1)S(1)}, u32[]{:S(2)}, u32[]{:S(2)}) collective-permute-start(bf16[32,2048]{1,0:T(8,128)(2,1)S(1)} %fusion.12), channel_id=1, source_target_pairs={{8,40},{24,56},{40,8},{56,24},{72,104},{88,120},{104,72},{120,88},... | collective-permute-start | bytes 393224 | tf_op jit(solution)/shard_map/ppermute | solution.py:40
  84.8 5.7 %collective-permute-start.18 = (bf16[32,2048]{1,0:T(8,128)(2,1)S(1)}, bf16[32,2048]{1,0:T(8,128)(2,1)S(1)}, u32[]{:S(2)}, u32[]{:S(2)}) collective-permute-start(bf16[32,2048]{1,0:T(8,128)(2,1)S(1)} %fusion.12), channel_id=1, source_target_pairs={{8,56},{24,8},{40,24},{56,40},{72,120},{88,72},{104,88},{120,104},... | collective-permute-start | bytes 393224 | tf_op jit(solution)/shard_map/ppermute | solution.py:40
  87.8 5.1 %collective-permute-start.17 = (bf16[32,2048]{1,0:T(8,128)(2,1)S(1)}, bf16[32,2048]{1,0:T(8,128)(2,1)S(1)}, u32[]{:S(2)}, u32[]{:S(2)}) collective-permute-start(bf16[32,2048]{1,0:T(8,128)(2,1)S(1)} %fusion.12), channel_id=1, source_target_pairs={{0,64},{8,24},{16,80},{24,40},{32,96},{40,56},{48,112},{56,8},{64,... | collective-permute-start | bytes 393224 | tf_op jit(solution)/shard_map/ppermute | solution.py:37
  93.0 2.7 %collective-permute-start.22 = (bf16[32,2048]{1,0:T(8,128)(2,1)S(1)}, bf16[32,2048]{1,0:T(8,128)(2,1)S(1)}, u32[]{:S(2)}, u32[]{:S(2)}) collective-permute-start(bf16[32,2048]{1,0:T(8,128)(2,1)S(1)} %fusion.37), channel_id=1, source_target_pairs={{0,32},{16,48},{32,0},{48,16},{64,96},{80,112},{96,64},{112,80},{1... | collective-permute-start | bytes 393224 | tf_op jit(solution)/shard_map/ppermute | solution.py:40
  94.4 3.9 %collective-permute-start.20 = (bf16[32,2048]{1,0:T(8,128)(2,1)S(1)}, bf16[32,2048]{1,0:T(8,128)(2,1)S(1)}, u32[]{:S(2)}, u32[]{:S(2)}) collective-permute-start(bf16[32,2048]{1,0:T(8,128)(2,1)S(1)} %fusion.37), channel_id=1, source_target_pairs={{0,16},{8,72},{16,32},{24,88},{32,48},{40,104},{48,0},{56,120},{64... | collective-permute-start | bytes 393224 | tf_op jit(solution)/shard_map/ppermute | solution.py:37
  98.4 4.4 %collective-permute-start.23 = (bf16[32,2048]{1,0:T(8,128)(2,1)S(1)}, bf16[32,2048]{1,0:T(8,128)(2,1)S(1)}, u32[]{:S(2)}, u32[]{:S(2)}) collective-permute-start(bf16[32,2048]{1,0:T(8,128)(2,1)S(1)} %fusion.5), channel_id=1, source_target_pairs={{0,8},{8,0},{16,24},{24,16},{32,40},{40,32},{48,56},{56,48},{64,72... | collective-permute-start | bytes 393224 | tf_op jit(solution)/shard_map/ppermute | solution.py:23
  106.5 7.2 %collective-permute-start.27 = (bf16[32,2048]{1,0:T(8,128)(2,1)S(1)}, bf16[32,2048]{1,0:T(8,128)(2,1)S(1)}, u32[]{:S(2)}, u32[]{:S(2)}) collective-permute-start(bf16[32,2048]{1,0:T(8,128)(2,1)S(1)} %fusion.13), channel_id=1, source_target_pairs={{8,40},{24,56},{40,8},{56,24},{72,104},{88,120},{104,72},{120,88},... | collective-permute-start | bytes 393224 | tf_op jit(solution)/shard_map/ppermute | solution.py:40
  108.8 5.7 %collective-permute-start.26 = (bf16[32,2048]{1,0:T(8,128)(2,1)S(1)}, bf16[32,2048]{1,0:T(8,128)(2,1)S(1)}, u32[]{:S(2)}, u32[]{:S(2)}) collective-permute-start(bf16[32,2048]{1,0:T(8,128)(2,1)S(1)} %fusion.13), channel_id=1, source_target_pairs={{8,56},{24,8},{40,24},{56,40},{72,120},{88,72},{104,88},{120,104},... | collective-permute-start | bytes 393224 | tf_op jit(solution)/shard_map/ppermute | solution.py:40
  111.6 5.1 %collective-permute-start.25 = (bf16[32,2048]{1,0:T(8,128)(2,1)S(1)}, bf16[32,2048]{1,0:T(8,128)(2,1)S(1)}, u32[]{:S(2)}, u32[]{:S(2)}) collective-permute-start(bf16[32,2048]{1,0:T(8,128)(2,1)S(1)} %fusion.13), channel_id=1, source_target_pairs={{0,64},{8,24},{16,80},{24,40},{32,96},{40,56},{48,112},{56,8},{64,... | collective-permute-start | bytes 393224 | tf_op jit(solution)/shard_map/ppermute | solution.py:37
  116.7 2.7 %collective-permute-start.30 = (bf16[32,2048]{1,0:T(8,128)(2,1)S(1)}, bf16[32,2048]{1,0:T(8,128)(2,1)S(1)}, u32[]{:S(2)}, u32[]{:S(2)}) collective-permute-start(bf16[32,2048]{1,0:T(8,128)(2,1)S(1)} %fusion.38), channel_id=1, source_target_pairs={{0,32},{16,48},{32,0},{48,16},{64,96},{80,112},{96,64},{112,80},{1... | collective-permute-start | bytes 393224 | tf_op jit(solution)/shard_map/ppermute | solution.py:40
  118.1 4.0 %collective-permute-start.28 = (bf16[32,2048]{1,0:T(8,128)(2,1)S(1)}, bf16[32,2048]{1,0:T(8,128)(2,1)S(1)}, u32[]{:S(2)}, u32[]{:S(2)}) collective-permute-start(bf16[32,2048]{1,0:T(8,128)(2,1)S(1)} %fusion.38), channel_id=1, source_target_pairs={{0,16},{8,72},{16,32},{24,88},{32,48},{40,104},{48,0},{56,120},{64... | collective-permute-start | bytes 393224 | tf_op jit(solution)/shard_map/ppermute | solution.py:37
  122.3 4.5 %collective-permute-start.31 = (bf16[32,2048]{1,0:T(8,128)(2,1)S(1)}, bf16[32,2048]{1,0:T(8,128)(2,1)S(1)}, u32[]{:S(2)}, u32[]{:S(2)}) collective-permute-start(bf16[32,2048]{1,0:T(8,128)(2,1)S(1)} %fusion.6), channel_id=1, source_target_pairs={{0,8},{8,0},{16,24},{24,16},{32,40},{40,32},{48,56},{56,48},{64,72... | collective-permute-start | bytes 393224 | tf_op jit(solution)/shard_map/ppermute | solution.py:23
  130.4 7.2 %collective-permute-start.35 = (bf16[32,2048]{1,0:T(8,128)(2,1)S(1)}, bf16[32,2048]{1,0:T(8,128)(2,1)S(1)}, u32[]{:S(2)}, u32[]{:S(2)}) collective-permute-start(bf16[32,2048]{1,0:T(8,128)(2,1)S(1)} %fusion.14), channel_id=1, source_target_pairs={{8,40},{24,56},{40,8},{56,24},{72,104},{88,120},{104,72},{120,88},... | collective-permute-start | bytes 393224 | tf_op jit(solution)/shard_map/ppermute | solution.py:40
  133.2 5.7 %collective-permute-start.34 = (bf16[32,2048]{1,0:T(8,128)(2,1)S(1)}, bf16[32,2048]{1,0:T(8,128)(2,1)S(1)}, u32[]{:S(2)}, u32[]{:S(2)}) collective-permute-start(bf16[32,2048]{1,0:T(8,128)(2,1)S(1)} %fusion.14), channel_id=1, source_target_pairs={{8,56},{24,8},{40,24},{56,40},{72,120},{88,72},{104,88},{120,104},... | collective-permute-start | bytes 393224 | tf_op jit(solution)/shard_map/ppermute | solution.py:40
  136.0 5.1 %collective-permute-start.33 = (bf16[32,2048]{1,0:T(8,128)(2,1)S(1)}, bf16[32,2048]{1,0:T(8,128)(2,1)S(1)}, u32[]{:S(2)}, u32[]{:S(2)}) collective-permute-start(bf16[32,2048]{1,0:T(8,128)(2,1)S(1)} %fusion.14), channel_id=1, source_target_pairs={{0,64},{8,24},{16,80},{24,40},{32,96},{40,56},{48,112},{56,8},{64,... | collective-permute-start | bytes 393224 | tf_op jit(solution)/shard_map/ppermute | solution.py:37
  141.2 2.7 %collective-permute-start.38 = (bf16[32,2048]{1,0:T(8,128)(2,1)S(1)}, bf16[32,2048]{1,0:T(8,128)(2,1)S(1)}, u32[]{:S(2)}, u32[]{:S(2)}) collective-permute-start(bf16[32,2048]{1,0:T(8,128)(2,1)S(1)} %fusion.39), channel_id=1, source_target_pairs={{0,32},{16,48},{32,0},{48,16},{64,96},{80,112},{96,64},{112,80},{1... | collective-permute-start | bytes 393224 | tf_op jit(solution)/shard_map/ppermute | solution.py:40
  142.6 4.0 %collective-permute-start.36 = (bf16[32,2048]{1,0:T(8,128)(2,1)S(1)}, bf16[32,2048]{1,0:T(8,128)(2,1)S(1)}, u32[]{:S(2)}, u32[]{:S(2)}) collective-permute-start(bf16[32,2048]{1,0:T(8,128)(2,1)S(1)} %fusion.39), channel_id=1, source_target_pairs={{0,16},{8,72},{16,32},{24,88},{32,48},{40,104},{48,0},{56,120},{64... | collective-permute-start | bytes 393224 | tf_op jit(solution)/shard_map/ppermute | solution.py:37
  146.7 6.5 %collective-permute-start.39 = (bf16[32,2048]{1,0:T(8,128)(2,1)S(1)}, bf16[32,2048]{1,0:T(8,128)(2,1)S(1)}, u32[]{:S(2)}, u32[]{:S(2)}) collective-permute-start(bf16[32,2048]{1,0:T(8,128)(2,1)S(1)} %fusion.8), channel_id=1, source_target_pairs={{0,8},{8,0},{16,24},{24,16},{32,40},{40,32},{48,56},{56,48},{64,72... | collective-permute-start | bytes 393224 | tf_op jit(solution)/shard_map/ppermute | solution.py:23
  (16 other events, 61.8 us)

commit v5 on v4

--- a/solution.py
+++ b/solution.py
@@ -25,23 +25,12 @@
     def to_other_core(array):
         return move(array, lambda r: r ^ 1)
 
-    def y_of(r):
-        return r ^ 8
+    rounds = ((8, 2), (2, 6), (6, 8))
 
-    def z_of(r, hops):
-        return (r & 9) | ((r + 2 * hops) & 6)
-
-    def exchanged(array, z_core):
-        sent = array.astype(bf16)
-        pairs = [(r, z_of(r, 1) if r % 2 == z_core else y_of(r)) for r in range(row_count)]
-        total = array + lax.ppermute(sent, "row", pairs).astype(f32)
-        for hops in (3, 2):
-            pairs = [(r, z_of(r, hops)) for r in range(row_count) if r % 2 == z_core]
-            total = total + lax.ppermute(sent, "row", pairs).astype(f32)
+    def over_chips(total):
+        for bits in rounds:
+            total = total + move(total.astype(bf16), lambda r: r ^ bits[r % 2]).astype(f32)
         return total
-
-    def over_chips(array):
-        return exchanged(exchanged(array, 1), 0)
 
     mine = lax.dynamic_index_in_dim(
         directions.reshape(2 * STEPS, 3, row_count, own_waves), col_index, 3, keepdims=False
@@ -78,8 +67,8 @@
     def half_of(array, which, axis):
         return lax.dynamic_slice_in_dim(array, which * width, width, axis)
 
-    basis_own, rest = lax.optimization_barrier((half_of(mode_basis, core, 1), mode_basis))
-    basis_other = lax.optimization_barrier(half_of(rest, 1 - core, 1))
+    basis_own = half_of(mode_basis, core, 1)
+    basis_other = half_of(mode_basis, 1 - core, 1)
     rates = half_of(decay_rates, core, 0)[None, :]
     field = half_of(every, core, 1)
     field_other = half_of(every, 1 - core, 1)

time: 175 us -> 167 us (0.954)
  starting transfers between devices: 72.7 us -> 37 us
  waiting for transfers between devices: 38.4 us -> 70.3 us
  local copies, waits for them, and re-layouts: 13.5 us -> 3.89 us
  matrix products: 30.4 us -> 39.3 us
  blocking collectives: 16.8 us -> 13.4 us
    ppermute x10 -> x25, waiting for transfers between devices: 2.24 us -> 61.9 us  [move(): lax.ppermute(array, 'row', [(r, target(r)) for r in range(row_count)])]
    ppermute x30 -> x0, starting transfers between devices: 44.4 us -> none  [the longest x20 35.1 us: exchanged(): total = total + lax.ppermute(sent, 'row', pairs).astype(f32)]
    ppermute x30 -> x0, waiting for transfers between devices: 36.2 us -> none  [the longest x10 24.9 us: exchanged(): total = array + lax.ppermute(sent, 'row', pairs).astype(f32)]
    dynamic_slice x2 -> x0, local copies, waits for them, and re-layouts: 9.57 us -> none  [half_of(): return lax.dynamic_slice_in_dim(array, which * width, width, axis)]
    ppermute x10 -> x25, starting transfers between devices: 16.8 us -> 25.5 us  [move(): lax.ppermute(array, 'row', [(r, target(r)) for r in range(row_count)])]
    all_to_all x1, waiting for transfers between devices: 0.01 us -> 8.42 us  [on_device(): every = lax.all_to_all(sent, ('row', 'col'), 0, 0)]
    dot_general x12, matrix products: 20.5 us -> 24.9 us  [to_nodes(): lax.dot_general(array, basis, (((1,), (1,)), ((), ())), preferred_element...]
    dot_general x12, matrix products: 9.95 us -> 14.3 us  [to_modes(): lax.dot_general(nodes, basis, (((1,), (0,)), ((), ())), preferred_element...]
  transfers between devices with their start and end apart: 41 -> 26, of which waited for: 24 -> 21; matrix products, arithmetic and copies ran while one was open for 14% -> 9% of each run, Pallas kernels for 0% -> 0%
where the time goes in v5:
time: 167 us
  waiting for transfers between devices  70.3 us (42%)
  matrix products  39.3 us (24%)
  starting transfers between devices  37 us (22%)
  blocking collectives  13.4 us (8%)
  local copies, waits for them, and re-layouts  3.89 us (2%)
  other arithmetic  2.62 us (2%)
    ppermute x25, waiting for transfers between devices, move(): lax.ppermute(array, 'row', [(r, target(r)) for r in range(row_count)])  61.9 us
    ppermute x25, starting transfers between devices, move(): lax.ppermute(array, 'row', [(r, target(r)) for r in range(row_count)])  25.5 us
    dot_general x12, matrix products, to_nodes(): lax.dot_general(array, basis, (((1,), (1,)), ((), ())), preferred_element...  24.9 us
    dot_general x12, matrix products, to_modes(): lax.dot_general(nodes, basis, (((1,), (0,)), ((), ())), preferred_element...  14.3 us
    all_to_all x1, blocking collectives, on_device(): every = lax.all_to_all(sent, ('row', 'col'), 0, 0)  13.4 us
    all_to_all x1, starting transfers between devices, on_device(): every = lax.all_to_all(sent, ('row', 'col'), 0, 0)  11.5 us
    all_to_all x1, waiting for transfers between devices, on_device(): every = lax.all_to_all(sent, ('row', 'col'), 0, 0)  8.42 us
  transfers between devices with their start and end apart: 26, of which 21 were waited for; matrix products, arithmetic and copies ran while one was open for 9% of the time, Pallas kernels for 0%

profile of v5, /device:TPU:1, one launch (start us, length us, event | category | flops | bytes accessed | tf_op | source)
XLA Modules:
  0.0 166.9 jit_solution(3703932068738605205)
XLA Ops:
  1.6 11.5 %all-to-all-start = ((bf16[128,2,512]{2,1,0:T(2,128)(2,1)}), bf16[128,2,512]{2,1,0:T(2,128)(2,1)S(1)}, u32[]{:S(2)}, u32[]{:S(2)}) async-start(bf16[128,2,512]{2,1,0:T(2,128)(2,1)} %bitcast.4), calls=%async_computation | async-start | bytes 524288 | tf_op jit(solution)/shard_map/all_to_all | solution.py:44
  15.2 8.4 %all-to-all-done = bf16[128,2,512]{2,1,0:T(2,128)(2,1)S(1)} async-done(((bf16[128,2,512]{2,1,0:T(2,128)(2,1)}), bf16[128,2,512]{2,1,0:T(2,128)(2,1)S(1)}, u32[]{:S(2)}, u32[]{:S(2)}) %all-to-all-start) | async-done | bytes 262176 | tf_op jit(solution)/shard_map/all_to_all | solution.py:44
  23.8 3.7 %fusion.21 = f32[32,1024]{1,0:T(8,128)S(1)} fusion(bf16[32,4096]{1,0:T(8,128)(2,1)S(1)} %bitcast.78, s32[]{:T(128)S(6)} %select_n.43, bf16[1024,4096]{1,0:T(8,128)(2,1)} %param.6), kind=kOutput, calls=%fused_computation.60 | convolution fusion | flops 134217728 | bytes 4457472 | tf_op jit(solution)/shard_map/dot_general | solution.py:51
  27.4 3.5 %convolution_add_fusion.6 = f32[32,1024]{1,0:T(8,128)S(1)} fusion(f32[32,1024]{1,0:T(8,128)S(1)} %fusion.21, bf16[32,4096]{1,0:T(8,128)(2,1)S(1)} %bitcast.79, s32[]{:T(128)S(6)} %select_n.44, bf16[1024,4096]{1,0:T(8,128)(2,1)} %param.6), kind=kOutput, calls=%fused_computation.14 | convolution fusion | flops 134250496 | bytes 4588544 | tf_op jit(solution)/shard_map/dot_general | solution.py:51
  31.9 1.4 collective-permute-start
  35.0 3.6 %collective-permute-done.1 = bf16[32,2048]{1,0:T(8,128)(2,1)S(1)} collective-permute-done((bf16[32,2048]{1,0:T(8,128)(2,1)S(1)}, bf16[32,2048]{1,0:T(8,128)(2,1)S(1)}, u32[]{:S(2)}, u32[]{:S(2)}) %collective-permute-start.1) | collective-permute-done | bytes 131104 | tf_op jit(solution)/shard_map/ppermute | solution.py:23
  39.2 4.5 %collective-permute-done.2 = bf16[32,2048]{1,0:T(8,128)(2,1)S(1)} collective-permute-done((bf16[32,2048]{1,0:T(8,128)(2,1)S(1)}, bf16[32,2048]{1,0:T(8,128)(2,1)S(1)}, u32[]{:S(2)}, u32[]{:S(2)}) %collective-permute-start.2) | collective-permute-done | bytes 131104 | tf_op jit(solution)/shard_map/ppermute | solution.py:23
  44.2 3.5 %collective-permute-done.3 = bf16[32,2048]{1,0:T(8,128)(2,1)S(1)} collective-permute-done((bf16[32,2048]{1,0:T(8,128)(2,1)S(1)}, bf16[32,2048]{1,0:T(8,128)(2,1)S(1)}, u32[]{:S(2)}, u32[]{:S(2)}) %collective-permute-start.3) | collective-permute-done | bytes 131104 | tf_op jit(solution)/shard_map/ppermute | solution.py:23
  47.8 3.6 %collective-permute-start.4 = (bf16[32,2048]{1,0:T(8,128)(2,1)S(1)}, bf16[32,2048]{1,0:T(8,128)(2,1)S(1)}, u32[]{:S(2)}, u32[]{:S(2)}) collective-permute-start(bf16[32,2048]{1,0:T(8,128)(2,1)S(1)} %fusion.2), channel_id=1, source_target_pairs={{0,8},{8,0},{16,24},{24,16},{32,40},{40,32},{48,56},{56,48},{64,72... | collective-permute-start | bytes 393224 | tf_op jit(solution)/shard_map/ppermute | solution.py:23
  52.7 1.3 convolution_add_fusion.5
  56.4 4.1 %collective-permute-done.6 = bf16[32,2048]{1,0:T(8,128)(2,1)S(1)} collective-permute-done((bf16[32,2048]{1,0:T(8,128)(2,1)S(1)}, bf16[32,2048]{1,0:T(8,128)(2,1)S(1)}, u32[]{:S(2)}, u32[]{:S(2)}) %collective-permute-start.6) | collective-permute-done | bytes 131104 | tf_op jit(solution)/shard_map/ppermute | solution.py:23
  61.2 4.5 %collective-permute-done.7 = bf16[32,2048]{1,0:T(8,128)(2,1)S(1)} collective-permute-done((bf16[32,2048]{1,0:T(8,128)(2,1)S(1)}, bf16[32,2048]{1,0:T(8,128)(2,1)S(1)}, u32[]{:S(2)}, u32[]{:S(2)}) %collective-permute-start.7) | collective-permute-done | bytes 131104 | tf_op jit(solution)/shard_map/ppermute | solution.py:23
  66.2 3.5 %collective-permute-done.8 = bf16[32,2048]{1,0:T(8,128)(2,1)S(1)} collective-permute-done((bf16[32,2048]{1,0:T(8,128)(2,1)S(1)}, bf16[32,2048]{1,0:T(8,128)(2,1)S(1)}, u32[]{:S(2)}, u32[]{:S(2)}) %collective-permute-start.8) | collective-permute-done | bytes 131104 | tf_op jit(solution)/shard_map/ppermute | solution.py:23
  69.8 3.6 %collective-permute-start.9 = (bf16[32,2048]{1,0:T(8,128)(2,1)S(1)}, bf16[32,2048]{1,0:T(8,128)(2,1)S(1)}, u32[]{:S(2)}, u32[]{:S(2)}) collective-permute-start(bf16[32,2048]{1,0:T(8,128)(2,1)S(1)} %fusion.3), channel_id=1, source_target_pairs={{0,8},{8,0},{16,24},{24,16},{32,40},{40,32},{48,56},{56,48},{64,72... | collective-permute-start | bytes 393224 | tf_op jit(solution)/shard_map/ppermute | solution.py:23
  78.4 4.1 %collective-permute-done.11 = bf16[32,2048]{1,0:T(8,128)(2,1)S(1)} collective-permute-done((bf16[32,2048]{1,0:T(8,128)(2,1)S(1)}, bf16[32,2048]{1,0:T(8,128)(2,1)S(1)}, u32[]{:S(2)}, u32[]{:S(2)}) %collective-permute-start.11) | collective-permute-done | bytes 131104 | tf_op jit(solution)/shard_map/ppermute | solution.py:23
  83.2 4.5 %collective-permute-done.12 = bf16[32,2048]{1,0:T(8,128)(2,1)S(1)} collective-permute-done((bf16[32,2048]{1,0:T(8,128)(2,1)S(1)}, bf16[32,2048]{1,0:T(8,128)(2,1)S(1)}, u32[]{:S(2)}, u32[]{:S(2)}) %collective-permute-start.12) | collective-permute-done | bytes 131104 | tf_op jit(solution)/shard_map/ppermute | solution.py:23
  88.2 3.5 %collective-permute-done.13 = bf16[32,2048]{1,0:T(8,128)(2,1)S(1)} collective-permute-done((bf16[32,2048]{1,0:T(8,128)(2,1)S(1)}, bf16[32,2048]{1,0:T(8,128)(2,1)S(1)}, u32[]{:S(2)}, u32[]{:S(2)}) %collective-permute-start.13) | collective-permute-done | bytes 131104 | tf_op jit(solution)/shard_map/ppermute | solution.py:23
  91.8 3.4 %collective-permute-start.14 = (bf16[32,2048]{1,0:T(8,128)(2,1)S(1)}, bf16[32,2048]{1,0:T(8,128)(2,1)S(1)}, u32[]{:S(2)}, u32[]{:S(2)}) collective-permute-start(bf16[32,2048]{1,0:T(8,128)(2,1)S(1)} %fusion.5), channel_id=1, source_target_pairs={{0,8},{8,0},{16,24},{24,16},{32,40},{40,32},{48,56},{56,48},{64,72... | collective-permute-start | bytes 393224 | tf_op jit(solution)/shard_map/ppermute | solution.py:23
  100.3 4.1 %collective-permute-done.16 = bf16[32,2048]{1,0:T(8,128)(2,1)S(1)} collective-permute-done((bf16[32,2048]{1,0:T(8,128)(2,1)S(1)}, bf16[32,2048]{1,0:T(8,128)(2,1)S(1)}, u32[]{:S(2)}, u32[]{:S(2)}) %collective-permute-start.16) | collective-permute-done | bytes 131104 | tf_op jit(solution)/shard_map/ppermute | solution.py:23
  105.1 4.5 %collective-permute-done.17 = bf16[32,2048]{1,0:T(8,128)(2,1)S(1)} collective-permute-done((bf16[32,2048]{1,0:T(8,128)(2,1)S(1)}, bf16[32,2048]{1,0:T(8,128)(2,1)S(1)}, u32[]{:S(2)}, u32[]{:S(2)}) %collective-permute-start.17) | collective-permute-done | bytes 131104 | tf_op jit(solution)/shard_map/ppermute | solution.py:23
  110.0 3.5 %collective-permute-done.18 = bf16[32,2048]{1,0:T(8,128)(2,1)S(1)} collective-permute-done((bf16[32,2048]{1,0:T(8,128)(2,1)S(1)}, bf16[32,2048]{1,0:T(8,128)(2,1)S(1)}, u32[]{:S(2)}, u32[]{:S(2)}) %collective-permute-start.18) | collective-permute-done | bytes 131104 | tf_op jit(solution)/shard_map/ppermute | solution.py:23
  113.6 3.4 %collective-permute-start.19 = (bf16[32,2048]{1,0:T(8,128)(2,1)S(1)}, bf16[32,2048]{1,0:T(8,128)(2,1)S(1)}, u32[]{:S(2)}, u32[]{:S(2)}) collective-permute-start(bf16[32,2048]{1,0:T(8,128)(2,1)S(1)} %fusion.6), channel_id=1, source_target_pairs={{0,8},{8,0},{16,24},{24,16},{32,40},{40,32},{48,56},{56,48},{64,72... | collective-permute-start | bytes 393224 | tf_op jit(solution)/shard_map/ppermute | solution.py:23
  118.4 1.3 convolution_add_fusion.2
  122.3 4.1 %collective-permute-done.21 = bf16[32,2048]{1,0:T(8,128)(2,1)S(1)} collective-permute-done((bf16[32,2048]{1,0:T(8,128)(2,1)S(1)}, bf16[32,2048]{1,0:T(8,128)(2,1)S(1)}, u32[]{:S(2)}, u32[]{:S(2)}) %collective-permute-start.21) | collective-permute-done | bytes 131104 | tf_op jit(solution)/shard_map/ppermute | solution.py:23
  127.1 4.5 %collective-permute-done.22 = bf16[32,2048]{1,0:T(8,128)(2,1)S(1)} collective-permute-done((bf16[32,2048]{1,0:T(8,128)(2,1)S(1)}, bf16[32,2048]{1,0:T(8,128)(2,1)S(1)}, u32[]{:S(2)}, u32[]{:S(2)}) %collective-permute-start.22) | collective-permute-done | bytes 131104 | tf_op jit(solution)/shard_map/ppermute | solution.py:23
  132.1 3.5 %collective-permute-done.23 = bf16[32,2048]{1,0:T(8,128)(2,1)S(1)} collective-permute-done((bf16[32,2048]{1,0:T(8,128)(2,1)S(1)}, bf16[32,2048]{1,0:T(8,128)(2,1)S(1)}, u32[]{:S(2)}, u32[]{:S(2)}) %collective-permute-start.23) | collective-permute-done | bytes 131104 | tf_op jit(solution)/shard_map/ppermute | solution.py:23
  135.6 3.4 %collective-permute-start.24 = (bf16[32,2048]{1,0:T(8,128)(2,1)S(1)}, bf16[32,2048]{1,0:T(8,128)(2,1)S(1)}, u32[]{:S(2)}, u32[]{:S(2)}) collective-permute-start(bf16[32,2048]{1,0:T(8,128)(2,1)S(1)} %fusion.8), channel_id=1, source_target_pairs={{0,8},{8,0},{16,24},{24,16},{32,40},{40,32},{48,56},{56,48},{64,72... | collective-permute-start | bytes 393224 | tf_op jit(solution)/shard_map/ppermute | solution.py:23
  139.0 3.5 %fusion.45 = f32[32,1024]{1,0:T(8,128)S(1)} fusion(bf16[32,2048]{1,0:T(8,128)(2,1)S(1)} %fusion.8, bf16[1024,4096]{1,0:T(8,128)(2,1)} %param.6, s32[]{:T(128)S(6)} %select_n.43), kind=kOutput, calls=%fused_computation.114 | convolution fusion | flops 134217728 | bytes 4456452 | tf_op jit(solution)/shard_map/dot_general | solution.py:51
  142.6 3.5 %convolution_add_fusion.1 = f32[32,1024]{1,0:T(8,128)S(1)} fusion(f32[32,1024]{1,0:T(8,128)S(1)} %fusion.45, bf16[32,2048]{1,0:T(8,128)(2,1)S(1)} %collective-permute-done.24, bf16[1024,4096]{1,0:T(8,128)(2,1)} %param.6, s32[]{:T(128)S(6)} %select_n.44), kind=kOutput, calls=%fused_computation.9 | convolution fusion | flops 134250496 | bytes 4587524 | tf_op jit(solution)/shard_map/dot_general | solution.py:51
  146.1 3.0 %convolution_convert_fusion = bf16[32,2048]{1,0:T(8,128)(2,1)S(1)} fusion(bf16[32,1024]{1,0:T(8,128)(2,1)S(1)} %pad_maximum_fusion.6, bf16[1024,4096]{1,0:T(8,128)(2,1)} %param.6, s32[]{:T(128)S(6)} %select_n.44), kind=kOutput, calls=%fused_computation.2 | convolution fusion | flops 134283264 | bytes 4390916 | tf_op jit(solution)/shard_map/dot_general | solution.py:56
  149.1 3.0 %broadcast_select_fusion.1 = (bf16[32,2048]{1,0:T(8,128)(2,1)S(1)}, bf16[32,2048]{1,0:T(8,128)(2,1)S(1)}) fusion(bf16[32,2048]{1,0:T(8,128)(2,1)S(1)} %convolution_convert_fusion, pred[]{:T(512)S(6)} %eq.6, bf16[32,2048]{1,0:T(8,128)(2,1)S(1)} %fusion.8, f32[2048]{0:T(1024)S(1)} %get-tuple-element.19, bf16[32,2048]{1,0:T(8,128)(2,1)S(1)} %fusion.6, ...), kind=kOutput, calls=%fused_computation.59 | convolution fusion | flops 134807552 | bytes 4923398 | tf_op jit(solution)/shard_map/dot_general | solution.py:56
  152.6 13.4 %all_to_all.10 = bf16[128,2,512]{2,1,0:T(2,128)(2,1)S(1)} all-to-all(bf16[128,2,512]{2,1,0:T(2,128)(2,1)S(1)} %bitcast.87), channel_id=1, replica_groups=mesh['row'=16,'col'=8] {'row','col'}, dimensions={0} | all-to-all | bytes 524288 | tf_op jit(solution)/shard_map/all_to_all | solution.py:103
  (98 shorter events, 31.8 us)
Async XLA Ops:
  1.6 22.0 %all-to-all-start = ((bf16[128,2,512]{2,1,0:T(2,128)(2,1)}), bf16[128,2,512]{2,1,0:T(2,128)(2,1)S(1)}, u32[]{:S(2)}, u32[]{:S(2)}) async-start(bf16[128,2,512]{2,1,0:T(2,128)(2,1)} %bitcast.4), calls=%async_computation | async-start | bytes 524288 | tf_op jit(solution)/shard_map/all_to_all | solution.py:44
  23.8 7.3 %copy-start = (bf16[1024,4096]{1,0:T(8,128)(2,1)S(1)}, bf16[1024,4096]{1,0:T(8,128)(2,1)}, u32[]{:S(2)}) copy-start(bf16[1024,4096]{1,0:T(8,128)(2,1)} %param.6) | copy-start | bytes 25165828
  31.9 12.3 %copy-start.1 = (f32[4096]{0:T(1024)S(1)}, f32[4096]{0:T(1024)}, u32[]{:S(2)}) copy-start(f32[4096]{0:T(1024)} %param.10) | copy-start | bytes 49156
  31.9 2.4 %collective-permute-start = (bf16[32,2048]{1,0:T(8,128)(2,1)S(1)}, bf16[32,2048]{1,0:T(8,128)(2,1)S(1)}, u32[]{:S(2)}, u32[]{:S(2)}) collective-permute-start(bf16[32,2048]{1,0:T(8,128)(2,1)S(1)} %convolution_convert_fusion.5), channel_id=1, source_target_pairs={{0,8},{8,0},{16,24},{24,16},{32,40},{40,32},{48,56},{56,48},{64,72... | collective-permute-start | bytes 393224 | tf_op jit(solution)/shard_map/ppermute | solution.py:23
  34.3 4.2 %collective-permute-start.1 = (bf16[32,2048]{1,0:T(8,128)(2,1)S(1)}, bf16[32,2048]{1,0:T(8,128)(2,1)S(1)}, u32[]{:S(2)}, u32[]{:S(2)}) collective-permute-start(bf16[32,2048]{1,0:T(8,128)(2,1)S(1)} %fusion.10), channel_id=1, source_target_pairs={{0,64},{8,24},{16,80},{24,8},{32,96},{40,56},{48,112},{56,40},{64,... | collective-permute-start | bytes 393224 | tf_op jit(solution)/shard_map/ppermute | solution.py:23
  38.6 5.1 %collective-permute-start.2 = (bf16[32,2048]{1,0:T(8,128)(2,1)S(1)}, bf16[32,2048]{1,0:T(8,128)(2,1)S(1)}, u32[]{:S(2)}, u32[]{:S(2)}) collective-permute-start(bf16[32,2048]{1,0:T(8,128)(2,1)S(1)} %fusion.40), channel_id=1, source_target_pairs={{0,16},{8,56},{16,0},{24,40},{32,48},{40,24},{48,32},{56,8},{64,80... | collective-permute-start | bytes 393224 | tf_op jit(solution)/shard_map/ppermute | solution.py:23
  43.8 3.9 %collective-permute-start.3 = (bf16[32,2048]{1,0:T(8,128)(2,1)S(1)}, bf16[32,2048]{1,0:T(8,128)(2,1)S(1)}, u32[]{:S(2)}, u32[]{:S(2)}) collective-permute-start(bf16[32,2048]{1,0:T(8,128)(2,1)S(1)} %fusion.11), channel_id=1, source_target_pairs={{0,48},{8,72},{16,32},{24,88},{32,16},{40,104},{48,0},{56,120},{64... | collective-permute-start | bytes 393224 | tf_op jit(solution)/shard_map/ppermute | solution.py:23
  47.8 4.9 %collective-permute-start.4 = (bf16[32,2048]{1,0:T(8,128)(2,1)S(1)}, bf16[32,2048]{1,0:T(8,128)(2,1)S(1)}, u32[]{:S(2)}, u32[]{:S(2)}) collective-permute-start(bf16[32,2048]{1,0:T(8,128)(2,1)S(1)} %fusion.2), channel_id=1, source_target_pairs={{0,8},{8,0},{16,24},{24,16},{32,40},{40,32},{48,56},{56,48},{64,72... | collective-permute-start | bytes 393224 | tf_op jit(solution)/shard_map/ppermute | solution.py:23
  54.9 1.4 collective-permute-start.5
  56.4 4.2 %collective-permute-start.6 = (bf16[32,2048]{1,0:T(8,128)(2,1)S(1)}, bf16[32,2048]{1,0:T(8,128)(2,1)S(1)}, u32[]{:S(2)}, u32[]{:S(2)}) collective-permute-start(bf16[32,2048]{1,0:T(8,128)(2,1)S(1)} %fusion.12), channel_id=1, source_target_pairs={{0,64},{8,24},{16,80},{24,8},{32,96},{40,56},{48,112},{56,40},{64,... | collective-permute-start | bytes 393224 | tf_op jit(solution)/shard_map/ppermute | solution.py:23
  60.6 5.1 %collective-permute-start.7 = (bf16[32,2048]{1,0:T(8,128)(2,1)S(1)}, bf16[32,2048]{1,0:T(8,128)(2,1)S(1)}, u32[]{:S(2)}, u32[]{:S(2)}) collective-permute-start(bf16[32,2048]{1,0:T(8,128)(2,1)S(1)} %fusion.41), channel_id=1, source_target_pairs={{0,16},{8,56},{16,0},{24,40},{32,48},{40,24},{48,32},{56,8},{64,80... | collective-permute-start | bytes 393224 | tf_op jit(solution)/shard_map/ppermute | solution.py:23
  65.8 3.9 %collective-permute-start.8 = (bf16[32,2048]{1,0:T(8,128)(2,1)S(1)}, bf16[32,2048]{1,0:T(8,128)(2,1)S(1)}, u32[]{:S(2)}, u32[]{:S(2)}) collective-permute-start(bf16[32,2048]{1,0:T(8,128)(2,1)S(1)} %fusion.13), channel_id=1, source_target_pairs={{0,48},{8,72},{16,32},{24,88},{32,16},{40,104},{48,0},{56,120},{64... | collective-permute-start | bytes 393224 | tf_op jit(solution)/shard_map/ppermute | solution.py:23
  69.8 4.9 %collective-permute-start.9 = (bf16[32,2048]{1,0:T(8,128)(2,1)S(1)}, bf16[32,2048]{1,0:T(8,128)(2,1)S(1)}, u32[]{:S(2)}, u32[]{:S(2)}) collective-permute-start(bf16[32,2048]{1,0:T(8,128)(2,1)S(1)} %fusion.3), channel_id=1, source_target_pairs={{0,8},{8,0},{16,24},{24,16},{32,40},{40,32},{48,56},{56,48},{64,72... | collective-permute-start | bytes 393224 | tf_op jit(solution)/shard_map/ppermute | solution.py:23
  76.9 1.4 collective-permute-start.10
  78.4 4.2 %collective-permute-start.11 = (bf16[32,2048]{1,0:T(8,128)(2,1)S(1)}, bf16[32,2048]{1,0:T(8,128)(2,1)S(1)}, u32[]{:S(2)}, u32[]{:S(2)}) collective-permute-start(bf16[32,2048]{1,0:T(8,128)(2,1)S(1)} %fusion.14), channel_id=1, source_target_pairs={{0,64},{8,24},{16,80},{24,8},{32,96},{40,56},{48,112},{56,40},{64,... | collective-permute-start | bytes 393224 | tf_op jit(solution)/shard_map/ppermute | solution.py:23
  82.6 5.1 %collective-permute-start.12 = (bf16[32,2048]{1,0:T(8,128)(2,1)S(1)}, bf16[32,2048]{1,0:T(8,128)(2,1)S(1)}, u32[]{:S(2)}, u32[]{:S(2)}) collective-permute-start(bf16[32,2048]{1,0:T(8,128)(2,1)S(1)} %fusion.42), channel_id=1, source_target_pairs={{0,16},{8,56},{16,0},{24,40},{32,48},{40,24},{48,32},{56,8},{64,80... | collective-permute-start | bytes 393224 | tf_op jit(solution)/shard_map/ppermute | solution.py:23
  87.8 3.9 %collective-permute-start.13 = (bf16[32,2048]{1,0:T(8,128)(2,1)S(1)}, bf16[32,2048]{1,0:T(8,128)(2,1)S(1)}, u32[]{:S(2)}, u32[]{:S(2)}) collective-permute-start(bf16[32,2048]{1,0:T(8,128)(2,1)S(1)} %fusion.15), channel_id=1, source_target_pairs={{0,48},{8,72},{16,32},{24,88},{32,16},{40,104},{48,0},{56,120},{64... | collective-permute-start | bytes 393224 | tf_op jit(solution)/shard_map/ppermute | solution.py:23
  91.8 4.7 %collective-permute-start.14 = (bf16[32,2048]{1,0:T(8,128)(2,1)S(1)}, bf16[32,2048]{1,0:T(8,128)(2,1)S(1)}, u32[]{:S(2)}, u32[]{:S(2)}) collective-permute-start(bf16[32,2048]{1,0:T(8,128)(2,1)S(1)} %fusion.5), channel_id=1, source_target_pairs={{0,8},{8,0},{16,24},{24,16},{32,40},{40,32},{48,56},{56,48},{64,72... | collective-permute-start | bytes 393224 | tf_op jit(solution)/shard_map/ppermute | solution.py:23
  98.7 1.4 collective-permute-start.15
  100.2 4.2 %collective-permute-start.16 = (bf16[32,2048]{1,0:T(8,128)(2,1)S(1)}, bf16[32,2048]{1,0:T(8,128)(2,1)S(1)}, u32[]{:S(2)}, u32[]{:S(2)}) collective-permute-start(bf16[32,2048]{1,0:T(8,128)(2,1)S(1)} %fusion.16), channel_id=1, source_target_pairs={{0,64},{8,24},{16,80},{24,8},{32,96},{40,56},{48,112},{56,40},{64,... | collective-permute-start | bytes 393224 | tf_op jit(solution)/shard_map/ppermute | solution.py:23
  104.4 5.1 %collective-permute-start.17 = (bf16[32,2048]{1,0:T(8,128)(2,1)S(1)}, bf16[32,2048]{1,0:T(8,128)(2,1)S(1)}, u32[]{:S(2)}, u32[]{:S(2)}) collective-permute-start(bf16[32,2048]{1,0:T(8,128)(2,1)S(1)} %fusion.43), channel_id=1, source_target_pairs={{0,16},{8,56},{16,0},{24,40},{32,48},{40,24},{48,32},{56,8},{64,80... | collective-permute-start | bytes 393224 | tf_op jit(solution)/shard_map/ppermute | solution.py:23
  109.6 3.9 %collective-permute-start.18 = (bf16[32,2048]{1,0:T(8,128)(2,1)S(1)}, bf16[32,2048]{1,0:T(8,128)(2,1)S(1)}, u32[]{:S(2)}, u32[]{:S(2)}) collective-permute-start(bf16[32,2048]{1,0:T(8,128)(2,1)S(1)} %fusion.17), channel_id=1, source_target_pairs={{0,48},{8,72},{16,32},{24,88},{32,16},{40,104},{48,0},{56,120},{64... | collective-permute-start | bytes 393224 | tf_op jit(solution)/shard_map/ppermute | solution.py:23
  113.6 4.7 %collective-permute-start.19 = (bf16[32,2048]{1,0:T(8,128)(2,1)S(1)}, bf16[32,2048]{1,0:T(8,128)(2,1)S(1)}, u32[]{:S(2)}, u32[]{:S(2)}) collective-permute-start(bf16[32,2048]{1,0:T(8,128)(2,1)S(1)} %fusion.6), channel_id=1, source_target_pairs={{0,8},{8,0},{16,24},{24,16},{32,40},{40,32},{48,56},{56,48},{64,72... | collective-permute-start | bytes 393224 | tf_op jit(solution)/shard_map/ppermute | solution.py:23
  120.6 1.6 collective-permute-start.20
  122.2 4.2 %collective-permute-start.21 = (bf16[32,2048]{1,0:T(8,128)(2,1)S(1)}, bf16[32,2048]{1,0:T(8,128)(2,1)S(1)}, u32[]{:S(2)}, u32[]{:S(2)}) collective-permute-start(bf16[32,2048]{1,0:T(8,128)(2,1)S(1)} %fusion.18), channel_id=1, source_target_pairs={{0,64},{8,24},{16,80},{24,8},{32,96},{40,56},{48,112},{56,40},{64,... | collective-permute-start | bytes 393224 | tf_op jit(solution)/shard_map/ppermute | solution.py:23
  126.5 5.1 %collective-permute-start.22 = (bf16[32,2048]{1,0:T(8,128)(2,1)S(1)}, bf16[32,2048]{1,0:T(8,128)(2,1)S(1)}, u32[]{:S(2)}, u32[]{:S(2)}) collective-permute-start(bf16[32,2048]{1,0:T(8,128)(2,1)S(1)} %fusion.44), channel_id=1, source_target_pairs={{0,16},{8,56},{16,0},{24,40},{32,48},{40,24},{48,32},{56,8},{64,80... | collective-permute-start | bytes 393224 | tf_op jit(solution)/shard_map/ppermute | solution.py:23
  131.6 3.9 %collective-permute-start.23 = (bf16[32,2048]{1,0:T(8,128)(2,1)S(1)}, bf16[32,2048]{1,0:T(8,128)(2,1)S(1)}, u32[]{:S(2)}, u32[]{:S(2)}) collective-permute-start(bf16[32,2048]{1,0:T(8,128)(2,1)S(1)} %fusion.19), channel_id=1, source_target_pairs={{0,48},{8,72},{16,32},{24,88},{32,16},{40,104},{48,0},{56,120},{64... | collective-permute-start | bytes 393224 | tf_op jit(solution)/shard_map/ppermute | solution.py:23
  135.6 6.9 %collective-permute-start.24 = (bf16[32,2048]{1,0:T(8,128)(2,1)S(1)}, bf16[32,2048]{1,0:T(8,128)(2,1)S(1)}, u32[]{:S(2)}, u32[]{:S(2)}) collective-permute-start(bf16[32,2048]{1,0:T(8,128)(2,1)S(1)} %fusion.8), channel_id=1, source_target_pairs={{0,8},{8,0},{16,24},{24,16},{32,40},{40,32},{48,56},{56,48},{64,72... | collective-permute-start | bytes 393224 | tf_op jit(solution)/shard_map/ppermute | solution.py:23

commit v6 on v5

--- a/solution.py
+++ b/solution.py
@@ -25,11 +25,17 @@
     def to_other_core(array):
         return move(array, lambda r: r ^ 1)
 
-    rounds = ((8, 2), (2, 6), (6, 8))
+    def along_y(array):
+        return move(array, lambda r: r ^ 8)
+
+    def along_z(array, hops):
+        return move(array, lambda r: (r & 9) | ((r + 2 * hops) & 6))
 
     def over_chips(total):
-        for bits in rounds:
-            total = total + move(total.astype(bf16), lambda r: r ^ bits[r % 2]).astype(f32)
+        total = total + along_y(total.astype(bf16)).astype(f32)
+        sent = total.astype(bf16)
+        for hops in (1, 3, 2):
+            total = total + along_z(sent, hops).astype(f32)
         return total
 
     mine = lax.dynamic_index_in_dim(
@@ -41,6 +47,16 @@
     sent = jnp.transpose(magnetization, (2, 0, 1))
     sent = jnp.broadcast_to(sent[None], (row_count,) + sent.shape)
     sent = sent.reshape(row_count * col_count, parts, col_width)
+    first_core, first_chip = core == 0, row_index < 2
+
+    def half_of(array, which, axis):
+        return lax.dynamic_slice_in_dim(array, which * width, width, axis)
+
+    rates = jnp.stack([half_of(decay_rates, core, 0), half_of(decay_rates, 1 - core, 0)])
+    sent, rates, first_core, first_chip = lax.optimization_barrier(
+        (sent, rates, first_core, first_chip)
+    )
+    rates = rates[:1]
     every = lax.all_to_all(sent, ("row", "col"), 0, 0)
     every = every.reshape(row_count, col_count, parts, col_width)
     every = lax.optimization_barrier(
@@ -64,12 +80,8 @@
         rows = jnp.concatenate([scale * imag, -scale * real], axis=0)
         return lax.optimization_barrier(rows.astype(bf16))
 
-    def half_of(array, which, axis):
-        return lax.dynamic_slice_in_dim(array, which * width, width, axis)
-
     basis_own = half_of(mode_basis, core, 1)
     basis_other = half_of(mode_basis, 1 - core, 1)
-    rates = half_of(decay_rates, core, 0)[None, :]
     field = half_of(every, core, 1)
     field_other = half_of(every, 1 - core, 1)
 
@@ -92,11 +104,11 @@
             field_other = to_other_core(field)
 
     local = field.astype(f32) + (0.0 - 1.0 * rates) * half.astype(f32)
-    local = jnp.where(row_index < 2, local, 0.0)
+    local = jnp.where(first_chip, local, 0.0)
     part_own = (to_modes(nodes, basis_own) + local).astype(bf16)
     part_other = to_modes(nodes, basis_other).astype(bf16)
-    low = jnp.where(core == 0, part_own, part_other)
-    high = jnp.where(core == 0, part_other, part_own)
+    low = jnp.where(first_core, part_own, part_other)
+    high = jnp.where(first_core, part_other, part_own)
     sent = jnp.concatenate([low, high], axis=1)
     sent = sent.reshape(parts, row_count, col_count, col_width)
     sent = jnp.transpose(sent, (1, 2, 0, 3)).reshape(row_count * col_count, parts, col_width)

time: 167 us -> 154 us (0.922)
  matrix products: 39.3 us -> 30.5 us
  starting transfers between devices: 37 us -> 33.9 us
  waiting for transfers between devices: 70.3 us -> 67.8 us
    dot_general x12, matrix products: 24.9 us -> 20.6 us  [to_nodes(): lax.dot_general(array, basis, (((1,), (1,)), ((), ())), preferred_element...]
    dot_general x12, matrix products: 14.3 us -> 9.98 us  [to_modes(): lax.dot_general(nodes, basis, (((1,), (0,)), ((), ())), preferred_element...]
    ppermute x25 -> x30, starting transfers between devices: 25.5 us -> 22.4 us  [move(): lax.ppermute(array, 'row', [(r, target(r)) for r in range(row_count)])]
    ppermute x25 -> x30, waiting for transfers between devices: 61.9 us -> 59.3 us  [move(): lax.ppermute(array, 'row', [(r, target(r)) for r in range(row_count)])]
  transfers between devices with their start and end apart: 26 -> 31, of which waited for: 21 -> 26; matrix products, arithmetic and copies ran while one was open for 9% -> 8% of each run, Pallas kernels for 0% -> 0%
where the time goes in v6:
time: 154 us; the launch traced here: 153 us
  waiting for transfers between devices  67.8 us (44%)
  starting transfers between devices  33.9 us (22%)
  matrix products  30.5 us (20%)
  blocking collectives  13.4 us (9%)
  local copies, waits for them, and re-layouts  4.59 us (3%)
  other arithmetic  2.42 us (2%)
    ppermute x30, waiting for transfers between devices, move(): lax.ppermute(array, 'row', [(r, target(r)) for r in range(row_count)])  59.3 us
    ppermute x30, starting transfers between devices, move(): lax.ppermute(array, 'row', [(r, target(r)) for r in range(row_count)])  22.4 us
    dot_general x12, matrix products, to_nodes(): lax.dot_general(array, basis, (((1,), (1,)), ((), ())), preferred_element...  20.6 us
    all_to_all x1, blocking collectives, on_device(): every = lax.all_to_all(sent, ('row', 'col'), 0, 0)  13.4 us
    all_to_all x1, starting transfers between devices, on_device(): every = lax.all_to_all(sent, ('row', 'col'), 0, 0)  11.5 us
    dot_general x12, matrix products, to_modes(): lax.dot_general(nodes, basis, (((1,), (0,)), ((), ())), preferred_element...  9.98 us
    all_to_all x1, waiting for transfers between devices, on_device(): every = lax.all_to_all(sent, ('row', 'col'), 0, 0)  8.44 us
  transfers between devices with their start and end apart: 31, of which 26 were waited for; matrix products, arithmetic and copies ran while one was open for 8% of the time, Pallas kernels for 0%

profile of v6, /device:TPU:1, one launch (start us, length us, event | category | flops | bytes accessed | tf_op | source)
XLA Modules:
  0.0 153.0 jit_solution(14284831678599552069)
XLA Ops:
  2.4 11.5 %all-to-all-start = ((bf16[128,2,512]{2,1,0:T(2,128)(2,1)}), bf16[128,2,512]{2,1,0:T(2,128)(2,1)S(1)}, u32[]{:S(2)}, u32[]{:S(2)}) async-start(bf16[128,2,512]{2,1,0:T(2,128)(2,1)} %bitcast.1), calls=%async_computation | async-start | bytes 524288 | tf_op jit(solution)/shard_map/all_to_all | solution.py:60
  15.9 8.4 %all-to-all-done = bf16[128,2,512]{2,1,0:T(2,128)(2,1)S(1)} async-done(((bf16[128,2,512]{2,1,0:T(2,128)(2,1)}), bf16[128,2,512]{2,1,0:T(2,128)(2,1)S(1)}, u32[]{:S(2)}, u32[]{:S(2)}) %all-to-all-start) | async-done | bytes 262176 | tf_op jit(solution)/shard_map/all_to_all | solution.py:60
  24.5 3.7 %fusion.21 = f32[32,1024]{1,0:T(8,128)S(1)} fusion(bf16[32,4096]{1,0:T(8,128)(2,1)S(1)} %bitcast.82, s32[]{:T(128)S(6)} %select_n.42, bf16[1024,4096]{1,0:T(8,128)(2,1)} %param.6), kind=kOutput, calls=%fused_computation.55 | convolution fusion | flops 134217728 | bytes 4457472 | tf_op jit(solution)/shard_map/dot_general | solution.py:67
  28.2 3.5 %convolution_add_fusion.6 = f32[32,1024]{1,0:T(8,128)S(1)} fusion(f32[32,1024]{1,0:T(8,128)S(1)} %fusion.21, bf16[32,4096]{1,0:T(8,128)(2,1)S(1)} %bitcast.83, s32[]{:T(128)S(6)} %select_n.43, bf16[1024,4096]{1,0:T(8,128)(2,1)} %param.6), kind=kOutput, calls=%fused_computation.14 | convolution fusion | flops 134250496 | bytes 4588544 | tf_op jit(solution)/shard_map/dot_general | solution.py:67
  32.6 1.4 collective-permute-start
  35.5 4.4 %collective-permute-done.1 = bf16[32,2048]{1,0:T(8,128)(2,1)S(1)} collective-permute-done((bf16[32,2048]{1,0:T(8,128)(2,1)S(1)}, bf16[32,2048]{1,0:T(8,128)(2,1)S(1)}, u32[]{:S(2)}, u32[]{:S(2)}) %collective-permute-start.1) | collective-permute-done | bytes 131104 | tf_op jit(solution)/shard_map/ppermute | solution.py:23
  40.7 2.2 %collective-permute-start.3 = (bf16[32,2048]{1,0:T(8,128)(2,1)S(1)}, bf16[32,2048]{1,0:T(8,128)(2,1)S(1)}, u32[]{:S(2)}, u32[]{:S(2)}) collective-permute-start(bf16[32,2048]{1,0:T(8,128)(2,1)S(1)} %fusion.16), channel_id=1, source_target_pairs={{0,48},{8,56},{16,0},{24,8},{32,16},{40,24},{48,32},{56,40},{64,11... | collective-permute-start | bytes 393224 | tf_op jit(solution)/shard_map/ppermute | solution.py:23
  42.9 2.4 %collective-permute-done.4 = bf16[32,2048]{1,0:T(8,128)(2,1)S(1)} collective-permute-done((bf16[32,2048]{1,0:T(8,128)(2,1)S(1)}, bf16[32,2048]{1,0:T(8,128)(2,1)S(1)}, u32[]{:S(2)}, u32[]{:S(2)}) %collective-permute-start.4) | collective-permute-done | bytes 131104 | tf_op jit(solution)/shard_map/ppermute | solution.py:23
  46.3 2.9 %collective-permute-done.2 = bf16[32,2048]{1,0:T(8,128)(2,1)S(1)} collective-permute-done((bf16[32,2048]{1,0:T(8,128)(2,1)S(1)}, bf16[32,2048]{1,0:T(8,128)(2,1)S(1)}, u32[]{:S(2)}, u32[]{:S(2)}) %collective-permute-start.2) | collective-permute-done | bytes 131104 | tf_op jit(solution)/shard_map/ppermute | solution.py:23
  49.3 1.8 %collective-permute-start.5 = (bf16[32,2048]{1,0:T(8,128)(2,1)S(1)}, bf16[32,2048]{1,0:T(8,128)(2,1)S(1)}, u32[]{:S(2)}, u32[]{:S(2)}) collective-permute-start(bf16[32,2048]{1,0:T(8,128)(2,1)S(1)} %fusion.2), channel_id=1, source_target_pairs={{0,8},{8,0},{16,24},{24,16},{32,40},{40,32},{48,56},{56,48},{64,72... | collective-permute-start | bytes 393224 | tf_op jit(solution)/shard_map/ppermute | solution.py:23
  52.5 1.3 convolution_add_fusion.5
  56.6 4.6 %collective-permute-done.7 = bf16[32,2048]{1,0:T(8,128)(2,1)S(1)} collective-permute-done((bf16[32,2048]{1,0:T(8,128)(2,1)S(1)}, bf16[32,2048]{1,0:T(8,128)(2,1)S(1)}, u32[]{:S(2)}, u32[]{:S(2)}) %collective-permute-start.7) | collective-permute-done | bytes 131104 | tf_op jit(solution)/shard_map/ppermute | solution.py:23
  63.2 3.4 %collective-permute-done.10 = bf16[32,2048]{1,0:T(8,128)(2,1)S(1)} collective-permute-done((bf16[32,2048]{1,0:T(8,128)(2,1)S(1)}, bf16[32,2048]{1,0:T(8,128)(2,1)S(1)}, u32[]{:S(2)}, u32[]{:S(2)}) %collective-permute-start.10) | collective-permute-done | bytes 131104 | tf_op jit(solution)/shard_map/ppermute | solution.py:23
  67.6 2.7 %collective-permute-done.8 = bf16[32,2048]{1,0:T(8,128)(2,1)S(1)} collective-permute-done((bf16[32,2048]{1,0:T(8,128)(2,1)S(1)}, bf16[32,2048]{1,0:T(8,128)(2,1)S(1)}, u32[]{:S(2)}, u32[]{:S(2)}) %collective-permute-start.8) | collective-permute-done | bytes 131104 | tf_op jit(solution)/shard_map/ppermute | solution.py:23
  70.4 1.5 collective-permute-start.11
  73.3 1.3 convolution_add_fusion.4
  77.3 4.6 %collective-permute-done.13 = bf16[32,2048]{1,0:T(8,128)(2,1)S(1)} collective-permute-done((bf16[32,2048]{1,0:T(8,128)(2,1)S(1)}, bf16[32,2048]{1,0:T(8,128)(2,1)S(1)}, u32[]{:S(2)}, u32[]{:S(2)}) %collective-permute-start.13) | collective-permute-done | bytes 131104 | tf_op jit(solution)/shard_map/ppermute | solution.py:23
  84.0 3.4 %collective-permute-done.16 = bf16[32,2048]{1,0:T(8,128)(2,1)S(1)} collective-permute-done((bf16[32,2048]{1,0:T(8,128)(2,1)S(1)}, bf16[32,2048]{1,0:T(8,128)(2,1)S(1)}, u32[]{:S(2)}, u32[]{:S(2)}) %collective-permute-start.16) | collective-permute-done | bytes 131104 | tf_op jit(solution)/shard_map/ppermute | solution.py:23
  88.3 2.7 %collective-permute-done.14 = bf16[32,2048]{1,0:T(8,128)(2,1)S(1)} collective-permute-done((bf16[32,2048]{1,0:T(8,128)(2,1)S(1)}, bf16[32,2048]{1,0:T(8,128)(2,1)S(1)}, u32[]{:S(2)}, u32[]{:S(2)}) %collective-permute-start.14) | collective-permute-done | bytes 131104 | tf_op jit(solution)/shard_map/ppermute | solution.py:23
  91.2 1.4 collective-permute-start.17
  93.9 1.3 convolution_add_fusion.3
  97.9 4.6 %collective-permute-done.19 = bf16[32,2048]{1,0:T(8,128)(2,1)S(1)} collective-permute-done((bf16[32,2048]{1,0:T(8,128)(2,1)S(1)}, bf16[32,2048]{1,0:T(8,128)(2,1)S(1)}, u32[]{:S(2)}, u32[]{:S(2)}) %collective-permute-start.19) | collective-permute-done | bytes 131104 | tf_op jit(solution)/shard_map/ppermute | solution.py:23
  104.6 3.4 %collective-permute-done.22 = bf16[32,2048]{1,0:T(8,128)(2,1)S(1)} collective-permute-done((bf16[32,2048]{1,0:T(8,128)(2,1)S(1)}, bf16[32,2048]{1,0:T(8,128)(2,1)S(1)}, u32[]{:S(2)}, u32[]{:S(2)}) %collective-permute-start.22) | collective-permute-done | bytes 131104 | tf_op jit(solution)/shard_map/ppermute | solution.py:23
  108.9 2.7 %collective-permute-done.20 = bf16[32,2048]{1,0:T(8,128)(2,1)S(1)} collective-permute-done((bf16[32,2048]{1,0:T(8,128)(2,1)S(1)}, bf16[32,2048]{1,0:T(8,128)(2,1)S(1)}, u32[]{:S(2)}, u32[]{:S(2)}) %collective-permute-start.20) | collective-permute-done | bytes 131104 | tf_op jit(solution)/shard_map/ppermute | solution.py:23
  111.7 1.6 %collective-permute-start.23 = (bf16[32,2048]{1,0:T(8,128)(2,1)S(1)}, bf16[32,2048]{1,0:T(8,128)(2,1)S(1)}, u32[]{:S(2)}, u32[]{:S(2)}) collective-permute-start(bf16[32,2048]{1,0:T(8,128)(2,1)S(1)} %fusion.6), channel_id=1, source_target_pairs={{0,8},{8,0},{16,24},{24,16},{32,40},{40,32},{48,56},{56,48},{64,72... | collective-permute-start | bytes 393224 | tf_op jit(solution)/shard_map/ppermute | solution.py:23
  114.7 1.3 convolution_add_fusion.2
  118.7 4.6 %collective-permute-done.25 = bf16[32,2048]{1,0:T(8,128)(2,1)S(1)} collective-permute-done((bf16[32,2048]{1,0:T(8,128)(2,1)S(1)}, bf16[32,2048]{1,0:T(8,128)(2,1)S(1)}, u32[]{:S(2)}, u32[]{:S(2)}) %collective-permute-start.25) | collective-permute-done | bytes 131104 | tf_op jit(solution)/shard_map/ppermute | solution.py:23
  125.4 3.4 %collective-permute-done.28 = bf16[32,2048]{1,0:T(8,128)(2,1)S(1)} collective-permute-done((bf16[32,2048]{1,0:T(8,128)(2,1)S(1)}, bf16[32,2048]{1,0:T(8,128)(2,1)S(1)}, u32[]{:S(2)}, u32[]{:S(2)}) %collective-permute-start.28) | collective-permute-done | bytes 131104 | tf_op jit(solution)/shard_map/ppermute | solution.py:23
  129.7 2.7 %collective-permute-done.26 = bf16[32,2048]{1,0:T(8,128)(2,1)S(1)} collective-permute-done((bf16[32,2048]{1,0:T(8,128)(2,1)S(1)}, bf16[32,2048]{1,0:T(8,128)(2,1)S(1)}, u32[]{:S(2)}, u32[]{:S(2)}) %collective-permute-start.26) | collective-permute-done | bytes 131104 | tf_op jit(solution)/shard_map/ppermute | solution.py:23
  132.5 1.4 collective-permute-start.29
  135.3 1.3 convolution_add_fusion.1
  138.8 13.4 %all_to_all.10 = bf16[128,2,512]{2,1,0:T(2,128)(2,1)S(1)} all-to-all(bf16[128,2,512]{2,1,0:T(2,128)(2,1)S(1)} %bitcast.91), channel_id=1, replica_groups=mesh['row'=16,'col'=8] {'row','col'}, dimensions={0} | all-to-all | bytes 524288 | tf_op jit(solution)/shard_map/all_to_all | solution.py:115
  (103 shorter events, 41.7 us)
Async XLA Ops:
  2.4 22.0 %all-to-all-start = ((bf16[128,2,512]{2,1,0:T(2,128)(2,1)}), bf16[128,2,512]{2,1,0:T(2,128)(2,1)S(1)}, u32[]{:S(2)}, u32[]{:S(2)}) async-start(bf16[128,2,512]{2,1,0:T(2,128)(2,1)} %bitcast.1), calls=%async_computation | async-start | bytes 524288 | tf_op jit(solution)/shard_map/all_to_all | solution.py:60
  24.5 7.3 %copy-start = (bf16[1024,4096]{1,0:T(8,128)(2,1)S(1)}, bf16[1024,4096]{1,0:T(8,128)(2,1)}, u32[]{:S(2)}) copy-start(bf16[1024,4096]{1,0:T(8,128)(2,1)} %param.6) | copy-start | bytes 25165828
  32.6 2.4 %collective-permute-start = (bf16[32,2048]{1,0:T(8,128)(2,1)S(1)}, bf16[32,2048]{1,0:T(8,128)(2,1)S(1)}, u32[]{:S(2)}, u32[]{:S(2)}) collective-permute-start(bf16[32,2048]{1,0:T(8,128)(2,1)S(1)} %convolution_convert_fusion.5), channel_id=1, source_target_pairs={{0,8},{8,0},{16,24},{24,16},{32,40},{40,32},{48,56},{56,48},{64,72... | collective-permute-start | bytes 393224 | tf_op jit(solution)/shard_map/ppermute | solution.py:23
  35.0 4.8 %collective-permute-start.1 = (bf16[32,2048]{1,0:T(8,128)(2,1)S(1)}, bf16[32,2048]{1,0:T(8,128)(2,1)S(1)}, u32[]{:S(2)}, u32[]{:S(2)}) collective-permute-start(bf16[32,2048]{1,0:T(8,128)(2,1)S(1)} %fusion.10), channel_id=1, source_target_pairs={{0,64},{8,72},{16,80},{24,88},{32,96},{40,104},{48,112},{56,120},{... | collective-permute-start | bytes 393224 | tf_op jit(solution)/shard_map/ppermute | solution.py:23
  39.9 5.4 %collective-permute-start.4 = (bf16[32,2048]{1,0:T(8,128)(2,1)S(1)}, bf16[32,2048]{1,0:T(8,128)(2,1)S(1)}, u32[]{:S(2)}, u32[]{:S(2)}) collective-permute-start(bf16[32,2048]{1,0:T(8,128)(2,1)S(1)} %fusion.16), channel_id=1, source_target_pairs={{0,32},{8,40},{16,48},{24,56},{32,0},{40,8},{48,16},{56,24},{64,96... | collective-permute-start | bytes 393224 | tf_op jit(solution)/shard_map/ppermute | solution.py:23
  40.7 5.6 %collective-permute-start.3 = (bf16[32,2048]{1,0:T(8,128)(2,1)S(1)}, bf16[32,2048]{1,0:T(8,128)(2,1)S(1)}, u32[]{:S(2)}, u32[]{:S(2)}) collective-permute-start(bf16[32,2048]{1,0:T(8,128)(2,1)S(1)} %fusion.16), channel_id=1, source_target_pairs={{0,48},{8,56},{16,0},{24,8},{32,16},{40,24},{48,32},{56,40},{64,11... | collective-permute-start | bytes 393224 | tf_op jit(solution)/shard_map/ppermute | solution.py:23
  42.9 6.3 %collective-permute-start.2 = (bf16[32,2048]{1,0:T(8,128)(2,1)S(1)}, bf16[32,2048]{1,0:T(8,128)(2,1)S(1)}, u32[]{:S(2)}, u32[]{:S(2)}) collective-permute-start(bf16[32,2048]{1,0:T(8,128)(2,1)S(1)} %fusion.16), channel_id=1, source_target_pairs={{0,16},{8,24},{16,32},{24,40},{32,48},{40,56},{48,0},{56,8},{64,80... | collective-permute-start | bytes 393224 | tf_op jit(solution)/shard_map/ppermute | solution.py:23
  49.3 3.2 %collective-permute-start.5 = (bf16[32,2048]{1,0:T(8,128)(2,1)S(1)}, bf16[32,2048]{1,0:T(8,128)(2,1)S(1)}, u32[]{:S(2)}, u32[]{:S(2)}) collective-permute-start(bf16[32,2048]{1,0:T(8,128)(2,1)S(1)} %fusion.2), channel_id=1, source_target_pairs={{0,8},{8,0},{16,24},{24,16},{32,40},{40,32},{48,56},{56,48},{64,72... | collective-permute-start | bytes 393224 | tf_op jit(solution)/shard_map/ppermute | solution.py:23
  54.7 1.4 collective-permute-start.6
  56.1 5.0 %collective-permute-start.7 = (bf16[32,2048]{1,0:T(8,128)(2,1)S(1)}, bf16[32,2048]{1,0:T(8,128)(2,1)S(1)}, u32[]{:S(2)}, u32[]{:S(2)}) collective-permute-start(bf16[32,2048]{1,0:T(8,128)(2,1)S(1)} %fusion.11), channel_id=1, source_target_pairs={{0,64},{8,72},{16,80},{24,88},{32,96},{40,104},{48,112},{56,120},{... | collective-permute-start | bytes 393224 | tf_op jit(solution)/shard_map/ppermute | solution.py:23
  61.2 5.4 %collective-permute-start.10 = (bf16[32,2048]{1,0:T(8,128)(2,1)S(1)}, bf16[32,2048]{1,0:T(8,128)(2,1)S(1)}, u32[]{:S(2)}, u32[]{:S(2)}) collective-permute-start(bf16[32,2048]{1,0:T(8,128)(2,1)S(1)} %fusion.17), channel_id=1, source_target_pairs={{0,32},{8,40},{16,48},{24,56},{32,0},{40,8},{48,16},{56,24},{64,96... | collective-permute-start | bytes 393224 | tf_op jit(solution)/shard_map/ppermute | solution.py:23
  61.7 5.8 %collective-permute-start.9 = (bf16[32,2048]{1,0:T(8,128)(2,1)S(1)}, bf16[32,2048]{1,0:T(8,128)(2,1)S(1)}, u32[]{:S(2)}, u32[]{:S(2)}) collective-permute-start(bf16[32,2048]{1,0:T(8,128)(2,1)S(1)} %fusion.17), channel_id=1, source_target_pairs={{0,48},{8,56},{16,0},{24,8},{32,16},{40,24},{48,32},{56,40},{64,11... | collective-permute-start | bytes 393224 | tf_op jit(solution)/shard_map/ppermute | solution.py:23
  62.6 7.6 %collective-permute-start.8 = (bf16[32,2048]{1,0:T(8,128)(2,1)S(1)}, bf16[32,2048]{1,0:T(8,128)(2,1)S(1)}, u32[]{:S(2)}, u32[]{:S(2)}) collective-permute-start(bf16[32,2048]{1,0:T(8,128)(2,1)S(1)} %fusion.17), channel_id=1, source_target_pairs={{0,16},{8,24},{16,32},{24,40},{32,48},{40,56},{48,0},{56,8},{64,80... | collective-permute-start | bytes 393224 | tf_op jit(solution)/shard_map/ppermute | solution.py:23
  70.4 2.9 %collective-permute-start.11 = (bf16[32,2048]{1,0:T(8,128)(2,1)S(1)}, bf16[32,2048]{1,0:T(8,128)(2,1)S(1)}, u32[]{:S(2)}, u32[]{:S(2)}) collective-permute-start(bf16[32,2048]{1,0:T(8,128)(2,1)S(1)} %fusion.3), channel_id=1, source_target_pairs={{0,8},{8,0},{16,24},{24,16},{32,40},{40,32},{48,56},{56,48},{64,72... | collective-permute-start | bytes 393224 | tf_op jit(solution)/shard_map/ppermute | solution.py:23
  75.5 1.4 collective-permute-start.12
  76.9 5.0 %collective-permute-start.13 = (bf16[32,2048]{1,0:T(8,128)(2,1)S(1)}, bf16[32,2048]{1,0:T(8,128)(2,1)S(1)}, u32[]{:S(2)}, u32[]{:S(2)}) collective-permute-start(bf16[32,2048]{1,0:T(8,128)(2,1)S(1)} %fusion.12), channel_id=1, source_target_pairs={{0,64},{8,72},{16,80},{24,88},{32,96},{40,104},{48,112},{56,120},{... | collective-permute-start | bytes 393224 | tf_op jit(solution)/shard_map/ppermute | solution.py:23
  82.0 5.4 %collective-permute-start.16 = (bf16[32,2048]{1,0:T(8,128)(2,1)S(1)}, bf16[32,2048]{1,0:T(8,128)(2,1)S(1)}, u32[]{:S(2)}, u32[]{:S(2)}) collective-permute-start(bf16[32,2048]{1,0:T(8,128)(2,1)S(1)} %fusion.18), channel_id=1, source_target_pairs={{0,32},{8,40},{16,48},{24,56},{32,0},{40,8},{48,16},{56,24},{64,96... | collective-permute-start | bytes 393224 | tf_op jit(solution)/shard_map/ppermute | solution.py:23
  82.5 5.8 %collective-permute-start.15 = (bf16[32,2048]{1,0:T(8,128)(2,1)S(1)}, bf16[32,2048]{1,0:T(8,128)(2,1)S(1)}, u32[]{:S(2)}, u32[]{:S(2)}) collective-permute-start(bf16[32,2048]{1,0:T(8,128)(2,1)S(1)} %fusion.18), channel_id=1, source_target_pairs={{0,48},{8,56},{16,0},{24,8},{32,16},{40,24},{48,32},{56,40},{64,11... | collective-permute-start | bytes 393224 | tf_op jit(solution)/shard_map/ppermute | solution.py:23
  83.4 7.6 %collective-permute-start.14 = (bf16[32,2048]{1,0:T(8,128)(2,1)S(1)}, bf16[32,2048]{1,0:T(8,128)(2,1)S(1)}, u32[]{:S(2)}, u32[]{:S(2)}) collective-permute-start(bf16[32,2048]{1,0:T(8,128)(2,1)S(1)} %fusion.18), channel_id=1, source_target_pairs={{0,16},{8,24},{16,32},{24,40},{32,48},{40,56},{48,0},{56,8},{64,80... | collective-permute-start | bytes 393224 | tf_op jit(solution)/shard_map/ppermute | solution.py:23
  91.2 2.7 %collective-permute-start.17 = (bf16[32,2048]{1,0:T(8,128)(2,1)S(1)}, bf16[32,2048]{1,0:T(8,128)(2,1)S(1)}, u32[]{:S(2)}, u32[]{:S(2)}) collective-permute-start(bf16[32,2048]{1,0:T(8,128)(2,1)S(1)} %fusion.5), channel_id=1, source_target_pairs={{0,8},{8,0},{16,24},{24,16},{32,40},{40,32},{48,56},{56,48},{64,72... | collective-permute-start | bytes 393224 | tf_op jit(solution)/shard_map/ppermute | solution.py:23
  96.1 1.4 collective-permute-start.18
  97.5 5.0 %collective-permute-start.19 = (bf16[32,2048]{1,0:T(8,128)(2,1)S(1)}, bf16[32,2048]{1,0:T(8,128)(2,1)S(1)}, u32[]{:S(2)}, u32[]{:S(2)}) collective-permute-start(bf16[32,2048]{1,0:T(8,128)(2,1)S(1)} %fusion.13), channel_id=1, source_target_pairs={{0,64},{8,72},{16,80},{24,88},{32,96},{40,104},{48,112},{56,120},{... | collective-permute-start | bytes 393224 | tf_op jit(solution)/shard_map/ppermute | solution.py:23
  102.6 5.4 %collective-permute-start.22 = (bf16[32,2048]{1,0:T(8,128)(2,1)S(1)}, bf16[32,2048]{1,0:T(8,128)(2,1)S(1)}, u32[]{:S(2)}, u32[]{:S(2)}) collective-permute-start(bf16[32,2048]{1,0:T(8,128)(2,1)S(1)} %fusion.19), channel_id=1, source_target_pairs={{0,32},{8,40},{16,48},{24,56},{32,0},{40,8},{48,16},{56,24},{64,96... | collective-permute-start | bytes 393224 | tf_op jit(solution)/shard_map/ppermute | solution.py:23
  103.1 5.8 %collective-permute-start.21 = (bf16[32,2048]{1,0:T(8,128)(2,1)S(1)}, bf16[32,2048]{1,0:T(8,128)(2,1)S(1)}, u32[]{:S(2)}, u32[]{:S(2)}) collective-permute-start(bf16[32,2048]{1,0:T(8,128)(2,1)S(1)} %fusion.19), channel_id=1, source_target_pairs={{0,48},{8,56},{16,0},{24,8},{32,16},{40,24},{48,32},{56,40},{64,11... | collective-permute-start | bytes 393224 | tf_op jit(solution)/shard_map/ppermute | solution.py:23
  104.0 7.6 %collective-permute-start.20 = (bf16[32,2048]{1,0:T(8,128)(2,1)S(1)}, bf16[32,2048]{1,0:T(8,128)(2,1)S(1)}, u32[]{:S(2)}, u32[]{:S(2)}) collective-permute-start(bf16[32,2048]{1,0:T(8,128)(2,1)S(1)} %fusion.19), channel_id=1, source_target_pairs={{0,16},{8,24},{16,32},{24,40},{32,48},{40,56},{48,0},{56,8},{64,80... | collective-permute-start | bytes 393224 | tf_op jit(solution)/shard_map/ppermute | solution.py:23
  111.7 2.9 %collective-permute-start.23 = (bf16[32,2048]{1,0:T(8,128)(2,1)S(1)}, bf16[32,2048]{1,0:T(8,128)(2,1)S(1)}, u32[]{:S(2)}, u32[]{:S(2)}) collective-permute-start(bf16[32,2048]{1,0:T(8,128)(2,1)S(1)} %fusion.6), channel_id=1, source_target_pairs={{0,8},{8,0},{16,24},{24,16},{32,40},{40,32},{48,56},{56,48},{64,72... | collective-permute-start | bytes 393224 | tf_op jit(solution)/shard_map/ppermute | solution.py:23
  116.9 1.4 collective-permute-start.24
  118.3 5.0 %collective-permute-start.25 = (bf16[32,2048]{1,0:T(8,128)(2,1)S(1)}, bf16[32,2048]{1,0:T(8,128)(2,1)S(1)}, u32[]{:S(2)}, u32[]{:S(2)}) collective-permute-start(bf16[32,2048]{1,0:T(8,128)(2,1)S(1)} %fusion.14), channel_id=1, source_target_pairs={{0,64},{8,72},{16,80},{24,88},{32,96},{40,104},{48,112},{56,120},{... | collective-permute-start | bytes 393224 | tf_op jit(solution)/shard_map/ppermute | solution.py:23
  123.4 5.4 %collective-permute-start.28 = (bf16[32,2048]{1,0:T(8,128)(2,1)S(1)}, bf16[32,2048]{1,0:T(8,128)(2,1)S(1)}, u32[]{:S(2)}, u32[]{:S(2)}) collective-permute-start(bf16[32,2048]{1,0:T(8,128)(2,1)S(1)} %fusion.20), channel_id=1, source_target_pairs={{0,32},{8,40},{16,48},{24,56},{32,0},{40,8},{48,16},{56,24},{64,96... | collective-permute-start | bytes 393224 | tf_op jit(solution)/shard_map/ppermute | solution.py:23
  123.9 5.8 %collective-permute-start.27 = (bf16[32,2048]{1,0:T(8,128)(2,1)S(1)}, bf16[32,2048]{1,0:T(8,128)(2,1)S(1)}, u32[]{:S(2)}, u32[]{:S(2)}) collective-permute-start(bf16[32,2048]{1,0:T(8,128)(2,1)S(1)} %fusion.20), channel_id=1, source_target_pairs={{0,48},{8,56},{16,0},{24,8},{32,16},{40,24},{48,32},{56,40},{64,11... | collective-permute-start | bytes 393224 | tf_op jit(solution)/shard_map/ppermute | solution.py:23
  124.8 7.6 %collective-permute-start.26 = (bf16[32,2048]{1,0:T(8,128)(2,1)S(1)}, bf16[32,2048]{1,0:T(8,128)(2,1)S(1)}, u32[]{:S(2)}, u32[]{:S(2)}) collective-permute-start(bf16[32,2048]{1,0:T(8,128)(2,1)S(1)} %fusion.20), channel_id=1, source_target_pairs={{0,16},{8,24},{16,32},{24,40},{32,48},{40,56},{48,0},{56,8},{64,80... | collective-permute-start | bytes 393224 | tf_op jit(solution)/shard_map/ppermute | solution.py:23
  132.5 2.7 %collective-permute-start.29 = (bf16[32,2048]{1,0:T(8,128)(2,1)S(1)}, bf16[32,2048]{1,0:T(8,128)(2,1)S(1)}, u32[]{:S(2)}, u32[]{:S(2)}) collective-permute-start(bf16[32,2048]{1,0:T(8,128)(2,1)S(1)} %fusion.8), channel_id=1, source_target_pairs={{0,8},{8,0},{16,24},{24,16},{32,40},{40,32},{48,56},{56,48},{64,72... | collective-permute-start | bytes 393224 | tf_op jit(solution)/shard_map/ppermute | solution.py:23

commit v7 on v6

--- a/solution.py
+++ b/solution.py
@@ -1,9 +1,93 @@
 import jax
 import jax.numpy as jnp
 from jax import lax
+from jax.experimental import pallas as pl
+from jax.experimental.pallas import tpu as pltpu
 from jax.sharding import PartitionSpec as P
 
 STEPS = 3
+LOADS = 8
+
+NN = (((1,), (0,)), ((), ()))
+NT = (((1,), (1,)), ((), ()))
+
+
+def product(left, right, dims):
+    return lax.dot_general(left, right, dims, preferred_element_type=jnp.float32)
+
+
+def first_kernel(field_ref, scale_ref, basis_ref, own_ref, other_ref, *held):
+    *held, loaded = held
+    core = lax.rem(lax.axis_index("row"), 2)
+    width = held[0].shape[1]
+    chunk = 2 * width // LOADS
+    copies = []
+    for h, which in enumerate((core, 1 - core)):
+        for k in range(LOADS // 2):
+            start = pl.multiple_of(which * width + k * chunk, chunk)
+            copies.append(
+                pltpu.make_async_copy(
+                    basis_ref.at[:, pl.ds(start, chunk)],
+                    held[h].at[:, pl.ds(k * chunk, chunk)],
+                    loaded.at[h * (LOADS // 2) + k],
+                )
+            )
+    for copy in copies:
+        copy.start()
+    nodes = jnp.zeros((field_ref.shape[1], held[0].shape[0]), jnp.float32)
+    for k, copy in enumerate(copies):
+        copy.wait()
+        h, place = k // (LOADS // 2), pl.ds(k % (LOADS // 2) * chunk, chunk)
+        nodes += product(field_ref[h, :, place], held[h][:, place], NT)
+    half = nodes.shape[0] // 2
+    scale = scale_ref[...]
+    nodes = jnp.concatenate([scale * nodes[half:], -scale * nodes[:half]], axis=0)
+    nodes = nodes.astype(jnp.bfloat16)
+    for k in range(LOADS // 2):
+        place = pl.ds(k * chunk, chunk)
+        other_ref[:, place] = product(nodes, held[1][:, place], NN).astype(jnp.bfloat16)
+        own_ref[:, place] = product(nodes, held[0][:, place], NN)
+
+
+def first_operator(field, scale, basis):
+    _, rows, width = field.shape
+    nodes, modes = basis.shape
+    in_vmem = pl.BlockSpec(memory_space=pltpu.VMEM)
+    return pl.pallas_call(
+        first_kernel,
+        out_shape=(
+            jax.ShapeDtypeStruct((rows, width), jnp.float32),
+            jax.ShapeDtypeStruct((rows, width), jnp.bfloat16),
+            jax.ShapeDtypeStruct((nodes, width), basis.dtype),
+            jax.ShapeDtypeStruct((nodes, width), basis.dtype),
+        ),
+        in_specs=[in_vmem, in_vmem, pl.BlockSpec(memory_space=pl.ANY)],
+        out_specs=(in_vmem,) * 4,
+        scratch_shapes=[pltpu.SemaphoreType.DMA((LOADS,))],
+        compiler_params=pltpu.CompilerParams(vmem_limit_bytes=44 << 20),
+        cost_estimate=pl.CostEstimate(
+            flops=4 * rows * modes * nodes, bytes_accessed=2 * modes * nodes, transcendentals=0
+        ),
+    )(field, scale, basis)
+
+
+def turn_kernel(basis_ref, turned_ref):
+    turned_ref[...] = basis_ref[...].T
+
+
+def turned(basis, block=512):
+    nodes, width = basis.shape
+    return pl.pallas_call(
+        turn_kernel,
+        out_shape=jax.ShapeDtypeStruct((width, nodes), basis.dtype),
+        grid=(width // block,),
+        in_specs=[pl.BlockSpec((nodes, block), lambda j: (0, j))],
+        out_specs=pl.BlockSpec((block, nodes), lambda j: (j, 0)),
+        compiler_params=pltpu.CompilerParams(vmem_limit_bytes=10 << 20),
+        cost_estimate=pl.CostEstimate(
+            flops=0, bytes_accessed=4 * width * nodes, transcendentals=0
+        ),
+    )(basis)
 
 
 def on_device(mode_basis, node_coords, quad_weights, magnetization, decay_rates, directions):
@@ -63,50 +147,42 @@
         jnp.transpose(every, (2, 0, 1, 3)).reshape(columns, mode_count)
     )
 
-    def to_nodes(array, basis):
-        return lax.dot_general(
-            array, basis, (((1,), (1,)), ((), ())), preferred_element_type=f32
-        )
-
-    def to_modes(nodes, basis):
-        return lax.dot_general(
-            nodes, basis, (((1,), (0,)), ((), ())), preferred_element_type=f32
-        )
-
-    def turned(nodes, half_step):
+    def mixed(nodes, half_step):
         factor = 0.5 if half_step % 2 == 0 else 1.0
         scale = factor * weights[half_step]
         real, imag = nodes[:row_count], nodes[row_count:]
         rows = jnp.concatenate([scale * imag, -scale * real], axis=0)
         return lax.optimization_barrier(rows.astype(bf16))
 
-    basis_own = half_of(mode_basis, core, 1)
-    basis_other = half_of(mode_basis, 1 - core, 1)
     field = half_of(every, core, 1)
-    field_other = half_of(every, 1 - core, 1)
+    both = jnp.stack([field, half_of(every, 1 - core, 1)])
+
+    kept, sent, basis_own, basis_other = first_operator(both, 0.5 * weights[0], mode_basis)
+    turned_own, turned_other = turned(basis_own), turned(basis_other)
+    sums = over_chips(kept + to_other_core(sent).astype(f32))
 
     def weighted(own, other, half_step):
-        kept = lax.optimization_barrier(to_nodes(own, basis_own))
-        return turned(kept + to_nodes(other, basis_other), half_step)
+        kept = lax.optimization_barrier(product(own, turned_own, NN))
+        return mixed(kept + product(other, turned_other, NN), half_step)
 
     def summed(nodes):
-        arrived = to_other_core(to_modes(nodes, basis_other).astype(bf16))
-        kept = lax.optimization_barrier(to_modes(nodes, basis_own))
+        arrived = to_other_core(product(nodes, basis_other, NN).astype(bf16))
+        kept = lax.optimization_barrier(product(nodes, basis_own, NN))
         return over_chips(kept + arrived.astype(f32))
 
     for step in range(STEPS):
-        sums = summed(weighted(field, field_other, 2 * step))
+        if step > 0:
+            sums = summed(weighted(field, to_other_core(field), 2 * step))
         half = (sums + (1.0 - 0.5 * rates) * field.astype(f32)).astype(bf16)
         nodes = weighted(half, to_other_core(half), 2 * step + 1)
         if step + 1 < STEPS:
             update = summed(nodes) + (0.0 - 1.0 * rates) * half.astype(f32)
             field = (field.astype(f32) + update).astype(bf16)
-            field_other = to_other_core(field)
 
     local = field.astype(f32) + (0.0 - 1.0 * rates) * half.astype(f32)
     local = jnp.where(first_chip, local, 0.0)
-    part_own = (to_modes(nodes, basis_own) + local).astype(bf16)
-    part_other = to_modes(nodes, basis_other).astype(bf16)
+    part_own = (product(nodes, basis_own, NN) + local).astype(bf16)
+    part_other = product(nodes, basis_other, NN).astype(bf16)
     low = jnp.where(first_core, part_own, part_other)
     high = jnp.where(first_core, part_other, part_own)
     sent = jnp.concatenate([low, high], axis=1)

time: 154 us -> 146 us (0.948)
  matrix products: 30.5 us -> 16.5 us
  Pallas kernels: 0 us -> 9.21 us
  waiting for transfers between devices: 67.8 us -> 62.5 us
  starting transfers between devices: 33.9 us -> 36.5 us
    dot_general x24 -> x20, matrix products: 30.5 us -> 16.5 us  [product(): lax.dot_general(left, right, dims, preferred_element_type=jnp.float32)]
    pallas_call x0 -> x3, Pallas kernels: none -> 9.21 us  [the longest x1 5.7 us: first_operator(): pl.pallas_call(first_kernel, out_shape=(jax.ShapeDtypeStruct((rows, width...]
    ppermute x30, waiting for transfers between devices: 59.3 us -> 54 us  [move(): lax.ppermute(array, 'row', [(r, target(r)) for r in range(row_count)])]
    ppermute x30, starting transfers between devices: 22.4 us -> 25 us  [move(): lax.ppermute(array, 'row', [(r, target(r)) for r in range(row_count)])]
  transfers between devices with their start and end apart: 31 -> 31, of which waited for: 26 -> 29; matrix products, arithmetic and copies ran while one was open for 8% -> 6% of each run, Pallas kernels for 0% -> 2%
where the time goes in v7:
time: 146 us
  waiting for transfers between devices  62.5 us (43%)
  starting transfers between devices  36.5 us (25%)
  matrix products  16.5 us (11%)
  blocking collectives  13.8 us (9%)
  Pallas kernels  9.21 us (6%)
  local copies, waits for them, and re-layouts  4.61 us (3%)
  other arithmetic  2.37 us (2%)
    ppermute x30, waiting for transfers between devices, move(): lax.ppermute(array, 'row', [(r, target(r)) for r in range(row_count)])  54 us
    ppermute x30, starting transfers between devices, move(): lax.ppermute(array, 'row', [(r, target(r)) for r in range(row_count)])  25 us
    dot_general x20, matrix products, product(): lax.dot_general(left, right, dims, preferred_element_type=jnp.float32)  16.5 us
    all_to_all x1, blocking collectives, on_device(): every = lax.all_to_all(sent, ('row', 'col'), 0, 0)  13.8 us
    all_to_all x1, starting transfers between devices, on_device(): every = lax.all_to_all(sent, ('row', 'col'), 0, 0)  11.5 us
    all_to_all x1, waiting for transfers between devices, on_device(): every = lax.all_to_all(sent, ('row', 'col'), 0, 0)  8.42 us
    pallas_call x1, Pallas kernels, first_operator(): pl.pallas_call(first_kernel, out_shape=(jax.ShapeDtypeStruct((rows, width...  5.7 us
    pallas_call x2, Pallas kernels, turned(): pl.pallas_call(turn_kernel, out_shape=jax.ShapeDtypeStruct((width, nodes)...  3.51 us
  transfers between devices with their start and end apart: 31, of which 29 were waited for; matrix products, arithmetic and copies ran while one was open for 6% of the time, Pallas kernels for 2%

profile of v7, /device:TPU:1, one launch (start us, length us, event | category | flops | bytes accessed | tf_op | source)
XLA Modules:
  0.0 145.7 jit_solution(12186094730578976655)
XLA Ops:
  1.5 0.9 broadcast_in_dim.5
  2.4 11.5 %all-to-all-start = ((bf16[128,2,512]{2,1,0:T(2,128)(2,1)}), bf16[128,2,512]{2,1,0:T(2,128)(2,1)S(1)}, u32[]{:S(2)}, u32[]{:S(2)}) async-start(bf16[128,2,512]{2,1,0:T(2,128)(2,1)} %bitcast.1), calls=%async_computation | async-start | bytes 524288 | tf_op jit(solution)/shard_map/all_to_all | solution.py:144
  16.0 8.4 %all-to-all-done = bf16[128,2,512]{2,1,0:T(2,128)(2,1)S(1)} async-done(((bf16[128,2,512]{2,1,0:T(2,128)(2,1)}), bf16[128,2,512]{2,1,0:T(2,128)(2,1)S(1)}, u32[]{:S(2)}, u32[]{:S(2)}) %all-to-all-start) | async-done | bytes 262176 | tf_op jit(solution)/shard_map/all_to_all | solution.py:144
  24.6 5.7 %shard_map.64 = (f32[32,2048]{1,0:T(8,128)S(1)}, bf16[32,2048]{1,0:T(8,128)(2,1)S(1)}, bf16[1024,2048]{1,0:T(8,128)(2,1)S(1)}, bf16[1024,2048]{1,0:T(8,128)(2,1)S(1)}) custom-call(bf16[2,32,2048]{2,1,0:T(8,128)(2,1)S(1)} %pad_maximum_fusion.field_ref, f32[16,1024]{1,0:T(8,128)S(1)} %fusion.31.scale_ref, bf16[1024,4096]{1,0:T(8,128)(2,1)} %basis_ref.1), custom_call_target="tpu_custom_call" | custom-call | flops 536870912 | bytes 8388608 | tf_op jit(solution)/shard_map/pallas_call | solution.py:56
  30.3 1.4 collective-permute-start
  31.7 1.0 collective-permute-done
  33.2 4.4 %collective-permute-done.1 = bf16[32,2048]{1,0:T(8,128)(2,1)S(1)} collective-permute-done((bf16[32,2048]{1,0:T(8,128)(2,1)S(1)}, bf16[32,2048]{1,0:T(8,128)(2,1)S(1)}, u32[]{:S(2)}, u32[]{:S(2)}) %collective-permute-start.1) | collective-permute-done | bytes 131104 | tf_op jit(solution)/shard_map/ppermute | solution.py:107
  38.4 2.2 %collective-permute-start.3 = (bf16[32,2048]{1,0:T(8,128)(2,1)S(1)}, bf16[32,2048]{1,0:T(8,128)(2,1)S(1)}, u32[]{:S(2)}, u32[]{:S(2)}) collective-permute-start(bf16[32,2048]{1,0:T(8,128)(2,1)S(1)} %fusion.15), channel_id=1, source_target_pairs={{0,48},{8,56},{16,0},{24,8},{32,16},{40,24},{48,32},{56,40},{64,11... | collective-permute-start | bytes 393224 | tf_op jit(solution)/shard_map/ppermute | solution.py:107
  40.6 1.8 %shard_map.65 = bf16[2048,1024]{1,0:T(8,128)(2,1)S(1)} custom-call(bf16[1024,2048]{1,0:T(8,128)(2,1)S(1)} %get-tuple-element.18.basis_ref), custom_call_target="tpu_custom_call" | custom-call | bytes 8388608 | tf_op jit(solution)/shard_map/pallas_call | solution.py:80
  42.4 1.8 %shard_map.66 = bf16[2048,1024]{1,0:T(8,128)(2,1)S(1)} custom-call(bf16[1024,2048]{1,0:T(8,128)(2,1)S(1)} %get-tuple-element.19.basis_ref), custom_call_target="tpu_custom_call" | custom-call | bytes 8388608 | tf_op jit(solution)/shard_map/pallas_call | solution.py:80
  44.2 2.7 %collective-permute-done.2 = bf16[32,2048]{1,0:T(8,128)(2,1)S(1)} collective-permute-done((bf16[32,2048]{1,0:T(8,128)(2,1)S(1)}, bf16[32,2048]{1,0:T(8,128)(2,1)S(1)}, u32[]{:S(2)}, u32[]{:S(2)}) %collective-permute-start.2) | collective-permute-done | bytes 131104 | tf_op jit(solution)/shard_map/ppermute | solution.py:107
  47.0 1.9 %collective-permute-start.5 = (bf16[32,2048]{1,0:T(8,128)(2,1)S(1)}, bf16[32,2048]{1,0:T(8,128)(2,1)S(1)}, u32[]{:S(2)}, u32[]{:S(2)}) collective-permute-start(bf16[32,2048]{1,0:T(8,128)(2,1)S(1)} %fusion.2), channel_id=1, source_target_pairs={{0,8},{8,0},{16,24},{24,16},{32,40},{40,32},{48,56},{56,48},{64,72... | collective-permute-start | bytes 393224 | tf_op jit(solution)/shard_map/ppermute | solution.py:107
  53.4 4.4 %collective-permute-done.7 = bf16[32,2048]{1,0:T(8,128)(2,1)S(1)} collective-permute-done((bf16[32,2048]{1,0:T(8,128)(2,1)S(1)}, bf16[32,2048]{1,0:T(8,128)(2,1)S(1)}, u32[]{:S(2)}, u32[]{:S(2)}) %collective-permute-start.7) | collective-permute-done | bytes 131104 | tf_op jit(solution)/shard_map/ppermute | solution.py:107
  59.8 3.4 %collective-permute-done.10 = bf16[32,2048]{1,0:T(8,128)(2,1)S(1)} collective-permute-done((bf16[32,2048]{1,0:T(8,128)(2,1)S(1)}, bf16[32,2048]{1,0:T(8,128)(2,1)S(1)}, u32[]{:S(2)}, u32[]{:S(2)}) %collective-permute-start.10) | collective-permute-done | bytes 131104 | tf_op jit(solution)/shard_map/ppermute | solution.py:107
  63.9 2.7 %collective-permute-done.8 = bf16[32,2048]{1,0:T(8,128)(2,1)S(1)} collective-permute-done((bf16[32,2048]{1,0:T(8,128)(2,1)S(1)}, bf16[32,2048]{1,0:T(8,128)(2,1)S(1)}, u32[]{:S(2)}, u32[]{:S(2)}) %collective-permute-start.8) | collective-permute-done | bytes 131104 | tf_op jit(solution)/shard_map/ppermute | solution.py:107
  66.7 1.8 %collective-permute-start.11 = (bf16[32,2048]{1,0:T(8,128)(2,1)S(1)}, bf16[32,2048]{1,0:T(8,128)(2,1)S(1)}, u32[]{:S(2)}, u32[]{:S(2)}) collective-permute-start(bf16[32,2048]{1,0:T(8,128)(2,1)S(1)} %fusion.3), channel_id=1, source_target_pairs={{0,8},{8,0},{16,24},{24,16},{32,40},{40,32},{48,56},{56,48},{64,72... | collective-permute-start | bytes 393224 | tf_op jit(solution)/shard_map/ppermute | solution.py:107
  73.0 4.4 %collective-permute-done.13 = bf16[32,2048]{1,0:T(8,128)(2,1)S(1)} collective-permute-done((bf16[32,2048]{1,0:T(8,128)(2,1)S(1)}, bf16[32,2048]{1,0:T(8,128)(2,1)S(1)}, u32[]{:S(2)}, u32[]{:S(2)}) %collective-permute-start.13) | collective-permute-done | bytes 131104 | tf_op jit(solution)/shard_map/ppermute | solution.py:107
  78.0 0.9 collective-permute-start.15
  79.5 3.4 %collective-permute-done.16 = bf16[32,2048]{1,0:T(8,128)(2,1)S(1)} collective-permute-done((bf16[32,2048]{1,0:T(8,128)(2,1)S(1)}, bf16[32,2048]{1,0:T(8,128)(2,1)S(1)}, u32[]{:S(2)}, u32[]{:S(2)}) %collective-permute-start.16) | collective-permute-done | bytes 131104 | tf_op jit(solution)/shard_map/ppermute | solution.py:107
  83.6 2.6 %collective-permute-done.14 = bf16[32,2048]{1,0:T(8,128)(2,1)S(1)} collective-permute-done((bf16[32,2048]{1,0:T(8,128)(2,1)S(1)}, bf16[32,2048]{1,0:T(8,128)(2,1)S(1)}, u32[]{:S(2)}, u32[]{:S(2)}) %collective-permute-start.14) | collective-permute-done | bytes 131104 | tf_op jit(solution)/shard_map/ppermute | solution.py:107
  86.3 1.6 %collective-permute-start.17 = (bf16[32,2048]{1,0:T(8,128)(2,1)S(1)}, bf16[32,2048]{1,0:T(8,128)(2,1)S(1)}, u32[]{:S(2)}, u32[]{:S(2)}) collective-permute-start(bf16[32,2048]{1,0:T(8,128)(2,1)S(1)} %fusion.5), channel_id=1, source_target_pairs={{0,8},{8,0},{16,24},{24,16},{32,40},{40,32},{48,56},{56,48},{64,72... | collective-permute-start | bytes 393224 | tf_op jit(solution)/shard_map/ppermute | solution.py:107
  92.5 4.4 %collective-permute-done.19 = bf16[32,2048]{1,0:T(8,128)(2,1)S(1)} collective-permute-done((bf16[32,2048]{1,0:T(8,128)(2,1)S(1)}, bf16[32,2048]{1,0:T(8,128)(2,1)S(1)}, u32[]{:S(2)}, u32[]{:S(2)}) %collective-permute-start.19) | collective-permute-done | bytes 131104 | tf_op jit(solution)/shard_map/ppermute | solution.py:107
  97.5 1.0 collective-permute-start.21
  98.9 3.4 %collective-permute-done.22 = bf16[32,2048]{1,0:T(8,128)(2,1)S(1)} collective-permute-done((bf16[32,2048]{1,0:T(8,128)(2,1)S(1)}, bf16[32,2048]{1,0:T(8,128)(2,1)S(1)}, u32[]{:S(2)}, u32[]{:S(2)}) %collective-permute-start.22) | collective-permute-done | bytes 131104 | tf_op jit(solution)/shard_map/ppermute | solution.py:107
  103.1 2.6 %collective-permute-done.20 = bf16[32,2048]{1,0:T(8,128)(2,1)S(1)} collective-permute-done((bf16[32,2048]{1,0:T(8,128)(2,1)S(1)}, bf16[32,2048]{1,0:T(8,128)(2,1)S(1)}, u32[]{:S(2)}, u32[]{:S(2)}) %collective-permute-start.20) | collective-permute-done | bytes 131104 | tf_op jit(solution)/shard_map/ppermute | solution.py:107
  105.8 1.6 %collective-permute-start.23 = (bf16[32,2048]{1,0:T(8,128)(2,1)S(1)}, bf16[32,2048]{1,0:T(8,128)(2,1)S(1)}, u32[]{:S(2)}, u32[]{:S(2)}) collective-permute-start(bf16[32,2048]{1,0:T(8,128)(2,1)S(1)} %fusion.6), channel_id=1, source_target_pairs={{0,8},{8,0},{16,24},{24,16},{32,40},{40,32},{48,56},{56,48},{64,72... | collective-permute-start | bytes 393224 | tf_op jit(solution)/shard_map/ppermute | solution.py:107
  112.0 4.4 %collective-permute-done.25 = bf16[32,2048]{1,0:T(8,128)(2,1)S(1)} collective-permute-done((bf16[32,2048]{1,0:T(8,128)(2,1)S(1)}, bf16[32,2048]{1,0:T(8,128)(2,1)S(1)}, u32[]{:S(2)}, u32[]{:S(2)}) %collective-permute-start.25) | collective-permute-done | bytes 131104 | tf_op jit(solution)/shard_map/ppermute | solution.py:107
  117.1 1.0 collective-permute-start.27
  118.6 3.4 %collective-permute-done.28 = bf16[32,2048]{1,0:T(8,128)(2,1)S(1)} collective-permute-done((bf16[32,2048]{1,0:T(8,128)(2,1)S(1)}, bf16[32,2048]{1,0:T(8,128)(2,1)S(1)}, u32[]{:S(2)}, u32[]{:S(2)}) %collective-permute-start.28) | collective-permute-done | bytes 131104 | tf_op jit(solution)/shard_map/ppermute | solution.py:107
  122.7 2.6 %collective-permute-done.26 = bf16[32,2048]{1,0:T(8,128)(2,1)S(1)} collective-permute-done((bf16[32,2048]{1,0:T(8,128)(2,1)S(1)}, bf16[32,2048]{1,0:T(8,128)(2,1)S(1)}, u32[]{:S(2)}, u32[]{:S(2)}) %collective-permute-start.26) | collective-permute-done | bytes 131104 | tf_op jit(solution)/shard_map/ppermute | solution.py:107
  125.5 1.6 %collective-permute-start.29 = (bf16[32,2048]{1,0:T(8,128)(2,1)S(1)}, bf16[32,2048]{1,0:T(8,128)(2,1)S(1)}, u32[]{:S(2)}, u32[]{:S(2)}) collective-permute-start(bf16[32,2048]{1,0:T(8,128)(2,1)S(1)} %fusion.8), channel_id=1, source_target_pairs={{0,8},{8,0},{16,24},{24,16},{32,40},{40,32},{48,56},{56,48},{64,72... | collective-permute-start | bytes 393224 | tf_op jit(solution)/shard_map/ppermute | solution.py:107
  131.1 13.8 %all_to_all.10 = bf16[128,2,512]{2,1,0:T(2,128)(2,1)S(1)} all-to-all(bf16[128,2,512]{2,1,0:T(2,128)(2,1)S(1)} %bitcast.108), channel_id=1, replica_groups=mesh['row'=16,'col'=8] {'row','col'}, dimensions={0} | all-to-all | bytes 524288 | tf_op jit(solution)/shard_map/all_to_all | solution.py:191
  (101 shorter events, 36.8 us)
Async XLA Ops:
  2.4 22.0 %all-to-all-start = ((bf16[128,2,512]{2,1,0:T(2,128)(2,1)}), bf16[128,2,512]{2,1,0:T(2,128)(2,1)S(1)}, u32[]{:S(2)}, u32[]{:S(2)}) async-start(bf16[128,2,512]{2,1,0:T(2,128)(2,1)} %bitcast.1), calls=%async_computation | async-start | bytes 524288 | tf_op jit(solution)/shard_map/all_to_all | solution.py:144
  30.3 2.4 %collective-permute-start = (bf16[32,2048]{1,0:T(8,128)(2,1)S(1)}, bf16[32,2048]{1,0:T(8,128)(2,1)S(1)}, u32[]{:S(2)}, u32[]{:S(2)}) collective-permute-start(bf16[32,2048]{1,0:T(8,128)(2,1)S(1)} %get-tuple-element.16), channel_id=1, source_target_pairs={{0,8},{8,0},{16,24},{24,16},{32,40},{40,32},{48,56},{56,48},{64,72... | collective-permute-start | bytes 393224 | tf_op jit(solution)/shard_map/ppermute | solution.py:107
  32.7 4.8 %collective-permute-start.1 = (bf16[32,2048]{1,0:T(8,128)(2,1)S(1)}, bf16[32,2048]{1,0:T(8,128)(2,1)S(1)}, u32[]{:S(2)}, u32[]{:S(2)}) collective-permute-start(bf16[32,2048]{1,0:T(8,128)(2,1)S(1)} %fusion.10), channel_id=1, source_target_pairs={{0,64},{8,72},{16,80},{24,88},{32,96},{40,104},{48,112},{56,120},{... | collective-permute-start | bytes 393224 | tf_op jit(solution)/shard_map/ppermute | solution.py:107
  37.6 6.6 %collective-permute-start.4 = (bf16[32,2048]{1,0:T(8,128)(2,1)S(1)}, bf16[32,2048]{1,0:T(8,128)(2,1)S(1)}, u32[]{:S(2)}, u32[]{:S(2)}) collective-permute-start(bf16[32,2048]{1,0:T(8,128)(2,1)S(1)} %fusion.15), channel_id=1, source_target_pairs={{0,32},{8,40},{16,48},{24,56},{32,0},{40,8},{48,16},{56,24},{64,96... | collective-permute-start | bytes 393224 | tf_op jit(solution)/shard_map/ppermute | solution.py:107
  38.4 5.8 %collective-permute-start.3 = (bf16[32,2048]{1,0:T(8,128)(2,1)S(1)}, bf16[32,2048]{1,0:T(8,128)(2,1)S(1)}, u32[]{:S(2)}, u32[]{:S(2)}) collective-permute-start(bf16[32,2048]{1,0:T(8,128)(2,1)S(1)} %fusion.15), channel_id=1, source_target_pairs={{0,48},{8,56},{16,0},{24,8},{32,16},{40,24},{48,32},{56,40},{64,11... | collective-permute-start | bytes 393224 | tf_op jit(solution)/shard_map/ppermute | solution.py:107
  40.6 6.3 %collective-permute-start.2 = (bf16[32,2048]{1,0:T(8,128)(2,1)S(1)}, bf16[32,2048]{1,0:T(8,128)(2,1)S(1)}, u32[]{:S(2)}, u32[]{:S(2)}) collective-permute-start(bf16[32,2048]{1,0:T(8,128)(2,1)S(1)} %fusion.15), channel_id=1, source_target_pairs={{0,16},{8,24},{16,32},{24,40},{32,48},{40,56},{48,0},{56,8},{64,80... | collective-permute-start | bytes 393224 | tf_op jit(solution)/shard_map/ppermute | solution.py:107
  47.0 2.8 %collective-permute-start.5 = (bf16[32,2048]{1,0:T(8,128)(2,1)S(1)}, bf16[32,2048]{1,0:T(8,128)(2,1)S(1)}, u32[]{:S(2)}, u32[]{:S(2)}) collective-permute-start(bf16[32,2048]{1,0:T(8,128)(2,1)S(1)} %fusion.2), channel_id=1, source_target_pairs={{0,8},{8,0},{16,24},{24,16},{32,40},{40,32},{48,56},{56,48},{64,72... | collective-permute-start | bytes 393224 | tf_op jit(solution)/shard_map/ppermute | solution.py:107
  51.5 1.4 collective-permute-start.6
  52.9 4.8 %collective-permute-start.7 = (bf16[32,2048]{1,0:T(8,128)(2,1)S(1)}, bf16[32,2048]{1,0:T(8,128)(2,1)S(1)}, u32[]{:S(2)}, u32[]{:S(2)}) collective-permute-start(bf16[32,2048]{1,0:T(8,128)(2,1)S(1)} %fusion.11), channel_id=1, source_target_pairs={{0,64},{8,72},{16,80},{24,88},{32,96},{40,104},{48,112},{56,120},{... | collective-permute-start | bytes 393224 | tf_op jit(solution)/shard_map/ppermute | solution.py:107
  57.8 5.4 %collective-permute-start.10 = (bf16[32,2048]{1,0:T(8,128)(2,1)S(1)}, bf16[32,2048]{1,0:T(8,128)(2,1)S(1)}, u32[]{:S(2)}, u32[]{:S(2)}) collective-permute-start(bf16[32,2048]{1,0:T(8,128)(2,1)S(1)} %fusion.16), channel_id=1, source_target_pairs={{0,32},{8,40},{16,48},{24,56},{32,0},{40,8},{48,16},{56,24},{64,96... | collective-permute-start | bytes 393224 | tf_op jit(solution)/shard_map/ppermute | solution.py:107
  58.3 5.6 %collective-permute-start.9 = (bf16[32,2048]{1,0:T(8,128)(2,1)S(1)}, bf16[32,2048]{1,0:T(8,128)(2,1)S(1)}, u32[]{:S(2)}, u32[]{:S(2)}) collective-permute-start(bf16[32,2048]{1,0:T(8,128)(2,1)S(1)} %fusion.16), channel_id=1, source_target_pairs={{0,48},{8,56},{16,0},{24,8},{32,16},{40,24},{48,32},{56,40},{64,11... | collective-permute-start | bytes 393224 | tf_op jit(solution)/shard_map/ppermute | solution.py:107
  59.2 7.4 %collective-permute-start.8 = (bf16[32,2048]{1,0:T(8,128)(2,1)S(1)}, bf16[32,2048]{1,0:T(8,128)(2,1)S(1)}, u32[]{:S(2)}, u32[]{:S(2)}) collective-permute-start(bf16[32,2048]{1,0:T(8,128)(2,1)S(1)} %fusion.16), channel_id=1, source_target_pairs={{0,16},{8,24},{16,32},{24,40},{32,48},{40,56},{48,0},{56,8},{64,80... | collective-permute-start | bytes 393224 | tf_op jit(solution)/shard_map/ppermute | solution.py:107
  66.7 2.8 %collective-permute-start.11 = (bf16[32,2048]{1,0:T(8,128)(2,1)S(1)}, bf16[32,2048]{1,0:T(8,128)(2,1)S(1)}, u32[]{:S(2)}, u32[]{:S(2)}) collective-permute-start(bf16[32,2048]{1,0:T(8,128)(2,1)S(1)} %fusion.3), channel_id=1, source_target_pairs={{0,8},{8,0},{16,24},{24,16},{32,40},{40,32},{48,56},{56,48},{64,72... | collective-permute-start | bytes 393224 | tf_op jit(solution)/shard_map/ppermute | solution.py:107
  71.2 1.4 collective-permute-start.12
  72.6 4.8 %collective-permute-start.13 = (bf16[32,2048]{1,0:T(8,128)(2,1)S(1)}, bf16[32,2048]{1,0:T(8,128)(2,1)S(1)}, u32[]{:S(2)}, u32[]{:S(2)}) collective-permute-start(bf16[32,2048]{1,0:T(8,128)(2,1)S(1)} %fusion.12), channel_id=1, source_target_pairs={{0,64},{8,72},{16,80},{24,88},{32,96},{40,104},{48,112},{56,120},{... | collective-permute-start | bytes 393224 | tf_op jit(solution)/shard_map/ppermute | solution.py:107
  77.5 5.4 %collective-permute-start.16 = (bf16[32,2048]{1,0:T(8,128)(2,1)S(1)}, bf16[32,2048]{1,0:T(8,128)(2,1)S(1)}, u32[]{:S(2)}, u32[]{:S(2)}) collective-permute-start(bf16[32,2048]{1,0:T(8,128)(2,1)S(1)} %fusion.17), channel_id=1, source_target_pairs={{0,32},{8,40},{16,48},{24,56},{32,0},{40,8},{48,16},{56,24},{64,96... | collective-permute-start | bytes 393224 | tf_op jit(solution)/shard_map/ppermute | solution.py:107
  78.0 5.6 %collective-permute-start.15 = (bf16[32,2048]{1,0:T(8,128)(2,1)S(1)}, bf16[32,2048]{1,0:T(8,128)(2,1)S(1)}, u32[]{:S(2)}, u32[]{:S(2)}) collective-permute-start(bf16[32,2048]{1,0:T(8,128)(2,1)S(1)} %fusion.17), channel_id=1, source_target_pairs={{0,48},{8,56},{16,0},{24,8},{32,16},{40,24},{48,32},{56,40},{64,11... | collective-permute-start | bytes 393224 | tf_op jit(solution)/shard_map/ppermute | solution.py:107
  78.9 7.3 %collective-permute-start.14 = (bf16[32,2048]{1,0:T(8,128)(2,1)S(1)}, bf16[32,2048]{1,0:T(8,128)(2,1)S(1)}, u32[]{:S(2)}, u32[]{:S(2)}) collective-permute-start(bf16[32,2048]{1,0:T(8,128)(2,1)S(1)} %fusion.17), channel_id=1, source_target_pairs={{0,16},{8,24},{16,32},{24,40},{32,48},{40,56},{48,0},{56,8},{64,80... | collective-permute-start | bytes 393224 | tf_op jit(solution)/shard_map/ppermute | solution.py:107
  86.3 2.6 %collective-permute-start.17 = (bf16[32,2048]{1,0:T(8,128)(2,1)S(1)}, bf16[32,2048]{1,0:T(8,128)(2,1)S(1)}, u32[]{:S(2)}, u32[]{:S(2)}) collective-permute-start(bf16[32,2048]{1,0:T(8,128)(2,1)S(1)} %fusion.5), channel_id=1, source_target_pairs={{0,8},{8,0},{16,24},{24,16},{32,40},{40,32},{48,56},{56,48},{64,72... | collective-permute-start | bytes 393224 | tf_op jit(solution)/shard_map/ppermute | solution.py:107
  90.6 1.4 collective-permute-start.18
  92.1 4.8 %collective-permute-start.19 = (bf16[32,2048]{1,0:T(8,128)(2,1)S(1)}, bf16[32,2048]{1,0:T(8,128)(2,1)S(1)}, u32[]{:S(2)}, u32[]{:S(2)}) collective-permute-start(bf16[32,2048]{1,0:T(8,128)(2,1)S(1)} %fusion.13), channel_id=1, source_target_pairs={{0,64},{8,72},{16,80},{24,88},{32,96},{40,104},{48,112},{56,120},{... | collective-permute-start | bytes 393224 | tf_op jit(solution)/shard_map/ppermute | solution.py:107
  96.9 5.4 %collective-permute-start.22 = (bf16[32,2048]{1,0:T(8,128)(2,1)S(1)}, bf16[32,2048]{1,0:T(8,128)(2,1)S(1)}, u32[]{:S(2)}, u32[]{:S(2)}) collective-permute-start(bf16[32,2048]{1,0:T(8,128)(2,1)S(1)} %fusion.18), channel_id=1, source_target_pairs={{0,32},{8,40},{16,48},{24,56},{32,0},{40,8},{48,16},{56,24},{64,96... | collective-permute-start | bytes 393224 | tf_op jit(solution)/shard_map/ppermute | solution.py:107
  97.5 5.6 %collective-permute-start.21 = (bf16[32,2048]{1,0:T(8,128)(2,1)S(1)}, bf16[32,2048]{1,0:T(8,128)(2,1)S(1)}, u32[]{:S(2)}, u32[]{:S(2)}) collective-permute-start(bf16[32,2048]{1,0:T(8,128)(2,1)S(1)} %fusion.18), channel_id=1, source_target_pairs={{0,48},{8,56},{16,0},{24,8},{32,16},{40,24},{48,32},{56,40},{64,11... | collective-permute-start | bytes 393224 | tf_op jit(solution)/shard_map/ppermute | solution.py:107
  98.4 7.3 %collective-permute-start.20 = (bf16[32,2048]{1,0:T(8,128)(2,1)S(1)}, bf16[32,2048]{1,0:T(8,128)(2,1)S(1)}, u32[]{:S(2)}, u32[]{:S(2)}) collective-permute-start(bf16[32,2048]{1,0:T(8,128)(2,1)S(1)} %fusion.18), channel_id=1, source_target_pairs={{0,16},{8,24},{16,32},{24,40},{32,48},{40,56},{48,0},{56,8},{64,80... | collective-permute-start | bytes 393224 | tf_op jit(solution)/shard_map/ppermute | solution.py:107
  105.8 2.6 %collective-permute-start.23 = (bf16[32,2048]{1,0:T(8,128)(2,1)S(1)}, bf16[32,2048]{1,0:T(8,128)(2,1)S(1)}, u32[]{:S(2)}, u32[]{:S(2)}) collective-permute-start(bf16[32,2048]{1,0:T(8,128)(2,1)S(1)} %fusion.6), channel_id=1, source_target_pairs={{0,8},{8,0},{16,24},{24,16},{32,40},{40,32},{48,56},{56,48},{64,72... | collective-permute-start | bytes 393224 | tf_op jit(solution)/shard_map/ppermute | solution.py:107
  110.1 1.4 collective-permute-start.24
  111.5 4.8 %collective-permute-start.25 = (bf16[32,2048]{1,0:T(8,128)(2,1)S(1)}, bf16[32,2048]{1,0:T(8,128)(2,1)S(1)}, u32[]{:S(2)}, u32[]{:S(2)}) collective-permute-start(bf16[32,2048]{1,0:T(8,128)(2,1)S(1)} %fusion.14), channel_id=1, source_target_pairs={{0,64},{8,72},{16,80},{24,88},{32,96},{40,104},{48,112},{56,120},{... | collective-permute-start | bytes 393224 | tf_op jit(solution)/shard_map/ppermute | solution.py:107
  116.4 5.7 %collective-permute-start.28 = (bf16[32,2048]{1,0:T(8,128)(2,1)S(1)}, bf16[32,2048]{1,0:T(8,128)(2,1)S(1)}, u32[]{:S(2)}, u32[]{:S(2)}) collective-permute-start(bf16[32,2048]{1,0:T(8,128)(2,1)S(1)} %fusion.19), channel_id=1, source_target_pairs={{0,32},{8,40},{16,48},{24,56},{32,0},{40,8},{48,16},{56,24},{64,96... | collective-permute-start | bytes 393224 | tf_op jit(solution)/shard_map/ppermute | solution.py:107
  117.1 5.6 %collective-permute-start.27 = (bf16[32,2048]{1,0:T(8,128)(2,1)S(1)}, bf16[32,2048]{1,0:T(8,128)(2,1)S(1)}, u32[]{:S(2)}, u32[]{:S(2)}) collective-permute-start(bf16[32,2048]{1,0:T(8,128)(2,1)S(1)} %fusion.19), channel_id=1, source_target_pairs={{0,48},{8,56},{16,0},{24,8},{32,16},{40,24},{48,32},{56,40},{64,11... | collective-permute-start | bytes 393224 | tf_op jit(solution)/shard_map/ppermute | solution.py:107
  118.1 7.3 %collective-permute-start.26 = (bf16[32,2048]{1,0:T(8,128)(2,1)S(1)}, bf16[32,2048]{1,0:T(8,128)(2,1)S(1)}, u32[]{:S(2)}, u32[]{:S(2)}) collective-permute-start(bf16[32,2048]{1,0:T(8,128)(2,1)S(1)} %fusion.19), channel_id=1, source_target_pairs={{0,16},{8,24},{16,32},{24,40},{32,48},{40,56},{48,0},{56,8},{64,80... | collective-permute-start | bytes 393224 | tf_op jit(solution)/shard_map/ppermute | solution.py:107
  125.5 2.6 %collective-permute-start.29 = (bf16[32,2048]{1,0:T(8,128)(2,1)S(1)}, bf16[32,2048]{1,0:T(8,128)(2,1)S(1)}, u32[]{:S(2)}, u32[]{:S(2)}) collective-permute-start(bf16[32,2048]{1,0:T(8,128)(2,1)S(1)} %fusion.8), channel_id=1, source_target_pairs={{0,8},{8,0},{16,24},{24,16},{32,40},{40,32},{48,56},{56,48},{64,72... | collective-permute-start | bytes 393224 | tf_op jit(solution)/shard_map/ppermute | solution.py:107

commit v8 on v7

--- a/solution.py
+++ b/solution.py
@@ -90,6 +90,39 @@
     )(basis)
 
 
+def spread_kernel(waves_ref, sent_ref):
+    for wave in range(waves_ref.shape[1]):
+        for part in range(waves_ref.shape[0]):
+            line = waves_ref[part, wave : wave + 1, :]
+            sent_ref[:, wave, part : part + 1, :] = jnp.broadcast_to(
+                line[None], (sent_ref.shape[0],) + line.shape
+            )
+
+
+def spread(waves, row_count):
+    parts, waves_here, width = waves.shape
+    return pl.pallas_call(
+        spread_kernel,
+        out_shape=jax.ShapeDtypeStruct((row_count, waves_here, parts, width), waves.dtype),
+        compiler_params=pltpu.CompilerParams(vmem_limit_bytes=8 << 20),
+    )(waves)
+
+
+def gather_kernel(arrived_ref, final_ref):
+    total = jnp.sum(arrived_ref[...].astype(jnp.float32), axis=0)
+    for part in range(final_ref.shape[0]):
+        final_ref[part] = total[:, part, :].astype(final_ref.dtype)
+
+
+def gathered(arrived):
+    _, waves_here, parts, width = arrived.shape
+    return pl.pallas_call(
+        gather_kernel,
+        out_shape=jax.ShapeDtypeStruct((parts, waves_here, width), arrived.dtype),
+        compiler_params=pltpu.CompilerParams(vmem_limit_bytes=8 << 20),
+    )(arrived)
+
+
 def on_device(mode_basis, node_coords, quad_weights, magnetization, decay_rates, directions):
     row_count = lax.axis_size("row")
     col_count = lax.axis_size("col")
@@ -128,19 +161,15 @@
     moments = node_coords * quad_weights[None, :]
     weights = jnp.sum(mine[:, :, :, None] * moments[None, :, None, :], axis=1)
 
-    sent = jnp.transpose(magnetization, (2, 0, 1))
-    sent = jnp.broadcast_to(sent[None], (row_count,) + sent.shape)
+    sent = spread(jnp.transpose(magnetization, (0, 2, 1)), row_count)
     sent = sent.reshape(row_count * col_count, parts, col_width)
     first_core, first_chip = core == 0, row_index < 2
 
     def half_of(array, which, axis):
         return lax.dynamic_slice_in_dim(array, which * width, width, axis)
 
-    rates = jnp.stack([half_of(decay_rates, core, 0), half_of(decay_rates, 1 - core, 0)])
-    sent, rates, first_core, first_chip = lax.optimization_barrier(
-        (sent, rates, first_core, first_chip)
-    )
-    rates = rates[:1]
+    rates = half_of(decay_rates, core, 0)[None, :]
+    sent, first_core, first_chip = lax.optimization_barrier((sent, first_core, first_chip))
     every = lax.all_to_all(sent, ("row", "col"), 0, 0)
     every = every.reshape(row_count, col_count, parts, col_width)
     every = lax.optimization_barrier(
@@ -190,8 +219,7 @@
     sent = jnp.transpose(sent, (1, 2, 0, 3)).reshape(row_count * col_count, parts, col_width)
     every = lax.all_to_all(sent, ("row", "col"), 0, 0)
     every = every.reshape(row_count, col_count, parts, col_width)
-    final = jnp.sum(every.astype(f32), axis=0).astype(bf16)
-    return jnp.transpose(final, (1, 2, 0))
+    return jnp.transpose(gathered(every), (0, 2, 1))
 
 
 def solution(mesh):

time: 146 us -> 145 us (level)
  local copies, waits for them, and re-layouts: 4.61 us -> 2.37 us
  Pallas kernels: 9.21 us -> 10.9 us
    pallas_call x0 -> x2, Pallas kernels: none -> 1.73 us  [the longest x1 0.89 us: gathered(): pl.pallas_call(gather_kernel, out_shape=jax.ShapeDtypeStruct((parts, wave...]
where the time goes in v8:
time: 145 us
  waiting for transfers between devices  62.5 us (43%)
  starting transfers between devices  36.5 us (25%)
  matrix products  16.5 us (11%)
  blocking collectives  13.8 us (10%)
  Pallas kernels  10.9 us (8%)
  local copies, waits for them, and re-layouts  2.37 us (2%)
  other arithmetic  2.12 us (1%)
    ppermute x30, waiting for transfers between devices, move(): lax.ppermute(array, 'row', [(r, target(r)) for r in range(row_count)])  54 us
    ppermute x30, starting transfers between devices, move(): lax.ppermute(array, 'row', [(r, target(r)) for r in range(row_count)])  25 us
    dot_general x20, matrix products, product(): lax.dot_general(left, right, dims, preferred_element_type=jnp.float32)  16.5 us
    all_to_all x1, blocking collectives, on_device(): every = lax.all_to_all(sent, ('row', 'col'), 0, 0)  13.8 us
    all_to_all x1, starting transfers between devices, on_device(): every = lax.all_to_all(sent, ('row', 'col'), 0, 0)  11.5 us
    all_to_all x1, waiting for transfers between devices, on_device(): every = lax.all_to_all(sent, ('row', 'col'), 0, 0)  8.41 us
    pallas_call x1, Pallas kernels, first_operator(): pl.pallas_call(first_kernel, out_shape=(jax.ShapeDtypeStruct((rows, width...  5.7 us
    pallas_call x2, Pallas kernels, turned(): pl.pallas_call(turn_kernel, out_shape=jax.ShapeDtypeStruct((width, nodes)...  3.51 us
  transfers between devices with their start and end apart: 31, of which 29 were waited for; matrix products, arithmetic and copies ran while one was open for 6% of the time, Pallas kernels for 2%

profile of v8, /device:TPU:1, one launch (start us, length us, event | category | flops | bytes accessed | tf_op | source)
XLA Modules:
  0.0 144.9 jit_solution(10217282436214152780)
XLA Ops:
  1.6 11.5 %all-to-all-start = ((bf16[128,2,512]{2,1,0:T(2,128)(2,1)}), bf16[128,2,512]{2,1,0:T(2,128)(2,1)S(1)}, u32[]{:S(2)}, u32[]{:S(2)}) async-start(bf16[128,2,512]{2,1,0:T(2,128)(2,1)} %bitcast.1), calls=%async_computation | async-start | bytes 524288 | tf_op jit(solution)/shard_map/all_to_all | solution.py:173
  15.1 8.4 %all-to-all-done = bf16[128,2,512]{2,1,0:T(2,128)(2,1)S(1)} async-done(((bf16[128,2,512]{2,1,0:T(2,128)(2,1)}), bf16[128,2,512]{2,1,0:T(2,128)(2,1)S(1)}, u32[]{:S(2)}, u32[]{:S(2)}) %all-to-all-start) | async-done | bytes 262176 | tf_op jit(solution)/shard_map/all_to_all | solution.py:173
  23.8 5.7 %shard_map.65 = (f32[32,2048]{1,0:T(8,128)S(1)}, bf16[32,2048]{1,0:T(8,128)(2,1)S(1)}, bf16[1024,2048]{1,0:T(8,128)(2,1)S(1)}, bf16[1024,2048]{1,0:T(8,128)(2,1)S(1)}) custom-call(bf16[2,32,2048]{2,1,0:T(8,128)(2,1)S(1)} %pad_maximum_fusion.field_ref, f32[16,1024]{1,0:T(8,128)S(1)} %fusion.31.scale_ref, bf16[1024,4096]{1,0:T(8,128)(2,1)} %basis_ref.1), custom_call_target="tpu_custom_call" | custom-call | flops 536870912 | bytes 8388608 | tf_op jit(solution)/shard_map/pallas_call | solution.py:56
  29.5 1.4 collective-permute-start
  30.9 1.0 collective-permute-done
  32.4 4.4 %collective-permute-done.1 = bf16[32,2048]{1,0:T(8,128)(2,1)S(1)} collective-permute-done((bf16[32,2048]{1,0:T(8,128)(2,1)S(1)}, bf16[32,2048]{1,0:T(8,128)(2,1)S(1)}, u32[]{:S(2)}, u32[]{:S(2)}) %collective-permute-start.1) | collective-permute-done | bytes 131104 | tf_op jit(solution)/shard_map/ppermute | solution.py:140
  37.6 2.2 %collective-permute-start.3 = (bf16[32,2048]{1,0:T(8,128)(2,1)S(1)}, bf16[32,2048]{1,0:T(8,128)(2,1)S(1)}, u32[]{:S(2)}, u32[]{:S(2)}) collective-permute-start(bf16[32,2048]{1,0:T(8,128)(2,1)S(1)} %fusion.15), channel_id=1, source_target_pairs={{0,48},{8,56},{16,0},{24,8},{32,16},{40,24},{48,32},{56,40},{64,11... | collective-permute-start | bytes 393224 | tf_op jit(solution)/shard_map/ppermute | solution.py:140
  39.8 1.8 %shard_map.66 = bf16[2048,1024]{1,0:T(8,128)(2,1)S(1)} custom-call(bf16[1024,2048]{1,0:T(8,128)(2,1)S(1)} %get-tuple-element.16.basis_ref), custom_call_target="tpu_custom_call" | custom-call | bytes 8388608 | tf_op jit(solution)/shard_map/pallas_call | solution.py:80
  41.6 1.8 %shard_map.67 = bf16[2048,1024]{1,0:T(8,128)(2,1)S(1)} custom-call(bf16[1024,2048]{1,0:T(8,128)(2,1)S(1)} %get-tuple-element.17.basis_ref), custom_call_target="tpu_custom_call" | custom-call | bytes 8388608 | tf_op jit(solution)/shard_map/pallas_call | solution.py:80
  43.4 2.7 %collective-permute-done.2 = bf16[32,2048]{1,0:T(8,128)(2,1)S(1)} collective-permute-done((bf16[32,2048]{1,0:T(8,128)(2,1)S(1)}, bf16[32,2048]{1,0:T(8,128)(2,1)S(1)}, u32[]{:S(2)}, u32[]{:S(2)}) %collective-permute-start.2) | collective-permute-done | bytes 131104 | tf_op jit(solution)/shard_map/ppermute | solution.py:140
  46.2 1.9 %collective-permute-start.5 = (bf16[32,2048]{1,0:T(8,128)(2,1)S(1)}, bf16[32,2048]{1,0:T(8,128)(2,1)S(1)}, u32[]{:S(2)}, u32[]{:S(2)}) collective-permute-start(bf16[32,2048]{1,0:T(8,128)(2,1)S(1)} %fusion.2), channel_id=1, source_target_pairs={{0,8},{8,0},{16,24},{24,16},{32,40},{40,32},{48,56},{56,48},{64,72... | collective-permute-start | bytes 393224 | tf_op jit(solution)/shard_map/ppermute | solution.py:140
  52.6 4.4 %collective-permute-done.7 = bf16[32,2048]{1,0:T(8,128)(2,1)S(1)} collective-permute-done((bf16[32,2048]{1,0:T(8,128)(2,1)S(1)}, bf16[32,2048]{1,0:T(8,128)(2,1)S(1)}, u32[]{:S(2)}, u32[]{:S(2)}) %collective-permute-start.7) | collective-permute-done | bytes 131104 | tf_op jit(solution)/shard_map/ppermute | solution.py:140
  59.0 3.4 %collective-permute-done.10 = bf16[32,2048]{1,0:T(8,128)(2,1)S(1)} collective-permute-done((bf16[32,2048]{1,0:T(8,128)(2,1)S(1)}, bf16[32,2048]{1,0:T(8,128)(2,1)S(1)}, u32[]{:S(2)}, u32[]{:S(2)}) %collective-permute-start.10) | collective-permute-done | bytes 131104 | tf_op jit(solution)/shard_map/ppermute | solution.py:140
  63.1 2.7 %collective-permute-done.8 = bf16[32,2048]{1,0:T(8,128)(2,1)S(1)} collective-permute-done((bf16[32,2048]{1,0:T(8,128)(2,1)S(1)}, bf16[32,2048]{1,0:T(8,128)(2,1)S(1)}, u32[]{:S(2)}, u32[]{:S(2)}) %collective-permute-start.8) | collective-permute-done | bytes 131104 | tf_op jit(solution)/shard_map/ppermute | solution.py:140
  65.9 1.8 %collective-permute-start.11 = (bf16[32,2048]{1,0:T(8,128)(2,1)S(1)}, bf16[32,2048]{1,0:T(8,128)(2,1)S(1)}, u32[]{:S(2)}, u32[]{:S(2)}) collective-permute-start(bf16[32,2048]{1,0:T(8,128)(2,1)S(1)} %fusion.3), channel_id=1, source_target_pairs={{0,8},{8,0},{16,24},{24,16},{32,40},{40,32},{48,56},{56,48},{64,72... | collective-permute-start | bytes 393224 | tf_op jit(solution)/shard_map/ppermute | solution.py:140
  72.2 4.4 %collective-permute-done.13 = bf16[32,2048]{1,0:T(8,128)(2,1)S(1)} collective-permute-done((bf16[32,2048]{1,0:T(8,128)(2,1)S(1)}, bf16[32,2048]{1,0:T(8,128)(2,1)S(1)}, u32[]{:S(2)}, u32[]{:S(2)}) %collective-permute-start.13) | collective-permute-done | bytes 131104 | tf_op jit(solution)/shard_map/ppermute | solution.py:140
  77.2 0.9 collective-permute-start.15
  78.6 3.4 %collective-permute-done.16 = bf16[32,2048]{1,0:T(8,128)(2,1)S(1)} collective-permute-done((bf16[32,2048]{1,0:T(8,128)(2,1)S(1)}, bf16[32,2048]{1,0:T(8,128)(2,1)S(1)}, u32[]{:S(2)}, u32[]{:S(2)}) %collective-permute-start.16) | collective-permute-done | bytes 131104 | tf_op jit(solution)/shard_map/ppermute | solution.py:140
  82.8 2.6 %collective-permute-done.14 = bf16[32,2048]{1,0:T(8,128)(2,1)S(1)} collective-permute-done((bf16[32,2048]{1,0:T(8,128)(2,1)S(1)}, bf16[32,2048]{1,0:T(8,128)(2,1)S(1)}, u32[]{:S(2)}, u32[]{:S(2)}) %collective-permute-start.14) | collective-permute-done | bytes 131104 | tf_op jit(solution)/shard_map/ppermute | solution.py:140
  85.5 1.6 %collective-permute-start.17 = (bf16[32,2048]{1,0:T(8,128)(2,1)S(1)}, bf16[32,2048]{1,0:T(8,128)(2,1)S(1)}, u32[]{:S(2)}, u32[]{:S(2)}) collective-permute-start(bf16[32,2048]{1,0:T(8,128)(2,1)S(1)} %fusion.5), channel_id=1, source_target_pairs={{0,8},{8,0},{16,24},{24,16},{32,40},{40,32},{48,56},{56,48},{64,72... | collective-permute-start | bytes 393224 | tf_op jit(solution)/shard_map/ppermute | solution.py:140
  91.7 4.4 %collective-permute-done.19 = bf16[32,2048]{1,0:T(8,128)(2,1)S(1)} collective-permute-done((bf16[32,2048]{1,0:T(8,128)(2,1)S(1)}, bf16[32,2048]{1,0:T(8,128)(2,1)S(1)}, u32[]{:S(2)}, u32[]{:S(2)}) %collective-permute-start.19) | collective-permute-done | bytes 131104 | tf_op jit(solution)/shard_map/ppermute | solution.py:140
  96.6 1.0 collective-permute-start.21
  98.1 3.4 %collective-permute-done.22 = bf16[32,2048]{1,0:T(8,128)(2,1)S(1)} collective-permute-done((bf16[32,2048]{1,0:T(8,128)(2,1)S(1)}, bf16[32,2048]{1,0:T(8,128)(2,1)S(1)}, u32[]{:S(2)}, u32[]{:S(2)}) %collective-permute-start.22) | collective-permute-done | bytes 131104 | tf_op jit(solution)/shard_map/ppermute | solution.py:140
  102.2 2.6 %collective-permute-done.20 = bf16[32,2048]{1,0:T(8,128)(2,1)S(1)} collective-permute-done((bf16[32,2048]{1,0:T(8,128)(2,1)S(1)}, bf16[32,2048]{1,0:T(8,128)(2,1)S(1)}, u32[]{:S(2)}, u32[]{:S(2)}) %collective-permute-start.20) | collective-permute-done | bytes 131104 | tf_op jit(solution)/shard_map/ppermute | solution.py:140
  105.0 1.6 %collective-permute-start.23 = (bf16[32,2048]{1,0:T(8,128)(2,1)S(1)}, bf16[32,2048]{1,0:T(8,128)(2,1)S(1)}, u32[]{:S(2)}, u32[]{:S(2)}) collective-permute-start(bf16[32,2048]{1,0:T(8,128)(2,1)S(1)} %fusion.6), channel_id=1, source_target_pairs={{0,8},{8,0},{16,24},{24,16},{32,40},{40,32},{48,56},{56,48},{64,72... | collective-permute-start | bytes 393224 | tf_op jit(solution)/shard_map/ppermute | solution.py:140
  111.1 4.4 %collective-permute-done.25 = bf16[32,2048]{1,0:T(8,128)(2,1)S(1)} collective-permute-done((bf16[32,2048]{1,0:T(8,128)(2,1)S(1)}, bf16[32,2048]{1,0:T(8,128)(2,1)S(1)}, u32[]{:S(2)}, u32[]{:S(2)}) %collective-permute-start.25) | collective-permute-done | bytes 131104 | tf_op jit(solution)/shard_map/ppermute | solution.py:140
  116.3 1.0 collective-permute-start.27
  117.8 3.4 %collective-permute-done.28 = bf16[32,2048]{1,0:T(8,128)(2,1)S(1)} collective-permute-done((bf16[32,2048]{1,0:T(8,128)(2,1)S(1)}, bf16[32,2048]{1,0:T(8,128)(2,1)S(1)}, u32[]{:S(2)}, u32[]{:S(2)}) %collective-permute-start.28) | collective-permute-done | bytes 131104 | tf_op jit(solution)/shard_map/ppermute | solution.py:140
  121.9 2.6 %collective-permute-done.26 = bf16[32,2048]{1,0:T(8,128)(2,1)S(1)} collective-permute-done((bf16[32,2048]{1,0:T(8,128)(2,1)S(1)}, bf16[32,2048]{1,0:T(8,128)(2,1)S(1)}, u32[]{:S(2)}, u32[]{:S(2)}) %collective-permute-start.26) | collective-permute-done | bytes 131104 | tf_op jit(solution)/shard_map/ppermute | solution.py:140
  124.7 1.6 %collective-permute-start.29 = (bf16[32,2048]{1,0:T(8,128)(2,1)S(1)}, bf16[32,2048]{1,0:T(8,128)(2,1)S(1)}, u32[]{:S(2)}, u32[]{:S(2)}) collective-permute-start(bf16[32,2048]{1,0:T(8,128)(2,1)S(1)} %fusion.8), channel_id=1, source_target_pairs={{0,8},{8,0},{16,24},{24,16},{32,40},{40,32},{48,56},{56,48},{64,72... | collective-permute-start | bytes 393224 | tf_op jit(solution)/shard_map/ppermute | solution.py:140
  130.3 13.8 %all_to_all.10 = bf16[128,2,512]{2,1,0:T(2,128)(2,1)S(1)} all-to-all(bf16[128,2,512]{2,1,0:T(2,128)(2,1)S(1)} %bitcast.105), channel_id=1, replica_groups=mesh['row'=16,'col'=8] {'row','col'}, dimensions={0} | all-to-all | bytes 524288 | tf_op jit(solution)/shard_map/all_to_all | solution.py:220
  144.0 0.9 shard_map.68
  (101 shorter events, 36.0 us)
Async XLA Ops:
  1.6 22.0 %all-to-all-start = ((bf16[128,2,512]{2,1,0:T(2,128)(2,1)}), bf16[128,2,512]{2,1,0:T(2,128)(2,1)S(1)}, u32[]{:S(2)}, u32[]{:S(2)}) async-start(bf16[128,2,512]{2,1,0:T(2,128)(2,1)} %bitcast.1), calls=%async_computation | async-start | bytes 524288 | tf_op jit(solution)/shard_map/all_to_all | solution.py:173
  23.7 16.1 %copy-start.1 = (f32[4096]{0:T(1024)S(1)}, f32[4096]{0:T(1024)}, u32[]{:S(2)}) copy-start(f32[4096]{0:T(1024)} %param.10) | copy-start | bytes 49156
  29.5 2.4 %collective-permute-start = (bf16[32,2048]{1,0:T(8,128)(2,1)S(1)}, bf16[32,2048]{1,0:T(8,128)(2,1)S(1)}, u32[]{:S(2)}, u32[]{:S(2)}) collective-permute-start(bf16[32,2048]{1,0:T(8,128)(2,1)S(1)} %get-tuple-element.15), channel_id=1, source_target_pairs={{0,8},{8,0},{16,24},{24,16},{32,40},{40,32},{48,56},{56,48},{64,72... | collective-permute-start | bytes 393224 | tf_op jit(solution)/shard_map/ppermute | solution.py:140
  31.9 4.8 %collective-permute-start.1 = (bf16[32,2048]{1,0:T(8,128)(2,1)S(1)}, bf16[32,2048]{1,0:T(8,128)(2,1)S(1)}, u32[]{:S(2)}, u32[]{:S(2)}) collective-permute-start(bf16[32,2048]{1,0:T(8,128)(2,1)S(1)} %fusion.10), channel_id=1, source_target_pairs={{0,64},{8,72},{16,80},{24,88},{32,96},{40,104},{48,112},{56,120},{... | collective-permute-start | bytes 393224 | tf_op jit(solution)/shard_map/ppermute | solution.py:140
  36.8 6.6 %collective-permute-start.4 = (bf16[32,2048]{1,0:T(8,128)(2,1)S(1)}, bf16[32,2048]{1,0:T(8,128)(2,1)S(1)}, u32[]{:S(2)}, u32[]{:S(2)}) collective-permute-start(bf16[32,2048]{1,0:T(8,128)(2,1)S(1)} %fusion.15), channel_id=1, source_target_pairs={{0,32},{8,40},{16,48},{24,56},{32,0},{40,8},{48,16},{56,24},{64,96... | collective-permute-start | bytes 393224 | tf_op jit(solution)/shard_map/ppermute | solution.py:140
  37.6 5.8 %collective-permute-start.3 = (bf16[32,2048]{1,0:T(8,128)(2,1)S(1)}, bf16[32,2048]{1,0:T(8,128)(2,1)S(1)}, u32[]{:S(2)}, u32[]{:S(2)}) collective-permute-start(bf16[32,2048]{1,0:T(8,128)(2,1)S(1)} %fusion.15), channel_id=1, source_target_pairs={{0,48},{8,56},{16,0},{24,8},{32,16},{40,24},{48,32},{56,40},{64,11... | collective-permute-start | bytes 393224 | tf_op jit(solution)/shard_map/ppermute | solution.py:140
  39.8 6.3 %collective-permute-start.2 = (bf16[32,2048]{1,0:T(8,128)(2,1)S(1)}, bf16[32,2048]{1,0:T(8,128)(2,1)S(1)}, u32[]{:S(2)}, u32[]{:S(2)}) collective-permute-start(bf16[32,2048]{1,0:T(8,128)(2,1)S(1)} %fusion.15), channel_id=1, source_target_pairs={{0,16},{8,24},{16,32},{24,40},{32,48},{40,56},{48,0},{56,8},{64,80... | collective-permute-start | bytes 393224 | tf_op jit(solution)/shard_map/ppermute | solution.py:140
  46.2 2.8 %collective-permute-start.5 = (bf16[32,2048]{1,0:T(8,128)(2,1)S(1)}, bf16[32,2048]{1,0:T(8,128)(2,1)S(1)}, u32[]{:S(2)}, u32[]{:S(2)}) collective-permute-start(bf16[32,2048]{1,0:T(8,128)(2,1)S(1)} %fusion.2), channel_id=1, source_target_pairs={{0,8},{8,0},{16,24},{24,16},{32,40},{40,32},{48,56},{56,48},{64,72... | collective-permute-start | bytes 393224 | tf_op jit(solution)/shard_map/ppermute | solution.py:140
  50.7 1.4 collective-permute-start.6
  52.1 4.8 %collective-permute-start.7 = (bf16[32,2048]{1,0:T(8,128)(2,1)S(1)}, bf16[32,2048]{1,0:T(8,128)(2,1)S(1)}, u32[]{:S(2)}, u32[]{:S(2)}) collective-permute-start(bf16[32,2048]{1,0:T(8,128)(2,1)S(1)} %fusion.11), channel_id=1, source_target_pairs={{0,64},{8,72},{16,80},{24,88},{32,96},{40,104},{48,112},{56,120},{... | collective-permute-start | bytes 393224 | tf_op jit(solution)/shard_map/ppermute | solution.py:140
  57.0 5.4 %collective-permute-start.10 = (bf16[32,2048]{1,0:T(8,128)(2,1)S(1)}, bf16[32,2048]{1,0:T(8,128)(2,1)S(1)}, u32[]{:S(2)}, u32[]{:S(2)}) collective-permute-start(bf16[32,2048]{1,0:T(8,128)(2,1)S(1)} %fusion.16), channel_id=1, source_target_pairs={{0,32},{8,40},{16,48},{24,56},{32,0},{40,8},{48,16},{56,24},{64,96... | collective-permute-start | bytes 393224 | tf_op jit(solution)/shard_map/ppermute | solution.py:140
  57.5 5.6 %collective-permute-start.9 = (bf16[32,2048]{1,0:T(8,128)(2,1)S(1)}, bf16[32,2048]{1,0:T(8,128)(2,1)S(1)}, u32[]{:S(2)}, u32[]{:S(2)}) collective-permute-start(bf16[32,2048]{1,0:T(8,128)(2,1)S(1)} %fusion.16), channel_id=1, source_target_pairs={{0,48},{8,56},{16,0},{24,8},{32,16},{40,24},{48,32},{56,40},{64,11... | collective-permute-start | bytes 393224 | tf_op jit(solution)/shard_map/ppermute | solution.py:140
  58.4 7.4 %collective-permute-start.8 = (bf16[32,2048]{1,0:T(8,128)(2,1)S(1)}, bf16[32,2048]{1,0:T(8,128)(2,1)S(1)}, u32[]{:S(2)}, u32[]{:S(2)}) collective-permute-start(bf16[32,2048]{1,0:T(8,128)(2,1)S(1)} %fusion.16), channel_id=1, source_target_pairs={{0,16},{8,24},{16,32},{24,40},{32,48},{40,56},{48,0},{56,8},{64,80... | collective-permute-start | bytes 393224 | tf_op jit(solution)/shard_map/ppermute | solution.py:140
  65.9 2.8 %collective-permute-start.11 = (bf16[32,2048]{1,0:T(8,128)(2,1)S(1)}, bf16[32,2048]{1,0:T(8,128)(2,1)S(1)}, u32[]{:S(2)}, u32[]{:S(2)}) collective-permute-start(bf16[32,2048]{1,0:T(8,128)(2,1)S(1)} %fusion.3), channel_id=1, source_target_pairs={{0,8},{8,0},{16,24},{24,16},{32,40},{40,32},{48,56},{56,48},{64,72... | collective-permute-start | bytes 393224 | tf_op jit(solution)/shard_map/ppermute | solution.py:140
  70.4 1.4 collective-permute-start.12
  71.8 4.8 %collective-permute-start.13 = (bf16[32,2048]{1,0:T(8,128)(2,1)S(1)}, bf16[32,2048]{1,0:T(8,128)(2,1)S(1)}, u32[]{:S(2)}, u32[]{:S(2)}) collective-permute-start(bf16[32,2048]{1,0:T(8,128)(2,1)S(1)} %fusion.12), channel_id=1, source_target_pairs={{0,64},{8,72},{16,80},{24,88},{32,96},{40,104},{48,112},{56,120},{... | collective-permute-start | bytes 393224 | tf_op jit(solution)/shard_map/ppermute | solution.py:140
  76.6 5.4 %collective-permute-start.16 = (bf16[32,2048]{1,0:T(8,128)(2,1)S(1)}, bf16[32,2048]{1,0:T(8,128)(2,1)S(1)}, u32[]{:S(2)}, u32[]{:S(2)}) collective-permute-start(bf16[32,2048]{1,0:T(8,128)(2,1)S(1)} %fusion.17), channel_id=1, source_target_pairs={{0,32},{8,40},{16,48},{24,56},{32,0},{40,8},{48,16},{56,24},{64,96... | collective-permute-start | bytes 393224 | tf_op jit(solution)/shard_map/ppermute | solution.py:140
  77.2 5.6 %collective-permute-start.15 = (bf16[32,2048]{1,0:T(8,128)(2,1)S(1)}, bf16[32,2048]{1,0:T(8,128)(2,1)S(1)}, u32[]{:S(2)}, u32[]{:S(2)}) collective-permute-start(bf16[32,2048]{1,0:T(8,128)(2,1)S(1)} %fusion.17), channel_id=1, source_target_pairs={{0,48},{8,56},{16,0},{24,8},{32,16},{40,24},{48,32},{56,40},{64,11... | collective-permute-start | bytes 393224 | tf_op jit(solution)/shard_map/ppermute | solution.py:140
  78.1 7.3 %collective-permute-start.14 = (bf16[32,2048]{1,0:T(8,128)(2,1)S(1)}, bf16[32,2048]{1,0:T(8,128)(2,1)S(1)}, u32[]{:S(2)}, u32[]{:S(2)}) collective-permute-start(bf16[32,2048]{1,0:T(8,128)(2,1)S(1)} %fusion.17), channel_id=1, source_target_pairs={{0,16},{8,24},{16,32},{24,40},{32,48},{40,56},{48,0},{56,8},{64,80... | collective-permute-start | bytes 393224 | tf_op jit(solution)/shard_map/ppermute | solution.py:140
  85.5 2.6 %collective-permute-start.17 = (bf16[32,2048]{1,0:T(8,128)(2,1)S(1)}, bf16[32,2048]{1,0:T(8,128)(2,1)S(1)}, u32[]{:S(2)}, u32[]{:S(2)}) collective-permute-start(bf16[32,2048]{1,0:T(8,128)(2,1)S(1)} %fusion.5), channel_id=1, source_target_pairs={{0,8},{8,0},{16,24},{24,16},{32,40},{40,32},{48,56},{56,48},{64,72... | collective-permute-start | bytes 393224 | tf_op jit(solution)/shard_map/ppermute | solution.py:140
  89.8 1.4 collective-permute-start.18
  91.2 4.8 %collective-permute-start.19 = (bf16[32,2048]{1,0:T(8,128)(2,1)S(1)}, bf16[32,2048]{1,0:T(8,128)(2,1)S(1)}, u32[]{:S(2)}, u32[]{:S(2)}) collective-permute-start(bf16[32,2048]{1,0:T(8,128)(2,1)S(1)} %fusion.13), channel_id=1, source_target_pairs={{0,64},{8,72},{16,80},{24,88},{32,96},{40,104},{48,112},{56,120},{... | collective-permute-start | bytes 393224 | tf_op jit(solution)/shard_map/ppermute | solution.py:140
  96.1 5.4 %collective-permute-start.22 = (bf16[32,2048]{1,0:T(8,128)(2,1)S(1)}, bf16[32,2048]{1,0:T(8,128)(2,1)S(1)}, u32[]{:S(2)}, u32[]{:S(2)}) collective-permute-start(bf16[32,2048]{1,0:T(8,128)(2,1)S(1)} %fusion.18), channel_id=1, source_target_pairs={{0,32},{8,40},{16,48},{24,56},{32,0},{40,8},{48,16},{56,24},{64,96... | collective-permute-start | bytes 393224 | tf_op jit(solution)/shard_map/ppermute | solution.py:140
  96.6 5.6 %collective-permute-start.21 = (bf16[32,2048]{1,0:T(8,128)(2,1)S(1)}, bf16[32,2048]{1,0:T(8,128)(2,1)S(1)}, u32[]{:S(2)}, u32[]{:S(2)}) collective-permute-start(bf16[32,2048]{1,0:T(8,128)(2,1)S(1)} %fusion.18), channel_id=1, source_target_pairs={{0,48},{8,56},{16,0},{24,8},{32,16},{40,24},{48,32},{56,40},{64,11... | collective-permute-start | bytes 393224 | tf_op jit(solution)/shard_map/ppermute | solution.py:140
  97.6 7.3 %collective-permute-start.20 = (bf16[32,2048]{1,0:T(8,128)(2,1)S(1)}, bf16[32,2048]{1,0:T(8,128)(2,1)S(1)}, u32[]{:S(2)}, u32[]{:S(2)}) collective-permute-start(bf16[32,2048]{1,0:T(8,128)(2,1)S(1)} %fusion.18), channel_id=1, source_target_pairs={{0,16},{8,24},{16,32},{24,40},{32,48},{40,56},{48,0},{56,8},{64,80... | collective-permute-start | bytes 393224 | tf_op jit(solution)/shard_map/ppermute | solution.py:140
  105.0 2.6 %collective-permute-start.23 = (bf16[32,2048]{1,0:T(8,128)(2,1)S(1)}, bf16[32,2048]{1,0:T(8,128)(2,1)S(1)}, u32[]{:S(2)}, u32[]{:S(2)}) collective-permute-start(bf16[32,2048]{1,0:T(8,128)(2,1)S(1)} %fusion.6), channel_id=1, source_target_pairs={{0,8},{8,0},{16,24},{24,16},{32,40},{40,32},{48,56},{56,48},{64,72... | collective-permute-start | bytes 393224 | tf_op jit(solution)/shard_map/ppermute | solution.py:140
  109.3 1.4 collective-permute-start.24
  110.7 4.8 %collective-permute-start.25 = (bf16[32,2048]{1,0:T(8,128)(2,1)S(1)}, bf16[32,2048]{1,0:T(8,128)(2,1)S(1)}, u32[]{:S(2)}, u32[]{:S(2)}) collective-permute-start(bf16[32,2048]{1,0:T(8,128)(2,1)S(1)} %fusion.14), channel_id=1, source_target_pairs={{0,64},{8,72},{16,80},{24,88},{32,96},{40,104},{48,112},{56,120},{... | collective-permute-start | bytes 393224 | tf_op jit(solution)/shard_map/ppermute | solution.py:140
  115.6 5.7 %collective-permute-start.28 = (bf16[32,2048]{1,0:T(8,128)(2,1)S(1)}, bf16[32,2048]{1,0:T(8,128)(2,1)S(1)}, u32[]{:S(2)}, u32[]{:S(2)}) collective-permute-start(bf16[32,2048]{1,0:T(8,128)(2,1)S(1)} %fusion.19), channel_id=1, source_target_pairs={{0,32},{8,40},{16,48},{24,56},{32,0},{40,8},{48,16},{56,24},{64,96... | collective-permute-start | bytes 393224 | tf_op jit(solution)/shard_map/ppermute | solution.py:140
  116.3 5.6 %collective-permute-start.27 = (bf16[32,2048]{1,0:T(8,128)(2,1)S(1)}, bf16[32,2048]{1,0:T(8,128)(2,1)S(1)}, u32[]{:S(2)}, u32[]{:S(2)}) collective-permute-start(bf16[32,2048]{1,0:T(8,128)(2,1)S(1)} %fusion.19), channel_id=1, source_target_pairs={{0,48},{8,56},{16,0},{24,8},{32,16},{40,24},{48,32},{56,40},{64,11... | collective-permute-start | bytes 393224 | tf_op jit(solution)/shard_map/ppermute | solution.py:140
  117.3 7.3 %collective-permute-start.26 = (bf16[32,2048]{1,0:T(8,128)(2,1)S(1)}, bf16[32,2048]{1,0:T(8,128)(2,1)S(1)}, u32[]{:S(2)}, u32[]{:S(2)}) collective-permute-start(bf16[32,2048]{1,0:T(8,128)(2,1)S(1)} %fusion.19), channel_id=1, source_target_pairs={{0,16},{8,24},{16,32},{24,40},{32,48},{40,56},{48,0},{56,8},{64,80... | collective-permute-start | bytes 393224 | tf_op jit(solution)/shard_map/ppermute | solution.py:140
  124.7 2.6 %collective-permute-start.29 = (bf16[32,2048]{1,0:T(8,128)(2,1)S(1)}, bf16[32,2048]{1,0:T(8,128)(2,1)S(1)}, u32[]{:S(2)}, u32[]{:S(2)}) collective-permute-start(bf16[32,2048]{1,0:T(8,128)(2,1)S(1)} %fusion.8), channel_id=1, source_target_pairs={{0,8},{8,0},{16,24},{24,16},{32,40},{40,32},{48,56},{56,48},{64,72... | collective-permute-start | bytes 393224 | tf_op jit(solution)/shard_map/ppermute | solution.py:140
  (1 other events, 0.7 us)

commit v9 on v8

--- a/solution.py
+++ b/solution.py
@@ -6,7 +6,6 @@
 from jax.sharding import PartitionSpec as P
 
 STEPS = 3
-LOADS = 8
 
 NN = (((1,), (0,)), ((), ()))
 NT = (((1,), (1,)), ((), ()))
@@ -16,78 +15,27 @@
     return lax.dot_general(left, right, dims, preferred_element_type=jnp.float32)
 
 
-def first_kernel(field_ref, scale_ref, basis_ref, own_ref, other_ref, *held):
-    *held, loaded = held
-    core = lax.rem(lax.axis_index("row"), 2)
-    width = held[0].shape[1]
-    chunk = 2 * width // LOADS
-    copies = []
-    for h, which in enumerate((core, 1 - core)):
-        for k in range(LOADS // 2):
-            start = pl.multiple_of(which * width + k * chunk, chunk)
-            copies.append(
-                pltpu.make_async_copy(
-                    basis_ref.at[:, pl.ds(start, chunk)],
-                    held[h].at[:, pl.ds(k * chunk, chunk)],
-                    loaded.at[h * (LOADS // 2) + k],
-                )
-            )
-    for copy in copies:
-        copy.start()
-    nodes = jnp.zeros((field_ref.shape[1], held[0].shape[0]), jnp.float32)
-    for k, copy in enumerate(copies):
-        copy.wait()
-        h, place = k // (LOADS // 2), pl.ds(k % (LOADS // 2) * chunk, chunk)
-        nodes += product(field_ref[h, :, place], held[h][:, place], NT)
-    half = nodes.shape[0] // 2
-    scale = scale_ref[...]
-    nodes = jnp.concatenate([scale * nodes[half:], -scale * nodes[:half]], axis=0)
-    nodes = nodes.astype(jnp.bfloat16)
-    for k in range(LOADS // 2):
-        place = pl.ds(k * chunk, chunk)
-        other_ref[:, place] = product(nodes, held[1][:, place], NN).astype(jnp.bfloat16)
-        own_ref[:, place] = product(nodes, held[0][:, place], NN)
-
-
-def first_operator(field, scale, basis):
-    _, rows, width = field.shape
+def turn_kernel(from_ref, basis_ref, turned_ref):
+    turned_ref[...] = basis_ref[...].T
+
+
+def turned(basis, start, block=512):
     nodes, modes = basis.shape
-    in_vmem = pl.BlockSpec(memory_space=pltpu.VMEM)
-    return pl.pallas_call(
-        first_kernel,
-        out_shape=(
-            jax.ShapeDtypeStruct((rows, width), jnp.float32),
-            jax.ShapeDtypeStruct((rows, width), jnp.bfloat16),
-            jax.ShapeDtypeStruct((nodes, width), basis.dtype),
-            jax.ShapeDtypeStruct((nodes, width), basis.dtype),
-        ),
-        in_specs=[in_vmem, in_vmem, pl.BlockSpec(memory_space=pl.ANY)],
-        out_specs=(in_vmem,) * 4,
-        scratch_shapes=[pltpu.SemaphoreType.DMA((LOADS,))],
-        compiler_params=pltpu.CompilerParams(vmem_limit_bytes=44 << 20),
-        cost_estimate=pl.CostEstimate(
-            flops=4 * rows * modes * nodes, bytes_accessed=2 * modes * nodes, transcendentals=0
-        ),
-    )(field, scale, basis)
-
-
-def turn_kernel(basis_ref, turned_ref):
-    turned_ref[...] = basis_ref[...].T
-
-
-def turned(basis, block=512):
-    nodes, width = basis.shape
+    width = modes // 2
     return pl.pallas_call(
         turn_kernel,
         out_shape=jax.ShapeDtypeStruct((width, nodes), basis.dtype),
-        grid=(width // block,),
-        in_specs=[pl.BlockSpec((nodes, block), lambda j: (0, j))],
-        out_specs=pl.BlockSpec((block, nodes), lambda j: (j, 0)),
+        grid_spec=pltpu.PrefetchScalarGridSpec(
+            num_scalar_prefetch=1,
+            grid=(width // block,),
+            in_specs=[pl.BlockSpec((nodes, block), lambda j, w: (0, w[0] // block + j))],
+            out_specs=pl.BlockSpec((block, nodes), lambda j, w: (j, 0)),
+        ),
         compiler_params=pltpu.CompilerParams(vmem_limit_bytes=10 << 20),
         cost_estimate=pl.CostEstimate(
             flops=0, bytes_accessed=4 * width * nodes, transcendentals=0
         ),
-    )(basis)
+    )(start, basis)
 
 
 def spread_kernel(waves_ref, sent_ref):
@@ -104,8 +52,35 @@
     return pl.pallas_call(
         spread_kernel,
         out_shape=jax.ShapeDtypeStruct((row_count, waves_here, parts, width), waves.dtype),
-        compiler_params=pltpu.CompilerParams(vmem_limit_bytes=8 << 20),
+        compiler_params=pltpu.CompilerParams(vmem_limit_bytes=32 << 20),
+        cost_estimate=pl.CostEstimate(flops=1 << 34, bytes_accessed=1 << 20, transcendentals=0),
     )(waves)
+
+
+def weights_kernel(coords_ref, quad_ref, turns_ref, weights_ref):
+    half_steps, axes, waves = turns_ref.shape
+    rows = weights_ref.shape[1]
+    shape = (rows, waves)
+    lane = lax.broadcasted_iota(jnp.int32, shape, 1)
+    wanted = lax.broadcasted_iota(jnp.int32, shape, 0) * (waves // rows)
+    wanted += lax.axis_index("col")
+    moments = coords_ref[...] * quad_ref[...]
+    for a in range(half_steps):
+        total = None
+        for k in range(axes):
+            line = jnp.broadcast_to(turns_ref[a, k : k + 1, :], shape)
+            turn = jnp.sum(jnp.where(lane == wanted, line, 0.0), axis=1, keepdims=True)
+            term = turn * moments[k : k + 1, :]
+            total = term if total is None else total + term
+        weights_ref[a] = total
+
+
+def node_weights(coords, quad, turns, row_count):
+    return pl.pallas_call(
+        weights_kernel,
+        out_shape=jax.ShapeDtypeStruct((turns.shape[0], row_count, coords.shape[1]), coords.dtype),
+        compiler_params=pltpu.CompilerParams(vmem_limit_bytes=16 << 20),
+    )(coords, quad, turns)
 
 
 def gather_kernel(arrived_ref, final_ref):
@@ -155,26 +130,28 @@
             total = total + along_z(sent, hops).astype(f32)
         return total
 
-    mine = lax.dynamic_index_in_dim(
-        directions.reshape(2 * STEPS, 3, row_count, own_waves), col_index, 3, keepdims=False
+    waves = jnp.transpose(magnetization, (0, 2, 1))
+    own_from, other_from = (core * width).reshape(1), ((1 - core) * width).reshape(1)
+    first_core, first_chip = core == 0, row_index < 2
+    waves, own_from, other_from, first_core, first_chip = lax.optimization_barrier(
+        (waves, own_from, other_from, first_core, first_chip)
     )
-    moments = node_coords * quad_weights[None, :]
-    weights = jnp.sum(mine[:, :, :, None] * moments[None, :, None, :], axis=1)
-
-    sent = spread(jnp.transpose(magnetization, (0, 2, 1)), row_count)
+    sent = spread(waves, row_count)
     sent = sent.reshape(row_count * col_count, parts, col_width)
-    first_core, first_chip = core == 0, row_index < 2
-
     def half_of(array, which, axis):
-        return lax.dynamic_slice_in_dim(array, which * width, width, axis)
+        starts = [jnp.int32(0)] * array.ndim
+        sizes = list(array.shape)
+        starts[axis], sizes[axis] = which * width, width
+        return lax.dynamic_slice_p.bind(array, *starts, slice_sizes=tuple(sizes))
 
     rates = half_of(decay_rates, core, 0)[None, :]
-    sent, first_core, first_chip = lax.optimization_barrier((sent, first_core, first_chip))
     every = lax.all_to_all(sent, ("row", "col"), 0, 0)
     every = every.reshape(row_count, col_count, parts, col_width)
-    every = lax.optimization_barrier(
-        jnp.transpose(every, (2, 0, 1, 3)).reshape(columns, mode_count)
+    every = jnp.transpose(every, (2, 0, 1, 3)).reshape(columns, mode_count)
+    every, coords, quad, turns = lax.optimization_barrier(
+        (every, node_coords, quad_weights[None, :], directions)
     )
+    weights = node_weights(coords, quad, turns, row_count)
 
     def mixed(nodes, half_step):
         factor = 0.5 if half_step % 2 == 0 else 1.0
@@ -184,10 +161,13 @@
         return lax.optimization_barrier(rows.astype(bf16))
 
     field = half_of(every, core, 1)
-    both = jnp.stack([field, half_of(every, 1 - core, 1)])
-
-    kept, sent, basis_own, basis_other = first_operator(both, 0.5 * weights[0], mode_basis)
-    turned_own, turned_other = turned(basis_own), turned(basis_other)
+    basis_own, basis_other = half_of(mode_basis, core, 1), half_of(mode_basis, 1 - core, 1)
+
+    kept = lax.optimization_barrier(product(field, basis_own, NT))
+    nodes = mixed(kept + product(half_of(every, 1 - core, 1), basis_other, NT), 0)
+    sent = product(nodes, basis_other, NN).astype(bf16)
+    kept = lax.optimization_barrier(product(nodes, basis_own, NN))
+    turned_own, turned_other = turned(mode_basis, own_from), turned(mode_basis, other_from)
     sums = over_chips(kept + to_other_core(sent).astype(f32))
 
     def weighted(own, other, half_step):

time: 145 us -> 142 us (0.979)
  blocking collectives: 13.8 us -> 35.5 us
  starting transfers between devices: 36.5 us -> 24.9 us
  waiting for transfers between devices: 62.5 us -> 53 us
  Pallas kernels: 10.9 us -> 4.82 us
  matrix products: 16.5 us -> 20.9 us
    all_to_all x1 -> x2, blocking collectives: 13.8 us -> 35.5 us  [on_device(): every = lax.all_to_all(sent, ('row', 'col'), 0, 0)]
    all_to_all x1 -> x0, starting transfers between devices: 11.5 us -> none  [on_device(): every = lax.all_to_all(sent, ('row', 'col'), 0, 0)]
    all_to_all x1 -> x0, waiting for transfers between devices: 8.41 us -> none  [on_device(): every = lax.all_to_all(sent, ('row', 'col'), 0, 0)]
    pallas_call x1, Pallas kernels: 5.7 us -> 0.16 us  [node_weights(): pl.pallas_call(weights_kernel, out_shape=jax.ShapeDtypeStruct((turns.shap...]
    dot_general x20 -> x24, matrix products: 16.5 us -> 20.9 us  [product(): lax.dot_general(left, right, dims, preferred_element_type=jnp.float32)]
  transfers between devices with their start and end apart: 31 -> 30, of which waited for: 29 -> 28; matrix products, arithmetic and copies ran while one was open for 6% -> 6% of each run, Pallas kernels for 2% -> 3%
where the time goes in v9:
time: 142 us
  waiting for transfers between devices  53 us (37%)
  blocking collectives  35.5 us (25%)
  starting transfers between devices  24.9 us (18%)
  matrix products  20.9 us (15%)
  Pallas kernels  4.82 us (3%)
    ppermute x30, waiting for transfers between devices, move(): lax.ppermute(array, 'row', [(r, target(r)) for r in range(row_count)])  53 us
    all_to_all x2, blocking collectives, on_device(): every = lax.all_to_all(sent, ('row', 'col'), 0, 0)  35.5 us
    ppermute x30, starting transfers between devices, move(): lax.ppermute(array, 'row', [(r, target(r)) for r in range(row_count)])  24.9 us
    dot_general x24, matrix products, product(): lax.dot_general(left, right, dims, preferred_element_type=jnp.float32)  20.9 us
    pallas_call x2, Pallas kernels, turned(): pl.pallas_call(turn_kernel, out_shape=jax.ShapeDtypeStruct((width, nodes)...  3.65 us
  transfers between devices with their start and end apart: 30, of which 28 were waited for; matrix products, arithmetic and copies ran while one was open for 6% of the time, Pallas kernels for 3%

profile of v9, /device:TPU:1, one launch (start us, length us, event | category | flops | bytes accessed | tf_op | source)
XLA Modules:
  0.0 142.0 jit_solution(16775906268347738495)
XLA Ops:
  0.8 21.8 %all_to_all.10 = bf16[128,2,512]{2,1,0:T(2,128)(2,1)S(1)} all-to-all(bf16[128,2,512]{2,1,0:T(2,128)(2,1)S(1)} %bitcast.89), channel_id=1, replica_groups=mesh['row'=16,'col'=8] {'row','col'}, dimensions={0} | all-to-all | bytes 524288 | tf_op jit(solution)/shard_map/all_to_all | solution.py:148
  22.8 1.3 fusion.20
  24.1 1.3 fusion.22
  26.6 1.4 collective-permute-start
  29.4 4.4 %collective-permute-done.1 = bf16[32,2048]{1,0:T(8,128)(2,1)S(1)} collective-permute-done((bf16[32,2048]{1,0:T(8,128)(2,1)S(1)}, bf16[32,2048]{1,0:T(8,128)(2,1)S(1)}, u32[]{:S(2)}, u32[]{:S(2)}) %collective-permute-start.1) | collective-permute-done | bytes 131104 | tf_op jit(solution)/shard_map/ppermute | solution.py:115
  33.8 0.9 collective-permute-start.4
  34.8 2.1 %collective-permute-start.3 = (bf16[32,2048]{1,0:T(8,128)(2,1)S(1)}, bf16[32,2048]{1,0:T(8,128)(2,1)S(1)}, u32[]{:S(2)}, u32[]{:S(2)}) collective-permute-start(bf16[32,2048]{1,0:T(8,128)(2,1)S(1)} %fusion.40), channel_id=1, source_target_pairs={{0,48},{8,56},{16,0},{24,8},{32,16},{40,24},{48,32},{56,40},{64,11... | collective-permute-start | bytes 393224 | tf_op jit(solution)/shard_map/ppermute | solution.py:115
  36.9 1.8 %shard_map.66 = bf16[2048,1024]{1,0:T(8,128)(2,1)S(1)} custom-call(s32[1]{0:T(128)} %bitcast.1.from_ref, bf16[1024,4096]{1,0:T(8,128)(2,1)S(1)} %copy-done), custom_call_target="tpu_custom_call" | custom-call | bytes 8388608 | tf_op jit(solution)/shard_map/pallas_call | solution.py:25
  38.7 1.8 %shard_map.67 = bf16[2048,1024]{1,0:T(8,128)(2,1)S(1)} custom-call(s32[1]{0:T(128)} %bitcast.2.from_ref, bf16[1024,4096]{1,0:T(8,128)(2,1)S(1)} %copy-done), custom_call_target="tpu_custom_call" | custom-call | bytes 8388608 | tf_op jit(solution)/shard_map/pallas_call | solution.py:25
  40.6 2.5 %collective-permute-done.2 = bf16[32,2048]{1,0:T(8,128)(2,1)S(1)} collective-permute-done((bf16[32,2048]{1,0:T(8,128)(2,1)S(1)}, bf16[32,2048]{1,0:T(8,128)(2,1)S(1)}, u32[]{:S(2)}, u32[]{:S(2)}) %collective-permute-start.2) | collective-permute-done | bytes 131104 | tf_op jit(solution)/shard_map/ppermute | solution.py:115
  43.3 1.8 %collective-permute-start.5 = (bf16[32,2048]{1,0:T(8,128)(2,1)S(1)}, bf16[32,2048]{1,0:T(8,128)(2,1)S(1)}, u32[]{:S(2)}, u32[]{:S(2)}) collective-permute-start(bf16[32,2048]{1,0:T(8,128)(2,1)S(1)} %fusion.26), channel_id=1, source_target_pairs={{0,8},{8,0},{16,24},{24,16},{32,40},{40,32},{48,56},{56,48},{64,72... | collective-permute-start | bytes 393224 | tf_op jit(solution)/shard_map/ppermute | solution.py:115
  49.6 4.4 %collective-permute-done.7 = bf16[32,2048]{1,0:T(8,128)(2,1)S(1)} collective-permute-done((bf16[32,2048]{1,0:T(8,128)(2,1)S(1)}, bf16[32,2048]{1,0:T(8,128)(2,1)S(1)}, u32[]{:S(2)}, u32[]{:S(2)}) %collective-permute-start.7) | collective-permute-done | bytes 131104 | tf_op jit(solution)/shard_map/ppermute | solution.py:115
  56.0 3.4 %collective-permute-done.10 = bf16[32,2048]{1,0:T(8,128)(2,1)S(1)} collective-permute-done((bf16[32,2048]{1,0:T(8,128)(2,1)S(1)}, bf16[32,2048]{1,0:T(8,128)(2,1)S(1)}, u32[]{:S(2)}, u32[]{:S(2)}) %collective-permute-start.10) | collective-permute-done | bytes 131104 | tf_op jit(solution)/shard_map/ppermute | solution.py:115
  60.3 2.6 %collective-permute-done.8 = bf16[32,2048]{1,0:T(8,128)(2,1)S(1)} collective-permute-done((bf16[32,2048]{1,0:T(8,128)(2,1)S(1)}, bf16[32,2048]{1,0:T(8,128)(2,1)S(1)}, u32[]{:S(2)}, u32[]{:S(2)}) %collective-permute-start.8) | collective-permute-done | bytes 131104 | tf_op jit(solution)/shard_map/ppermute | solution.py:115
  63.0 1.8 %collective-permute-start.11 = (bf16[32,2048]{1,0:T(8,128)(2,1)S(1)}, bf16[32,2048]{1,0:T(8,128)(2,1)S(1)}, u32[]{:S(2)}, u32[]{:S(2)}) collective-permute-start(bf16[32,2048]{1,0:T(8,128)(2,1)S(1)} %fusion.27), channel_id=1, source_target_pairs={{0,8},{8,0},{16,24},{24,16},{32,40},{40,32},{48,56},{56,48},{64,72... | collective-permute-start | bytes 393224 | tf_op jit(solution)/shard_map/ppermute | solution.py:115
  69.3 4.4 %collective-permute-done.13 = bf16[32,2048]{1,0:T(8,128)(2,1)S(1)} collective-permute-done((bf16[32,2048]{1,0:T(8,128)(2,1)S(1)}, bf16[32,2048]{1,0:T(8,128)(2,1)S(1)}, u32[]{:S(2)}, u32[]{:S(2)}) %collective-permute-start.13) | collective-permute-done | bytes 131104 | tf_op jit(solution)/shard_map/ppermute | solution.py:115
  74.2 0.9 collective-permute-start.15
  75.7 3.4 %collective-permute-done.16 = bf16[32,2048]{1,0:T(8,128)(2,1)S(1)} collective-permute-done((bf16[32,2048]{1,0:T(8,128)(2,1)S(1)}, bf16[32,2048]{1,0:T(8,128)(2,1)S(1)}, u32[]{:S(2)}, u32[]{:S(2)}) %collective-permute-start.16) | collective-permute-done | bytes 131104 | tf_op jit(solution)/shard_map/ppermute | solution.py:115
  79.9 2.5 %collective-permute-done.14 = bf16[32,2048]{1,0:T(8,128)(2,1)S(1)} collective-permute-done((bf16[32,2048]{1,0:T(8,128)(2,1)S(1)}, bf16[32,2048]{1,0:T(8,128)(2,1)S(1)}, u32[]{:S(2)}, u32[]{:S(2)}) %collective-permute-start.14) | collective-permute-done | bytes 131104 | tf_op jit(solution)/shard_map/ppermute | solution.py:115
  82.6 1.6 %collective-permute-start.17 = (bf16[32,2048]{1,0:T(8,128)(2,1)S(1)}, bf16[32,2048]{1,0:T(8,128)(2,1)S(1)}, u32[]{:S(2)}, u32[]{:S(2)}) collective-permute-start(bf16[32,2048]{1,0:T(8,128)(2,1)S(1)} %fusion.29), channel_id=1, source_target_pairs={{0,8},{8,0},{16,24},{24,16},{32,40},{40,32},{48,56},{56,48},{64,72... | collective-permute-start | bytes 393224 | tf_op jit(solution)/shard_map/ppermute | solution.py:115
  88.7 4.4 %collective-permute-done.19 = bf16[32,2048]{1,0:T(8,128)(2,1)S(1)} collective-permute-done((bf16[32,2048]{1,0:T(8,128)(2,1)S(1)}, bf16[32,2048]{1,0:T(8,128)(2,1)S(1)}, u32[]{:S(2)}, u32[]{:S(2)}) %collective-permute-start.19) | collective-permute-done | bytes 131104 | tf_op jit(solution)/shard_map/ppermute | solution.py:115
  93.7 1.0 collective-permute-start.21
  95.2 3.4 %collective-permute-done.22 = bf16[32,2048]{1,0:T(8,128)(2,1)S(1)} collective-permute-done((bf16[32,2048]{1,0:T(8,128)(2,1)S(1)}, bf16[32,2048]{1,0:T(8,128)(2,1)S(1)}, u32[]{:S(2)}, u32[]{:S(2)}) %collective-permute-start.22) | collective-permute-done | bytes 131104 | tf_op jit(solution)/shard_map/ppermute | solution.py:115
  99.4 2.5 %collective-permute-done.20 = bf16[32,2048]{1,0:T(8,128)(2,1)S(1)} collective-permute-done((bf16[32,2048]{1,0:T(8,128)(2,1)S(1)}, bf16[32,2048]{1,0:T(8,128)(2,1)S(1)}, u32[]{:S(2)}, u32[]{:S(2)}) %collective-permute-start.20) | collective-permute-done | bytes 131104 | tf_op jit(solution)/shard_map/ppermute | solution.py:115
  102.1 1.6 %collective-permute-start.23 = (bf16[32,2048]{1,0:T(8,128)(2,1)S(1)}, bf16[32,2048]{1,0:T(8,128)(2,1)S(1)}, u32[]{:S(2)}, u32[]{:S(2)}) collective-permute-start(bf16[32,2048]{1,0:T(8,128)(2,1)S(1)} %fusion.30), channel_id=1, source_target_pairs={{0,8},{8,0},{16,24},{24,16},{32,40},{40,32},{48,56},{56,48},{64,72... | collective-permute-start | bytes 393224 | tf_op jit(solution)/shard_map/ppermute | solution.py:115
  108.2 4.4 %collective-permute-done.25 = bf16[32,2048]{1,0:T(8,128)(2,1)S(1)} collective-permute-done((bf16[32,2048]{1,0:T(8,128)(2,1)S(1)}, bf16[32,2048]{1,0:T(8,128)(2,1)S(1)}, u32[]{:S(2)}, u32[]{:S(2)}) %collective-permute-start.25) | collective-permute-done | bytes 131104 | tf_op jit(solution)/shard_map/ppermute | solution.py:115
  113.4 1.0 collective-permute-start.27
  114.9 3.4 %collective-permute-done.28 = bf16[32,2048]{1,0:T(8,128)(2,1)S(1)} collective-permute-done((bf16[32,2048]{1,0:T(8,128)(2,1)S(1)}, bf16[32,2048]{1,0:T(8,128)(2,1)S(1)}, u32[]{:S(2)}, u32[]{:S(2)}) %collective-permute-start.28) | collective-permute-done | bytes 131104 | tf_op jit(solution)/shard_map/ppermute | solution.py:115
  119.1 2.5 %collective-permute-done.26 = bf16[32,2048]{1,0:T(8,128)(2,1)S(1)} collective-permute-done((bf16[32,2048]{1,0:T(8,128)(2,1)S(1)}, bf16[32,2048]{1,0:T(8,128)(2,1)S(1)}, u32[]{:S(2)}, u32[]{:S(2)}) %collective-permute-start.26) | collective-permute-done | bytes 131104 | tf_op jit(solution)/shard_map/ppermute | solution.py:115
  121.7 1.6 %collective-permute-start.29 = (bf16[32,2048]{1,0:T(8,128)(2,1)S(1)}, bf16[32,2048]{1,0:T(8,128)(2,1)S(1)}, u32[]{:S(2)}, u32[]{:S(2)}) collective-permute-start(bf16[32,2048]{1,0:T(8,128)(2,1)S(1)} %fusion.32), channel_id=1, source_target_pairs={{0,8},{8,0},{16,24},{24,16},{32,40},{40,32},{48,56},{56,48},{64,72... | collective-permute-start | bytes 393224 | tf_op jit(solution)/shard_map/ppermute | solution.py:115
  127.3 13.8 %all_to_all.11 = bf16[128,2,512]{2,1,0:T(2,128)(2,1)S(1)} all-to-all(bf16[128,2,512]{2,1,0:T(2,128)(2,1)S(1)} %bitcast.100), channel_id=1, replica_groups=mesh['row'=16,'col'=8] {'row','col'}, dimensions={0} | all-to-all | bytes 524288 | tf_op jit(solution)/shard_map/all_to_all | solution.py:200
  141.1 0.9 shard_map.68
  (105 shorter events, 34.8 us)
Async XLA Ops:
  0.7 22.0 %copy-start = (bf16[1024,4096]{1,0:T(8,128)(2,1)S(1)}, bf16[1024,4096]{1,0:T(8,128)(2,1)}, u32[]{:S(2)}) copy-start(bf16[1024,4096]{1,0:T(8,128)(2,1)} %basis_ref.3) | copy-start | bytes 25165828
  22.8 2.7 %copy-start.1 = (f32[3,1024]{1,0:T(4,128)S(1)}, f32[3,1024]{1,0:T(4,128)}, u32[]{:S(2)}) copy-start(f32[3,1024]{1,0:T(4,128)} %coords_ref) | copy-start | bytes 36868
  26.6 2.4 %collective-permute-start = (bf16[32,2048]{1,0:T(8,128)(2,1)S(1)}, bf16[32,2048]{1,0:T(8,128)(2,1)S(1)}, u32[]{:S(2)}, u32[]{:S(2)}) collective-permute-start(bf16[32,2048]{1,0:T(8,128)(2,1)S(1)} %convolution_convert_fusion.5), channel_id=1, source_target_pairs={{0,8},{8,0},{16,24},{24,16},{32,40},{40,32},{48,56},{56,48},{64,72... | collective-permute-start | bytes 393224 | tf_op jit(solution)/shard_map/ppermute | solution.py:115
  29.0 4.8 %collective-permute-start.1 = (bf16[32,2048]{1,0:T(8,128)(2,1)S(1)}, bf16[32,2048]{1,0:T(8,128)(2,1)S(1)}, u32[]{:S(2)}, u32[]{:S(2)}) collective-permute-start(bf16[32,2048]{1,0:T(8,128)(2,1)S(1)} %fusion.34), channel_id=1, source_target_pairs={{0,64},{8,72},{16,80},{24,88},{32,96},{40,104},{48,112},{56,120},{... | collective-permute-start | bytes 393224 | tf_op jit(solution)/shard_map/ppermute | solution.py:115
  33.8 6.7 %collective-permute-start.4 = (bf16[32,2048]{1,0:T(8,128)(2,1)S(1)}, bf16[32,2048]{1,0:T(8,128)(2,1)S(1)}, u32[]{:S(2)}, u32[]{:S(2)}) collective-permute-start(bf16[32,2048]{1,0:T(8,128)(2,1)S(1)} %fusion.40), channel_id=1, source_target_pairs={{0,32},{8,40},{16,48},{24,56},{32,0},{40,8},{48,16},{56,24},{64,96... | collective-permute-start | bytes 393224 | tf_op jit(solution)/shard_map/ppermute | solution.py:115
  34.8 5.8 %collective-permute-start.3 = (bf16[32,2048]{1,0:T(8,128)(2,1)S(1)}, bf16[32,2048]{1,0:T(8,128)(2,1)S(1)}, u32[]{:S(2)}, u32[]{:S(2)}) collective-permute-start(bf16[32,2048]{1,0:T(8,128)(2,1)S(1)} %fusion.40), channel_id=1, source_target_pairs={{0,48},{8,56},{16,0},{24,8},{32,16},{40,24},{48,32},{56,40},{64,11... | collective-permute-start | bytes 393224 | tf_op jit(solution)/shard_map/ppermute | solution.py:115
  36.9 6.3 %collective-permute-start.2 = (bf16[32,2048]{1,0:T(8,128)(2,1)S(1)}, bf16[32,2048]{1,0:T(8,128)(2,1)S(1)}, u32[]{:S(2)}, u32[]{:S(2)}) collective-permute-start(bf16[32,2048]{1,0:T(8,128)(2,1)S(1)} %fusion.40), channel_id=1, source_target_pairs={{0,16},{8,24},{16,32},{24,40},{32,48},{40,56},{48,0},{56,8},{64,80... | collective-permute-start | bytes 393224 | tf_op jit(solution)/shard_map/ppermute | solution.py:115
  43.3 2.8 %collective-permute-start.5 = (bf16[32,2048]{1,0:T(8,128)(2,1)S(1)}, bf16[32,2048]{1,0:T(8,128)(2,1)S(1)}, u32[]{:S(2)}, u32[]{:S(2)}) collective-permute-start(bf16[32,2048]{1,0:T(8,128)(2,1)S(1)} %fusion.26), channel_id=1, source_target_pairs={{0,8},{8,0},{16,24},{24,16},{32,40},{40,32},{48,56},{56,48},{64,72... | collective-permute-start | bytes 393224 | tf_op jit(solution)/shard_map/ppermute | solution.py:115
  47.8 1.4 collective-permute-start.6
  49.2 4.8 %collective-permute-start.7 = (bf16[32,2048]{1,0:T(8,128)(2,1)S(1)}, bf16[32,2048]{1,0:T(8,128)(2,1)S(1)}, u32[]{:S(2)}, u32[]{:S(2)}) collective-permute-start(bf16[32,2048]{1,0:T(8,128)(2,1)S(1)} %fusion.35), channel_id=1, source_target_pairs={{0,64},{8,72},{16,80},{24,88},{32,96},{40,104},{48,112},{56,120},{... | collective-permute-start | bytes 393224 | tf_op jit(solution)/shard_map/ppermute | solution.py:115
  54.0 5.4 %collective-permute-start.10 = (bf16[32,2048]{1,0:T(8,128)(2,1)S(1)}, bf16[32,2048]{1,0:T(8,128)(2,1)S(1)}, u32[]{:S(2)}, u32[]{:S(2)}) collective-permute-start(bf16[32,2048]{1,0:T(8,128)(2,1)S(1)} %fusion.41), channel_id=1, source_target_pairs={{0,32},{8,40},{16,48},{24,56},{32,0},{40,8},{48,16},{56,24},{64,96... | collective-permute-start | bytes 393224 | tf_op jit(solution)/shard_map/ppermute | solution.py:115
  54.6 5.7 %collective-permute-start.9 = (bf16[32,2048]{1,0:T(8,128)(2,1)S(1)}, bf16[32,2048]{1,0:T(8,128)(2,1)S(1)}, u32[]{:S(2)}, u32[]{:S(2)}) collective-permute-start(bf16[32,2048]{1,0:T(8,128)(2,1)S(1)} %fusion.41), channel_id=1, source_target_pairs={{0,48},{8,56},{16,0},{24,8},{32,16},{40,24},{48,32},{56,40},{64,11... | collective-permute-start | bytes 393224 | tf_op jit(solution)/shard_map/ppermute | solution.py:115
  55.5 7.4 %collective-permute-start.8 = (bf16[32,2048]{1,0:T(8,128)(2,1)S(1)}, bf16[32,2048]{1,0:T(8,128)(2,1)S(1)}, u32[]{:S(2)}, u32[]{:S(2)}) collective-permute-start(bf16[32,2048]{1,0:T(8,128)(2,1)S(1)} %fusion.41), channel_id=1, source_target_pairs={{0,16},{8,24},{16,32},{24,40},{32,48},{40,56},{48,0},{56,8},{64,80... | collective-permute-start | bytes 393224 | tf_op jit(solution)/shard_map/ppermute | solution.py:115
  63.0 2.8 %collective-permute-start.11 = (bf16[32,2048]{1,0:T(8,128)(2,1)S(1)}, bf16[32,2048]{1,0:T(8,128)(2,1)S(1)}, u32[]{:S(2)}, u32[]{:S(2)}) collective-permute-start(bf16[32,2048]{1,0:T(8,128)(2,1)S(1)} %fusion.27), channel_id=1, source_target_pairs={{0,8},{8,0},{16,24},{24,16},{32,40},{40,32},{48,56},{56,48},{64,72... | collective-permute-start | bytes 393224 | tf_op jit(solution)/shard_map/ppermute | solution.py:115
  67.4 1.4 collective-permute-start.12
  68.8 4.8 %collective-permute-start.13 = (bf16[32,2048]{1,0:T(8,128)(2,1)S(1)}, bf16[32,2048]{1,0:T(8,128)(2,1)S(1)}, u32[]{:S(2)}, u32[]{:S(2)}) collective-permute-start(bf16[32,2048]{1,0:T(8,128)(2,1)S(1)} %fusion.36), channel_id=1, source_target_pairs={{0,64},{8,72},{16,80},{24,88},{32,96},{40,104},{48,112},{56,120},{... | collective-permute-start | bytes 393224 | tf_op jit(solution)/shard_map/ppermute | solution.py:115
  73.7 5.4 %collective-permute-start.16 = (bf16[32,2048]{1,0:T(8,128)(2,1)S(1)}, bf16[32,2048]{1,0:T(8,128)(2,1)S(1)}, u32[]{:S(2)}, u32[]{:S(2)}) collective-permute-start(bf16[32,2048]{1,0:T(8,128)(2,1)S(1)} %fusion.42), channel_id=1, source_target_pairs={{0,32},{8,40},{16,48},{24,56},{32,0},{40,8},{48,16},{56,24},{64,96... | collective-permute-start | bytes 393224 | tf_op jit(solution)/shard_map/ppermute | solution.py:115
  74.2 5.7 %collective-permute-start.15 = (bf16[32,2048]{1,0:T(8,128)(2,1)S(1)}, bf16[32,2048]{1,0:T(8,128)(2,1)S(1)}, u32[]{:S(2)}, u32[]{:S(2)}) collective-permute-start(bf16[32,2048]{1,0:T(8,128)(2,1)S(1)} %fusion.42), channel_id=1, source_target_pairs={{0,48},{8,56},{16,0},{24,8},{32,16},{40,24},{48,32},{56,40},{64,11... | collective-permute-start | bytes 393224 | tf_op jit(solution)/shard_map/ppermute | solution.py:115
  75.2 7.3 %collective-permute-start.14 = (bf16[32,2048]{1,0:T(8,128)(2,1)S(1)}, bf16[32,2048]{1,0:T(8,128)(2,1)S(1)}, u32[]{:S(2)}, u32[]{:S(2)}) collective-permute-start(bf16[32,2048]{1,0:T(8,128)(2,1)S(1)} %fusion.42), channel_id=1, source_target_pairs={{0,16},{8,24},{16,32},{24,40},{32,48},{40,56},{48,0},{56,8},{64,80... | collective-permute-start | bytes 393224 | tf_op jit(solution)/shard_map/ppermute | solution.py:115
  82.6 2.6 %collective-permute-start.17 = (bf16[32,2048]{1,0:T(8,128)(2,1)S(1)}, bf16[32,2048]{1,0:T(8,128)(2,1)S(1)}, u32[]{:S(2)}, u32[]{:S(2)}) collective-permute-start(bf16[32,2048]{1,0:T(8,128)(2,1)S(1)} %fusion.29), channel_id=1, source_target_pairs={{0,8},{8,0},{16,24},{24,16},{32,40},{40,32},{48,56},{56,48},{64,72... | collective-permute-start | bytes 393224 | tf_op jit(solution)/shard_map/ppermute | solution.py:115
  86.9 1.4 collective-permute-start.18
  88.3 4.8 %collective-permute-start.19 = (bf16[32,2048]{1,0:T(8,128)(2,1)S(1)}, bf16[32,2048]{1,0:T(8,128)(2,1)S(1)}, u32[]{:S(2)}, u32[]{:S(2)}) collective-permute-start(bf16[32,2048]{1,0:T(8,128)(2,1)S(1)} %fusion.37), channel_id=1, source_target_pairs={{0,64},{8,72},{16,80},{24,88},{32,96},{40,104},{48,112},{56,120},{... | collective-permute-start | bytes 393224 | tf_op jit(solution)/shard_map/ppermute | solution.py:115
  93.2 5.4 %collective-permute-start.22 = (bf16[32,2048]{1,0:T(8,128)(2,1)S(1)}, bf16[32,2048]{1,0:T(8,128)(2,1)S(1)}, u32[]{:S(2)}, u32[]{:S(2)}) collective-permute-start(bf16[32,2048]{1,0:T(8,128)(2,1)S(1)} %fusion.43), channel_id=1, source_target_pairs={{0,32},{8,40},{16,48},{24,56},{32,0},{40,8},{48,16},{56,24},{64,96... | collective-permute-start | bytes 393224 | tf_op jit(solution)/shard_map/ppermute | solution.py:115
  93.7 5.7 %collective-permute-start.21 = (bf16[32,2048]{1,0:T(8,128)(2,1)S(1)}, bf16[32,2048]{1,0:T(8,128)(2,1)S(1)}, u32[]{:S(2)}, u32[]{:S(2)}) collective-permute-start(bf16[32,2048]{1,0:T(8,128)(2,1)S(1)} %fusion.43), channel_id=1, source_target_pairs={{0,48},{8,56},{16,0},{24,8},{32,16},{40,24},{48,32},{56,40},{64,11... | collective-permute-start | bytes 393224 | tf_op jit(solution)/shard_map/ppermute | solution.py:115
  94.7 7.3 %collective-permute-start.20 = (bf16[32,2048]{1,0:T(8,128)(2,1)S(1)}, bf16[32,2048]{1,0:T(8,128)(2,1)S(1)}, u32[]{:S(2)}, u32[]{:S(2)}) collective-permute-start(bf16[32,2048]{1,0:T(8,128)(2,1)S(1)} %fusion.43), channel_id=1, source_target_pairs={{0,16},{8,24},{16,32},{24,40},{32,48},{40,56},{48,0},{56,8},{64,80... | collective-permute-start | bytes 393224 | tf_op jit(solution)/shard_map/ppermute | solution.py:115
  102.1 2.6 %collective-permute-start.23 = (bf16[32,2048]{1,0:T(8,128)(2,1)S(1)}, bf16[32,2048]{1,0:T(8,128)(2,1)S(1)}, u32[]{:S(2)}, u32[]{:S(2)}) collective-permute-start(bf16[32,2048]{1,0:T(8,128)(2,1)S(1)} %fusion.30), channel_id=1, source_target_pairs={{0,8},{8,0},{16,24},{24,16},{32,40},{40,32},{48,56},{56,48},{64,72... | collective-permute-start | bytes 393224 | tf_op jit(solution)/shard_map/ppermute | solution.py:115
  106.4 1.4 collective-permute-start.24
  107.8 4.8 %collective-permute-start.25 = (bf16[32,2048]{1,0:T(8,128)(2,1)S(1)}, bf16[32,2048]{1,0:T(8,128)(2,1)S(1)}, u32[]{:S(2)}, u32[]{:S(2)}) collective-permute-start(bf16[32,2048]{1,0:T(8,128)(2,1)S(1)} %fusion.38), channel_id=1, source_target_pairs={{0,64},{8,72},{16,80},{24,88},{32,96},{40,104},{48,112},{56,120},{... | collective-permute-start | bytes 393224 | tf_op jit(solution)/shard_map/ppermute | solution.py:115
  112.6 5.7 %collective-permute-start.28 = (bf16[32,2048]{1,0:T(8,128)(2,1)S(1)}, bf16[32,2048]{1,0:T(8,128)(2,1)S(1)}, u32[]{:S(2)}, u32[]{:S(2)}) collective-permute-start(bf16[32,2048]{1,0:T(8,128)(2,1)S(1)} %fusion.44), channel_id=1, source_target_pairs={{0,32},{8,40},{16,48},{24,56},{32,0},{40,8},{48,16},{56,24},{64,96... | collective-permute-start | bytes 393224 | tf_op jit(solution)/shard_map/ppermute | solution.py:115
  113.4 5.7 %collective-permute-start.27 = (bf16[32,2048]{1,0:T(8,128)(2,1)S(1)}, bf16[32,2048]{1,0:T(8,128)(2,1)S(1)}, u32[]{:S(2)}, u32[]{:S(2)}) collective-permute-start(bf16[32,2048]{1,0:T(8,128)(2,1)S(1)} %fusion.44), channel_id=1, source_target_pairs={{0,48},{8,56},{16,0},{24,8},{32,16},{40,24},{48,32},{56,40},{64,11... | collective-permute-start | bytes 393224 | tf_op jit(solution)/shard_map/ppermute | solution.py:115
  114.3 7.3 %collective-permute-start.26 = (bf16[32,2048]{1,0:T(8,128)(2,1)S(1)}, bf16[32,2048]{1,0:T(8,128)(2,1)S(1)}, u32[]{:S(2)}, u32[]{:S(2)}) collective-permute-start(bf16[32,2048]{1,0:T(8,128)(2,1)S(1)} %fusion.44), channel_id=1, source_target_pairs={{0,16},{8,24},{16,32},{24,40},{32,48},{40,56},{48,0},{56,8},{64,80... | collective-permute-start | bytes 393224 | tf_op jit(solution)/shard_map/ppermute | solution.py:115
  121.7 2.6 %collective-permute-start.29 = (bf16[32,2048]{1,0:T(8,128)(2,1)S(1)}, bf16[32,2048]{1,0:T(8,128)(2,1)S(1)}, u32[]{:S(2)}, u32[]{:S(2)}) collective-permute-start(bf16[32,2048]{1,0:T(8,128)(2,1)S(1)} %fusion.32), channel_id=1, source_target_pairs={{0,8},{8,0},{16,24},{24,16},{32,40},{40,32},{48,56},{56,48},{64,72... | collective-permute-start | bytes 393224 | tf_op jit(solution)/shard_map/ppermute | solution.py:115
  (4 other events, 8.0 us)

commit v10 on v9

--- a/solution.py
+++ b/solution.py
@@ -121,10 +121,13 @@
         return move(array, lambda r: r ^ 8)
 
     def along_z(array, hops):
-        return move(array, lambda r: (r & 9) | ((r + 2 * hops) & 6))
-
-    def over_chips(total):
-        total = total + along_y(total.astype(bf16)).astype(f32)
+        return move(array, lambda r: r ^ (2 * hops))
+
+    def over_chips(total, beside=None):
+        arrived = along_y(total.astype(bf16))
+        if beside is not None:
+            arrived, _ = lax.optimization_barrier((arrived, beside))
+        total = total + arrived.astype(f32)
         sent = total.astype(bf16)
         for hops in (1, 3, 2):
             total = total + along_z(sent, hops).astype(f32)
@@ -168,7 +171,7 @@
     sent = product(nodes, basis_other, NN).astype(bf16)
     kept = lax.optimization_barrier(product(nodes, basis_own, NN))
     turned_own, turned_other = turned(mode_basis, own_from), turned(mode_basis, other_from)
-    sums = over_chips(kept + to_other_core(sent).astype(f32))
+    sums = over_chips(kept + to_other_core(sent).astype(f32), turned_own)
 
     def weighted(own, other, half_step):
         kept = lax.optimization_barrier(product(own, turned_own, NN))

time: 142 us -> 142 us (level)
  transfers between devices with their start and end apart: 30 -> 30, of which waited for: 28 -> 25; matrix products, arithmetic and copies ran while one was open for 6% -> 6% of each run, Pallas kernels for 3% -> 3%
where the time goes in v10:
time: 142 us
  waiting for transfers between devices  51.8 us (36%)
  blocking collectives  36.1 us (25%)
  starting transfers between devices  25.2 us (18%)
  matrix products  20.9 us (15%)
  Pallas kernels  4.79 us (3%)
    ppermute x30, waiting for transfers between devices, move(): lax.ppermute(array, 'row', [(r, target(r)) for r in range(row_count)])  51.8 us
    all_to_all x2, blocking collectives, on_device(): every = lax.all_to_all(sent, ('row', 'col'), 0, 0)  36.1 us
    ppermute x30, starting transfers between devices, move(): lax.ppermute(array, 'row', [(r, target(r)) for r in range(row_count)])  25.2 us
    dot_general x24, matrix products, product(): lax.dot_general(left, right, dims, preferred_element_type=jnp.float32)  20.9 us
    pallas_call x2, Pallas kernels, turned(): pl.pallas_call(turn_kernel, out_shape=jax.ShapeDtypeStruct((width, nodes)...  3.62 us
  transfers between devices with their start and end apart: 30, of which 25 were waited for; matrix products, arithmetic and copies ran while one was open for 6% of the time, Pallas kernels for 3%

profile of v10, /device:TPU:1, one launch (start us, length us, event | category | flops | bytes accessed | tf_op | source)
XLA Modules:
  0.0 141.6 jit_solution(13785681832302923172)
XLA Ops:
  0.8 21.8 %all_to_all.10 = bf16[128,2,512]{2,1,0:T(2,128)(2,1)S(1)} all-to-all(bf16[128,2,512]{2,1,0:T(2,128)(2,1)S(1)} %bitcast.89), channel_id=1, replica_groups=mesh['row'=16,'col'=8] {'row','col'}, dimensions={0} | all-to-all | bytes 524288 | tf_op jit(solution)/shard_map/all_to_all | solution.py:151
  22.8 1.3 fusion.20
  24.1 1.3 fusion.22
  26.6 1.4 collective-permute-start
  29.4 1.8 %shard_map.66 = bf16[2048,1024]{1,0:T(8,128)(2,1)S(1)} custom-call(s32[1]{0:T(128)} %bitcast.1.from_ref, bf16[1024,4096]{1,0:T(8,128)(2,1)S(1)} %copy-done), custom_call_target="tpu_custom_call" | custom-call | bytes 8388608 | tf_op jit(solution)/shard_map/pallas_call | solution.py:25
  31.2 2.6 %collective-permute-done.1 = bf16[32,2048]{1,0:T(8,128)(2,1)S(1)} collective-permute-done((bf16[32,2048]{1,0:T(8,128)(2,1)S(1)}, bf16[32,2048]{1,0:T(8,128)(2,1)S(1)}, u32[]{:S(2)}, u32[]{:S(2)}) %collective-permute-start.1) | collective-permute-done | bytes 131104 | tf_op jit(solution)/shard_map/ppermute | solution.py:115
  34.8 2.1 %collective-permute-start.3 = (bf16[32,2048]{1,0:T(8,128)(2,1)S(1)}, bf16[32,2048]{1,0:T(8,128)(2,1)S(1)}, u32[]{:S(2)}, u32[]{:S(2)}) collective-permute-start(bf16[32,2048]{1,0:T(8,128)(2,1)S(1)} %fusion.40), channel_id=1, source_target_pairs={{0,48},{8,56},{16,32},{24,40},{32,16},{40,24},{48,0},{56,8},{64,11... | collective-permute-start | bytes 393224 | tf_op jit(solution)/shard_map/ppermute | solution.py:115
  36.9 1.8 %shard_map.67 = bf16[2048,1024]{1,0:T(8,128)(2,1)S(1)} custom-call(s32[1]{0:T(128)} %bitcast.2.from_ref, bf16[1024,4096]{1,0:T(8,128)(2,1)S(1)} %copy-done), custom_call_target="tpu_custom_call" | custom-call | bytes 8388608 | tf_op jit(solution)/shard_map/pallas_call | solution.py:25
  39.3 3.7 %collective-permute-done.3 = bf16[32,2048]{1,0:T(8,128)(2,1)S(1)} collective-permute-done((bf16[32,2048]{1,0:T(8,128)(2,1)S(1)}, bf16[32,2048]{1,0:T(8,128)(2,1)S(1)}, u32[]{:S(2)}, u32[]{:S(2)}) %collective-permute-start.3) | collective-permute-done | bytes 131104 | tf_op jit(solution)/shard_map/ppermute | solution.py:115
  43.2 1.2 collective-permute-start.5
  48.9 4.4 %collective-permute-done.7 = bf16[32,2048]{1,0:T(8,128)(2,1)S(1)} collective-permute-done((bf16[32,2048]{1,0:T(8,128)(2,1)S(1)}, bf16[32,2048]{1,0:T(8,128)(2,1)S(1)}, u32[]{:S(2)}, u32[]{:S(2)}) %collective-permute-start.7) | collective-permute-done | bytes 131104 | tf_op jit(solution)/shard_map/ppermute | solution.py:115
  53.3 1.3 collective-permute-start.10
  56.0 2.7 %collective-permute-done.10 = bf16[32,2048]{1,0:T(8,128)(2,1)S(1)} collective-permute-done((bf16[32,2048]{1,0:T(8,128)(2,1)S(1)}, bf16[32,2048]{1,0:T(8,128)(2,1)S(1)}, u32[]{:S(2)}, u32[]{:S(2)}) %collective-permute-start.10) | collective-permute-done | bytes 131104 | tf_op jit(solution)/shard_map/ppermute | solution.py:115
  58.8 3.7 %collective-permute-done.9 = bf16[32,2048]{1,0:T(8,128)(2,1)S(1)} collective-permute-done((bf16[32,2048]{1,0:T(8,128)(2,1)S(1)}, bf16[32,2048]{1,0:T(8,128)(2,1)S(1)}, u32[]{:S(2)}, u32[]{:S(2)}) %collective-permute-start.9) | collective-permute-done | bytes 131104 | tf_op jit(solution)/shard_map/ppermute | solution.py:115
  62.6 1.4 collective-permute-start.11
  68.5 4.4 %collective-permute-done.13 = bf16[32,2048]{1,0:T(8,128)(2,1)S(1)} collective-permute-done((bf16[32,2048]{1,0:T(8,128)(2,1)S(1)}, bf16[32,2048]{1,0:T(8,128)(2,1)S(1)}, u32[]{:S(2)}, u32[]{:S(2)}) %collective-permute-start.13) | collective-permute-done | bytes 131104 | tf_op jit(solution)/shard_map/ppermute | solution.py:115
  73.0 1.3 collective-permute-start.16
  74.2 0.9 collective-permute-start.15
  75.7 2.7 %collective-permute-done.16 = bf16[32,2048]{1,0:T(8,128)(2,1)S(1)} collective-permute-done((bf16[32,2048]{1,0:T(8,128)(2,1)S(1)}, bf16[32,2048]{1,0:T(8,128)(2,1)S(1)}, u32[]{:S(2)}, u32[]{:S(2)}) %collective-permute-start.16) | collective-permute-done | bytes 131104 | tf_op jit(solution)/shard_map/ppermute | solution.py:115
  78.4 3.7 %collective-permute-done.15 = bf16[32,2048]{1,0:T(8,128)(2,1)S(1)} collective-permute-done((bf16[32,2048]{1,0:T(8,128)(2,1)S(1)}, bf16[32,2048]{1,0:T(8,128)(2,1)S(1)}, u32[]{:S(2)}, u32[]{:S(2)}) %collective-permute-start.15) | collective-permute-done | bytes 131104 | tf_op jit(solution)/shard_map/ppermute | solution.py:115
  82.3 1.2 collective-permute-start.17
  88.0 4.4 %collective-permute-done.19 = bf16[32,2048]{1,0:T(8,128)(2,1)S(1)} collective-permute-done((bf16[32,2048]{1,0:T(8,128)(2,1)S(1)}, bf16[32,2048]{1,0:T(8,128)(2,1)S(1)}, u32[]{:S(2)}, u32[]{:S(2)}) %collective-permute-start.19) | collective-permute-done | bytes 131104 | tf_op jit(solution)/shard_map/ppermute | solution.py:115
  92.4 1.3 collective-permute-start.22
  95.1 2.7 %collective-permute-done.22 = bf16[32,2048]{1,0:T(8,128)(2,1)S(1)} collective-permute-done((bf16[32,2048]{1,0:T(8,128)(2,1)S(1)}, bf16[32,2048]{1,0:T(8,128)(2,1)S(1)}, u32[]{:S(2)}, u32[]{:S(2)}) %collective-permute-start.22) | collective-permute-done | bytes 131104 | tf_op jit(solution)/shard_map/ppermute | solution.py:115
  97.9 3.7 %collective-permute-done.21 = bf16[32,2048]{1,0:T(8,128)(2,1)S(1)} collective-permute-done((bf16[32,2048]{1,0:T(8,128)(2,1)S(1)}, bf16[32,2048]{1,0:T(8,128)(2,1)S(1)}, u32[]{:S(2)}, u32[]{:S(2)}) %collective-permute-start.21) | collective-permute-done | bytes 131104 | tf_op jit(solution)/shard_map/ppermute | solution.py:115
  101.7 1.2 collective-permute-start.23
  107.5 4.4 %collective-permute-done.25 = bf16[32,2048]{1,0:T(8,128)(2,1)S(1)} collective-permute-done((bf16[32,2048]{1,0:T(8,128)(2,1)S(1)}, bf16[32,2048]{1,0:T(8,128)(2,1)S(1)}, u32[]{:S(2)}, u32[]{:S(2)}) %collective-permute-start.25) | collective-permute-done | bytes 131104 | tf_op jit(solution)/shard_map/ppermute | solution.py:115
  111.9 1.3 collective-permute-start.28
  114.6 2.7 %collective-permute-done.28 = bf16[32,2048]{1,0:T(8,128)(2,1)S(1)} collective-permute-done((bf16[32,2048]{1,0:T(8,128)(2,1)S(1)}, bf16[32,2048]{1,0:T(8,128)(2,1)S(1)}, u32[]{:S(2)}, u32[]{:S(2)}) %collective-permute-start.28) | collective-permute-done | bytes 131104 | tf_op jit(solution)/shard_map/ppermute | solution.py:115
  117.3 3.7 %collective-permute-done.27 = bf16[32,2048]{1,0:T(8,128)(2,1)S(1)} collective-permute-done((bf16[32,2048]{1,0:T(8,128)(2,1)S(1)}, bf16[32,2048]{1,0:T(8,128)(2,1)S(1)}, u32[]{:S(2)}, u32[]{:S(2)}) %collective-permute-start.27) | collective-permute-done | bytes 131104 | tf_op jit(solution)/shard_map/ppermute | solution.py:115
  121.2 1.2 collective-permute-start.29
  126.4 14.3 %all_to_all.11 = bf16[128,2,512]{2,1,0:T(2,128)(2,1)S(1)} all-to-all(bf16[128,2,512]{2,1,0:T(2,128)(2,1)S(1)} %bitcast.100), channel_id=1, replica_groups=mesh['row'=16,'col'=8] {'row','col'}, dimensions={0} | all-to-all | bytes 524288 | tf_op jit(solution)/shard_map/all_to_all | solution.py:203
  (105 shorter events, 33.6 us)
Async XLA Ops:
  0.7 22.0 %copy-start = (bf16[1024,4096]{1,0:T(8,128)(2,1)S(1)}, bf16[1024,4096]{1,0:T(8,128)(2,1)}, u32[]{:S(2)}) copy-start(bf16[1024,4096]{1,0:T(8,128)(2,1)} %basis_ref.3) | copy-start | bytes 25165828
  26.6 2.4 %collective-permute-start = (bf16[32,2048]{1,0:T(8,128)(2,1)S(1)}, bf16[32,2048]{1,0:T(8,128)(2,1)S(1)}, u32[]{:S(2)}, u32[]{:S(2)}) collective-permute-start(bf16[32,2048]{1,0:T(8,128)(2,1)S(1)} %convolution_convert_fusion.5), channel_id=1, source_target_pairs={{0,8},{8,0},{16,24},{24,16},{32,40},{40,32},{48,56},{56,48},{64,72... | collective-permute-start | bytes 393224 | tf_op jit(solution)/shard_map/ppermute | solution.py:115
  29.0 4.8 %collective-permute-start.1 = (bf16[32,2048]{1,0:T(8,128)(2,1)S(1)}, bf16[32,2048]{1,0:T(8,128)(2,1)S(1)}, u32[]{:S(2)}, u32[]{:S(2)}) collective-permute-start(bf16[32,2048]{1,0:T(8,128)(2,1)S(1)} %fusion.34), channel_id=1, source_target_pairs={{0,64},{8,72},{16,80},{24,88},{32,96},{40,104},{48,112},{56,120},{... | collective-permute-start | bytes 393224 | tf_op jit(solution)/shard_map/ppermute | solution.py:115
  33.8 4.9 %copy-start.5 = (f32[4096]{0:T(1024)S(1)}, f32[4096]{0:T(1024)}, u32[]{:S(2)}) copy-start(f32[4096]{0:T(1024)} %param.10) | copy-start | bytes 49156
  33.8 5.5 %collective-permute-start.4 = (bf16[32,2048]{1,0:T(8,128)(2,1)S(1)}, bf16[32,2048]{1,0:T(8,128)(2,1)S(1)}, u32[]{:S(2)}, u32[]{:S(2)}) collective-permute-start(bf16[32,2048]{1,0:T(8,128)(2,1)S(1)} %fusion.40), channel_id=1, source_target_pairs={{0,32},{8,40},{16,48},{24,56},{32,0},{40,8},{48,16},{56,24},{64,96... | collective-permute-start | bytes 393224 | tf_op jit(solution)/shard_map/ppermute | solution.py:115
  34.8 8.3 %collective-permute-start.3 = (bf16[32,2048]{1,0:T(8,128)(2,1)S(1)}, bf16[32,2048]{1,0:T(8,128)(2,1)S(1)}, u32[]{:S(2)}, u32[]{:S(2)}) collective-permute-start(bf16[32,2048]{1,0:T(8,128)(2,1)S(1)} %fusion.40), channel_id=1, source_target_pairs={{0,48},{8,56},{16,32},{24,40},{32,16},{40,24},{48,0},{56,8},{64,11... | collective-permute-start | bytes 393224 | tf_op jit(solution)/shard_map/ppermute | solution.py:115
  36.9 6.2 %collective-permute-start.2 = (bf16[32,2048]{1,0:T(8,128)(2,1)S(1)}, bf16[32,2048]{1,0:T(8,128)(2,1)S(1)}, u32[]{:S(2)}, u32[]{:S(2)}) collective-permute-start(bf16[32,2048]{1,0:T(8,128)(2,1)S(1)} %fusion.40), channel_id=1, source_target_pairs={{0,16},{8,24},{16,0},{24,8},{32,48},{40,56},{48,32},{56,40},{64,80... | collective-permute-start | bytes 393224 | tf_op jit(solution)/shard_map/ppermute | solution.py:115
  43.2 2.1 %collective-permute-start.5 = (bf16[32,2048]{1,0:T(8,128)(2,1)S(1)}, bf16[32,2048]{1,0:T(8,128)(2,1)S(1)}, u32[]{:S(2)}, u32[]{:S(2)}) collective-permute-start(bf16[32,2048]{1,0:T(8,128)(2,1)S(1)} %fusion.26), channel_id=1, source_target_pairs={{0,8},{8,0},{16,24},{24,16},{32,40},{40,32},{48,56},{56,48},{64,72... | collective-permute-start | bytes 393224 | tf_op jit(solution)/shard_map/ppermute | solution.py:115
  47.0 1.4 collective-permute-start.6
  48.4 4.8 %collective-permute-start.7 = (bf16[32,2048]{1,0:T(8,128)(2,1)S(1)}, bf16[32,2048]{1,0:T(8,128)(2,1)S(1)}, u32[]{:S(2)}, u32[]{:S(2)}) collective-permute-start(bf16[32,2048]{1,0:T(8,128)(2,1)S(1)} %fusion.35), channel_id=1, source_target_pairs={{0,64},{8,72},{16,80},{24,88},{32,96},{40,104},{48,112},{56,120},{... | collective-permute-start | bytes 393224 | tf_op jit(solution)/shard_map/ppermute | solution.py:115
  53.3 5.5 %collective-permute-start.10 = (bf16[32,2048]{1,0:T(8,128)(2,1)S(1)}, bf16[32,2048]{1,0:T(8,128)(2,1)S(1)}, u32[]{:S(2)}, u32[]{:S(2)}) collective-permute-start(bf16[32,2048]{1,0:T(8,128)(2,1)S(1)} %fusion.41), channel_id=1, source_target_pairs={{0,32},{8,40},{16,48},{24,56},{32,0},{40,8},{48,16},{56,24},{64,96... | collective-permute-start | bytes 393224 | tf_op jit(solution)/shard_map/ppermute | solution.py:115
  54.6 7.9 %collective-permute-start.9 = (bf16[32,2048]{1,0:T(8,128)(2,1)S(1)}, bf16[32,2048]{1,0:T(8,128)(2,1)S(1)}, u32[]{:S(2)}, u32[]{:S(2)}) collective-permute-start(bf16[32,2048]{1,0:T(8,128)(2,1)S(1)} %fusion.41), channel_id=1, source_target_pairs={{0,48},{8,56},{16,32},{24,40},{32,16},{40,24},{48,0},{56,8},{64,11... | collective-permute-start | bytes 393224 | tf_op jit(solution)/shard_map/ppermute | solution.py:115
  55.5 7.0 %collective-permute-start.8 = (bf16[32,2048]{1,0:T(8,128)(2,1)S(1)}, bf16[32,2048]{1,0:T(8,128)(2,1)S(1)}, u32[]{:S(2)}, u32[]{:S(2)}) collective-permute-start(bf16[32,2048]{1,0:T(8,128)(2,1)S(1)} %fusion.41), channel_id=1, source_target_pairs={{0,16},{8,24},{16,0},{24,8},{32,48},{40,56},{48,32},{56,40},{64,80... | collective-permute-start | bytes 393224 | tf_op jit(solution)/shard_map/ppermute | solution.py:115
  62.6 2.4 %collective-permute-start.11 = (bf16[32,2048]{1,0:T(8,128)(2,1)S(1)}, bf16[32,2048]{1,0:T(8,128)(2,1)S(1)}, u32[]{:S(2)}, u32[]{:S(2)}) collective-permute-start(bf16[32,2048]{1,0:T(8,128)(2,1)S(1)} %fusion.27), channel_id=1, source_target_pairs={{0,8},{8,0},{16,24},{24,16},{32,40},{40,32},{48,56},{56,48},{64,72... | collective-permute-start | bytes 393224 | tf_op jit(solution)/shard_map/ppermute | solution.py:115
  66.7 1.4 collective-permute-start.12
  68.1 4.8 %collective-permute-start.13 = (bf16[32,2048]{1,0:T(8,128)(2,1)S(1)}, bf16[32,2048]{1,0:T(8,128)(2,1)S(1)}, u32[]{:S(2)}, u32[]{:S(2)}) collective-permute-start(bf16[32,2048]{1,0:T(8,128)(2,1)S(1)} %fusion.36), channel_id=1, source_target_pairs={{0,64},{8,72},{16,80},{24,88},{32,96},{40,104},{48,112},{56,120},{... | collective-permute-start | bytes 393224 | tf_op jit(solution)/shard_map/ppermute | solution.py:115
  73.0 5.5 %collective-permute-start.16 = (bf16[32,2048]{1,0:T(8,128)(2,1)S(1)}, bf16[32,2048]{1,0:T(8,128)(2,1)S(1)}, u32[]{:S(2)}, u32[]{:S(2)}) collective-permute-start(bf16[32,2048]{1,0:T(8,128)(2,1)S(1)} %fusion.42), channel_id=1, source_target_pairs={{0,32},{8,40},{16,48},{24,56},{32,0},{40,8},{48,16},{56,24},{64,96... | collective-permute-start | bytes 393224 | tf_op jit(solution)/shard_map/ppermute | solution.py:115
  74.2 7.9 %collective-permute-start.15 = (bf16[32,2048]{1,0:T(8,128)(2,1)S(1)}, bf16[32,2048]{1,0:T(8,128)(2,1)S(1)}, u32[]{:S(2)}, u32[]{:S(2)}) collective-permute-start(bf16[32,2048]{1,0:T(8,128)(2,1)S(1)} %fusion.42), channel_id=1, source_target_pairs={{0,48},{8,56},{16,32},{24,40},{32,16},{40,24},{48,0},{56,8},{64,11... | collective-permute-start | bytes 393224 | tf_op jit(solution)/shard_map/ppermute | solution.py:115
  75.2 7.0 %collective-permute-start.14 = (bf16[32,2048]{1,0:T(8,128)(2,1)S(1)}, bf16[32,2048]{1,0:T(8,128)(2,1)S(1)}, u32[]{:S(2)}, u32[]{:S(2)}) collective-permute-start(bf16[32,2048]{1,0:T(8,128)(2,1)S(1)} %fusion.42), channel_id=1, source_target_pairs={{0,16},{8,24},{16,0},{24,8},{32,48},{40,56},{48,32},{56,40},{64,80... | collective-permute-start | bytes 393224 | tf_op jit(solution)/shard_map/ppermute | solution.py:115
  82.3 2.2 %collective-permute-start.17 = (bf16[32,2048]{1,0:T(8,128)(2,1)S(1)}, bf16[32,2048]{1,0:T(8,128)(2,1)S(1)}, u32[]{:S(2)}, u32[]{:S(2)}) collective-permute-start(bf16[32,2048]{1,0:T(8,128)(2,1)S(1)} %fusion.29), channel_id=1, source_target_pairs={{0,8},{8,0},{16,24},{24,16},{32,40},{40,32},{48,56},{56,48},{64,72... | collective-permute-start | bytes 393224 | tf_op jit(solution)/shard_map/ppermute | solution.py:115
  86.2 1.4 collective-permute-start.18
  87.6 4.8 %collective-permute-start.19 = (bf16[32,2048]{1,0:T(8,128)(2,1)S(1)}, bf16[32,2048]{1,0:T(8,128)(2,1)S(1)}, u32[]{:S(2)}, u32[]{:S(2)}) collective-permute-start(bf16[32,2048]{1,0:T(8,128)(2,1)S(1)} %fusion.37), channel_id=1, source_target_pairs={{0,64},{8,72},{16,80},{24,88},{32,96},{40,104},{48,112},{56,120},{... | collective-permute-start | bytes 393224 | tf_op jit(solution)/shard_map/ppermute | solution.py:115
  92.4 5.5 %collective-permute-start.22 = (bf16[32,2048]{1,0:T(8,128)(2,1)S(1)}, bf16[32,2048]{1,0:T(8,128)(2,1)S(1)}, u32[]{:S(2)}, u32[]{:S(2)}) collective-permute-start(bf16[32,2048]{1,0:T(8,128)(2,1)S(1)} %fusion.43), channel_id=1, source_target_pairs={{0,32},{8,40},{16,48},{24,56},{32,0},{40,8},{48,16},{56,24},{64,96... | collective-permute-start | bytes 393224 | tf_op jit(solution)/shard_map/ppermute | solution.py:115
  93.7 7.9 %collective-permute-start.21 = (bf16[32,2048]{1,0:T(8,128)(2,1)S(1)}, bf16[32,2048]{1,0:T(8,128)(2,1)S(1)}, u32[]{:S(2)}, u32[]{:S(2)}) collective-permute-start(bf16[32,2048]{1,0:T(8,128)(2,1)S(1)} %fusion.43), channel_id=1, source_target_pairs={{0,48},{8,56},{16,32},{24,40},{32,16},{40,24},{48,0},{56,8},{64,11... | collective-permute-start | bytes 393224 | tf_op jit(solution)/shard_map/ppermute | solution.py:115
  94.6 7.0 %collective-permute-start.20 = (bf16[32,2048]{1,0:T(8,128)(2,1)S(1)}, bf16[32,2048]{1,0:T(8,128)(2,1)S(1)}, u32[]{:S(2)}, u32[]{:S(2)}) collective-permute-start(bf16[32,2048]{1,0:T(8,128)(2,1)S(1)} %fusion.43), channel_id=1, source_target_pairs={{0,16},{8,24},{16,0},{24,8},{32,48},{40,56},{48,32},{56,40},{64,80... | collective-permute-start | bytes 393224 | tf_op jit(solution)/shard_map/ppermute | solution.py:115
  101.7 2.2 %collective-permute-start.23 = (bf16[32,2048]{1,0:T(8,128)(2,1)S(1)}, bf16[32,2048]{1,0:T(8,128)(2,1)S(1)}, u32[]{:S(2)}, u32[]{:S(2)}) collective-permute-start(bf16[32,2048]{1,0:T(8,128)(2,1)S(1)} %fusion.30), channel_id=1, source_target_pairs={{0,8},{8,0},{16,24},{24,16},{32,40},{40,32},{48,56},{56,48},{64,72... | collective-permute-start | bytes 393224 | tf_op jit(solution)/shard_map/ppermute | solution.py:115
  105.6 1.4 collective-permute-start.24
  107.0 4.8 %collective-permute-start.25 = (bf16[32,2048]{1,0:T(8,128)(2,1)S(1)}, bf16[32,2048]{1,0:T(8,128)(2,1)S(1)}, u32[]{:S(2)}, u32[]{:S(2)}) collective-permute-start(bf16[32,2048]{1,0:T(8,128)(2,1)S(1)} %fusion.38), channel_id=1, source_target_pairs={{0,64},{8,72},{16,80},{24,88},{32,96},{40,104},{48,112},{56,120},{... | collective-permute-start | bytes 393224 | tf_op jit(solution)/shard_map/ppermute | solution.py:115
  111.9 5.5 %collective-permute-start.28 = (bf16[32,2048]{1,0:T(8,128)(2,1)S(1)}, bf16[32,2048]{1,0:T(8,128)(2,1)S(1)}, u32[]{:S(2)}, u32[]{:S(2)}) collective-permute-start(bf16[32,2048]{1,0:T(8,128)(2,1)S(1)} %fusion.44), channel_id=1, source_target_pairs={{0,32},{8,40},{16,48},{24,56},{32,0},{40,8},{48,16},{56,24},{64,96... | collective-permute-start | bytes 393224 | tf_op jit(solution)/shard_map/ppermute | solution.py:115
  113.2 7.9 %collective-permute-start.27 = (bf16[32,2048]{1,0:T(8,128)(2,1)S(1)}, bf16[32,2048]{1,0:T(8,128)(2,1)S(1)}, u32[]{:S(2)}, u32[]{:S(2)}) collective-permute-start(bf16[32,2048]{1,0:T(8,128)(2,1)S(1)} %fusion.44), channel_id=1, source_target_pairs={{0,48},{8,56},{16,32},{24,40},{32,16},{40,24},{48,0},{56,8},{64,11... | collective-permute-start | bytes 393224 | tf_op jit(solution)/shard_map/ppermute | solution.py:115
  114.1 7.0 %collective-permute-start.26 = (bf16[32,2048]{1,0:T(8,128)(2,1)S(1)}, bf16[32,2048]{1,0:T(8,128)(2,1)S(1)}, u32[]{:S(2)}, u32[]{:S(2)}) collective-permute-start(bf16[32,2048]{1,0:T(8,128)(2,1)S(1)} %fusion.44), channel_id=1, source_target_pairs={{0,16},{8,24},{16,0},{24,8},{32,48},{40,56},{48,32},{56,40},{64,80... | collective-permute-start | bytes 393224 | tf_op jit(solution)/shard_map/ppermute | solution.py:115
  121.2 2.2 %collective-permute-start.29 = (bf16[32,2048]{1,0:T(8,128)(2,1)S(1)}, bf16[32,2048]{1,0:T(8,128)(2,1)S(1)}, u32[]{:S(2)}, u32[]{:S(2)}) collective-permute-start(bf16[32,2048]{1,0:T(8,128)(2,1)S(1)} %fusion.32), channel_id=1, source_target_pairs={{0,8},{8,0},{16,24},{24,16},{32,40},{40,32},{48,56},{56,48},{64,72... | collective-permute-start | bytes 393224 | tf_op jit(solution)/shard_map/ppermute | solution.py:115
  (4 other events, 8.9 us)

commit v11 on v10

--- a/solution.py
+++ b/solution.py
@@ -36,6 +36,25 @@
             flops=0, bytes_accessed=4 * width * nodes, transcendentals=0
         ),
     )(start, basis)
+
+
+def flip_kernel(array_ref, turned_ref):
+    turned_ref[...] = array_ref[...].T
+
+
+def flipped(array, block=512):
+    rows, width = array.shape
+    return pl.pallas_call(
+        flip_kernel,
+        out_shape=jax.ShapeDtypeStruct((width, rows), array.dtype),
+        grid=(rows // block,),
+        in_specs=[pl.BlockSpec((block, width), lambda j: (j, 0))],
+        out_specs=pl.BlockSpec((width, block), lambda j: (0, j)),
+        compiler_params=pltpu.CompilerParams(vmem_limit_bytes=10 << 20),
+        cost_estimate=pl.CostEstimate(
+            flops=0, bytes_accessed=4 * width * rows, transcendentals=0
+        ),
+    )(array)
 
 
 def spread_kernel(waves_ref, sent_ref):
@@ -156,7 +175,7 @@
     )
     weights = node_weights(coords, quad, turns, row_count)
 
-    def mixed(nodes, half_step):
+    def mixed(nodes, half_step, weights=weights):
         factor = 0.5 if half_step % 2 == 0 else 1.0
         scale = factor * weights[half_step]
         real, imag = nodes[:row_count], nodes[row_count:]
@@ -177,24 +196,41 @@
         kept = lax.optimization_barrier(product(own, turned_own, NN))
         return mixed(kept + product(other, turned_other, NN), half_step)
 
-    def summed(nodes):
+    def summed(nodes, beside):
         arrived = to_other_core(product(nodes, basis_other, NN).astype(bf16))
         kept = lax.optimization_barrier(product(nodes, basis_own, NN))
-        return over_chips(kept + arrived.astype(f32))
+        return over_chips(kept + arrived.astype(f32), beside)
+
+    turned_mate = to_other_core(turned_other)
+    weights_mate = to_other_core(weights)
+    basis_mate = flipped(turned_mate)
+
+    def reduced(own, half_step):
+        for_mate = lax.optimization_barrier(product(own, turned_mate, NN))
+        arrived = to_other_core(for_mate.astype(bf16))
+        for_own = lax.optimization_barrier(product(own, turned_own, NN))
+        arrived_mate = to_other_core(for_own.astype(bf16))
+        nodes = mixed(for_own + arrived.astype(f32), half_step)
+        kept = lax.optimization_barrier(product(nodes, basis_own, NN))
+        nodes = mixed(for_mate + arrived_mate.astype(f32), half_step, weights_mate)
+        return kept + product(nodes, basis_mate, NN)
 
     for step in range(STEPS):
         if step > 0:
-            sums = summed(weighted(field, to_other_core(field), 2 * step))
+            sums = over_chips(reduced(field, 2 * step))
         half = (sums + (1.0 - 0.5 * rates) * field.astype(f32)).astype(bf16)
-        nodes = weighted(half, to_other_core(half), 2 * step + 1)
+        if step == 0:
+            sums = summed(weighted(half, to_other_core(half), 1), (basis_mate, weights_mate))
+        elif step + 1 < STEPS:
+            sums = over_chips(reduced(half, 2 * step + 1))
         if step + 1 < STEPS:
-            update = summed(nodes) + (0.0 - 1.0 * rates) * half.astype(f32)
+            update = sums + (0.0 - 1.0 * rates) * half.astype(f32)
             field = (field.astype(f32) + update).astype(bf16)
 
     local = field.astype(f32) + (0.0 - 1.0 * rates) * half.astype(f32)
     local = jnp.where(first_chip, local, 0.0)
-    part_own = (product(nodes, basis_own, NN) + local).astype(bf16)
-    part_other = product(nodes, basis_other, NN).astype(bf16)
+    part_own = (reduced(half, 2 * STEPS - 1) + local).astype(bf16)
+    part_other = jnp.zeros_like(part_own)
     low = jnp.where(first_core, part_own, part_other)
     high = jnp.where(first_core, part_other, part_own)
     sent = jnp.concatenate([low, high], axis=1)

time: 142 us -> 164 us (1.15)
  blocking collectives: 36.1 us -> 15.7 us
  matrix products: 20.9 us -> 36.4 us
  starting transfers between devices: 25.2 us -> 38.1 us
  Pallas kernels: 4.79 us -> 10.8 us
  waiting for transfers between devices: 51.8 us -> 55.9 us
  local copies, waits for them, and re-layouts: 1.24 us -> 4.61 us
    all_to_all x2 -> x1, blocking collectives: 36.1 us -> 15.7 us  [on_device(): every = lax.all_to_all(sent, ('row', 'col'), 0, 0)]
    dot_general x24, matrix products: 20.9 us -> 36.4 us  [product(): lax.dot_general(left, right, dims, preferred_element_type=jnp.float32)]
    all_to_all x0 -> x1, starting transfers between devices: none -> 11.5 us  [on_device(): every = lax.all_to_all(sent, ('row', 'col'), 0, 0)]
    pallas_call x0 -> x1, Pallas kernels: none -> 3.76 us  [flipped(): pl.pallas_call(flip_kernel, out_shape=jax.ShapeDtypeStruct((width, rows),...]
    unnamed x14 -> x16, local copies, waits for them, and re-layouts: 0.92 us -> 4.29 us
    all_to_all x0 -> x1, waiting for transfers between devices: none -> 2.67 us  [on_device(): every = lax.all_to_all(sent, ('row', 'col'), 0, 0)]
    ppermute x30 -> x33, starting transfers between devices: 25.2 us -> 26.6 us  [move(): lax.ppermute(array, 'row', [(r, target(r)) for r in range(row_count)])]
    ppermute x30 -> x33, waiting for transfers between devices: 51.8 us -> 53.2 us  [move(): lax.ppermute(array, 'row', [(r, target(r)) for r in range(row_count)])]
  transfers between devices with their start and end apart: 30 -> 34, of which waited for: 25 -> 23; matrix products, arithmetic and copies ran while one was open for 6% -> 16% of each run, Pallas kernels for 3% -> 6%
where the time goes in v11:
time: 164 us; the launch traced here: 163 us
  waiting for transfers between devices  55.9 us (34%)
  starting transfers between devices  38.1 us (23%)
  matrix products  36.4 us (22%)
  blocking collectives  15.7 us (10%)
  Pallas kernels  10.8 us (7%)
  local copies, waits for them, and re-layouts  4.61 us (3%)
    ppermute x33, waiting for transfers between devices, move(): lax.ppermute(array, 'row', [(r, target(r)) for r in range(row_count)])  53.2 us
    dot_general x24, matrix products, product(): lax.dot_general(left, right, dims, preferred_element_type=jnp.float32)  36.4 us
    ppermute x33, starting transfers between devices, move(): lax.ppermute(array, 'row', [(r, target(r)) for r in range(row_count)])  26.6 us
    all_to_all x1, blocking collectives, on_device(): every = lax.all_to_all(sent, ('row', 'col'), 0, 0)  15.7 us
    all_to_all x1, starting transfers between devices, on_device(): every = lax.all_to_all(sent, ('row', 'col'), 0, 0)  11.5 us
    pallas_call x2, Pallas kernels, turned(): pl.pallas_call(turn_kernel, out_shape=jax.ShapeDtypeStruct((width, nodes)...  5.16 us
    unnamed x16, local copies, waits for them, and re-layouts  4.29 us
    pallas_call x1, Pallas kernels, flipped(): pl.pallas_call(flip_kernel, out_shape=jax.ShapeDtypeStruct((width, rows),...  3.76 us
  transfers between devices with their start and end apart: 34, of which 23 were waited for; matrix products, arithmetic and copies ran while one was open for 16% of the time, Pallas kernels for 6%

profile of v11, /device:TPU:1, one launch (start us, length us, event | category | flops | bytes accessed | tf_op | source)
XLA Modules:
  0.0 163.4 jit_solution(18218328848443675968)
XLA Ops:
  1.6 11.5 %all-to-all-start = ((bf16[128,2,512]{2,1,0:T(2,128)(2,1)}), bf16[128,2,512]{2,1,0:T(2,128)(2,1)S(1)}, u32[]{:S(2)}, u32[]{:S(2)}) async-start(bf16[128,2,512]{2,1,0:T(2,128)(2,1)} %bitcast.3), calls=%async_computation | async-start | bytes 524288 | tf_op jit(solution)/shard_map/all_to_all | solution.py:170
  13.1 3.4 %copy-done = bf16[1024,4096]{1,0:T(8,128)(2,1)S(1)} copy-done((bf16[1024,4096]{1,0:T(8,128)(2,1)S(1)}, bf16[1024,4096]{1,0:T(8,128)(2,1)}, u32[]{:S(2)}) %copy-start) | copy-done | bytes 8388632
  16.5 3.4 %shard_map.67 = bf16[2048,1024]{1,0:T(8,128)(2,1)} custom-call(s32[1]{0:T(128)} %bitcast.2.from_ref, bf16[1024,4096]{1,0:T(8,128)(2,1)S(1)} %copy-done), custom_call_target="tpu_custom_call" | custom-call | bytes 8388608 | tf_op jit(solution)/shard_map/pallas_call | solution.py:25
  20.9 2.7 %all-to-all-done = bf16[128,2,512]{2,1,0:T(2,128)(2,1)S(1)} async-done(((bf16[128,2,512]{2,1,0:T(2,128)(2,1)}), bf16[128,2,512]{2,1,0:T(2,128)(2,1)S(1)}, u32[]{:S(2)}, u32[]{:S(2)}) %all-to-all-start) | async-done | bytes 262176 | tf_op jit(solution)/shard_map/all_to_all | solution.py:170
  23.7 3.7 %fusion.26 = f32[32,1024]{1,0:T(8,128)S(1)} fusion(bf16[1024,4096]{1,0:T(8,128)(2,1)} %basis_ref.3, s32[]{:T(128)} %mul.147, bf16[32,4096]{1,0:T(8,128)(2,1)S(1)} %bitcast.119), kind=kOutput, calls=%fused_computation.26 | convolution fusion | flops 134217728 | bytes 4457472 | tf_op jit(solution)/shard_map/dot_general | solution.py:15
  27.4 3.5 %fusion.28 = f32[32,1024]{1,0:T(8,128)S(1)} fusion(f32[32,1024]{1,0:T(8,128)S(1)} %fusion.26, bf16[1024,4096]{1,0:T(8,128)(2,1)} %basis_ref.3, s32[]{:T(128)} %mul.148, bf16[32,4096]{1,0:T(8,128)(2,1)S(1)} %bitcast.120), kind=kOutput, calls=%fused_computation.29 | convolution fusion | flops 134250496 | bytes 4588544 | tf_op jit(solution)/shard_map/dot_general | solution.py:15
  32.0 1.4 collective-permute-start
  34.9 1.8 %shard_map.66 = bf16[2048,1024]{1,0:T(8,128)(2,1)S(1)} custom-call(s32[1]{0:T(128)} %bitcast.1.from_ref, bf16[1024,4096]{1,0:T(8,128)(2,1)S(1)} %copy-done.1), custom_call_target="tpu_custom_call" | custom-call | bytes 8388608 | tf_op jit(solution)/shard_map/pallas_call | solution.py:25
  36.7 2.6 %collective-permute-done.1 = bf16[32,2048]{1,0:T(8,128)(2,1)S(1)} collective-permute-done((bf16[32,2048]{1,0:T(8,128)(2,1)S(1)}, bf16[32,2048]{1,0:T(8,128)(2,1)S(1)}, u32[]{:S(2)}, u32[]{:S(2)}) %collective-permute-start.1) | collective-permute-done | bytes 131104 | tf_op jit(solution)/shard_map/ppermute | solution.py:134
  40.1 2.2 %collective-permute-start.3 = (bf16[32,2048]{1,0:T(8,128)(2,1)S(1)}, bf16[32,2048]{1,0:T(8,128)(2,1)S(1)}, u32[]{:S(2)}, u32[]{:S(2)}) collective-permute-start(bf16[32,2048]{1,0:T(8,128)(2,1)S(1)} %fusion.46), channel_id=1, source_target_pairs={{0,48},{8,56},{16,32},{24,40},{32,16},{40,24},{48,0},{56,8},{64,11... | collective-permute-start | bytes 393224 | tf_op jit(solution)/shard_map/ppermute | solution.py:134
  42.3 1.8 %collective-permute-start.9 = (f32[6,16,1024]{2,1,0:T(8,128)S(1)}, f32[6,16,1024]{2,1,0:T(8,128)S(1)}, u32[]{:S(2)}, u32[]{:S(2)}) collective-permute-start(f32[6,16,1024]{2,1,0:T(8,128)S(1)} %shard_map.65), channel_id=1, source_target_pairs={{0,8},{8,0},{16,24},{24,16},{32,40},{40,32},{48,56},{56,48},{64,72... | collective-permute-start | bytes 1179656 | tf_op jit(solution)/shard_map/ppermute | solution.py:134
  44.8 3.7 %collective-permute-done.3 = bf16[32,2048]{1,0:T(8,128)(2,1)S(1)} collective-permute-done((bf16[32,2048]{1,0:T(8,128)(2,1)S(1)}, bf16[32,2048]{1,0:T(8,128)(2,1)S(1)}, u32[]{:S(2)}, u32[]{:S(2)}) %collective-permute-start.3) | collective-permute-done | bytes 131104 | tf_op jit(solution)/shard_map/ppermute | solution.py:134
  50.8 3.0 %convolution_add_fusion.4 = f32[32,1024]{1,0:T(8,128)S(1)} fusion(f32[32,1024]{1,0:T(8,128)S(1)} %fusion.87, bf16[32,2048]{1,0:T(8,128)(2,1)S(1)} %collective-permute-done.5, bf16[2048,1024]{1,0:T(8,128)(2,1)} %shard_map.67), kind=kOutput, calls=%fused_computation.28 | convolution fusion | flops 134250496 | bytes 4587520 | tf_op jit(solution)/shard_map/dot_general | solution.py:15
  56.6 3.8 %shard_map.68 = bf16[1024,2048]{1,0:T(8,128)(2,1)S(1)} custom-call(bf16[2048,1024]{1,0:T(8,128)(2,1)} %collective-permute-done.8.array_ref), custom_call_target="tpu_custom_call" | custom-call | bytes 8388608 | tf_op jit(solution)/shard_map/pallas_call | solution.py:47
  63.7 2.7 %collective-permute-done.12 = bf16[32,2048]{1,0:T(8,128)(2,1)S(1)} collective-permute-done((bf16[32,2048]{1,0:T(8,128)(2,1)S(1)}, bf16[32,2048]{1,0:T(8,128)(2,1)S(1)}, u32[]{:S(2)}, u32[]{:S(2)}) %collective-permute-start.12) | collective-permute-done | bytes 131104 | tf_op jit(solution)/shard_map/ppermute | solution.py:134
  66.4 3.7 %collective-permute-done.11 = bf16[32,2048]{1,0:T(8,128)(2,1)S(1)} collective-permute-done((bf16[32,2048]{1,0:T(8,128)(2,1)S(1)}, bf16[32,2048]{1,0:T(8,128)(2,1)S(1)}, u32[]{:S(2)}, u32[]{:S(2)}) %collective-permute-start.11) | collective-permute-done | bytes 131104 | tf_op jit(solution)/shard_map/ppermute | solution.py:134
  72.4 3.0 %fusion.89 = f32[32,1024]{1,0:T(8,128)S(1)} fusion(bf16[32,2048]{1,0:T(8,128)(2,1)S(1)} %fusion.33, bf16[2048,1024]{1,0:T(8,128)(2,1)} %collective-permute-done.8.array_ref), kind=kOutput, calls=%fused_computation.155 | convolution fusion | flops 134217728 | bytes 4456448 | tf_op jit(solution)/shard_map/dot_general | solution.py:15
  79.1 4.4 %collective-permute-done.15 = bf16[32,2048]{1,0:T(8,128)(2,1)S(1)} collective-permute-done((bf16[32,2048]{1,0:T(8,128)(2,1)S(1)}, bf16[32,2048]{1,0:T(8,128)(2,1)S(1)}, u32[]{:S(2)}, u32[]{:S(2)}) %collective-permute-start.15) | collective-permute-done | bytes 131104 | tf_op jit(solution)/shard_map/ppermute | solution.py:134
  86.3 2.7 %collective-permute-done.18 = bf16[32,2048]{1,0:T(8,128)(2,1)S(1)} collective-permute-done((bf16[32,2048]{1,0:T(8,128)(2,1)S(1)}, bf16[32,2048]{1,0:T(8,128)(2,1)S(1)}, u32[]{:S(2)}, u32[]{:S(2)}) %collective-permute-start.18) | collective-permute-done | bytes 131104 | tf_op jit(solution)/shard_map/ppermute | solution.py:134
  89.0 4.2 %collective-permute-done.17 = bf16[32,2048]{1,0:T(8,128)(2,1)S(1)} collective-permute-done((bf16[32,2048]{1,0:T(8,128)(2,1)S(1)}, bf16[32,2048]{1,0:T(8,128)(2,1)S(1)}, u32[]{:S(2)}, u32[]{:S(2)}) %collective-permute-start.17) | collective-permute-done | bytes 131104 | tf_op jit(solution)/shard_map/ppermute | solution.py:134
  94.9 3.0 %fusion.91 = f32[32,1024]{1,0:T(8,128)S(1)} fusion(bf16[32,2048]{1,0:T(8,128)(2,1)S(1)} %fusion.35, bf16[2048,1024]{1,0:T(8,128)(2,1)} %collective-permute-done.8.array_ref), kind=kOutput, calls=%fused_computation.157 | convolution fusion | flops 134217728 | bytes 4456448 | tf_op jit(solution)/shard_map/dot_general | solution.py:15
  101.6 4.4 %collective-permute-done.21 = bf16[32,2048]{1,0:T(8,128)(2,1)S(1)} collective-permute-done((bf16[32,2048]{1,0:T(8,128)(2,1)S(1)}, bf16[32,2048]{1,0:T(8,128)(2,1)S(1)}, u32[]{:S(2)}, u32[]{:S(2)}) %collective-permute-start.21) | collective-permute-done | bytes 131104 | tf_op jit(solution)/shard_map/ppermute | solution.py:134
  106.1 1.3 collective-permute-start.24
  108.8 2.7 %collective-permute-done.24 = bf16[32,2048]{1,0:T(8,128)(2,1)S(1)} collective-permute-done((bf16[32,2048]{1,0:T(8,128)(2,1)S(1)}, bf16[32,2048]{1,0:T(8,128)(2,1)S(1)}, u32[]{:S(2)}, u32[]{:S(2)}) %collective-permute-start.24) | collective-permute-done | bytes 131104 | tf_op jit(solution)/shard_map/ppermute | solution.py:134
  111.5 4.2 %collective-permute-done.23 = bf16[32,2048]{1,0:T(8,128)(2,1)S(1)} collective-permute-done((bf16[32,2048]{1,0:T(8,128)(2,1)S(1)}, bf16[32,2048]{1,0:T(8,128)(2,1)S(1)}, u32[]{:S(2)}, u32[]{:S(2)}) %collective-permute-start.23) | collective-permute-done | bytes 131104 | tf_op jit(solution)/shard_map/ppermute | solution.py:134
  117.4 3.0 %fusion.93 = f32[32,1024]{1,0:T(8,128)S(1)} fusion(bf16[32,2048]{1,0:T(8,128)(2,1)S(1)} %fusion.36, bf16[2048,1024]{1,0:T(8,128)(2,1)} %collective-permute-done.8.array_ref), kind=kOutput, calls=%fused_computation.159 | convolution fusion | flops 134217728 | bytes 4456448 | tf_op jit(solution)/shard_map/dot_general | solution.py:15
  124.2 4.4 %collective-permute-done.27 = bf16[32,2048]{1,0:T(8,128)(2,1)S(1)} collective-permute-done((bf16[32,2048]{1,0:T(8,128)(2,1)S(1)}, bf16[32,2048]{1,0:T(8,128)(2,1)S(1)}, u32[]{:S(2)}, u32[]{:S(2)}) %collective-permute-start.27) | collective-permute-done | bytes 131104 | tf_op jit(solution)/shard_map/ppermute | solution.py:134
  128.6 1.5 collective-permute-start.30
  131.6 2.7 %collective-permute-done.30 = bf16[32,2048]{1,0:T(8,128)(2,1)S(1)} collective-permute-done((bf16[32,2048]{1,0:T(8,128)(2,1)S(1)}, bf16[32,2048]{1,0:T(8,128)(2,1)S(1)}, u32[]{:S(2)}, u32[]{:S(2)}) %collective-permute-start.30) | collective-permute-done | bytes 131104 | tf_op jit(solution)/shard_map/ppermute | solution.py:134
  134.3 4.2 %collective-permute-done.29 = bf16[32,2048]{1,0:T(8,128)(2,1)S(1)} collective-permute-done((bf16[32,2048]{1,0:T(8,128)(2,1)S(1)}, bf16[32,2048]{1,0:T(8,128)(2,1)S(1)}, u32[]{:S(2)}, u32[]{:S(2)}) %collective-permute-start.29) | collective-permute-done | bytes 131104 | tf_op jit(solution)/shard_map/ppermute | solution.py:134
  140.2 3.0 %fusion.95 = f32[32,1024]{1,0:T(8,128)S(1)} fusion(bf16[32,2048]{1,0:T(8,128)(2,1)S(1)} %fusion.38, bf16[2048,1024]{1,0:T(8,128)(2,1)} %collective-permute-done.8.array_ref), kind=kOutput, calls=%fused_computation.161 | convolution fusion | flops 134217728 | bytes 4456448 | tf_op jit(solution)/shard_map/dot_general | solution.py:15
  146.8 15.7 %all_to_all.10 = bf16[128,2,512]{2,1,0:T(2,128)(2,1)S(1)} all-to-all(bf16[128,2,512]{2,1,0:T(2,128)(2,1)S(1)} %bitcast.127), channel_id=1, replica_groups=mesh['row'=16,'col'=8] {'row','col'}, dimensions={0} | all-to-all | bytes 524288 | tf_op jit(solution)/shard_map/all_to_all | solution.py:239
  (132 shorter events, 43.6 us)
Async XLA Ops:
  1.6 22.0 %all-to-all-start = ((bf16[128,2,512]{2,1,0:T(2,128)(2,1)}), bf16[128,2,512]{2,1,0:T(2,128)(2,1)S(1)}, u32[]{:S(2)}, u32[]{:S(2)}) async-start(bf16[128,2,512]{2,1,0:T(2,128)(2,1)} %bitcast.3), calls=%async_computation | async-start | bytes 524288 | tf_op jit(solution)/shard_map/all_to_all | solution.py:170
  19.8 36.7 %collective-permute-start.8 = (bf16[2048,1024]{1,0:T(8,128)(2,1)}, bf16[2048,1024]{1,0:T(8,128)(2,1)}, u32[]{:S(2)}, u32[]{:S(2)}) collective-permute-start(bf16[2048,1024]{1,0:T(8,128)(2,1)} %shard_map.67), channel_id=1, source_target_pairs={{0,8},{8,0},{16,24},{24,16},{32,40},{40,32},{48,56},{56,48},{64,72... | collective-permute-start | bytes 12582920 | tf_op jit(solution)/shard_map/ppermute | solution.py:134
  32.0 2.4 %collective-permute-start = (bf16[32,2048]{1,0:T(8,128)(2,1)S(1)}, bf16[32,2048]{1,0:T(8,128)(2,1)S(1)}, u32[]{:S(2)}, u32[]{:S(2)}) collective-permute-start(bf16[32,2048]{1,0:T(8,128)(2,1)S(1)} %fusion.7), channel_id=1, source_target_pairs={{0,8},{8,0},{16,24},{24,16},{32,40},{40,32},{48,56},{56,48},{64,72... | collective-permute-start | bytes 393224 | tf_op jit(solution)/shard_map/ppermute | solution.py:134
  34.5 4.8 %collective-permute-start.1 = (bf16[32,2048]{1,0:T(8,128)(2,1)S(1)}, bf16[32,2048]{1,0:T(8,128)(2,1)S(1)}, u32[]{:S(2)}, u32[]{:S(2)}) collective-permute-start(bf16[32,2048]{1,0:T(8,128)(2,1)S(1)} %fusion.40), channel_id=1, source_target_pairs={{0,64},{8,72},{16,80},{24,88},{32,96},{40,104},{48,112},{56,120},{... | collective-permute-start | bytes 393224 | tf_op jit(solution)/shard_map/ppermute | solution.py:134
  39.3 5.5 %collective-permute-start.4 = (bf16[32,2048]{1,0:T(8,128)(2,1)S(1)}, bf16[32,2048]{1,0:T(8,128)(2,1)S(1)}, u32[]{:S(2)}, u32[]{:S(2)}) collective-permute-start(bf16[32,2048]{1,0:T(8,128)(2,1)S(1)} %fusion.46), channel_id=1, source_target_pairs={{0,32},{8,40},{16,48},{24,56},{32,0},{40,8},{48,16},{56,24},{64,96... | collective-permute-start | bytes 393224 | tf_op jit(solution)/shard_map/ppermute | solution.py:134
  40.1 8.4 %collective-permute-start.3 = (bf16[32,2048]{1,0:T(8,128)(2,1)S(1)}, bf16[32,2048]{1,0:T(8,128)(2,1)S(1)}, u32[]{:S(2)}, u32[]{:S(2)}) collective-permute-start(bf16[32,2048]{1,0:T(8,128)(2,1)S(1)} %fusion.46), channel_id=1, source_target_pairs={{0,48},{8,56},{16,32},{24,40},{32,16},{40,24},{48,0},{56,8},{64,11... | collective-permute-start | bytes 393224 | tf_op jit(solution)/shard_map/ppermute | solution.py:134
  42.3 6.2 %collective-permute-start.2 = (bf16[32,2048]{1,0:T(8,128)(2,1)S(1)}, bf16[32,2048]{1,0:T(8,128)(2,1)S(1)}, u32[]{:S(2)}, u32[]{:S(2)}) collective-permute-start(bf16[32,2048]{1,0:T(8,128)(2,1)S(1)} %fusion.46), channel_id=1, source_target_pairs={{0,16},{8,24},{16,0},{24,8},{32,48},{40,56},{48,32},{56,40},{64,80... | collective-permute-start | bytes 393224 | tf_op jit(solution)/shard_map/ppermute | solution.py:134
  42.3 18.0 %collective-permute-start.9 = (f32[6,16,1024]{2,1,0:T(8,128)S(1)}, f32[6,16,1024]{2,1,0:T(8,128)S(1)}, u32[]{:S(2)}, u32[]{:S(2)}) collective-permute-start(f32[6,16,1024]{2,1,0:T(8,128)S(1)} %shard_map.65), channel_id=1, source_target_pairs={{0,8},{8,0},{16,24},{24,16},{32,40},{40,32},{48,56},{56,48},{64,72... | collective-permute-start | bytes 1179656 | tf_op jit(solution)/shard_map/ppermute | solution.py:134
  48.7 2.1 %collective-permute-start.5 = (bf16[32,2048]{1,0:T(8,128)(2,1)S(1)}, bf16[32,2048]{1,0:T(8,128)(2,1)S(1)}, u32[]{:S(2)}, u32[]{:S(2)}) collective-permute-start(bf16[32,2048]{1,0:T(8,128)(2,1)S(1)} %fusion.32), channel_id=1, source_target_pairs={{0,8},{8,0},{16,24},{24,16},{32,40},{40,32},{48,56},{56,48},{64,72... | collective-permute-start | bytes 393224 | tf_op jit(solution)/shard_map/ppermute | solution.py:134
  54.7 1.4 collective-permute-start.6
  56.1 4.8 %collective-permute-start.7 = (bf16[32,2048]{1,0:T(8,128)(2,1)S(1)}, bf16[32,2048]{1,0:T(8,128)(2,1)S(1)}, u32[]{:S(2)}, u32[]{:S(2)}) collective-permute-start(bf16[32,2048]{1,0:T(8,128)(2,1)S(1)} %fusion.41), channel_id=1, source_target_pairs={{0,64},{8,72},{16,80},{24,88},{32,96},{40,104},{48,112},{56,120},{... | collective-permute-start | bytes 393224 | tf_op jit(solution)/shard_map/ppermute | solution.py:134
  61.0 5.5 %collective-permute-start.12 = (bf16[32,2048]{1,0:T(8,128)(2,1)S(1)}, bf16[32,2048]{1,0:T(8,128)(2,1)S(1)}, u32[]{:S(2)}, u32[]{:S(2)}) collective-permute-start(bf16[32,2048]{1,0:T(8,128)(2,1)S(1)} %fusion.47), channel_id=1, source_target_pairs={{0,32},{8,40},{16,48},{24,56},{32,0},{40,8},{48,16},{56,24},{64,96... | collective-permute-start | bytes 393224 | tf_op jit(solution)/shard_map/ppermute | solution.py:134
  62.3 7.9 %collective-permute-start.11 = (bf16[32,2048]{1,0:T(8,128)(2,1)S(1)}, bf16[32,2048]{1,0:T(8,128)(2,1)S(1)}, u32[]{:S(2)}, u32[]{:S(2)}) collective-permute-start(bf16[32,2048]{1,0:T(8,128)(2,1)S(1)} %fusion.47), channel_id=1, source_target_pairs={{0,48},{8,56},{16,32},{24,40},{32,16},{40,24},{48,0},{56,8},{64,11... | collective-permute-start | bytes 393224 | tf_op jit(solution)/shard_map/ppermute | solution.py:134
  63.1 7.0 %collective-permute-start.10 = (bf16[32,2048]{1,0:T(8,128)(2,1)S(1)}, bf16[32,2048]{1,0:T(8,128)(2,1)S(1)}, u32[]{:S(2)}, u32[]{:S(2)}) collective-permute-start(bf16[32,2048]{1,0:T(8,128)(2,1)S(1)} %fusion.47), channel_id=1, source_target_pairs={{0,16},{8,24},{16,0},{24,8},{32,48},{40,56},{48,32},{56,40},{64,80... | collective-permute-start | bytes 393224 | tf_op jit(solution)/shard_map/ppermute | solution.py:134
  71.2 4.2 %collective-permute-start.14 = (bf16[32,1024]{1,0:T(8,128)(2,1)S(1)}, bf16[32,1024]{1,0:T(8,128)(2,1)S(1)}, u32[]{:S(2)}, u32[]{:S(2)}) collective-permute-start(bf16[32,1024]{1,0:T(8,128)(2,1)S(1)} %convert_element_type.222), channel_id=1, source_target_pairs={{0,8},{8,0},{16,24},{24,16},{32,40},{40,32},{48,56},{56,48},{64,72... | collective-permute-start | bytes 196616 | tf_op jit(solution)/shard_map/ppermute | solution.py:134
  75.4 1.3 collective-permute-start.13
  78.5 5.0 %collective-permute-start.15 = (bf16[32,2048]{1,0:T(8,128)(2,1)S(1)}, bf16[32,2048]{1,0:T(8,128)(2,1)S(1)}, u32[]{:S(2)}, u32[]{:S(2)}) collective-permute-start(bf16[32,2048]{1,0:T(8,128)(2,1)S(1)} %get-tuple-element.59), channel_id=1, source_target_pairs={{0,64},{8,72},{16,80},{24,88},{32,96},{40,104},{48,112},{56,120},{... | collective-permute-start | bytes 393224 | tf_op jit(solution)/shard_map/ppermute | solution.py:134
  83.5 5.5 %collective-permute-start.18 = (bf16[32,2048]{1,0:T(8,128)(2,1)S(1)}, bf16[32,2048]{1,0:T(8,128)(2,1)S(1)}, u32[]{:S(2)}, u32[]{:S(2)}) collective-permute-start(bf16[32,2048]{1,0:T(8,128)(2,1)S(1)} %fusion.42), channel_id=1, source_target_pairs={{0,32},{8,40},{16,48},{24,56},{32,0},{40,8},{48,16},{56,24},{64,96... | collective-permute-start | bytes 393224 | tf_op jit(solution)/shard_map/ppermute | solution.py:134
  84.8 8.3 %collective-permute-start.17 = (bf16[32,2048]{1,0:T(8,128)(2,1)S(1)}, bf16[32,2048]{1,0:T(8,128)(2,1)S(1)}, u32[]{:S(2)}, u32[]{:S(2)}) collective-permute-start(bf16[32,2048]{1,0:T(8,128)(2,1)S(1)} %fusion.42), channel_id=1, source_target_pairs={{0,48},{8,56},{16,32},{24,40},{32,16},{40,24},{48,0},{56,8},{64,11... | collective-permute-start | bytes 393224 | tf_op jit(solution)/shard_map/ppermute | solution.py:134
  85.8 7.4 %collective-permute-start.16 = (bf16[32,2048]{1,0:T(8,128)(2,1)S(1)}, bf16[32,2048]{1,0:T(8,128)(2,1)S(1)}, u32[]{:S(2)}, u32[]{:S(2)}) collective-permute-start(bf16[32,2048]{1,0:T(8,128)(2,1)S(1)} %fusion.42), channel_id=1, source_target_pairs={{0,16},{8,24},{16,0},{24,8},{32,48},{40,56},{48,32},{56,40},{64,80... | collective-permute-start | bytes 393224 | tf_op jit(solution)/shard_map/ppermute | solution.py:134
  94.1 3.8 %collective-permute-start.20 = (bf16[32,1024]{1,0:T(8,128)(2,1)S(1)}, bf16[32,1024]{1,0:T(8,128)(2,1)S(1)}, u32[]{:S(2)}, u32[]{:S(2)}) collective-permute-start(bf16[32,1024]{1,0:T(8,128)(2,1)S(1)} %convert_element_type.233), channel_id=1, source_target_pairs={{0,8},{8,0},{16,24},{24,16},{32,40},{40,32},{48,56},{56,48},{64,72... | collective-permute-start | bytes 196616 | tf_op jit(solution)/shard_map/ppermute | solution.py:134
  101.0 5.0 %collective-permute-start.21 = (bf16[32,2048]{1,0:T(8,128)(2,1)S(1)}, bf16[32,2048]{1,0:T(8,128)(2,1)S(1)}, u32[]{:S(2)}, u32[]{:S(2)}) collective-permute-start(bf16[32,2048]{1,0:T(8,128)(2,1)S(1)} %get-tuple-element.61), channel_id=1, source_target_pairs={{0,64},{8,72},{16,80},{24,88},{32,96},{40,104},{48,112},{56,120},{... | collective-permute-start | bytes 393224 | tf_op jit(solution)/shard_map/ppermute | solution.py:134
  106.1 5.5 %collective-permute-start.24 = (bf16[32,2048]{1,0:T(8,128)(2,1)S(1)}, bf16[32,2048]{1,0:T(8,128)(2,1)S(1)}, u32[]{:S(2)}, u32[]{:S(2)}) collective-permute-start(bf16[32,2048]{1,0:T(8,128)(2,1)S(1)} %fusion.43), channel_id=1, source_target_pairs={{0,32},{8,40},{16,48},{24,56},{32,0},{40,8},{48,16},{56,24},{64,96... | collective-permute-start | bytes 393224 | tf_op jit(solution)/shard_map/ppermute | solution.py:134
  107.4 8.3 %collective-permute-start.23 = (bf16[32,2048]{1,0:T(8,128)(2,1)S(1)}, bf16[32,2048]{1,0:T(8,128)(2,1)S(1)}, u32[]{:S(2)}, u32[]{:S(2)}) collective-permute-start(bf16[32,2048]{1,0:T(8,128)(2,1)S(1)} %fusion.43), channel_id=1, source_target_pairs={{0,48},{8,56},{16,32},{24,40},{32,16},{40,24},{48,0},{56,8},{64,11... | collective-permute-start | bytes 393224 | tf_op jit(solution)/shard_map/ppermute | solution.py:134
  108.3 7.4 %collective-permute-start.22 = (bf16[32,2048]{1,0:T(8,128)(2,1)S(1)}, bf16[32,2048]{1,0:T(8,128)(2,1)S(1)}, u32[]{:S(2)}, u32[]{:S(2)}) collective-permute-start(bf16[32,2048]{1,0:T(8,128)(2,1)S(1)} %fusion.43), channel_id=1, source_target_pairs={{0,16},{8,24},{16,0},{24,8},{32,48},{40,56},{48,32},{56,40},{64,80... | collective-permute-start | bytes 393224 | tf_op jit(solution)/shard_map/ppermute | solution.py:134
  116.7 3.8 %collective-permute-start.26 = (bf16[32,1024]{1,0:T(8,128)(2,1)S(1)}, bf16[32,1024]{1,0:T(8,128)(2,1)S(1)}, u32[]{:S(2)}, u32[]{:S(2)}) collective-permute-start(bf16[32,1024]{1,0:T(8,128)(2,1)S(1)} %convert_element_type.245), channel_id=1, source_target_pairs={{0,8},{8,0},{16,24},{24,16},{32,40},{40,32},{48,56},{56,48},{64,72... | collective-permute-start | bytes 196616 | tf_op jit(solution)/shard_map/ppermute | solution.py:134
  123.6 5.0 %collective-permute-start.27 = (bf16[32,2048]{1,0:T(8,128)(2,1)S(1)}, bf16[32,2048]{1,0:T(8,128)(2,1)S(1)}, u32[]{:S(2)}, u32[]{:S(2)}) collective-permute-start(bf16[32,2048]{1,0:T(8,128)(2,1)S(1)} %get-tuple-element.63), channel_id=1, source_target_pairs={{0,64},{8,72},{16,80},{24,88},{32,96},{40,104},{48,112},{56,120},{... | collective-permute-start | bytes 393224 | tf_op jit(solution)/shard_map/ppermute | solution.py:134
  128.6 5.7 %collective-permute-start.30 = (bf16[32,2048]{1,0:T(8,128)(2,1)S(1)}, bf16[32,2048]{1,0:T(8,128)(2,1)S(1)}, u32[]{:S(2)}, u32[]{:S(2)}) collective-permute-start(bf16[32,2048]{1,0:T(8,128)(2,1)S(1)} %fusion.44), channel_id=1, source_target_pairs={{0,32},{8,40},{16,48},{24,56},{32,0},{40,8},{48,16},{56,24},{64,96... | collective-permute-start | bytes 393224 | tf_op jit(solution)/shard_map/ppermute | solution.py:134
  130.1 8.3 %collective-permute-start.29 = (bf16[32,2048]{1,0:T(8,128)(2,1)S(1)}, bf16[32,2048]{1,0:T(8,128)(2,1)S(1)}, u32[]{:S(2)}, u32[]{:S(2)}) collective-permute-start(bf16[32,2048]{1,0:T(8,128)(2,1)S(1)} %fusion.44), channel_id=1, source_target_pairs={{0,48},{8,56},{16,32},{24,40},{32,16},{40,24},{48,0},{56,8},{64,11... | collective-permute-start | bytes 393224 | tf_op jit(solution)/shard_map/ppermute | solution.py:134
  131.0 7.4 %collective-permute-start.28 = (bf16[32,2048]{1,0:T(8,128)(2,1)S(1)}, bf16[32,2048]{1,0:T(8,128)(2,1)S(1)}, u32[]{:S(2)}, u32[]{:S(2)}) collective-permute-start(bf16[32,2048]{1,0:T(8,128)(2,1)S(1)} %fusion.44), channel_id=1, source_target_pairs={{0,16},{8,24},{16,0},{24,8},{32,48},{40,56},{48,32},{56,40},{64,80... | collective-permute-start | bytes 393224 | tf_op jit(solution)/shard_map/ppermute | solution.py:134
  139.4 3.8 %collective-permute-start.32 = (bf16[32,1024]{1,0:T(8,128)(2,1)S(1)}, bf16[32,1024]{1,0:T(8,128)(2,1)S(1)}, u32[]{:S(2)}, u32[]{:S(2)}) collective-permute-start(bf16[32,1024]{1,0:T(8,128)(2,1)S(1)} %convert_element_type.257), channel_id=1, source_target_pairs={{0,8},{8,0},{16,24},{24,16},{32,40},{40,32},{48,56},{56,48},{64,72... | collective-permute-start | bytes 196616 | tf_op jit(solution)/shard_map/ppermute | solution.py:134
  143.2 1.3 collective-permute-start.31
  (9 other events, 43.9 us)

commit v12 on v10

--- a/solution.py
+++ b/solution.py
@@ -59,7 +59,7 @@
 
 def weights_kernel(coords_ref, quad_ref, turns_ref, weights_ref):
     half_steps, axes, waves = turns_ref.shape
-    rows = weights_ref.shape[1]
+    rows = weights_ref.shape[1] // 2
     shape = (rows, waves)
     lane = lax.broadcasted_iota(jnp.int32, shape, 1)
     wanted = lax.broadcasted_iota(jnp.int32, shape, 0) * (waves // rows)
@@ -72,13 +72,17 @@
             turn = jnp.sum(jnp.where(lane == wanted, line, 0.0), axis=1, keepdims=True)
             term = turn * moments[k : k + 1, :]
             total = term if total is None else total + term
-        weights_ref[a] = total
+        total = -0.5 * total if a % 2 == 0 else total
+        weights_ref[a, :rows] = total
+        weights_ref[a, rows:] = -total
 
 
 def node_weights(coords, quad, turns, row_count):
     return pl.pallas_call(
         weights_kernel,
-        out_shape=jax.ShapeDtypeStruct((turns.shape[0], row_count, coords.shape[1]), coords.dtype),
+        out_shape=jax.ShapeDtypeStruct(
+            (turns.shape[0], 2 * row_count, coords.shape[1]), coords.dtype
+        ),
         compiler_params=pltpu.CompilerParams(vmem_limit_bytes=16 << 20),
     )(coords, quad, turns)
 
@@ -147,31 +151,34 @@
         starts[axis], sizes[axis] = which * width, width
         return lax.dynamic_slice_p.bind(array, *starts, slice_sizes=tuple(sizes))
 
-    rates = half_of(decay_rates, core, 0)[None, :]
     every = lax.all_to_all(sent, ("row", "col"), 0, 0)
     every = every.reshape(row_count, col_count, parts, col_width)
     every = jnp.transpose(every, (2, 0, 1, 3)).reshape(columns, mode_count)
-    every, coords, quad, turns = lax.optimization_barrier(
-        (every, node_coords, quad_weights[None, :], directions)
+    every, coords, quad, turns, decay_rates = lax.optimization_barrier(
+        (every, node_coords, quad_weights[None, :], directions, decay_rates)
     )
     weights = node_weights(coords, quad, turns, row_count)
 
     def mixed(nodes, half_step):
-        factor = 0.5 if half_step % 2 == 0 else 1.0
-        scale = factor * weights[half_step]
-        real, imag = nodes[:row_count], nodes[row_count:]
-        rows = jnp.concatenate([scale * imag, -scale * real], axis=0)
-        return lax.optimization_barrier(rows.astype(bf16))
-
-    field = half_of(every, core, 1)
+        return lax.optimization_barrier((nodes * lax.index_in_dim(weights, half_step, 0, False)).astype(bf16))
+
+    def swapped(array):
+        rows = array.shape[0] // 2
+        return lax.optimization_barrier(jnp.concatenate([array[rows:], array[:rows]], axis=0))
+
+    rates = half_of(decay_rates, core, 0)[None, :]
+    field = lax.optimization_barrier(half_of(every, core, 1))
     basis_own, basis_other = half_of(mode_basis, core, 1), half_of(mode_basis, 1 - core, 1)
 
     kept = lax.optimization_barrier(product(field, basis_own, NT))
     nodes = mixed(kept + product(half_of(every, 1 - core, 1), basis_other, NT), 0)
     sent = product(nodes, basis_other, NN).astype(bf16)
     kept = lax.optimization_barrier(product(nodes, basis_own, NN))
+    total, own_from, other_from = lax.optimization_barrier(
+        (kept + to_other_core(sent).astype(f32), own_from, other_from)
+    )
     turned_own, turned_other = turned(mode_basis, own_from), turned(mode_basis, other_from)
-    sums = over_chips(kept + to_other_core(sent).astype(f32), turned_own)
+    sums = over_chips(total, turned_own)
 
     def weighted(own, other, half_step):
         kept = lax.optimization_barrier(product(own, turned_own, NN))
@@ -185,13 +192,13 @@
     for step in range(STEPS):
         if step > 0:
             sums = summed(weighted(field, to_other_core(field), 2 * step))
-        half = (sums + (1.0 - 0.5 * rates) * field.astype(f32)).astype(bf16)
+        half = (sums + (1.0 - 0.5 * rates) * swapped(field).astype(f32)).astype(bf16)
         nodes = weighted(half, to_other_core(half), 2 * step + 1)
         if step + 1 < STEPS:
-            update = summed(nodes) + (0.0 - 1.0 * rates) * half.astype(f32)
+            update = summed(nodes) + (0.0 - 1.0 * rates) * swapped(half).astype(f32)
             field = (field.astype(f32) + update).astype(bf16)
 
-    local = field.astype(f32) + (0.0 - 1.0 * rates) * half.astype(f32)
+    local = field.astype(f32) + (0.0 - 1.0 * rates) * swapped(half).astype(f32)
     local = jnp.where(first_chip, local, 0.0)
     part_own = (product(nodes, basis_own, NN) + local).astype(bf16)
     part_other = product(nodes, basis_other, NN).astype(bf16)

time: 142 us -> 142 us (level)
  transfers between devices with their start and end apart: 30 -> 30, of which waited for: 25 -> 25; matrix products, arithmetic and copies ran while one was open for 6% -> 5% of each run, Pallas kernels for 3% -> 3%
where the time goes in v12:
time: 142 us
  waiting for transfers between devices  52.4 us (37%)
  blocking collectives  36 us (25%)
  starting transfers between devices  25.2 us (18%)
  matrix products  20.9 us (15%)
  Pallas kernels  4.87 us (3%)
    ppermute x30, waiting for transfers between devices, move(): lax.ppermute(array, 'row', [(r, target(r)) for r in range(row_count)])  52.4 us
    all_to_all x2, blocking collectives, on_device(): every = lax.all_to_all(sent, ('row', 'col'), 0, 0)  36 us
    ppermute x30, starting transfers between devices, move(): lax.ppermute(array, 'row', [(r, target(r)) for r in range(row_count)])  25.2 us
    dot_general x24, matrix products, product(): lax.dot_general(left, right, dims, preferred_element_type=jnp.float32)  20.9 us
    pallas_call x2, Pallas kernels, turned(): pl.pallas_call(turn_kernel, out_shape=jax.ShapeDtypeStruct((width, nodes)...  3.68 us
  transfers between devices with their start and end apart: 30, of which 25 were waited for; matrix products, arithmetic and copies ran while one was open for 5% of the time, Pallas kernels for 3%

profile of v12, /device:TPU:1, one launch (start us, length us, event | category | flops | bytes accessed | tf_op | source)
XLA Modules:
  0.0 142.2 jit_solution(12858287335622407368)
XLA Ops:
  0.9 21.8 %all_to_all.10 = bf16[128,2,512]{2,1,0:T(2,128)(2,1)S(1)} all-to-all(bf16[128,2,512]{2,1,0:T(2,128)(2,1)S(1)} %bitcast.78), channel_id=1, replica_groups=mesh['row'=16,'col'=8] {'row','col'}, dimensions={0} | all-to-all | bytes 524288 | tf_op jit(solution)/shard_map/all_to_all | solution.py:154
  22.8 1.3 fusion.20
  24.4 1.4 fusion.33
  26.6 1.4 collective-permute-start
  29.5 1.8 %shard_map.66 = bf16[2048,1024]{1,0:T(8,128)(2,1)S(1)} custom-call(s32[1]{0:T(128)} %bitcast.1.from_ref, bf16[1024,4096]{1,0:T(8,128)(2,1)S(1)} %copy-done), custom_call_target="tpu_custom_call" | custom-call | bytes 8388608 | tf_op jit(solution)/shard_map/pallas_call | solution.py:25
  31.3 2.5 %collective-permute-done.1 = bf16[32,2048]{1,0:T(8,128)(2,1)S(1)} collective-permute-done((bf16[32,2048]{1,0:T(8,128)(2,1)S(1)}, bf16[32,2048]{1,0:T(8,128)(2,1)S(1)}, u32[]{:S(2)}, u32[]{:S(2)}) %collective-permute-start.1) | collective-permute-done | bytes 131104 | tf_op jit(solution)/shard_map/ppermute | solution.py:119
  34.8 2.1 %collective-permute-start.3 = (bf16[32,2048]{1,0:T(8,128)(2,1)S(1)}, bf16[32,2048]{1,0:T(8,128)(2,1)S(1)}, u32[]{:S(2)}, u32[]{:S(2)}) collective-permute-start(bf16[32,2048]{1,0:T(8,128)(2,1)S(1)} %fusion.41), channel_id=1, source_target_pairs={{0,48},{8,56},{16,32},{24,40},{32,16},{40,24},{48,0},{56,8},{64,11... | collective-permute-start | bytes 393224 | tf_op jit(solution)/shard_map/ppermute | solution.py:119
  36.9 1.8 %shard_map.67 = bf16[2048,1024]{1,0:T(8,128)(2,1)S(1)} custom-call(s32[1]{0:T(128)} %bitcast.2.from_ref, bf16[1024,4096]{1,0:T(8,128)(2,1)S(1)} %copy-done), custom_call_target="tpu_custom_call" | custom-call | bytes 8388608 | tf_op jit(solution)/shard_map/pallas_call | solution.py:25
  39.3 3.7 %collective-permute-done.3 = bf16[32,2048]{1,0:T(8,128)(2,1)S(1)} collective-permute-done((bf16[32,2048]{1,0:T(8,128)(2,1)S(1)}, bf16[32,2048]{1,0:T(8,128)(2,1)S(1)}, u32[]{:S(2)}, u32[]{:S(2)}) %collective-permute-start.3) | collective-permute-done | bytes 131104 | tf_op jit(solution)/shard_map/ppermute | solution.py:119
  43.2 1.2 collective-permute-start.5
  48.9 4.4 %collective-permute-done.7 = bf16[32,2048]{1,0:T(8,128)(2,1)S(1)} collective-permute-done((bf16[32,2048]{1,0:T(8,128)(2,1)S(1)}, bf16[32,2048]{1,0:T(8,128)(2,1)S(1)}, u32[]{:S(2)}, u32[]{:S(2)}) %collective-permute-start.7) | collective-permute-done | bytes 131104 | tf_op jit(solution)/shard_map/ppermute | solution.py:119
  53.3 1.3 collective-permute-start.10
  56.0 2.7 %collective-permute-done.10 = bf16[32,2048]{1,0:T(8,128)(2,1)S(1)} collective-permute-done((bf16[32,2048]{1,0:T(8,128)(2,1)S(1)}, bf16[32,2048]{1,0:T(8,128)(2,1)S(1)}, u32[]{:S(2)}, u32[]{:S(2)}) %collective-permute-start.10) | collective-permute-done | bytes 131104 | tf_op jit(solution)/shard_map/ppermute | solution.py:119
  58.7 3.7 %collective-permute-done.9 = bf16[32,2048]{1,0:T(8,128)(2,1)S(1)} collective-permute-done((bf16[32,2048]{1,0:T(8,128)(2,1)S(1)}, bf16[32,2048]{1,0:T(8,128)(2,1)S(1)}, u32[]{:S(2)}, u32[]{:S(2)}) %collective-permute-start.9) | collective-permute-done | bytes 131104 | tf_op jit(solution)/shard_map/ppermute | solution.py:119
  62.6 1.4 collective-permute-start.11
  68.5 4.4 %collective-permute-done.13 = bf16[32,2048]{1,0:T(8,128)(2,1)S(1)} collective-permute-done((bf16[32,2048]{1,0:T(8,128)(2,1)S(1)}, bf16[32,2048]{1,0:T(8,128)(2,1)S(1)}, u32[]{:S(2)}, u32[]{:S(2)}) %collective-permute-start.13) | collective-permute-done | bytes 131104 | tf_op jit(solution)/shard_map/ppermute | solution.py:119
  72.9 1.3 collective-permute-start.16
  75.6 2.7 %collective-permute-done.16 = bf16[32,2048]{1,0:T(8,128)(2,1)S(1)} collective-permute-done((bf16[32,2048]{1,0:T(8,128)(2,1)S(1)}, bf16[32,2048]{1,0:T(8,128)(2,1)S(1)}, u32[]{:S(2)}, u32[]{:S(2)}) %collective-permute-start.16) | collective-permute-done | bytes 131104 | tf_op jit(solution)/shard_map/ppermute | solution.py:119
  78.3 3.7 %collective-permute-done.15 = bf16[32,2048]{1,0:T(8,128)(2,1)S(1)} collective-permute-done((bf16[32,2048]{1,0:T(8,128)(2,1)S(1)}, bf16[32,2048]{1,0:T(8,128)(2,1)S(1)}, u32[]{:S(2)}, u32[]{:S(2)}) %collective-permute-start.15) | collective-permute-done | bytes 131104 | tf_op jit(solution)/shard_map/ppermute | solution.py:119
  82.2 1.2 collective-permute-start.17
  87.9 4.4 %collective-permute-done.19 = bf16[32,2048]{1,0:T(8,128)(2,1)S(1)} collective-permute-done((bf16[32,2048]{1,0:T(8,128)(2,1)S(1)}, bf16[32,2048]{1,0:T(8,128)(2,1)S(1)}, u32[]{:S(2)}, u32[]{:S(2)}) %collective-permute-start.19) | collective-permute-done | bytes 131104 | tf_op jit(solution)/shard_map/ppermute | solution.py:119
  92.3 1.3 collective-permute-start.22
  95.1 2.7 %collective-permute-done.22 = bf16[32,2048]{1,0:T(8,128)(2,1)S(1)} collective-permute-done((bf16[32,2048]{1,0:T(8,128)(2,1)S(1)}, bf16[32,2048]{1,0:T(8,128)(2,1)S(1)}, u32[]{:S(2)}, u32[]{:S(2)}) %collective-permute-start.22) | collective-permute-done | bytes 131104 | tf_op jit(solution)/shard_map/ppermute | solution.py:119
  97.8 3.7 %collective-permute-done.21 = bf16[32,2048]{1,0:T(8,128)(2,1)S(1)} collective-permute-done((bf16[32,2048]{1,0:T(8,128)(2,1)S(1)}, bf16[32,2048]{1,0:T(8,128)(2,1)S(1)}, u32[]{:S(2)}, u32[]{:S(2)}) %collective-permute-start.21) | collective-permute-done | bytes 131104 | tf_op jit(solution)/shard_map/ppermute | solution.py:119
  101.7 1.2 collective-permute-start.23
  107.4 4.4 %collective-permute-done.25 = bf16[32,2048]{1,0:T(8,128)(2,1)S(1)} collective-permute-done((bf16[32,2048]{1,0:T(8,128)(2,1)S(1)}, bf16[32,2048]{1,0:T(8,128)(2,1)S(1)}, u32[]{:S(2)}, u32[]{:S(2)}) %collective-permute-start.25) | collective-permute-done | bytes 131104 | tf_op jit(solution)/shard_map/ppermute | solution.py:119
  111.8 1.3 collective-permute-start.28
  114.5 2.7 %collective-permute-done.28 = bf16[32,2048]{1,0:T(8,128)(2,1)S(1)} collective-permute-done((bf16[32,2048]{1,0:T(8,128)(2,1)S(1)}, bf16[32,2048]{1,0:T(8,128)(2,1)S(1)}, u32[]{:S(2)}, u32[]{:S(2)}) %collective-permute-start.28) | collective-permute-done | bytes 131104 | tf_op jit(solution)/shard_map/ppermute | solution.py:119
  117.2 3.7 %collective-permute-done.27 = bf16[32,2048]{1,0:T(8,128)(2,1)S(1)} collective-permute-done((bf16[32,2048]{1,0:T(8,128)(2,1)S(1)}, bf16[32,2048]{1,0:T(8,128)(2,1)S(1)}, u32[]{:S(2)}, u32[]{:S(2)}) %collective-permute-start.27) | collective-permute-done | bytes 131104 | tf_op jit(solution)/shard_map/ppermute | solution.py:119
  121.9 1.2 collective-permute-start.29
  123.2 1.0 collective-permute-done.29
  127.1 14.3 %all_to_all.11 = bf16[128,2,512]{2,1,0:T(2,128)(2,1)S(1)} all-to-all(bf16[128,2,512]{2,1,0:T(2,128)(2,1)S(1)} %bitcast.87), channel_id=1, replica_groups=mesh['row'=16,'col'=8] {'row','col'}, dimensions={0} | all-to-all | bytes 524288 | tf_op jit(solution)/shard_map/all_to_all | solution.py:210
  (107 shorter events, 34.3 us)
Async XLA Ops:
  0.8 23.3 %copy-start.1 = (f32[3,1024]{1,0:T(4,128)S(1)}, f32[3,1024]{1,0:T(4,128)}, u32[]{:S(2)}) copy-start(f32[3,1024]{1,0:T(4,128)} %coords_ref) | copy-start | bytes 36868
  0.9 23.3 %copy-start.2 = (f32[6,3,128]{2,1,0:T(4,128)S(1)}, f32[6,3,128]{2,1,0:T(4,128)}, u32[]{:S(2)}) copy-start(f32[6,3,128]{2,1,0:T(4,128)} %turns_ref) | copy-start | bytes 27652
  26.6 2.4 %collective-permute-start = (bf16[32,2048]{1,0:T(8,128)(2,1)S(1)}, bf16[32,2048]{1,0:T(8,128)(2,1)S(1)}, u32[]{:S(2)}, u32[]{:S(2)}) collective-permute-start(bf16[32,2048]{1,0:T(8,128)(2,1)S(1)} %convolution_convert_fusion.5), channel_id=1, source_target_pairs={{0,8},{8,0},{16,24},{24,16},{32,40},{40,32},{48,56},{56,48},{64,72... | collective-permute-start | bytes 393224 | tf_op jit(solution)/shard_map/ppermute | solution.py:119
  29.0 4.8 %collective-permute-start.1 = (bf16[32,2048]{1,0:T(8,128)(2,1)S(1)}, bf16[32,2048]{1,0:T(8,128)(2,1)S(1)}, u32[]{:S(2)}, u32[]{:S(2)}) collective-permute-start(bf16[32,2048]{1,0:T(8,128)(2,1)S(1)} %convert_element_type.190), channel_id=1, source_target_pairs={{0,64},{8,72},{16,80},{24,88},{32,96},{40,104},{48,112},{56,120},{... | collective-permute-start | bytes 393224 | tf_op jit(solution)/shard_map/ppermute | solution.py:119
  33.9 5.5 %collective-permute-start.4 = (bf16[32,2048]{1,0:T(8,128)(2,1)S(1)}, bf16[32,2048]{1,0:T(8,128)(2,1)S(1)}, u32[]{:S(2)}, u32[]{:S(2)}) collective-permute-start(bf16[32,2048]{1,0:T(8,128)(2,1)S(1)} %fusion.41), channel_id=1, source_target_pairs={{0,32},{8,40},{16,48},{24,56},{32,0},{40,8},{48,16},{56,24},{64,96... | collective-permute-start | bytes 393224 | tf_op jit(solution)/shard_map/ppermute | solution.py:119
  34.8 8.3 %collective-permute-start.3 = (bf16[32,2048]{1,0:T(8,128)(2,1)S(1)}, bf16[32,2048]{1,0:T(8,128)(2,1)S(1)}, u32[]{:S(2)}, u32[]{:S(2)}) collective-permute-start(bf16[32,2048]{1,0:T(8,128)(2,1)S(1)} %fusion.41), channel_id=1, source_target_pairs={{0,48},{8,56},{16,32},{24,40},{32,16},{40,24},{48,0},{56,8},{64,11... | collective-permute-start | bytes 393224 | tf_op jit(solution)/shard_map/ppermute | solution.py:119
  36.9 6.2 %collective-permute-start.2 = (bf16[32,2048]{1,0:T(8,128)(2,1)S(1)}, bf16[32,2048]{1,0:T(8,128)(2,1)S(1)}, u32[]{:S(2)}, u32[]{:S(2)}) collective-permute-start(bf16[32,2048]{1,0:T(8,128)(2,1)S(1)} %fusion.41), channel_id=1, source_target_pairs={{0,16},{8,24},{16,0},{24,8},{32,48},{40,56},{48,32},{56,40},{64,80... | collective-permute-start | bytes 393224 | tf_op jit(solution)/shard_map/ppermute | solution.py:119
  43.2 2.1 %collective-permute-start.5 = (bf16[32,2048]{1,0:T(8,128)(2,1)S(1)}, bf16[32,2048]{1,0:T(8,128)(2,1)S(1)}, u32[]{:S(2)}, u32[]{:S(2)}) collective-permute-start(bf16[32,2048]{1,0:T(8,128)(2,1)S(1)} %add_convert_fusion.4), channel_id=1, source_target_pairs={{0,8},{8,0},{16,24},{24,16},{32,40},{40,32},{48,56},{56,48},{64,72... | collective-permute-start | bytes 393224 | tf_op jit(solution)/shard_map/ppermute | solution.py:119
  47.0 1.4 collective-permute-start.6
  48.4 4.8 %collective-permute-start.7 = (bf16[32,2048]{1,0:T(8,128)(2,1)S(1)}, bf16[32,2048]{1,0:T(8,128)(2,1)S(1)}, u32[]{:S(2)}, u32[]{:S(2)}) collective-permute-start(bf16[32,2048]{1,0:T(8,128)(2,1)S(1)} %fusion.42), channel_id=1, source_target_pairs={{0,64},{8,72},{16,80},{24,88},{32,96},{40,104},{48,112},{56,120},{... | collective-permute-start | bytes 393224 | tf_op jit(solution)/shard_map/ppermute | solution.py:119
  53.3 5.5 %collective-permute-start.10 = (bf16[32,2048]{1,0:T(8,128)(2,1)S(1)}, bf16[32,2048]{1,0:T(8,128)(2,1)S(1)}, u32[]{:S(2)}, u32[]{:S(2)}) collective-permute-start(bf16[32,2048]{1,0:T(8,128)(2,1)S(1)} %fusion.47), channel_id=1, source_target_pairs={{0,32},{8,40},{16,48},{24,56},{32,0},{40,8},{48,16},{56,24},{64,96... | collective-permute-start | bytes 393224 | tf_op jit(solution)/shard_map/ppermute | solution.py:119
  54.5 7.9 %collective-permute-start.9 = (bf16[32,2048]{1,0:T(8,128)(2,1)S(1)}, bf16[32,2048]{1,0:T(8,128)(2,1)S(1)}, u32[]{:S(2)}, u32[]{:S(2)}) collective-permute-start(bf16[32,2048]{1,0:T(8,128)(2,1)S(1)} %fusion.47), channel_id=1, source_target_pairs={{0,48},{8,56},{16,32},{24,40},{32,16},{40,24},{48,0},{56,8},{64,11... | collective-permute-start | bytes 393224 | tf_op jit(solution)/shard_map/ppermute | solution.py:119
  55.4 7.0 %collective-permute-start.8 = (bf16[32,2048]{1,0:T(8,128)(2,1)S(1)}, bf16[32,2048]{1,0:T(8,128)(2,1)S(1)}, u32[]{:S(2)}, u32[]{:S(2)}) collective-permute-start(bf16[32,2048]{1,0:T(8,128)(2,1)S(1)} %fusion.47), channel_id=1, source_target_pairs={{0,16},{8,24},{16,0},{24,8},{32,48},{40,56},{48,32},{56,40},{64,80... | collective-permute-start | bytes 393224 | tf_op jit(solution)/shard_map/ppermute | solution.py:119
  62.6 2.4 %collective-permute-start.11 = (bf16[32,2048]{1,0:T(8,128)(2,1)S(1)}, bf16[32,2048]{1,0:T(8,128)(2,1)S(1)}, u32[]{:S(2)}, u32[]{:S(2)}) collective-permute-start(bf16[32,2048]{1,0:T(8,128)(2,1)S(1)} %add_convert_fusion.3), channel_id=1, source_target_pairs={{0,8},{8,0},{16,24},{24,16},{32,40},{40,32},{48,56},{56,48},{64,72... | collective-permute-start | bytes 393224 | tf_op jit(solution)/shard_map/ppermute | solution.py:119
  66.6 1.4 collective-permute-start.12
  68.0 4.8 %collective-permute-start.13 = (bf16[32,2048]{1,0:T(8,128)(2,1)S(1)}, bf16[32,2048]{1,0:T(8,128)(2,1)S(1)}, u32[]{:S(2)}, u32[]{:S(2)}) collective-permute-start(bf16[32,2048]{1,0:T(8,128)(2,1)S(1)} %fusion.43), channel_id=1, source_target_pairs={{0,64},{8,72},{16,80},{24,88},{32,96},{40,104},{48,112},{56,120},{... | collective-permute-start | bytes 393224 | tf_op jit(solution)/shard_map/ppermute | solution.py:119
  72.9 5.5 %collective-permute-start.16 = (bf16[32,2048]{1,0:T(8,128)(2,1)S(1)}, bf16[32,2048]{1,0:T(8,128)(2,1)S(1)}, u32[]{:S(2)}, u32[]{:S(2)}) collective-permute-start(bf16[32,2048]{1,0:T(8,128)(2,1)S(1)} %fusion.48), channel_id=1, source_target_pairs={{0,32},{8,40},{16,48},{24,56},{32,0},{40,8},{48,16},{56,24},{64,96... | collective-permute-start | bytes 393224 | tf_op jit(solution)/shard_map/ppermute | solution.py:119
  74.2 7.9 %collective-permute-start.15 = (bf16[32,2048]{1,0:T(8,128)(2,1)S(1)}, bf16[32,2048]{1,0:T(8,128)(2,1)S(1)}, u32[]{:S(2)}, u32[]{:S(2)}) collective-permute-start(bf16[32,2048]{1,0:T(8,128)(2,1)S(1)} %fusion.48), channel_id=1, source_target_pairs={{0,48},{8,56},{16,32},{24,40},{32,16},{40,24},{48,0},{56,8},{64,11... | collective-permute-start | bytes 393224 | tf_op jit(solution)/shard_map/ppermute | solution.py:119
  75.1 7.0 %collective-permute-start.14 = (bf16[32,2048]{1,0:T(8,128)(2,1)S(1)}, bf16[32,2048]{1,0:T(8,128)(2,1)S(1)}, u32[]{:S(2)}, u32[]{:S(2)}) collective-permute-start(bf16[32,2048]{1,0:T(8,128)(2,1)S(1)} %fusion.48), channel_id=1, source_target_pairs={{0,16},{8,24},{16,0},{24,8},{32,48},{40,56},{48,32},{56,40},{64,80... | collective-permute-start | bytes 393224 | tf_op jit(solution)/shard_map/ppermute | solution.py:119
  82.2 2.2 %collective-permute-start.17 = (bf16[32,2048]{1,0:T(8,128)(2,1)S(1)}, bf16[32,2048]{1,0:T(8,128)(2,1)S(1)}, u32[]{:S(2)}, u32[]{:S(2)}) collective-permute-start(bf16[32,2048]{1,0:T(8,128)(2,1)S(1)} %add_convert_fusion.2), channel_id=1, source_target_pairs={{0,8},{8,0},{16,24},{24,16},{32,40},{40,32},{48,56},{56,48},{64,72... | collective-permute-start | bytes 393224 | tf_op jit(solution)/shard_map/ppermute | solution.py:119
  86.1 1.4 collective-permute-start.18
  87.5 4.8 %collective-permute-start.19 = (bf16[32,2048]{1,0:T(8,128)(2,1)S(1)}, bf16[32,2048]{1,0:T(8,128)(2,1)S(1)}, u32[]{:S(2)}, u32[]{:S(2)}) collective-permute-start(bf16[32,2048]{1,0:T(8,128)(2,1)S(1)} %fusion.44), channel_id=1, source_target_pairs={{0,64},{8,72},{16,80},{24,88},{32,96},{40,104},{48,112},{56,120},{... | collective-permute-start | bytes 393224 | tf_op jit(solution)/shard_map/ppermute | solution.py:119
  92.3 5.5 %collective-permute-start.22 = (bf16[32,2048]{1,0:T(8,128)(2,1)S(1)}, bf16[32,2048]{1,0:T(8,128)(2,1)S(1)}, u32[]{:S(2)}, u32[]{:S(2)}) collective-permute-start(bf16[32,2048]{1,0:T(8,128)(2,1)S(1)} %fusion.49), channel_id=1, source_target_pairs={{0,32},{8,40},{16,48},{24,56},{32,0},{40,8},{48,16},{56,24},{64,96... | collective-permute-start | bytes 393224 | tf_op jit(solution)/shard_map/ppermute | solution.py:119
  93.6 7.9 %collective-permute-start.21 = (bf16[32,2048]{1,0:T(8,128)(2,1)S(1)}, bf16[32,2048]{1,0:T(8,128)(2,1)S(1)}, u32[]{:S(2)}, u32[]{:S(2)}) collective-permute-start(bf16[32,2048]{1,0:T(8,128)(2,1)S(1)} %fusion.49), channel_id=1, source_target_pairs={{0,48},{8,56},{16,32},{24,40},{32,16},{40,24},{48,0},{56,8},{64,11... | collective-permute-start | bytes 393224 | tf_op jit(solution)/shard_map/ppermute | solution.py:119
  94.5 7.0 %collective-permute-start.20 = (bf16[32,2048]{1,0:T(8,128)(2,1)S(1)}, bf16[32,2048]{1,0:T(8,128)(2,1)S(1)}, u32[]{:S(2)}, u32[]{:S(2)}) collective-permute-start(bf16[32,2048]{1,0:T(8,128)(2,1)S(1)} %fusion.49), channel_id=1, source_target_pairs={{0,16},{8,24},{16,0},{24,8},{32,48},{40,56},{48,32},{56,40},{64,80... | collective-permute-start | bytes 393224 | tf_op jit(solution)/shard_map/ppermute | solution.py:119
  101.7 2.2 %collective-permute-start.23 = (bf16[32,2048]{1,0:T(8,128)(2,1)S(1)}, bf16[32,2048]{1,0:T(8,128)(2,1)S(1)}, u32[]{:S(2)}, u32[]{:S(2)}) collective-permute-start(bf16[32,2048]{1,0:T(8,128)(2,1)S(1)} %add_convert_fusion.1), channel_id=1, source_target_pairs={{0,8},{8,0},{16,24},{24,16},{32,40},{40,32},{48,56},{56,48},{64,72... | collective-permute-start | bytes 393224 | tf_op jit(solution)/shard_map/ppermute | solution.py:119
  105.5 1.4 collective-permute-start.24
  106.9 4.8 %collective-permute-start.25 = (bf16[32,2048]{1,0:T(8,128)(2,1)S(1)}, bf16[32,2048]{1,0:T(8,128)(2,1)S(1)}, u32[]{:S(2)}, u32[]{:S(2)}) collective-permute-start(bf16[32,2048]{1,0:T(8,128)(2,1)S(1)} %fusion.45), channel_id=1, source_target_pairs={{0,64},{8,72},{16,80},{24,88},{32,96},{40,104},{48,112},{56,120},{... | collective-permute-start | bytes 393224 | tf_op jit(solution)/shard_map/ppermute | solution.py:119
  111.8 5.5 %collective-permute-start.28 = (bf16[32,2048]{1,0:T(8,128)(2,1)S(1)}, bf16[32,2048]{1,0:T(8,128)(2,1)S(1)}, u32[]{:S(2)}, u32[]{:S(2)}) collective-permute-start(bf16[32,2048]{1,0:T(8,128)(2,1)S(1)} %fusion.50), channel_id=1, source_target_pairs={{0,32},{8,40},{16,48},{24,56},{32,0},{40,8},{48,16},{56,24},{64,96... | collective-permute-start | bytes 393224 | tf_op jit(solution)/shard_map/ppermute | solution.py:119
  113.1 7.9 %collective-permute-start.27 = (bf16[32,2048]{1,0:T(8,128)(2,1)S(1)}, bf16[32,2048]{1,0:T(8,128)(2,1)S(1)}, u32[]{:S(2)}, u32[]{:S(2)}) collective-permute-start(bf16[32,2048]{1,0:T(8,128)(2,1)S(1)} %fusion.50), channel_id=1, source_target_pairs={{0,48},{8,56},{16,32},{24,40},{32,16},{40,24},{48,0},{56,8},{64,11... | collective-permute-start | bytes 393224 | tf_op jit(solution)/shard_map/ppermute | solution.py:119
  114.0 7.0 %collective-permute-start.26 = (bf16[32,2048]{1,0:T(8,128)(2,1)S(1)}, bf16[32,2048]{1,0:T(8,128)(2,1)S(1)}, u32[]{:S(2)}, u32[]{:S(2)}) collective-permute-start(bf16[32,2048]{1,0:T(8,128)(2,1)S(1)} %fusion.50), channel_id=1, source_target_pairs={{0,16},{8,24},{16,0},{24,8},{32,48},{40,56},{48,32},{56,40},{64,80... | collective-permute-start | bytes 393224 | tf_op jit(solution)/shard_map/ppermute | solution.py:119
  121.9 2.2 %collective-permute-start.29 = (bf16[32,2048]{1,0:T(8,128)(2,1)S(1)}, bf16[32,2048]{1,0:T(8,128)(2,1)S(1)}, u32[]{:S(2)}, u32[]{:S(2)}) collective-permute-start(bf16[32,2048]{1,0:T(8,128)(2,1)S(1)} %add_convert_fusion), channel_id=1, source_target_pairs={{0,8},{8,0},{16,24},{24,16},{32,40},{40,32},{48,56},{56,48},{64,72... | collective-permute-start | bytes 393224 | tf_op jit(solution)/shard_map/ppermute | solution.py:119
  (4 other events, 53.6 us)
